TPU v7x, 32 devices: a whole 2x2x4 slice. The times are simulated.
32 devices in a mesh: feat: 4 (over y, x), seq: 4 (over z), dp: 2 (over core).
Axes of the slice: x: 2, y: 2, z: 4, core: 2. Of those that a mesh axis runs over, the one named last changes fastest.
Arguments:
- tokens: bfloat16 [4, 2, 1024, 2048], P('feat', 'dp', 'seq'), may hold values from -6 to 6
- segments: int32 [4, 2, 1024], P(None, 'dp', 'seq'), may hold values from 0 to 3, never falling along the last dimension, each value on 1 to 512 neighbouring positions
- norm1_gain: bfloat16 [2048], P(('feat', 'seq', 'dp')), may hold values from 0.5 to 1.5
- norm2_gain: bfloat16 [2048], P(('feat', 'seq', 'dp')), may hold values from 0.5 to 1.5
- w_query: bfloat16 [2048, 256], P(('feat', 'seq', 'dp')), may hold values from -0.25 to 0.25
- w_key: bfloat16 [2048, 256], P(('feat', 'seq', 'dp')), may hold values from -0.25 to 0.25
- w_value: bfloat16 [2048, 2048], P(('feat', 'seq', 'dp')), may hold values from -0.125 to 0.125
- w_out: bfloat16 [2048, 2048], P(None, ('feat', 'seq', 'dp')), may hold values from -0.375 to 0.375
- w_gate: bfloat16 [2048, 5632], P(('seq', 'dp'), 'feat'), may hold values from -0.125 to 0.125
- w_up: bfloat16 [2048, 5632], P(('seq', 'dp'), 'feat'), may hold values from -0.125 to 0.125
- w_down: bfloat16 [5632, 2048], P('feat', ('seq', 'dp')), may hold values from -0.078125 to 0.078125
- cotangent: bfloat16 [4, 2, 1024, 2048], P('feat', 'dp', 'seq'), may hold values from -6 to 6
Outputs:
- out: bfloat16 [4, 2, 1024, 2048], P('feat', 'dp', 'seq')
- x_grad: float32 [4, 2, 1024, 2048], P('feat', 'dp', 'seq')
- norm1_gain_grad: float32 [2048], P(('feat', 'seq', 'dp'))
- norm2_gain_grad: float32 [2048], P(('feat', 'seq', 'dp'))
- w_query_grad: float32 [2048, 256], P(('feat', 'seq', 'dp'))
- w_key_grad: float32 [2048, 256], P(('feat', 'seq', 'dp'))
- w_value_grad: float32 [2048, 2048], P(('feat', 'seq', 'dp'))
- w_out_grad: float32 [2048, 2048], P(None, ('feat', 'seq', 'dp'))
- w_gate_grad: float32 [2048, 5632], P(('seq', 'dp'), 'feat')
- w_up_grad: float32 [2048, 5632], P(('seq', 'dp'), 'feat')
- w_down_grad: float32 [5632, 2048], P('feat', ('seq', 'dp'))
Inputs may be any that keep to these rules, and one draw needn't show every extreme that they name: `segments`: along each sequence the segment numbers never fall; all 4 numbers occur, each on 1 to 512 tokens, and one on exactly 512.
All inputs are finite; a program needn't handle non-finite values.
Results may differ from a plain program's by a relative error of at most 0.019.
Values may be sent and summed in bfloat16 or wider, within the bound.
A program may use at most 256 MiB of HBM per device.

v0:
```python
import jax
import jax.numpy as jnp
from jax import lax
from jax.sharding import PartitionSpec as P

HEADS = 16
FDIM = 16
HV = 128


exact_mode = lax.Precision.HIGHEST
epsilon = 1e-05
quad_scale = 0.25 / 2.0**0.5


def carried_in(array, axis, join, neutral, backward):
    count = lax.axis_size(axis)
    place = lax.axis_index(axis)
    ahead = count - 1 - place if backward else place
    gathered = jax.tree.map(
        lambda a, kind: lax.all_gather(a.astype(kind), axis),
        array,
        (jnp.bfloat16, jnp.bfloat16, jnp.bfloat16),
    )
    state = jax.tree.map(lambda a, e: jnp.zeros_like(a) + jnp.asarray(e, a.dtype), array, neutral)

    def one(step, state):
        source = count - 1 - step if backward else step
        return join(
            state,
            jax.tree.map(
                lambda a, own: lax.dynamic_index_in_dim(a, source, 0, False).astype(own.dtype),
                gathered,
                array,
            ),
        )

    return lax.fori_loop(0, ahead, one, state)


def rms_norm(values, gain):
    inverse = lax.rsqrt(jnp.mean(values * values, axis=-1, keepdims=True) + epsilon)
    return values * inverse * gain


def gated(gate_in, up_in):
    return jax.nn.silu(gate_in) * up_in


def taylor_part(values, feat_index, rows_each):
    final_axis = values.ndim - 1
    picked = lax.dynamic_slice_in_dim(values, feat_index * rows_each, rows_each, final_axis)
    product_part = picked[..., :, None] * values[..., None, :] * quad_scale
    product_part = product_part.reshape(values.shape[:-1] + (rows_each * values.shape[-1],))
    leading = jnp.where(feat_index == 0, 1.0, 0.0).astype(jnp.float32)
    constant = jnp.zeros(values.shape[:-1] + (1,), jnp.float32) + leading
    return jnp.concatenate([product_part, constant, values * (0.5 * leading)], axis=-1)


def join_states(earlier, later_part):
    state_early, sum_early, mark_early = earlier
    state_late, sum_late, mark_late = later_part
    vacant = mark_late < 0.0
    agrees = mark_late == mark_early

    def select_part(part_early, part_late):
        shape = (1, mark_late.shape[0]) + (1,) * (part_late.ndim - 2)
        kept_early = jnp.where(agrees.reshape(shape), part_early, 0.0)
        return jnp.where(vacant.reshape(shape), part_early, part_late + kept_early)

    return (
        select_part(state_early, state_late),
        select_part(sum_early, sum_late),
        jnp.where(vacant, mark_early, mark_late),
    )


def local(
    tokens,
    segments,
    norm1_gain,
    norm2_gain,
    w_query,
    w_key,
    w_value,
    w_out,
    w_gate,
    w_up,
    w_down,
    cotangent,
):
    feat_index = lax.axis_index("feat")
    rows_each = FDIM // lax.axis_size("feat")
    block_len = tokens.shape[2]
    model_width = tokens.shape[3]
    gain_one, gain_two, query_w, key_w, value_w, out_w = (
        lax.all_gather(norm1_gain, ("feat", "seq", "dp"), axis=0, tiled=True),
        lax.all_gather(norm2_gain, ("feat", "seq", "dp"), axis=0, tiled=True),
        lax.all_gather(w_query, ("feat", "seq", "dp"), axis=0, tiled=True),
        lax.all_gather(w_key, ("feat", "seq", "dp"), axis=0, tiled=True),
        lax.all_gather(w_value, ("feat", "seq", "dp"), axis=0, tiled=True),
        lax.all_gather(w_out, ("feat", "seq", "dp"), axis=1, tiled=True),
    )
    gate_w, up_w, down_w = (
        lax.all_gather(w_gate, ("seq", "dp"), axis=0, tiled=True),
        lax.all_gather(w_up, ("seq", "dp"), axis=0, tiled=True),
        lax.all_gather(w_down, ("seq", "dp"), axis=1, tiled=True),
    )
    inputs = tokens.reshape(block_len, model_width).astype(jnp.float32)
    normed_one, norm_one_pull = jax.vjp(rms_norm, inputs, gain_one.astype(jnp.float32))
    normed_low = normed_one.astype(jnp.bfloat16)
    query_low = jnp.dot(normed_low, query_w, preferred_element_type=jnp.float32).astype(
        jnp.bfloat16
    )
    key_low = jnp.dot(normed_low, key_w, preferred_element_type=jnp.float32).astype(jnp.bfloat16)
    value_low = jnp.dot(normed_low, value_w, preferred_element_type=jnp.float32).astype(
        jnp.bfloat16
    )

    def features_of(entries):
        return taylor_part(entries, feat_index, rows_each)

    query_all, key_all, value_all = (
        lax.all_gather(query_low[None], "feat", axis=0, tiled=True),
        lax.all_gather(key_low[None], "feat", axis=0, tiled=True),
        lax.all_gather(value_low[None], "feat", axis=0, tiled=True),
    )
    seq_count = query_all.shape[0]

    def by_heads(source, per_head):
        return source.reshape(seq_count, block_len, HEADS, per_head).transpose(2, 0, 1, 3)

    query_heads = by_heads(query_all, FDIM)
    key_heads = by_heads(key_all, FDIM)
    value_heads = by_heads(value_all, HV)
    segment = segments.reshape(seq_count, block_len).astype(jnp.float32)
    position = jnp.arange(block_len)
    causal = position[None, :] <= position[:, None]
    allowed = (causal[None] & (segment[:, :, None] == segment[:, None, :])).astype(jnp.float32)
    tail_mark = segment[:, -1]
    head_mark = segment[:, 0]
    tail_mask = (segment == tail_mark[:, None]).astype(jnp.float32)
    lead_mask = (segment == head_mark[:, None]).astype(jnp.float32)

    def key_summary(element):
        key_h, value_h = element
        key_f = features_of(key_h.astype(jnp.float32)) * tail_mask[:, :, None]
        state = jnp.einsum("suf,sue->sfe", key_f, value_h.astype(jnp.float32), precision=exact_mode)
        return (state, jnp.sum(key_f, axis=1))

    tail_states, tail_sums = lax.map(key_summary, (key_heads, value_heads))
    carried, carried_sums, carried_mark = carried_in(
        (tail_states, tail_sums, tail_mark),
        "seq",
        join_states,
        (jnp.zeros_like(tail_states), jnp.zeros_like(tail_sums), jnp.full_like(tail_mark, -1.0)),
        False,
    )
    carry_query = (segment == carried_mark[:, None]).astype(jnp.float32)

    def forward_head(element):
        query_h, key_h, value_h, state_in, sum_in = element
        query_f = features_of(query_h.astype(jnp.float32))
        key_f = features_of(key_h.astype(jnp.float32))
        kernel = jnp.einsum("stf,suf->stu", query_f, key_f, precision=exact_mode) * allowed
        numerator = jnp.einsum(
            "stu,sue->ste", kernel, value_h.astype(jnp.float32), precision=exact_mode
        )
        numerator = numerator + carry_query[:, :, None] * jnp.einsum(
            "stf,sfe->ste", query_f, state_in, precision=exact_mode
        )
        denominator = jnp.sum(kernel, axis=2) + carry_query * jnp.einsum(
            "stf,sf->st", query_f, sum_in, precision=exact_mode
        )
        return (numerator, denominator)

    numer_parts, denom_parts = lax.map(
        forward_head, (query_heads, key_heads, value_heads, carried, carried_sums)
    )
    numer_own, denom_own = (
        lax.psum_scatter(numer_parts, "feat", scatter_dimension=1, tiled=True),
        lax.psum_scatter(denom_parts, "feat", scatter_dimension=1, tiled=True),
    )
    numer_own = numer_own[:, 0]
    denom_own = denom_own[:, 0]
    attended = numer_own / denom_own[:, :, None]
    attended_low = attended.transpose(1, 0, 2).reshape(block_len, HEADS * HV).astype(jnp.bfloat16)
    branch = jnp.dot(attended_low, out_w, preferred_element_type=jnp.float32)
    residual = inputs + branch
    normed_two, norm_two_pull = jax.vjp(rms_norm, residual, gain_two.astype(jnp.float32))
    rows_all, cot_all = (
        lax.all_gather(normed_two.astype(jnp.bfloat16)[None], "feat", axis=0, tiled=True),
        lax.all_gather(cotangent.reshape(1, block_len, model_width), "feat", axis=0, tiled=True),
    )
    rows_all = rows_all.reshape(seq_count * block_len, model_width)
    cot_all = cot_all.reshape(seq_count * block_len, model_width)
    gate_out = jnp.dot(rows_all, gate_w, preferred_element_type=jnp.float32)
    up_out = jnp.dot(rows_all, up_w, preferred_element_type=jnp.float32)
    mixed_value, mix_pull = jax.vjp(gated, gate_out, up_out)
    mixed_low = mixed_value.astype(jnp.bfloat16)
    down_parts = jnp.dot(mixed_low, down_w, preferred_element_type=jnp.float32).reshape(
        seq_count, block_len, model_width
    )
    down_own = lax.psum_scatter(
        down_parts.astype(jnp.bfloat16), "feat", scatter_dimension=0, tiled=True
    ).astype(jnp.float32)[0]
    output = (residual + down_own).astype(jnp.bfloat16).reshape(tokens.shape)
    grad_mixed = jnp.einsum("td,fd->tf", cot_all, down_w, preferred_element_type=jnp.float32)
    grad_gate, grad_up = mix_pull(grad_mixed)
    grad_gate = grad_gate.astype(jnp.bfloat16)
    grad_up = grad_up.astype(jnp.bfloat16)
    row_grads = jnp.einsum(
        "tf,df->td", grad_gate, gate_w, preferred_element_type=jnp.float32
    ) + jnp.einsum("tf,df->td", grad_up, up_w, preferred_element_type=jnp.float32)
    grad_normed_two = lax.psum_scatter(
        row_grads.reshape(seq_count, block_len, model_width).astype(jnp.bfloat16),
        "feat",
        scatter_dimension=0,
        tiled=True,
    ).astype(jnp.float32)[0]
    ffn_grads = lax.psum_scatter(
        jnp.concatenate(
            [
                jnp.einsum("td,tf->df", rows_all, grad_gate, preferred_element_type=jnp.float32),
                jnp.einsum("td,tf->df", rows_all, grad_up, preferred_element_type=jnp.float32),
                jnp.einsum("td,tf->df", cot_all, mixed_low, preferred_element_type=jnp.float32),
            ],
            axis=1,
        ).astype(jnp.bfloat16),
        ("seq", "dp"),
        scatter_dimension=0,
        tiled=True,
    ).astype(jnp.float32)
    hidden = w_gate.shape[1]
    grad_w_gate = ffn_grads[:, :hidden]
    grad_w_up = ffn_grads[:, hidden : 2 * hidden]
    grad_w_down = ffn_grads[:, 2 * hidden :].T
    grad_residual_norm, grad_gain_two = norm_two_pull(grad_normed_two)
    grad_residual = grad_residual_norm + cotangent.reshape(block_len, model_width).astype(
        jnp.float32
    )
    grad_branch = grad_residual.astype(jnp.bfloat16)
    attn_back = (
        lax.all_gather(w_query, ("feat", "seq", "dp"), axis=0, tiled=True),
        lax.all_gather(w_key, ("feat", "seq", "dp"), axis=0, tiled=True),
        lax.all_gather(w_value, ("feat", "seq", "dp"), axis=0, tiled=True),
        lax.all_gather(w_out, ("feat", "seq", "dp"), axis=1, tiled=True),
    )
    query_w, key_w, value_w, out_w = attn_back
    grad_attended = jnp.einsum("td,ed->te", grad_branch, out_w, preferred_element_type=jnp.float32)
    grad_attended = grad_attended.reshape(block_len, HEADS, HV)
    grad_by_head = grad_attended.transpose(1, 0, 2)
    grad_numer = (grad_by_head / denom_own[:, :, None]).astype(jnp.bfloat16)
    grad_denom = (-jnp.sum(grad_by_head * attended, axis=2) / denom_own).astype(jnp.bfloat16)
    numer_grads, denom_grads = (
        lax.all_gather(grad_numer[:, None], "feat", axis=1, tiled=True),
        lax.all_gather(grad_denom[:, None], "feat", axis=1, tiled=True),
    )

    def query_summary(element):
        query_h, numer_h, denom_h = element
        query_f = features_of(query_h.astype(jnp.float32)) * lead_mask[:, :, None]
        state = jnp.einsum(
            "stf,ste->sfe", query_f, numer_h.astype(jnp.float32), precision=exact_mode
        )
        return (
            state,
            jnp.einsum("stf,st->sf", query_f, denom_h.astype(jnp.float32), precision=exact_mode),
        )

    lead_states, lead_sums = lax.map(query_summary, (query_heads, numer_grads, denom_grads))
    back_states, back_sums, back_mark = carried_in(
        (lead_states, lead_sums, head_mark),
        "seq",
        join_states,
        (jnp.zeros_like(lead_states), jnp.zeros_like(lead_sums), jnp.full_like(head_mark, -1.0)),
        True,
    )
    carry_key = (segment == back_mark[:, None]).astype(jnp.float32)

    def backward_head(element):
        query_h, key_h, value_h, state_in, sum_in, numer_h, denom_h, back_in, back_sum = element
        query_f, query_pull = jax.vjp(features_of, query_h.astype(jnp.float32))
        key_f, key_pull = jax.vjp(features_of, key_h.astype(jnp.float32))
        value_f = value_h.astype(jnp.float32)
        numer_f = numer_h.astype(jnp.float32)
        denom_f = denom_h.astype(jnp.float32)
        kernel = jnp.einsum("stf,suf->stu", query_f, key_f, precision=exact_mode) * allowed
        grad_kernel = (
            jnp.einsum("ste,sue->stu", numer_f, value_f, precision=exact_mode) + denom_f[:, :, None]
        ) * allowed
        grad_query_f = jnp.einsum(
            "stu,suf->stf", grad_kernel, key_f, precision=exact_mode
        ) + carry_query[:, :, None] * (
            jnp.einsum("ste,sfe->stf", numer_f, state_in, precision=exact_mode)
            + denom_f[:, :, None] * sum_in[:, None, :]
        )
        grad_key_f = jnp.einsum(
            "stu,stf->suf", grad_kernel, query_f, precision=exact_mode
        ) + carry_key[:, :, None] * (
            jnp.einsum("sue,sfe->suf", value_f, back_in, precision=exact_mode)
            + back_sum[:, None, :]
        )
        grad_value = jnp.einsum("stu,ste->sue", kernel, numer_f, precision=exact_mode) + carry_key[
            :, :, None
        ] * jnp.einsum("suf,sfe->sue", key_f, back_in, precision=exact_mode)
        return (query_pull(grad_query_f)[0], key_pull(grad_key_f)[0], grad_value)

    query_parts, key_parts, value_parts = lax.map(
        backward_head,
        (
            query_heads,
            key_heads,
            value_heads,
            carried,
            carried_sums,
            numer_grads,
            denom_grads,
            back_states,
            back_sums,
        ),
    )
    query_own, key_own, value_own = (
        lax.psum_scatter(
            query_parts.astype(jnp.bfloat16), "feat", scatter_dimension=1, tiled=True
        ).astype(jnp.float32),
        lax.psum_scatter(
            key_parts.astype(jnp.bfloat16), "feat", scatter_dimension=1, tiled=True
        ).astype(jnp.float32),
        lax.psum_scatter(
            value_parts.astype(jnp.bfloat16), "feat", scatter_dimension=1, tiled=True
        ).astype(jnp.float32),
    )

    def by_tokens(source):
        return source[:, 0].transpose(1, 0, 2).reshape(block_len, -1).astype(jnp.bfloat16)

    grad_query = by_tokens(query_own)
    grad_key = by_tokens(key_own)
    grad_value = by_tokens(value_own)
    grad_normed_one = (
        jnp.einsum("tq,dq->td", grad_query, query_w, preferred_element_type=jnp.float32)
        + jnp.einsum("tq,dq->td", grad_key, key_w, preferred_element_type=jnp.float32)
        + jnp.einsum("te,de->td", grad_value, value_w, preferred_element_type=jnp.float32)
    )
    grad_inputs_norm, grad_gain_one = norm_one_pull(grad_normed_one)
    x_grad = (grad_residual + grad_inputs_norm).reshape(tokens.shape)
    weight_terms = (
        grad_gain_one,
        grad_gain_two,
        jnp.einsum("td,tq->dq", normed_low, grad_query, preferred_element_type=jnp.float32),
        jnp.einsum("td,tq->dq", normed_low, grad_key, preferred_element_type=jnp.float32),
        jnp.einsum("td,te->de", normed_low, grad_value, preferred_element_type=jnp.float32),
        jnp.einsum("te,td->ed", attended_low, grad_branch, preferred_element_type=jnp.float32),
    )
    gain_one_grad, gain_two_grad, query_grad, key_grad, value_grad, out_grad = (
        lax.psum_scatter(weight_terms[0], ("feat", "seq", "dp"), scatter_dimension=0, tiled=True),
        lax.psum_scatter(weight_terms[1], ("feat", "seq", "dp"), scatter_dimension=0, tiled=True),
        lax.psum_scatter(weight_terms[2], ("feat", "seq", "dp"), scatter_dimension=0, tiled=True),
        lax.psum_scatter(weight_terms[3], ("feat", "seq", "dp"), scatter_dimension=0, tiled=True),
        lax.psum_scatter(weight_terms[4], ("feat", "seq", "dp"), scatter_dimension=0, tiled=True),
        lax.psum_scatter(weight_terms[5], ("feat", "seq", "dp"), scatter_dimension=1, tiled=True),
    )
    return (
        output,
        x_grad,
        gain_one_grad,
        gain_two_grad,
        query_grad,
        key_grad,
        value_grad,
        out_grad,
        grad_w_gate,
        grad_w_up,
        grad_w_down,
    )


def solution(mesh):
    placed = (
        P("feat", "dp", "seq", None),
        P(None, "dp", "seq"),
        P(("feat", "seq", "dp")),
        P(("feat", "seq", "dp")),
        P(("feat", "seq", "dp"), None),
        P(("feat", "seq", "dp"), None),
        P(("feat", "seq", "dp"), None),
        P(None, ("feat", "seq", "dp")),
        P(("seq", "dp"), "feat"),
        P(("seq", "dp"), "feat"),
        P("feat", ("seq", "dp")),
        P("feat", "dp", "seq", None),
    )
    return jax.shard_map(
        local,
        mesh=mesh,
        in_specs=placed,
        out_specs=(
            P("feat", "dp", "seq", None),
            P("feat", "dp", "seq", None),
            P(("feat", "seq", "dp")),
            P(("feat", "seq", "dp")),
            P(("feat", "seq", "dp"), None),
            P(("feat", "seq", "dp"), None),
            P(("feat", "seq", "dp"), None),
            P(None, ("feat", "seq", "dp")),
            P(("seq", "dp"), "feat"),
            P(("seq", "dp"), "feat"),
            P("feat", ("seq", "dp")),
        ),
        check_vma=False,
    )
```

profile of v0, /device:TPU:0, one launch (start us, length us, event | category | flops | bytes accessed | tf_op | source)
XLA Modules:
  0.0 2654.5 jit_solution(12902337940406795394)
XLA Ops:
  10.4 43.2 %all-reduce.14 = (bf16[2048]{0:T(1024)(128)(2,1)S(1)}, bf16[2048]{0:T(1024)(128)(2,1)S(1)}) all-reduce(bf16[2048]{0:T(1024)(128)(2,1)S(1)} %dynamic-update-slice.8, bf16[2048]{0:T(1024)(128)(2,1)S(1)} %dynamic-update-slice.10), channel_id=1, replica_groups=mesh['feat'=4,'seq'=4,'dp'=2] {'feat','seq','dp'}, use_global_device_ids=true, to_apply=%add | all-reduce | flops 4096 | bytes 16384
  55.2 36.3 %all-gather.30.cloned.1.call-done = bf16[2048,2048]{1,0:T(8,128)(2,1)} async-done(((bf16[64,2048]{1,0:T(8,128)(2,1)}), bf16[2048,2048]{1,0:T(8,128)(2,1)}) %all-gather.30.cloned.1.call-update) | async-done | bytes 8388624 | tf_op jit(solution)/shard_map/all_gather | solution.py:101
  91.6 7.1 convolution_convert_fusion.4
  99.6 47.4 %all-gather.28.cloned.1.call-done = bf16[2048,256]{1,0:T(8,128)(2,1)} async-done(((bf16[64,256]{1,0:T(8,128)(2,1)}), bf16[2048,256]{1,0:T(8,128)(2,1)}) %all-gather.28.cloned.1.call-update) | async-done | bytes 1048592 | tf_op jit(solution)/shard_map/all_gather | solution.py:100
  148.7 10.0 all-gather.1
  160.2 40.9 %all-gather.40.cloned.1.call-done = bf16[1024,2048]{1,0:T(8,128)(2,1)} async-done(((bf16[256,2048]{1,0:T(8,128)(2,1)}), bf16[1024,2048]{1,0:T(8,128)(2,1)}) %all-gather.40.cloned.1.call-update) | async-done | bytes 4194320 | tf_op jit(solution)/shard_map/all_gather | solution.py:126
  208.2 53.1 %while.96 = (s32[]{:T(128)}, bf16[16,4,81,128]{3,1,2,0:T(4,128)(2,1)S(1)}, bf16[16,4,81]{2,1,0:T(4,128)(2,1)S(1)}, bf16[16,4,256,16]{2,3,1,0:T(8,128)(2,1)}, s32...) while((s32[]{:T(128)}, ...), condition=%wide.region_3.4_spmd.clone, body=%wide.region_1.3_spmd.sunk.clone | while | flops 128162496 | bytes 1824477 | solution.py:151
  264.3 12.3 all-reduce.15
  280.7 10.6 all-gather
  292.8 14.7 all-gather.5
  307.5 55.2 %all-gather.42.cloned.1.call-done = bf16[64,4,81,128]{3,1,2,0:T(4,128)(2,1)} async-done(((bf16[16,4,81,128]{3,1,2,0:T(4,128)(2,1)}), bf16[64,4,81,128]{3,1,2,0:T(4,128)(2,1)}) %all-gather.42.cloned.1.call-update) | async-done | bytes 5308432 | tf_op jit(solution)/shard_map/all_gather | solution.py:21
  363.3 203.9 %while.100 = (s32[]{:T(128)}, f32[16,4,256,128]{2,3,0,1:T(8,128)}, f32[16,4,256]{2,0,1:T(8,128)}, bf16[16,4,256,16]{2,3,1,0:T(8,128)(2,1)}, s32[]{:T(128)}, /*in...) while((s32[]{:T(128)}, f32[16,4,256,128]{2,3,0,1:T(8,128)}, ...), condition=%wide.region_8.9_spmd.clone.clone, body=%wide.region_6.8_spmd.clone.sunk.clone | while | flops 788190208 | bytes 9967061 | solution.py:177
  570.2 28.1 %reduce-scatter.39.cloned.1.call-done = f32[16,1,256]{2,0,1:T(8,128)} async-done(((f32[16,4,256]{2,0,1:T(8,128)}), f32[16,1,256]{2,0,1:T(8,128)}) %reduce-scatter.39.cloned.1.call-update) | async-done | bytes 16400
  598.3 89.8 %reduce-scatter.37.cloned.1.call-done = f32[16,1,256,128]{2,3,0,1:T(8,128)} async-done(((f32[16,4,256,128]{2,3,0,1:T(8,128)}), f32[16,1,256,128]{2,3,0,1:T(8,128)}) %reduce-scatter.37.cloned.1.call-update) | async-done | bytes 2097168
  690.9 77.6 %all-gather.32.cloned.1.call-done = bf16[2048,2048]{0,1:T(8,128)(2,1)} async-done(((bf16[2048,64]{0,1:T(8,128)(2,1)}), bf16[2048,2048]{0,1:T(8,128)(2,1)}) %all-gather.32.cloned.1.call-update) | async-done | bytes 8388624 | tf_op jit(solution)/shard_map/all_gather | solution.py:102
  778.4 50.9 %all-gather.34.cloned.1.call-done = bf16[2048,1408]{1,0:T(8,128)(2,1)} async-done(((bf16[256,1408]{1,0:T(8,128)(2,1)}), bf16[2048,1408]{1,0:T(8,128)(2,1)}) %all-gather.34.cloned.1.call-update) | async-done | bytes 5767184 | tf_op jit(solution)/shard_map/all_gather | solution.py:105
  829.2 53.7 %all-gather.44.cloned.1.call-done = bf16[1024,2048]{1,0:T(8,128)(2,1)} async-done(((bf16[256,2048]{1,0:T(8,128)(2,1)}), bf16[1024,2048]{1,0:T(8,128)(2,1)}) %all-gather.44.cloned.1.call-update) | async-done | bytes 4194320 | tf_op jit(solution)/shard_map/all_gather | solution.py:192
  882.9 11.6 fusion.151
  894.6 50.5 %all-gather.36.cloned.1.call-done = bf16[2048,1408]{1,0:T(8,128)(2,1)} async-done(((bf16[256,1408]{1,0:T(8,128)(2,1)}), bf16[2048,1408]{1,0:T(8,128)(2,1)}) %all-gather.36.cloned.1.call-update) | async-done | bytes 5767184 | tf_op jit(solution)/shard_map/all_gather | solution.py:106
  945.0 11.7 fusion.152
  956.7 41.5 %all-gather.46.cloned.1.call-done = bf16[4,1,256,2048]{3,2,1,0:T(8,128)(2,1)} async-done(((bf16[1,1,256,2048]{3,2,1,0:T(8,128)(2,1)}), bf16[4,1,256,2048]{3,2,1,0:T(8,128)(2,1)}) %all-gather.46.cloned.1.call-update) | async-done | bytes 4194320 | tf_op jit(solution)/shard_map/all_gather | solution.py:193
  998.2 62.5 %all-gather.38.cloned.1.call-done = bf16[1408,2048]{1,0:T(8,128)(2,1)} async-done(((bf16[1408,256]{1,0:T(8,128)(2,1)}), bf16[1408,2048]{1,0:T(8,128)(2,1)}) %all-gather.38.cloned.1.call-update) | async-done | bytes 5767184 | tf_op jit(solution)/shard_map/all_gather | solution.py:107
  1060.6 15.6 multiply_convert_fusion
  1076.2 10.9 fusion.153
  1087.1 8.3 add_convert_fusion
  1095.9 11.0 convolution_convert_fusion.3
  1106.9 39.6 %reduce-scatter.43.cloned.1.call-done = bf16[1,256,2048]{2,1,0:T(8,128)(2,1)} async-done(((bf16[4,256,2048]{2,1,0:T(8,128)(2,1)}), bf16[1,256,2048]{2,1,0:T(8,128)(2,1)}) %reduce-scatter.43.cloned.1.call-update) | async-done | bytes 1048592
  1148.4 53.9 %reduce-scatter.41.cloned.1.call-done = bf16[1,256,2048]{2,1,0:T(8,128)(2,1)} async-done(((bf16[4,256,2048]{2,1,0:T(8,128)(2,1)}), bf16[1,256,2048]{2,1,0:T(8,128)(2,1)}) %reduce-scatter.41.cloned.1.call-update) | async-done | bytes 1048592
  1205.7 7.6 fusion.131
  1214.8 8.0 all_gather.104
  1222.9 44.6 %all-gather.48.cloned.1.call-done = bf16[16,1024,128]{1,2,0:T(8,128)(2,1)} async-done(((bf16[16,256,128]{1,2,0:T(8,128)(2,1)}), bf16[16,1024,128]{1,2,0:T(8,128)(2,1)}) %all-gather.48.cloned.1.call-update) | async-done | bytes 4194320 | tf_op jit(solution)/shard_map/all_gather | solution.py:256
  1274.2 55.5 %while.98 = (s32[]{:T(128)}, bf16[16,4,81,128]{3,1,2,0:T(4,128)(2,1)S(1)}, bf16[16,4,81]{2,1,0:T(4,128)(2,1)S(1)}, bf16[16,4,256,16]{2,3,1,0:T(8,128)(2,1)}, s32...) while((s32[]{:T(128)}, ...), condition=%wide.region_17.18_spmd.clone, body=%wide.region_16.17_spmd.sunk.clone | while | flops 129075200 | bytes 1833329 | solution.py:271
  1333.6 13.6 all-gather.11
  1347.2 83.3 %all-gather.50.cloned.1.call-done = bf16[64,4,81,128]{3,1,2,0:T(4,128)(2,1)} async-done(((bf16[16,4,81,128]{3,1,2,0:T(4,128)(2,1)}), bf16[64,4,81,128]{3,1,2,0:T(4,128)(2,1)}) %all-gather.50.cloned.1.call-update) | async-done | bytes 5308432 | tf_op jit(solution)/shard_map/all_gather | solution.py:21
  1430.8 9.3 while.99
  1440.2 276.2 %while.101 = (s32[]{:T(128)}, bf16[16,4,256,16]{2,3,1,0:T(8,128)(2,1)}, bf16[16,4,256,16]{2,3,1,0:T(8,128)(2,1)}, bf16[16,4,256,128]{2,3,0,1:T(8,128)(2,1)}, bf1...) while((s32[]{:T(128)}, ...), condition=%wide.region_25.26_spmd.clone.clone, body=%wide.region_20.25_spmd.clone.sunk.clone | while | flops 1620977664 | bytes 18148720 | solution.py:309
  1717.4 9.1 convolution_convert_fusion.1
  1739.6 7.6 pad_maximum_fusion.11
  1748.5 18.8 all-reduce.19.cloned.1.call-done
  1774.9 9.4 fusion.129
  1784.4 38.5 %reduce-scatter.45.cloned.1.call-done = bf16[16,1,256,128]{2,3,0,1:T(8,128)(2,1)} async-done(((bf16[16,4,256,128]{2,3,0,1:T(8,128)(2,1)}), bf16[16,1,256,128]{2,3,0,1:T(8,128)(2,1)}) %reduce-scatter.45.cloned.1.call-update) | async-done | bytes 1048592
  1823.0 10.1 fusion.139
  1843.0 41.3 %all-reduce.13 = (f32[2048]{0:T(1024)S(1)}, f32[2048]{0:T(1024)S(1)}) all-reduce(f32[2048]{0:T(1024)S(1)} %get-tuple-element.982, f32[2048]{0:T(1024)S(1)} %get-tuple-element.980), channel_id=21, replica_groups=mesh['feat'=4,'seq'=4,'dp'=2] {'feat','seq','dp'}, use_global_device_ids=true, to_apply=%region_31.32.clone | all-reduce | flops 4096 | bytes 32768
  1889.0 110.5 %reduce-scatter.35.cloned.1.call-done = bf16[256,4224]{0,1:T(8,128)(2,1)} async-done(((bf16[2048,4224]{0,1:T(8,128)(2,1)}), bf16[256,4224]{0,1:T(8,128)(2,1)}) %reduce-scatter.35.cloned.1.call-update) | async-done | bytes 2162704 | tf_op jit(solution)/shard_map/reduce_scatter | solution.py:221
  2010.2 128.0 %reduce-scatter.27.cloned.1.call-done = f32[64,256]{1,0:T(8,128)} async-done(((f32[2048,256]{1,0:T(8,128)}), f32[64,256]{1,0:T(8,128)}) %reduce-scatter.27.cloned.1.call-update) | async-done | bytes 65552 | tf_op jit(solution)/shard_map/reduce_scatter | solution.py:359
  2138.2 136.0 %reduce-scatter.29.cloned.1.call-done = f32[64,256]{1,0:T(8,128)} async-done(((f32[2048,256]{1,0:T(8,128)}), f32[64,256]{1,0:T(8,128)}) %reduce-scatter.29.cloned.1.call-update) | async-done | bytes 65552 | tf_op jit(solution)/shard_map/reduce_scatter | solution.py:360
  2274.2 185.8 %reduce-scatter.33.cloned.1.call-done = f32[2048,64]{0,1:T(8,128)} async-done(((f32[2048,2048]{0,1:T(8,128)}), f32[2048,64]{0,1:T(8,128)}) %reduce-scatter.33.cloned.1.call-update) | async-done | bytes 524304 | tf_op jit(solution)/shard_map/reduce_scatter | solution.py:362
  2460.0 187.3 %reduce-scatter.31.cloned.1.call-done = f32[64,2048]{1,0:T(8,128)} async-done(((f32[2048,2048]{1,0:T(8,128)}), f32[64,2048]{1,0:T(8,128)}) %reduce-scatter.31.cloned.1.call-update) | async-done | bytes 524304 | tf_op jit(solution)/shard_map/reduce_scatter | solution.py:361
  (1378 shorter events, 698.9 us)
Async XLA Ops:
  7.2 84.4 %all-gather.30.cloned.1.call-start = ((), (), s32[]{:S(2)}) async-start(), calls=%async_computation.12 | async-start | bytes 8650752 | tf_op jit(solution)/shard_map/all_gather | solution.py:101
  7.9 139.1 %all-gather.28.cloned.1.call-start = ((), (), s32[]{:S(2)}) async-start(), calls=%async_computation.11 | async-start | bytes 1081344 | tf_op jit(solution)/shard_map/all_gather | solution.py:100
  8.7 192.4 %all-gather.40.cloned.1.call-start = ((), (), s32[]{:S(2)}) async-start(), calls=%async_computation.22 | async-start | bytes 5242880 | tf_op jit(solution)/shard_map/all_gather | solution.py:126
  53.7 225.3 %copy-start.14 = (f32[2048]{0:T(1024)}, f32[2048]{0:T(1024)S(1)}, u32[]{:S(2)}) copy-start(f32[2048]{0:T(1024)S(1)} %convert_element_type.380) | copy-start | bytes 24580
  55.2 43.5 %copy-start.23 = (f32[256]{0:T(256)}, f32[256]{0:T(256)S(1)}, u32[]{:S(2)}) copy-start(f32[256]{0:T(256)S(1)} %fusion.117) | copy-start | bytes 3076
  55.2 223.8 %copy-start.21 = (f32[256]{0:T(256)}, f32[256]{0:T(256)S(1)}, u32[]{:S(2)}) copy-start(f32[256]{0:T(256)S(1)} %fusion.137) | copy-start | bytes 3076
  55.2 44.1 %copy-start.20 = (s32[4,1,256]{2,1,0:T(1,128)S(1)}, s32[4,1,256]{2,1,0:T(1,128)}, u32[]{:S(2)}) copy-start(s32[4,1,256]{2,1,0:T(1,128)} %param.25) | copy-start | bytes 12292
  55.2 91.7 %copy-start.1 = (bf16[1,1,256,2048]{3,2,1,0:T(8,128)(2,1)S(1)}, bf16[1,1,256,2048]{3,2,1,0:T(8,128)(2,1)}, u32[]{:S(2)}) copy-start(bf16[1,1,256,2048]{3,2,1,0:T(8,128)(2,1)} %param.24) | copy-start | bytes 3145732
  98.7 180.3 %all-gather.26.cloned.1.call-start = ((), (), s32[]{:S(2)}) async-start(), calls=%async_computation.10 | async-start | bytes 1081344 | tf_op jit(solution)/shard_map/all_gather | solution.py:99
  99.2 263.4 %all-gather.42.cloned.1.call-start = ((), (), s32[]{:S(2)}) async-start(), calls=%async_computation.23 | async-start | bytes 6635520 | tf_op jit(solution)/shard_map/all_gather | solution.py:21
  99.3 60.0 %copy-start.17 = (bf16[16,4,81]{2,1,0:T(4,128)(2,1)}, bf16[16,4,81]{2,1,0:T(4,128)(2,1)S(1)}, u32[]{:S(2)}) copy-start(bf16[16,4,81]{2,1,0:T(4,128)(2,1)S(1)} %fusion.150) | copy-start | bytes 31108
  208.1 54.3 %copy-start.30 = (u32[32]{0:T(128)S(1)}, u32[32]{0:T(128)}, u32[]{:S(2)}) copy-start(u32[32]{0:T(128)} %constant.291) | copy-start | bytes 388
  262.4 336.0 %reduce-scatter.39.cloned.1.call-start = ((), (), s32[]{:S(2)}) async-start(), calls=%async_computation.29 | async-start | bytes 81920
  567.2 120.9 %reduce-scatter.37.cloned.1.call-start = ((), (), s32[]{:S(2)}) async-start(), calls=%async_computation.28 | async-start | bytes 10485760
  568.7 199.8 %all-gather.32.cloned.1.call-start = ((), (), s32[]{:S(2)}) async-start(), calls=%async_computation.13 | async-start | bytes 8650752 | tf_op jit(solution)/shard_map/all_gather | solution.py:102
  568.7 199.8 %copy-start.2 = (bf16[1,1,256,2048]{3,2,1,0:T(8,128)(2,1)S(1)}, bf16[1,1,256,2048]{3,2,1,0:T(8,128)(2,1)}, u32[]{:S(2)}) copy-start(bf16[1,1,256,2048]{3,2,1,0:T(8,128)(2,1)} %param.24) | copy-start | bytes 3145732
  569.5 259.8 %all-gather.34.cloned.1.call-start = ((), (), s32[]{:S(2)}) async-start(), calls=%async_computation.14 | async-start | bytes 6488064 | tf_op jit(solution)/shard_map/all_gather | solution.py:105
  570.2 312.7 %all-gather.44.cloned.1.call-start = ((), (), s32[]{:S(2)}) async-start(), calls=%async_computation.24 | async-start | bytes 5242880 | tf_op jit(solution)/shard_map/all_gather | solution.py:192
  776.1 169.0 %all-gather.36.cloned.1.call-start = ((), (), s32[]{:S(2)}) async-start(), calls=%async_computation.15 | async-start | bytes 6488064 | tf_op jit(solution)/shard_map/all_gather | solution.py:106
  776.8 221.4 %all-gather.46.cloned.1.call-start = ((), (), s32[]{:S(2)}) async-start(), calls=%async_computation.25 | async-start | bytes 5242880 | tf_op jit(solution)/shard_map/all_gather | solution.py:193
  777.4 283.2 %all-gather.38.cloned.1.call-start = ((), (), s32[]{:S(2)}) async-start(), calls=%async_computation.16 | async-start | bytes 6488064 | tf_op jit(solution)/shard_map/all_gather | solution.py:107
  778.1 368.4 %reduce-scatter.43.cloned.1.call-start = ((), (), s32[]{:S(2)}) async-start(), calls=%async_computation.31 | async-start | bytes 5242880
  1076.2 10.9 copy-start.32
  1076.2 10.9 copy-start.34
  1076.2 10.9 copy-start.25
  1095.4 106.9 %reduce-scatter.41.cloned.1.call-start = ((), (), s32[]{:S(2)}) async-start(), calls=%async_computation.30 | async-start | bytes 5242880
  1106.9 95.5 %copy-start.11 = (bf16[1,1,256,2048]{3,2,1,0:T(8,128)(2,1)S(1)}, bf16[1,1,256,2048]{3,2,1,0:T(8,128)(2,1)}, u32[]{:S(2)}) copy-start(bf16[1,1,256,2048]{3,2,1,0:T(8,128)(2,1)} %param.35) | copy-start | bytes 3145732
  1106.9 160.6 %all-gather.48.cloned.1.call-start = ((), (), s32[]{:S(2)}) async-start(), calls=%async_computation.26 | async-start | bytes 5242880 | tf_op jit(solution)/shard_map/all_gather | solution.py:256
  1205.7 7.6 copy-start.5
  1205.7 7.6 copy-start.8
  1205.7 7.6 copy-start.16
  1214.8 215.7 %all-gather.50.cloned.1.call-start = ((), (), s32[]{:S(2)}) async-start(), calls=%async_computation.27 | async-start | bytes 6635520 | tf_op jit(solution)/shard_map/all_gather | solution.py:21
  1222.9 51.3 %copy-start.18 = (bf16[16,4,81]{2,1,0:T(4,128)(2,1)S(1)}, bf16[16,4,81]{2,1,0:T(4,128)(2,1)}, u32[]{:S(2)}) copy-start(bf16[16,4,81]{2,1,0:T(4,128)(2,1)} %copy-done.17) | copy-start | bytes 31108
  1274.2 56.7 %copy-start.29 = (bf16[16]{0:T(256)(128)(2,1)S(1)}, bf16[16]{0:T(256)(128)(2,1)}, u32[]{:S(2)}) copy-start(bf16[16]{0:T(256)(128)(2,1)} %get-tuple-element.1131) | copy-start | bytes 100
  1330.8 436.4 %all-reduce.19.cloned.1.call-start = ((), (), s32[]{:S(2)}) async-start(), calls=%async_computation.33 | async-start | bytes 2097152
  1716.4 106.6 %reduce-scatter.45.cloned.1.call-start = ((), (), s32[]{:S(2)}) async-start(), calls=%async_computation.32 | async-start | bytes 5242880
  1717.1 9.4 copy-start.33
  1717.1 282.4 %reduce-scatter.35.cloned.1.call-start = ((), (), s32[]{:S(2)}) async-start(), calls=%async_computation.21 | async-start | bytes 19464192 | tf_op jit(solution)/shard_map/reduce_scatter | solution.py:221
  1717.4 9.1 copy-start.26
  1726.5 6.6 copy-start.27
  1747.2 21.6 copy-start.3
  1747.2 21.6 copy-start.15
  1747.2 21.6 copy-start.22
  1747.3 390.9 %reduce-scatter.27.cloned.1.call-start = ((), (), s32[]{:S(2)}) async-start(), calls=%async_computation.17 | async-start | bytes 2162688 | tf_op jit(solution)/shard_map/reduce_scatter | solution.py:359
  1770.9 503.3 %reduce-scatter.29.cloned.1.call-start = ((), (), s32[]{:S(2)}) async-start(), calls=%async_computation.18 | async-start | bytes 2162688 | tf_op jit(solution)/shard_map/reduce_scatter | solution.py:360
  1774.6 685.4 %reduce-scatter.33.cloned.1.call-start = ((), (), s32[]{:S(2)}) async-start(), calls=%async_computation.20 | async-start | bytes 17301504 | tf_op jit(solution)/shard_map/reduce_scatter | solution.py:362
  1784.4 862.9 %reduce-scatter.31.cloned.1.call-start = ((), (), s32[]{:S(2)}) async-start(), calls=%async_computation.19 | async-start | bytes 17301504 | tf_op jit(solution)/shard_map/reduce_scatter | solution.py:361
  1840.8 44.8 %copy-start.24 = (f32[256]{0:T(256)S(1)}, f32[256]{0:T(256)}, u32[]{:S(2)}) copy-start(f32[256]{0:T(256)} %copy-done.23) | copy-start | bytes 3076
  (26 other events, 87.4 us)
Sparse Core Ops, SparseCore 0:
  11.0 80.5 all-gather.29
  94.6 52.3 all-gather.27
  149.4 51.6 all-gather.39
  204.0 53.8 all-gather.25
  262.5 100.1 all-gather.41
  567.3 30.9 reduce-scatter.38
  601.7 86.3 reduce-scatter.36
  691.1 77.3 all-gather.31
  770.2 59.0 all-gather.33
  831.5 51.3 all-gather.43
  884.6 60.4 all-gather.35
  946.7 51.3 all-gather.45
  999.7 60.8 all-gather.37
  1095.6 50.9 reduce-scatter.42
  1149.6 52.6 reduce-scatter.40
  1214.9 52.5 all-gather.47
  1331.0 99.4 all-gather.49
  1716.5 50.7 all-reduce.18
  1770.2 52.6 reduce-scatter.44
  1825.3 174.1 reduce-scatter.34
  2002.5 135.6 reduce-scatter.26
  2141.0 133.1 reduce-scatter.28
  2277.2 182.7 reduce-scatter.32
  2462.8 184.3 reduce-scatter.30
where the time goes:
time: 2680 us; the launch traced here: 2650 us
  waiting for transfers between devices  1670 us (62%)
  matrix products  486 us (18%)
  other arithmetic  166 us (6%)
  local copies, waits for them, and re-layouts  158 us (6%)
  blocking collectives  154 us (6%)
    unnamed x30, waiting for transfers between devices  275 us
    reduce_scatter x1, waiting for transfers between devices, local(): lax.psum_scatter(weight_terms[4], ('feat', 'seq', 'dp'), scatter_dimensio...  187 us
    reduce_scatter x1, waiting for transfers between devices, local(): lax.psum_scatter(weight_terms[5], ('feat', 'seq', 'dp'), scatter_dimensio...  186 us
    all_gather x2, waiting for transfers between devices, carried_in(): lax.all_gather(a.astype(kind), axis)  138 us
    reduce_scatter x1, waiting for transfers between devices, local(): lax.psum_scatter(weight_terms[3], ('feat', 'seq', 'dp'), scatter_dimensio...  136 us
    reduce_scatter x1, waiting for transfers between devices, local(): lax.psum_scatter(weight_terms[2], ('feat', 'seq', 'dp'), scatter_dimensio...  128 us
    reduce_scatter x1, waiting for transfers between devices, local(): lax.psum_scatter(jnp.concatenate([jnp.einsum('td,tf->df', rows_all, grad_...  110 us
    unnamed x3, blocking collectives  96.9 us
  transfers between devices with their start and end apart: 24, of which 23 were waited for; matrix products, arithmetic and copies ran while one was open for 8% of the time, Pallas kernels for 0%

commit v1 on v0

v1 whole, which is shorter than its diff:
```python
import functools

import jax
import jax.numpy as jnp
import numpy as np
from jax import lax
from jax.experimental import pallas as pl
from jax.experimental.pallas import tpu as pltpu
from jax.sharding import PartitionSpec as P

HEADS = 16
FDIM = 16
HV = 128
STATE = 160
LANES = 256
epsilon = 1e-05
MESH = pl.DeviceIdType.MESH
ALL = ("feat", "seq", "dp")
f32 = jnp.float32
bf16 = jnp.bfloat16


def dot(a, b):
    return lax.dot_general(a, b, (((1,), (0,)), ((), ())), preferred_element_type=f32)


def dot_nt(a, b):
    return lax.dot_general(a, b, (((1,), (1,)), ((), ())), preferred_element_type=f32)


def dot_tn(a, b):
    return lax.dot_general(a, b, (((0,), (0,)), ((), ())), preferred_element_type=f32)


def feature_tables(heads):
    pairs = [(i, j) for i in range(FDIM) for j in range(i, FDIM)]
    left = np.zeros((heads, heads * FDIM, LANES), np.float32)
    right = np.zeros((heads, heads * FDIM, LANES), np.float32)
    rows = np.zeros((8, LANES), np.float32)
    for h in range(heads):
        for p, (i, j) in enumerate(pairs):
            left[h, h * FDIM + i, p] = 1.0
            right[h, h * FDIM + j, p] = 1.0
            rows[2, p] = 0.25 / 2.0**0.5 if i == j else 0.25
        for i in range(FDIM):
            p = len(pairs) + i
            left[h, h * FDIM + i, p] = 1.0
            rows[1, p] = 1.0
            rows[2, p] = 0.5
        p = len(pairs) + FDIM
        rows[0, p] = rows[1, p] = rows[2, p] = 1.0
    return jnp.asarray(left, bf16), jnp.asarray(right, bf16), jnp.asarray(rows)


def both_sides(entries, h, left_ref, right_ref, rows_ref):
    one = dot(entries, left_ref[h]) + rows_ref[0:1, :]
    two = dot(entries, right_ref[h]) + rows_ref[1:2, :]
    return one, two * rows_ref[2:3, :]


def features(entries, h, left_ref, right_ref, rows_ref):
    one, two = both_sides(entries, h, left_ref, right_ref, rows_ref)
    return one * two


def pull_features(grad, entries, h, left_ref, right_ref, rows_ref):
    one, two = both_sides(entries, h, left_ref, right_ref, rows_ref)
    scaled = rows_ref[2:3, :]
    return dot_nt((grad * two).astype(bf16), left_ref[h]) + dot_nt(
        (grad * one * scaled).astype(bf16), right_ref[h]
    )


def only_head(entries, h):
    lane = lax.broadcasted_iota(jnp.int32, entries.shape, 1)
    keep = (lane >= h * FDIM) & (lane < (h + 1) * FDIM)
    return jnp.where(keep, entries, jnp.zeros_like(entries))


def padded_state(state):
    return jnp.concatenate([state, jnp.zeros((LANES - STATE, state.shape[1]), state.dtype)], 0)


def chain_barrier(place, count):
    barrier = pltpu.get_barrier_semaphore()
    for step in (1, count - 1):
        other = lax.rem(place + step, count)
        pl.semaphore_signal(barrier, inc=1, device_id={"seq": other}, device_id_type=MESH)
    pl.semaphore_wait(barrier, 2)


def allowed_of(segc, segr):
    block = segc.shape[0]
    row = lax.broadcasted_iota(jnp.int32, (block, block), 0)
    col = lax.broadcasted_iota(jnp.int32, (block, block), 1)
    return (row >= col) & (segc == segr)


def forward_kernel(
    count,
    heads,
    qkv_ref,
    segc_ref,
    segr_ref,
    left_ref,
    right_ref,
    rows_ref,
    att_ref,
    rden_ref,
    carry_ref,
    csum_ref,
    send_state,
    send_sum,
    part,
    send_sem,
    recv_sem,
):
    place = lax.axis_index("seq")
    groups, block = qkv_ref.shape[0], qkv_ref.shape[1]
    width = heads * FDIM
    tables = (left_ref, right_ref, rows_ref)

    def hop(g):
        target = {"seq": lax.rem(place + 1, count)}
        return [
            pltpu.make_async_remote_copy(
                src_ref=src.at[g],
                dst_ref=dst.at[g],
                send_sem=send_sem.at[i, g],
                recv_sem=recv_sem.at[i, g],
                device_id=target,
                device_id_type=MESH,
            )
            for i, (src, dst) in enumerate(((send_state, carry_ref), (send_sum, csum_ref)))
        ]

    def send(g):
        for copy in hop(g):
            copy.start()

    chain_barrier(place, count)

    @pl.when(place == 0)
    def _():
        carry_ref[...] = jnp.zeros_like(carry_ref)
        csum_ref[...] = jnp.full_like(csum_ref, -1.0)

    def summarize(g, none):
        segc, segr = segc_ref[g], segr_ref[g]
        tail = segr[:, block - 1 : block]
        at_tail = (segc == tail).astype(f32)
        send_sum[g, heads : heads + 1, :] = jnp.broadcast_to(tail, (1, LANES))
        for h in range(heads):
            key = qkv_ref[g, :, width : 2 * width]
            value = qkv_ref[g, :, 2 * width + h * HV : 2 * width + (h + 1) * HV]
            phi = (features(key, h, *tables) * at_tail).astype(bf16)
            send_state[g, h] = dot_tn(phi, value)[:STATE].astype(bf16)
            ones = jnp.ones((8, block), bf16)
            send_sum[g, h : h + 1, :] = dot(ones, phi)[0:1]

        @pl.when(place == 0)
        def _():
            send(g)

        return none

    lax.fori_loop(0, groups, summarize, 0)

    def attend(g, none):
        segc, segr = segc_ref[g], segr_ref[g]
        allowed = allowed_of(segc, segr)
        for h in range(heads):
            query = only_head(qkv_ref[g, :, 0:width], h)
            key = qkv_ref[g, :, width : 2 * width]
            value = qkv_ref[g, :, 2 * width + h * HV : 2 * width + (h + 1) * HV]
            c = dot_nt(query, key)
            kernel = jnp.where(allowed, 1.0 + c * (0.25 + c * 0.03125), 0.0).astype(bf16)
            wide = jnp.concatenate([value, jnp.ones_like(value)], axis=1)
            part[h] = dot(kernel, wide)

        @pl.when(place > 0)
        def _():
            for copy in hop(g):
                copy.wait_recv()

        mark = csum_ref[g, heads : heads + 1, 0:1]
        head, tail = segr[:, 0:1], segr[:, block - 1 : block]
        whole = ((head == tail) & (head == mark)).astype(f32)

        @pl.when((place > 0) & (place < count - 1))
        def _():
            for h in range(heads):
                send_state[g, h] = (
                    send_state[g, h].astype(f32) + whole * carry_ref[g, h].astype(f32)
                ).astype(bf16)
                send_sum[g, h : h + 1, :] = (
                    send_sum[g, h : h + 1, :] + whole * csum_ref[g, h : h + 1, :]
                )
            send(g)

        carried = (segc == mark).astype(f32)
        for h in range(heads):
            phi = features(qkv_ref[g, :, 0:width], h, *tables) * carried
            state = padded_state(carry_ref[g, h])
            both = part[h]
            numer = both[:, :HV] + dot(phi.astype(bf16), state)
            denom = both[:, HV:] + jnp.sum(
                phi * csum_ref[g, h : h + 1, :], axis=1, keepdims=True
            )
            inverse = 1.0 / denom
            att_ref[g, :, h * HV : (h + 1) * HV] = (numer * inverse).astype(bf16)
            rden_ref[g, :, h * HV : (h + 1) * HV] = inverse
        return none

    lax.fori_loop(0, groups, attend, 0)

    @pl.when(place < count - 1)
    def _():
        def finish(g, none):
            for copy in hop(g):
                copy.wait_send()
            return none

        lax.fori_loop(0, groups, finish, 0)


def backward_kernel(
    count,
    heads,
    qkv_ref,
    segc_ref,
    segr_ref,
    left_ref,
    right_ref,
    rows_ref,
    att_ref,
    rden_ref,
    carry_ref,
    csum_ref,
    ga_ref,
    out_ref,
    gn,
    send_state,
    send_sum,
    recv_state,
    recv_sum,
    dkey,
    dvalue,
    send_sem,
    recv_sem,
):
    place = lax.axis_index("seq")
    groups, block = qkv_ref.shape[0], qkv_ref.shape[1]
    width = heads * FDIM
    tables = (left_ref, right_ref, rows_ref)

    def hop(g):
        target = {"seq": lax.rem(place + count - 1, count)}
        return [
            pltpu.make_async_remote_copy(
                src_ref=src.at[g],
                dst_ref=dst.at[g],
                send_sem=send_sem.at[i, g],
                recv_sem=recv_sem.at[i, g],
                device_id=target,
                device_id_type=MESH,
            )
            for i, (src, dst) in enumerate(((send_state, recv_state), (send_sum, recv_sum)))
        ]

    def send(g):
        for copy in hop(g):
            copy.start()

    chain_barrier(place, count)

    @pl.when(place == count - 1)
    def _():
        recv_state[...] = jnp.zeros_like(recv_state)
        recv_sum[...] = jnp.full_like(recv_sum, -1.0)

    def summarize(g, none):
        segc, segr = segc_ref[g], segr_ref[g]
        head = segr[:, 0:1]
        at_head = (segc == head).astype(f32)
        send_sum[g, heads : heads + 1, :] = jnp.broadcast_to(head, (1, LANES))
        for h in range(heads):
            lanes = slice(h * HV, (h + 1) * HV)
            ga = ga_ref[g, :, lanes]
            inverse = rden_ref[g, :, lanes]
            numer = (ga * inverse).astype(bf16)
            dots = jnp.sum(ga * att_ref[g, :, lanes].astype(f32), axis=1, keepdims=True)
            lane = lax.broadcasted_iota(jnp.int32, (block, HV), 1)
            denom = jnp.where(lane == 0, -dots * inverse, 0.0).astype(bf16)
            gn[g, h, :, :HV] = numer
            gn[g, h, :, HV:] = denom
            phi = (features(qkv_ref[g, :, 0:width], h, *tables) * at_head).astype(bf16)
            send_state[g, h] = dot_tn(phi, numer)[:STATE].astype(bf16)
            send_sum[g, h : h + 1, :] = dot_tn(denom, phi)[0:1]

        @pl.when(place == count - 1)
        def _():
            send(g)

        return none

    lax.fori_loop(0, groups, summarize, 0)

    def pull(g, none):
        segc, segr = segc_ref[g], segr_ref[g]
        allowed = allowed_of(segc, segr)
        query_all = qkv_ref[g, :, 0:width]
        key_all = qkv_ref[g, :, width : 2 * width]
        carried = (segc == csum_ref[g, heads : heads + 1, 0:1]).astype(f32)
        dquery = jnp.zeros((block, width), f32)
        dkey[...] = jnp.zeros_like(dkey)
        for h in range(heads):
            query, key = only_head(query_all, h), only_head(key_all, h)
            value = qkv_ref[g, :, 2 * width + h * HV : 2 * width + (h + 1) * HV]
            wide = jnp.concatenate([value, jnp.ones_like(value)], axis=1)
            both = gn[g, h]
            c = dot_nt(query, key_all)
            kernel = jnp.where(allowed, 1.0 + c * (0.25 + c * 0.03125), 0.0).astype(bf16)
            grad = jnp.where(allowed, dot_nt(both, wide), 0.0)
            grad_c = (grad * (0.25 + c * 0.0625)).astype(bf16)
            dvalue[h] = dot_tn(kernel, both[:, :HV])
            dkey[...] += dot_tn(grad_c, query)
            dquery = dquery + dot(grad_c, key)
            state = padded_state(carry_ref[g, h])
            gphi = dot_nt(both[:, :HV], state) + both[:, HV : HV + 1].astype(f32) * csum_ref[
                g, h : h + 1, :
            ]
            dquery = dquery + pull_features(gphi * carried, query_all, h, *tables)
        out_ref[g, :, 0:width] = dquery.astype(bf16)

        @pl.when(place < count - 1)
        def _():
            for copy in hop(g):
                copy.wait_recv()

        mark = recv_sum[g, heads : heads + 1, 0:1]
        head, tail = segr[:, 0:1], segr[:, block - 1 : block]
        whole = ((head == tail) & (head == mark)).astype(f32)

        @pl.when((place > 0) & (place < count - 1))
        def _():
            for h in range(heads):
                send_state[g, h] = (
                    send_state[g, h].astype(f32) + whole * recv_state[g, h].astype(f32)
                ).astype(bf16)
                send_sum[g, h : h + 1, :] = (
                    send_sum[g, h : h + 1, :] + whole * recv_sum[g, h : h + 1, :]
                )
            send(g)

        later = (segc == mark).astype(f32)
        total = dkey[...]
        for h in range(heads):
            value = qkv_ref[g, :, 2 * width + h * HV : 2 * width + (h + 1) * HV]
            state = padded_state(recv_state[g, h])
            phi = (features(key_all, h, *tables) * later).astype(bf16)
            dv = dvalue[h] + dot(phi, state)
            out_ref[g, :, 2 * width + h * HV : 2 * width + (h + 1) * HV] = dv.astype(bf16)
            gphi = (dot_nt(value, state) + recv_sum[g, h : h + 1, :]) * later
            total = total + pull_features(gphi, key_all, h, *tables)
        out_ref[g, :, width : 2 * width] = total.astype(bf16)
        return none

    lax.fori_loop(0, groups, pull, 0)

    @pl.when(place > 0)
    def _():
        def finish(g, none):
            for copy in hop(g):
                copy.wait_send()
            return none

        lax.fori_loop(0, groups, finish, 0)


def whole_vmem(count):
    return [pl.BlockSpec(memory_space=pltpu.VMEM)] * count


def attention_forward(qkv, segc, segr, tables, heads):
    groups, block, _ = qkv.shape
    count = lax.axis_size("seq")
    states = (groups, heads, STATE, HV)
    sums = (groups, 8, LANES)
    return pl.pallas_call(
        functools.partial(forward_kernel, count, heads),
        out_shape=(
            jax.ShapeDtypeStruct((groups, block, heads * HV), bf16),
            jax.ShapeDtypeStruct((groups, block, heads * HV), f32),
            jax.ShapeDtypeStruct(states, bf16),
            jax.ShapeDtypeStruct(sums, f32),
        ),
        in_specs=whole_vmem(6),
        out_specs=tuple(whole_vmem(4)),
        scratch_shapes=[
            pltpu.VMEM(states, bf16),
            pltpu.VMEM(sums, f32),
            pltpu.VMEM((heads, block, 2 * HV), f32),
            pltpu.SemaphoreType.DMA((2, groups)),
            pltpu.SemaphoreType.DMA((2, groups)),
        ],
        compiler_params=pltpu.CompilerParams(
            collective_id=0, has_side_effects=True, vmem_limit_bytes=40 << 20
        ),
        name="attention_forward",
    )(qkv, segc, segr, *tables)


def attention_backward(qkv, segc, segr, tables, att, rden, carry, csum, ga, heads):
    groups, block, wide = qkv.shape
    count = lax.axis_size("seq")
    states = (groups, heads, STATE, HV)
    sums = (groups, 8, LANES)
    return pl.pallas_call(
        functools.partial(backward_kernel, count, heads),
        out_shape=jax.ShapeDtypeStruct((groups, block, wide), bf16),
        in_specs=whole_vmem(11),
        out_specs=whole_vmem(1)[0],
        scratch_shapes=[
            pltpu.VMEM((groups, heads, block, 2 * HV), bf16),
            pltpu.VMEM(states, bf16),
            pltpu.VMEM(sums, f32),
            pltpu.VMEM(states, bf16),
            pltpu.VMEM(sums, f32),
            pltpu.VMEM((block, heads * FDIM), f32),
            pltpu.VMEM((heads, block, HV), f32),
            pltpu.SemaphoreType.DMA((2, groups)),
            pltpu.SemaphoreType.DMA((2, groups)),
        ],
        compiler_params=pltpu.CompilerParams(
            collective_id=1, has_side_effects=True, vmem_limit_bytes=48 << 20
        ),
        name="attention_backward",
    )(qkv, segc, segr, *tables, att, rden, carry, csum, ga)


def inverse_rms(values):
    return lax.rsqrt(jnp.mean(values * values, axis=-1, keepdims=True) + epsilon)


def norm_back(grad, unit, inverse, gain):
    scaled = grad * gain
    return (scaled - unit * jnp.mean(scaled * unit, axis=-1, keepdims=True)) * inverse


def local(
    tokens,
    segments,
    norm1_gain,
    norm2_gain,
    w_query,
    w_key,
    w_value,
    w_out,
    w_gate,
    w_up,
    w_down,
    cotangent,
):
    parts = lax.axis_size("feat")
    heads = HEADS // parts
    block, width = tokens.shape[2], tokens.shape[3]
    rows_total = parts * block
    rows_each = w_query.shape[0]
    own = tokens.reshape(block, width)
    cot_own = cotangent.reshape(block, width)

    def by_share(w, per):
        return w.reshape(rows_each, parts, heads * per).transpose(1, 0, 2)

    pack = jnp.concatenate(
        [by_share(w_query, FDIM), by_share(w_key, FDIM), by_share(w_value, HV), by_share(w_out.T, HV)],
        axis=2,
    )
    pack_width = pack.shape[2]
    pack = lax.all_to_all(pack, "feat", 0, 0, tiled=True)
    pack = lax.all_gather(pack, ("seq", "dp"), axis=1, tiled=True)
    attn_w = pack.reshape(width, pack_width)
    qkv_width = pack_width - heads * HV
    qkv_w, out_w = attn_w[:, :qkv_width], attn_w[:, qkv_width:]
    gains = lax.all_gather(jnp.stack([norm1_gain, norm2_gain]), ALL, axis=1, tiled=True).astype(f32)
    gain_one, gain_two = gains[0], gains[1]

    x_all = lax.all_gather(own, "feat", axis=0, tiled=True)
    gate_w = lax.all_gather(w_gate, ("seq", "dp"), axis=0, tiled=True)
    up_w = lax.all_gather(w_up, ("seq", "dp"), axis=0, tiled=True)
    down_w = lax.all_gather(w_down.T, ("seq", "dp"), axis=0, tiled=True)
    cot_all = lax.all_gather(cot_own, "feat", axis=0, tiled=True)

    x_wide = x_all.astype(f32)
    normed = (x_wide * inverse_rms(x_wide) * gain_one).astype(bf16)
    qkv = dot(normed, qkv_w).astype(bf16).reshape(parts, block, qkv_width)
    segment = segments.reshape(parts, block).astype(f32)
    segc, segr = segment[:, :, None], segment[:, None, :]
    tables = feature_tables(heads)
    att, rden, carry, csum = attention_forward(qkv, segc, segr, tables, heads)
    att_rows = att.reshape(rows_total, heads * HV)
    branch = lax.psum_scatter(
        dot_nt(att_rows, out_w).astype(bf16), "feat", scatter_dimension=0, tiled=True
    )
    inputs = own.astype(f32)
    residual = inputs + branch.astype(f32)
    inverse_two = inverse_rms(residual)
    unit_two = residual * inverse_two
    rows_all = lax.all_gather((unit_two * gain_two).astype(bf16), "feat", axis=0, tiled=True)

    gate_out = dot(rows_all, gate_w)
    up_out = dot(rows_all, up_w)
    sig = jax.nn.sigmoid(gate_out)
    silu = gate_out * sig
    mixed = (silu * up_out).astype(bf16)
    down_own = lax.psum_scatter(
        dot_nt(mixed, down_w).astype(bf16), "feat", scatter_dimension=0, tiled=True
    )
    output = (residual + down_own.astype(f32)).astype(bf16).reshape(tokens.shape)
    grad_mixed = dot(cot_all, down_w)
    grad_gate = (grad_mixed * up_out * sig * (1.0 + gate_out * (1.0 - sig))).astype(bf16)
    grad_up = (grad_mixed * silu).astype(bf16)
    row_grads = dot_nt(grad_gate, gate_w) + dot_nt(grad_up, up_w)
    grad_normed_two = lax.psum_scatter(
        row_grads.astype(bf16), "feat", scatter_dimension=0, tiled=True
    ).astype(f32)

    def summed(term):
        return lax.psum_scatter(
            term.astype(bf16), ("seq", "dp"), scatter_dimension=0, tiled=True
        ).astype(f32)

    grad_w_down = summed(dot_tn(cot_all, mixed)).T
    grad_w_gate = summed(dot_tn(rows_all, grad_gate))
    grad_w_up = summed(dot_tn(rows_all, grad_up))

    gain_two_part = jnp.sum(grad_normed_two * unit_two, axis=0)
    grad_residual = cot_own.astype(f32) + norm_back(grad_normed_two, unit_two, inverse_two, gain_two)
    branch_all = lax.all_gather(grad_residual.astype(bf16), "feat", axis=0, tiled=True)
    ga = dot(branch_all, out_w).reshape(parts, block, heads * HV)
    dqkv = attention_backward(qkv, segc, segr, tables, att, rden, carry, csum, ga, heads)
    dqkv = dqkv.reshape(rows_total, qkv_width)
    grad_normed_one = lax.psum_scatter(
        dot_nt(dqkv, qkv_w).astype(bf16), "feat", scatter_dimension=0, tiled=True
    ).astype(f32)
    inverse_one = inverse_rms(inputs)
    unit_one = inputs * inverse_one
    x_grad = grad_residual + norm_back(grad_normed_one, unit_one, inverse_one, gain_one)
    gain_one_part = jnp.sum(grad_normed_one * unit_one, axis=0)

    attn_grads = jnp.concatenate([dot_tn(normed, dqkv), dot_tn(branch_all, att_rows)], axis=1)
    attn_grads = attn_grads.astype(bf16).reshape(parts, width // parts, pack_width)
    attn_grads = lax.psum_scatter(attn_grads, ("seq", "dp"), scatter_dimension=1, tiled=True)
    attn_grads = lax.all_to_all(attn_grads, "feat", 0, 0, tiled=True).astype(f32)

    def from_share(first, per):
        piece = attn_grads[:, :, first : first + heads * per]
        return piece.transpose(1, 0, 2).reshape(rows_each, HEADS * per)

    start_value = 2 * heads * FDIM
    query_grad = from_share(0, FDIM)
    key_grad = from_share(heads * FDIM, FDIM)
    value_grad = from_share(start_value, HV)
    out_grad = from_share(start_value + heads * HV, HV).T
    gain_grads = lax.psum_scatter(
        jnp.stack([gain_one_part, gain_two_part]), ALL, scatter_dimension=1, tiled=True
    )
    return (
        output,
        x_grad.reshape(tokens.shape),
        gain_grads[0],
        gain_grads[1],
        query_grad,
        key_grad,
        value_grad,
        out_grad,
        grad_w_gate,
        grad_w_up,
        grad_w_down,
    )


def solution(mesh):
    placed = (
        P("feat", "dp", "seq", None),
        P(None, "dp", "seq"),
        P(ALL),
        P(ALL),
        P(ALL, None),
        P(ALL, None),
        P(ALL, None),
        P(None, ALL),
        P(("seq", "dp"), "feat"),
        P(("seq", "dp"), "feat"),
        P("feat", ("seq", "dp")),
        P("feat", "dp", "seq", None),
    )
    return jax.shard_map(
        local,
        mesh=mesh,
        in_specs=placed,
        out_specs=(
            P("feat", "dp", "seq", None),
            P("feat", "dp", "seq", None),
            P(ALL),
            P(ALL),
            P(ALL, None),
            P(ALL, None),
            P(ALL, None),
            P(None, ALL),
            P(("seq", "dp"), "feat"),
            P(("seq", "dp"), "feat"),
            P("feat", ("seq", "dp")),
        ),
        check_vma=False,
    )
```

time: 2680 us -> 1200 us (0.45)
  waiting for transfers between devices: 1670 us -> 817 us
  matrix products: 486 us -> 133 us
  other arithmetic: 166 us -> 36.5 us
  local copies, waits for them, and re-layouts: 158 us -> 38.3 us
  blocking collectives: 154 us -> 59.7 us
  Pallas kernels: 0 us -> 84.9 us
    reduce_scatter x5 -> x8, waiting for transfers between devices: 748 us -> 354 us  [the longest x3 82.5 us: summed(): lax.psum_scatter(term.astype(bf16), ('seq', 'dp'), scatter_dimension=0, t...]
    dot_general x260 -> x15, matrix products: 478 us -> 133 us  [the longest x5 50 us: dot(): lax.dot_general(a, b, (((1,), (0,)), ((), ())), preferred_element_type=f32)]
    all_gather x13 -> x8, waiting for transfers between devices: 644 us -> 329 us  [the longest x1 62.5 us: local(): down_w = lax.all_gather(w_down.T, ('seq', 'dp'), axis=0, tiled=True)]
    unnamed x30 -> x18, waiting for transfers between devices: 275 us -> 135 us
    dynamic_update_slice x192 -> x0, local copies, waits for them, and re-layouts: 104 us -> none  [the longest x96 82.2 us: local(): lax.map(forward_head, (query_heads, key_heads, value_heads, carried, carr...]
    unnamed x3 -> x0, blocking collectives: 96.9 us -> none
    pallas_call x0 -> x2, Pallas kernels: none -> 84.9 us  [the longest x1 67.3 us: attention_backward(): pl.pallas_call(functools.partial(backward_kernel, count, heads), out_shap...]
    mul x208 -> x0, other arithmetic: 65.4 us -> none  [the longest x64 49.8 us: taylor_part(): values * (0.5 * leading)]
  transfers between devices with their start and end apart: 24 -> 18, of which waited for: 23 -> 15; matrix products, arithmetic and copies ran while one was open for 8% -> 12% of each run, Pallas kernels for 0% -> 6%
where the time goes in v1:
time: 1200 us; the launch traced here: 1190 us
  waiting for transfers between devices  817 us (68%)
  matrix products  133 us (11%)
  Pallas kernels  84.9 us (7%)
  blocking collectives  59.7 us (5%)
  local copies, waits for them, and re-layouts  38.3 us (3%)
  other arithmetic  36.5 us (3%)
  between operations  14.7 us (1%)
    unnamed x18, waiting for transfers between devices  135 us
    reduce_scatter x3, waiting for transfers between devices, summed(): lax.psum_scatter(term.astype(bf16), ('seq', 'dp'), scatter_dimension=0, t...  82.5 us
    pallas_call x1, Pallas kernels, attention_backward(): pl.pallas_call(functools.partial(backward_kernel, count, heads), out_shap...  67.3 us
    reduce_scatter x1, waiting for transfers between devices, local(): lax.psum_scatter(dot_nt(att_rows, out_w).astype(bf16), 'feat', scatter_di...  64.3 us
    all_gather x1, waiting for transfers between devices, local(): down_w = lax.all_gather(w_down.T, ('seq', 'dp'), axis=0, tiled=True)  62.5 us
    all_gather x1, waiting for transfers between devices, local(): up_w = lax.all_gather(w_up, ('seq', 'dp'), axis=0, tiled=True)  55.2 us
    all_gather x1, waiting for transfers between devices, local(): lax.all_gather((unit_two * gain_two).astype(bf16), 'feat', axis=0, tiled=...  53.8 us
    reduce_scatter x1, waiting for transfers between devices, local(): lax.psum_scatter(attn_grads, ('seq', 'dp'), scatter_dimension=1, tiled=True)  53.7 us
  transfers between devices with their start and end apart: 18, of which 15 were waited for; matrix products, arithmetic and copies ran while one was open for 12% of the time, Pallas kernels for 6%

profile of v1, /device:TPU:0, one launch (start us, length us, event | category | flops | bytes accessed | tf_op | source)
XLA Modules:
  0.0 1188.9 jit_solution(17093903954518308671)
XLA Ops:
  13.7 19.7 %all_to_all.10 = bf16[4,64,1152]{2,1,0:T(8,128)(2,1)S(1)} all-to-all(bf16[4,64,1152]{2,1,0:T(8,128)(2,1)S(1)} %copy.70), channel_id=1, replica_groups=mesh['feat'=4,'seq'=4,'dp'=2] {'feat'}, dimensions={0} | all-to-all | bytes 1179648 | tf_op jit(solution)/shard_map/all_to_all | solution.py:481
  34.7 40.0 %all-gather.2 = bf16[32,64,2]{1,2,0:T(2,128)(2,1)S(1)} all-gather(bf16[1,64,2]{1,2,0:T(2,128)(2,1)S(1)} %maximum_bitcast_fusion), channel_id=1, replica_groups=mesh['feat'=4,'seq'=4,'dp'=2] {'feat','seq','dp'}, dimensions={0}, use_global_device_ids=true | all-gather | bytes 8448 | tf_op jit(solution)/shard_map/all_gather | solution.py:486
  75.1 3.1 fusion
  78.2 45.1 %all-gather.12.cloned.1.call-done = bf16[4,512,1152]{2,0,1:T(4,128)(2,1)} async-done(((bf16[4,64,1152]{2,0,1:T(4,128)(2,1)}), bf16[4,512,1152]{2,0,1:T(4,128)(2,1)}) %all-gather.12.cloned.1.call-update) | async-done | bytes 4718608 | tf_op jit(solution)/shard_map/all_gather | solution.py:482
  123.3 3.1 copy.72
  126.9 3.5 fusion.31
  130.5 17.6 %attention_forward.1 = (bf16[4,256,512]{2,1,0:T(8,128)(2,1)S(1)}, f32[4,256,512]{2,1,0:T(8,128)S(1)}, bf16[4,4,160,128]{3,2,1,0:T(8,128)(2,1)S(1)}, f32[4,8,256]{2,1,0:T(8,128)S(1)}) custom-call(bf16[4,256,640]{2,1,0:T(8,128)(2,1)S(1)} %bitcast.121, f32[4,256,1]{2,1,0:T(8,128)S(1)} %copy.73.segc_ref, f32[4,1,256]{2,1,0:T(1,128)S(1)} %get-tuple-element.37.segr_ref, ...), custom_call_target="tpu_custom_call" | custom-call | tf_op jit(solution)/shard_map/attention_forward/pallas_call | solution.py:390
  150.2 4.3 convolution_convert_fusion.5
  156.2 64.3 %reduce-scatter.12.cloned.1.call-done = bf16[256,2048]{1,0:T(8,128)(2,1)} async-done(((bf16[1024,2048]{1,0:T(8,128)(2,1)}), bf16[256,2048]{1,0:T(8,128)(2,1)}) %reduce-scatter.12.cloned.1.call-update) | async-done | bytes 1048592 | tf_op jit(solution)/shard_map/reduce_scatter | solution.py:503
  222.2 2.6 multiply_convert_fusion.3
  227.4 55.2 %all-gather.18.cloned.1.call-done = bf16[2048,1408]{1,0:T(8,128)(2,1)} async-done(((bf16[256,1408]{1,0:T(8,128)(2,1)}), bf16[2048,1408]{1,0:T(8,128)(2,1)}) %all-gather.18.cloned.1.call-update) | async-done | bytes 5767184 | tf_op jit(solution)/shard_map/all_gather | solution.py:491
  282.6 53.8 %all-gather.14.cloned.1.call-done = bf16[1024,2048]{1,0:T(8,128)(2,1)} async-done(((bf16[256,2048]{1,0:T(8,128)(2,1)}), bf16[1024,2048]{1,0:T(8,128)(2,1)}) %all-gather.14.cloned.1.call-update) | async-done | bytes 4194320 | tf_op jit(solution)/shard_map/all_gather | solution.py:510
  336.4 11.7 fusion.42
  348.1 50.4 %all-gather.16.cloned.1.call-done = bf16[2048,1408]{1,0:T(8,128)(2,1)} async-done(((bf16[256,1408]{1,0:T(8,128)(2,1)}), bf16[2048,1408]{1,0:T(8,128)(2,1)}) %all-gather.16.cloned.1.call-update) | async-done | bytes 5767184 | tf_op jit(solution)/shard_map/all_gather | solution.py:490
  398.4 11.7 fusion.41
  410.2 41.7 %all-gather.26.cloned.1.call-done = bf16[1,1,1024,2048]{3,2,1,0:T(8,128)(2,1)} async-done(((bf16[1,1,256,2048]{3,2,1,0:T(8,128)(2,1)}), bf16[1,1,1024,2048]{3,2,1,0:T(8,128)(2,1)}) %all-gather.26.cloned.1.call-update) | async-done | bytes 4194320 | tf_op jit(solution)/shard_map/all_gather | solution.py:493
  451.9 62.5 %all-gather.20.cloned.1.call-done = bf16[2048,1408]{0,1:T(8,128)(2,1)} async-done(((bf16[256,1408]{0,1:T(8,128)(2,1)}), bf16[2048,1408]{0,1:T(8,128)(2,1)}) %all-gather.20.cloned.1.call-update) | async-done | bytes 5767184 | tf_op jit(solution)/shard_map/all_gather | solution.py:492
  514.4 16.6 %multiply_convert_fusion = (bf16[1024,1408]{1,0:T(8,128)(2,1)}, bf16[1024,1408]{1,0:T(8,128)(2,1)}, bf16[1024,1408]{1,0:T(8,128)(2,1)}) fusion(f32[1024,1408]{1,0:T(8,128)} %fusion.41, f32[1024,1408]{1,0:T(8,128)} %fusion.42, bf16[2048,1408]{0,1:T(8,128)(2,1)} %all-gather.20.cloned.1.call-done, bf16[1,1,1024,2048]{3,2,1,0:T(8,128)(2,1)} %all-gather.26.cloned.1.call-done), kind=kOutput, calls=%fused_computation.10 | convolution fusion | flops 5927206912 | bytes 30146560 | tf_op jit(solution)/shard_map/dot_general | solution.py:24
  531.1 8.6 fusion.43
  539.7 11.1 add_convert_fusion
  550.8 51.0 %reduce-scatter.16.cloned.1.call-done = bf16[256,2048]{1,0:T(8,128)(2,1)} async-done(((bf16[1024,2048]{1,0:T(8,128)(2,1)}), bf16[256,2048]{1,0:T(8,128)(2,1)}) %reduce-scatter.16.cloned.1.call-update) | async-done | bytes 1048592 | tf_op jit(solution)/shard_map/reduce_scatter | solution.py:525
  601.8 2.7 fusion.23
  604.5 3.8 fusion.37
  608.4 11.0 convolution_convert_fusion.1
  619.5 11.0 convolution_convert_fusion.2
  630.5 10.7 fusion.3
  641.3 20.0 %all-gather.22.cloned.1.call-done = bf16[1024,2048]{1,0:T(8,128)(2,1)} async-done(((bf16[256,2048]{1,0:T(8,128)(2,1)}), bf16[1024,2048]{1,0:T(8,128)(2,1)}) %all-gather.22.cloned.1.call-update) | async-done | bytes 4194320 | tf_op jit(solution)/shard_map/all_gather | solution.py:540
  661.3 6.5 fusion.28
  670.1 67.3 %attention_backward.1 = bf16[4,256,640]{2,1,0:T(8,128)(2,1)S(1)} custom-call(bf16[4,256,640]{2,1,0:T(8,128)(2,1)S(1)} %bitcast.122, f32[4,256,1]{2,1,0:T(8,128)S(1)} %copy.73.segc_ref, f32[4,1,256]{2,1,0:T(1,128)S(1)} %get-tuple-element.37.segr_ref, bf16[4,64,256]{2,1,0:T(8,128)(2,1)S(1)} %copy-done.7, bf16[4,64,256]{2,1,0:T(8,128)(2,1)S(1)} %copy-done.6, ...), custom_call_target="tpu_custom_call" | custom-call | tf_op jit(solution)/shard_map/attention_backward/pallas_call | solution.py:419
  737.5 6.8 convolution_convert_fusion.3
  744.4 5.2 fusion.34
  749.5 6.7 copy.85
  756.2 6.5 copy.86
  762.7 4.8 convolution_convert_fusion.7
  767.5 3.6 convolution_convert_fusion.6
  771.1 2.7 pad_maximum_fusion
  775.6 11.0 convolution_convert_fusion.4
  786.7 2.4 convert_element_type.124
  789.1 19.3 %reduce-scatter.22.cloned.1.call-done = bf16[256,1408]{1,0:T(8,128)(2,1)} async-done(((bf16[2048,1408]{1,0:T(8,128)(2,1)}), bf16[256,1408]{1,0:T(8,128)(2,1)}) %reduce-scatter.22.cloned.1.call-update) | async-done | bytes 720912 | tf_op jit(solution)/shard_map/reduce_scatter | solution.py:530
  808.4 2.3 convert_element_type.122
  810.7 63.2 %reduce-scatter.26.cloned.1.call-done = bf16[256,1408]{0,1:T(8,128)(2,1)} async-done(((bf16[2048,1408]{0,1:T(8,128)(2,1)}), bf16[256,1408]{0,1:T(8,128)(2,1)}) %reduce-scatter.26.cloned.1.call-update) | async-done | bytes 720912 | tf_op jit(solution)/shard_map/reduce_scatter | solution.py:530
  874.0 2.3 convert_bitcast_fusion
  876.3 51.6 %reduce-scatter.18.cloned.1.call-done = bf16[256,2048]{1,0:T(8,128)(2,1)} async-done(((bf16[1024,2048]{1,0:T(8,128)(2,1)}), bf16[256,2048]{1,0:T(8,128)(2,1)}) %reduce-scatter.18.cloned.1.call-update) | async-done | bytes 1048592 | tf_op jit(solution)/shard_map/reduce_scatter | solution.py:544
  931.4 53.7 %reduce-scatter.20.cloned.1.call-done = bf16[4,64,1152]{2,1,0:T(8,128)(2,1)} async-done(((bf16[4,512,1152]{2,1,0:T(8,128)(2,1)}), bf16[4,64,1152]{2,1,0:T(8,128)(2,1)}) %reduce-scatter.20.cloned.1.call-update) | async-done | bytes 589840 | tf_op jit(solution)/shard_map/reduce_scatter | solution.py:554
  985.1 3.6 all-to-all-start.1
  988.8 50.6 %reduce-scatter.14.cloned.1.call-done = bf16[256,2048]{1,0:T(8,128)(2,1)} async-done(((bf16[1024,2048]{1,0:T(8,128)(2,1)}), bf16[256,2048]{1,0:T(8,128)(2,1)}) %reduce-scatter.14.cloned.1.call-update) | async-done | bytes 1048592 | tf_op jit(solution)/shard_map/reduce_scatter | solution.py:517
  1039.3 5.6 fusion.19
  1044.9 131.3 %reduce-scatter.28.cloned.1.call-done = f32[64,2]{1,0:T(8,128)} async-done(((f32[2048,2]{1,0:T(8,128)}), f32[64,2]{1,0:T(8,128)}) %reduce-scatter.28.cloned.1.call-update) | async-done | bytes 528
  (113 shorter events, 30.5 us)
Async XLA Ops:
  7.2 27.5 %copy-start.17 = (bf16[64]{0:T(256)(128)(2,1)S(1)}, bf16[64]{0:T(256)(128)(2,1)}, u32[]{:S(2)}) copy-start(bf16[64]{0:T(256)(128)(2,1)} %param.18) | copy-start | bytes 388
  7.2 27.5 %copy-start.18 = (bf16[64]{0:T(256)(128)(2,1)S(1)}, bf16[64]{0:T(256)(128)(2,1)}, u32[]{:S(2)}) copy-start(bf16[64]{0:T(256)(128)(2,1)} %param.17) | copy-start | bytes 388
  7.2 67.6 %copy-start.15 = (s32[4,1,256]{2,1,0:T(1,128)S(1)}, s32[4,1,256]{2,1,0:T(1,128)}, u32[]{:S(2)}) copy-start(s32[4,1,256]{2,1,0:T(1,128)} %param.16) | copy-start | bytes 12292
  7.2 67.9 %all-gather.24.cloned.1.call-start = ((), (), s32[]{:S(2)}) async-start(), calls=%async_computation.25 | async-start | bytes 5242880 | tf_op jit(solution)/shard_map/all_gather | solution.py:489
  7.9 115.3 %all-gather.12.cloned.1.call-start = ((), (), s32[]{:S(2)}) async-start(), calls=%async_computation.11 | async-start | bytes 5308416 | tf_op jit(solution)/shard_map/all_gather | solution.py:482
  34.6 185.9 %reduce-scatter.12.cloned.1.call-start = ((), (), s32[]{:S(2)}) async-start(), calls=%async_computation.12 | async-start | bytes 5242880 | tf_op jit(solution)/shard_map/reduce_scatter | solution.py:503
  123.3 3.6 copy-start.12
  126.4 23.9 %copy-start.13 = (bf16[4,512,1152]{2,1,0:T(8,128)(2,1)}, bf16[4,512,1152]{2,1,0:T(8,128)(2,1)S(1)}, u32[]{:S(2)}) copy-start(bf16[4,512,1152]{2,1,0:T(8,128)(2,1)S(1)} %copy.72) | copy-start | bytes 14155780
  126.9 3.5 copy-start.6
  126.9 3.5 copy-start.7
  126.9 3.6 copy-start.8
  148.1 1.3 copy-start
  149.4 0.8 copy-start.4
  154.6 1.0 copy-start.1
  155.5 65.0 %copy-start.9 = (bf16[1,1,256,2048]{3,2,1,0:T(8,128)(2,1)S(1)}, bf16[1,1,256,2048]{3,2,1,0:T(8,128)(2,1)}, u32[]{:S(2)}) copy-start(bf16[1,1,256,2048]{3,2,1,0:T(8,128)(2,1)} %param.15) | copy-start | bytes 3145732
  155.6 127.0 %all-gather.18.cloned.1.call-start = ((), (), s32[]{:S(2)}) async-start(), calls=%async_computation.15 | async-start | bytes 6488064 | tf_op jit(solution)/shard_map/all_gather | solution.py:491
  156.1 180.3 %all-gather.14.cloned.1.call-start = ((), (), s32[]{:S(2)}) async-start(), calls=%async_computation.13 | async-start | bytes 5242880 | tf_op jit(solution)/shard_map/all_gather | solution.py:510
  224.8 173.6 %all-gather.16.cloned.1.call-start = ((), (), s32[]{:S(2)}) async-start(), calls=%async_computation.14 | async-start | bytes 6488064 | tf_op jit(solution)/shard_map/all_gather | solution.py:490
  225.4 226.5 %all-gather.26.cloned.1.call-start = ((), (), s32[]{:S(2)}) async-start(), calls=%async_computation.26 | async-start | bytes 5242880 | tf_op jit(solution)/shard_map/all_gather | solution.py:493
  226.1 288.3 %all-gather.20.cloned.1.call-start = ((), (), s32[]{:S(2)}) async-start(), calls=%async_computation.16 | async-start | bytes 6488064 | tf_op jit(solution)/shard_map/all_gather | solution.py:492
  226.9 375.0 %reduce-scatter.16.cloned.1.call-start = ((), (), s32[]{:S(2)}) async-start(), calls=%async_computation.18 | async-start | bytes 5242880 | tf_op jit(solution)/shard_map/reduce_scatter | solution.py:525
  514.4 16.6 %copy-start.16 = (bf16[2048,1408]{1,0:T(8,128)(2,1)S(1)}, bf16[2048,1408]{1,0:T(8,128)(2,1)}, u32[]{:S(2)}) copy-start(bf16[2048,1408]{1,0:T(8,128)(2,1)} %all-gather.16.cloned.1.call-done) | copy-start | bytes 17301508
  531.0 8.7 copy-start.20
  550.8 110.5 %all-gather.22.cloned.1.call-start = ((), (), s32[]{:S(2)}) async-start(), calls=%async_computation.19 | async-start | bytes 5242880 | tf_op jit(solution)/shard_map/all_gather | solution.py:540
  608.4 178.3 %reduce-scatter.24.cloned.1.call-start = ((), (), s32[]{:S(2)}) async-start(), calls=%async_computation.23 | async-start | bytes 6488064 | tf_op jit(solution)/shard_map/reduce_scatter | solution.py:530
  619.4 189.0 %reduce-scatter.22.cloned.1.call-start = ((), (), s32[]{:S(2)}) async-start(), calls=%async_computation.22 | async-start | bytes 6488064 | tf_op jit(solution)/shard_map/reduce_scatter | solution.py:530
  630.5 243.5 %reduce-scatter.26.cloned.1.call-start = ((), (), s32[]{:S(2)}) async-start(), calls=%async_computation.24 | async-start | bytes 6488064 | tf_op jit(solution)/shard_map/reduce_scatter | solution.py:530
  641.3 286.6 %reduce-scatter.18.cloned.1.call-start = ((), (), s32[]{:S(2)}) async-start(), calls=%async_computation.20 | async-start | bytes 5242880 | tf_op jit(solution)/shard_map/reduce_scatter | solution.py:544
  667.7 1.2 copy-start.2
  669.0 1.2 copy-start.5
  744.3 240.8 %reduce-scatter.20.cloned.1.call-start = ((), (), s32[]{:S(2)}) async-start(), calls=%async_computation.21 | async-start | bytes 5308416 | tf_op jit(solution)/shard_map/reduce_scatter | solution.py:554
  756.2 6.5 copy-start.3
  762.7 4.8 copy-start.14
  773.8 1.8 copy-start.19
  773.8 265.5 %reduce-scatter.14.cloned.1.call-start = ((), (), s32[]{:S(2)}) async-start(), calls=%async_computation.17 | async-start | bytes 5242880 | tf_op jit(solution)/shard_map/reduce_scatter | solution.py:517
  786.6 141.3 %copy-start.10 = (bf16[1,1,256,2048]{3,2,1,0:T(8,128)(2,1)S(1)}, bf16[1,1,256,2048]{3,2,1,0:T(8,128)(2,1)}, u32[]{:S(2)}) copy-start(bf16[1,1,256,2048]{3,2,1,0:T(8,128)(2,1)} %param.15) | copy-start | bytes 3145732
  786.7 389.6 %reduce-scatter.28.cloned.1.call-start = ((), (), s32[]{:S(2)}) async-start(), calls=%async_computation.27 | async-start | bytes 1081344
  810.7 228.6 %copy-start.11 = (bf16[256,2048]{1,0:T(8,128)(2,1)S(1)}, bf16[256,2048]{1,0:T(8,128)(2,1)}, u32[]{:S(2)}) copy-start(bf16[256,2048]{1,0:T(8,128)(2,1)} %reduce-scatter.12.cloned.1.call-done) | copy-start | bytes 3145732
  985.1 193.2 %all-to-all-start.1 = ((bf16[4,64,1152]{2,1,0:T(8,128)(2,1)}), bf16[4,64,1152]{2,1,0:T(8,128)(2,1)S(1)}, u32[]{:S(2)}, u32[]{:S(2)}) async-start(bf16[4,64,1152]{2,1,0:T(8,128)(2,1)} %reduce-scatter.20.cloned.1.call-done), calls=%async_computation.6 | async-start | bytes 1179648 | tf_op jit(solution)/shard_map/all_to_all | solution.py:555
Sparse Core Ops, SparseCore 0:
  9.9 59.4 all-gather.23
  71.6 51.6 all-gather.11
  155.7 64.7 reduce-scatter.11
  222.1 60.3 all-gather.17
  285.0 51.3 all-gather.13
  338.0 60.4 all-gather.15
  400.4 51.3 all-gather.25
  453.5 60.8 all-gather.19
  550.9 50.8 reduce-scatter.15
  608.5 52.7 all-gather.21
  663.6 79.5 reduce-scatter.23
  745.4 63.0 reduce-scatter.21
  810.7 63.1 reduce-scatter.25
  876.8 51.0 reduce-scatter.17
  930.1 54.9 reduce-scatter.19
  988.2 51.0 reduce-scatter.13
  1041.4 134.7 reduce-scatter.27

commit v2 on v1

--- a/solution.py
+++ b/solution.py
@@ -81,14 +81,6 @@
     return jnp.concatenate([state, jnp.zeros((LANES - STATE, state.shape[1]), state.dtype)], 0)
 
 
-def chain_barrier(place, count):
-    barrier = pltpu.get_barrier_semaphore()
-    for step in (1, count - 1):
-        other = lax.rem(place + step, count)
-        pl.semaphore_signal(barrier, inc=1, device_id={"seq": other}, device_id_type=MESH)
-    pl.semaphore_wait(barrier, 2)
-
-
 def allowed_of(segc, segr):
     block = segc.shape[0]
     row = lax.broadcasted_iota(jnp.int32, (block, block), 0)
@@ -105,17 +97,22 @@
     left_ref,
     right_ref,
     rows_ref,
+    cot_ref,
     att_ref,
     rden_ref,
     carry_ref,
     csum_ref,
+    cots_ref,
     send_state,
     send_sum,
     part,
     send_sem,
     recv_sem,
+    f_send,
+    f_recv,
+    local_sem,
 ):
-    place = lax.axis_index("seq")
+    place, f = lax.axis_index("seq"), lax.axis_index("feat")
     groups, block = qkv_ref.shape[0], qkv_ref.shape[1]
     width = heads * FDIM
     tables = (left_ref, right_ref, rows_ref)
@@ -138,7 +135,16 @@
         for copy in hop(g):
             copy.start()
 
-    chain_barrier(place, count)
+    chain = [lax.rem(place + 1, count), lax.rem(place + count - 1, count)]
+    greet([{"seq": c} for c in chain] + square_targets(f))
+    stay = pltpu.make_async_copy(cot_ref, cots_ref.at[f], local_sem.at[0])
+    stay.start()
+    cots = [
+        push(cot_ref, cots_ref.at[f], f_send.at[i], f_recv.at[i], {"feat": p})
+        for i, p in enumerate(peers(f))
+    ]
+    for c in cots:
+        c.start()
 
     @pl.when(place == 0)
     def _():
@@ -222,6 +228,12 @@
             return none
 
         lax.fori_loop(0, groups, finish, 0)
+
+    for c in cots:
+        c.wait_recv()
+    for c in cots:
+        c.wait_send()
+    stay.wait()
 
 
 def backward_kernel(
@@ -238,7 +250,10 @@
     carry_ref,
     csum_ref,
     ga_ref,
+    down_ref,
+    res_ref,
     out_ref,
+    final_ref,
     gn,
     send_state,
     send_sum,
@@ -246,10 +261,14 @@
     recv_sum,
     dkey,
     dvalue,
+    downs,
     send_sem,
     recv_sem,
+    f_send,
+    f_recv,
+    local_sem,
 ):
-    place = lax.axis_index("seq")
+    place, f = lax.axis_index("seq"), lax.axis_index("feat")
     groups, block = qkv_ref.shape[0], qkv_ref.shape[1]
     width = heads * FDIM
     tables = (left_ref, right_ref, rows_ref)
@@ -272,7 +291,16 @@
         for copy in hop(g):
             copy.start()
 
-    chain_barrier(place, count)
+    chain = [lax.rem(place + 1, count), lax.rem(place + count - 1, count)]
+    greet([{"seq": c} for c in chain] + square_targets(f))
+    stay = pltpu.make_async_copy(down_ref.at[f], downs.at[3], local_sem.at[0])
+    stay.start()
+    terms = [
+        push(down_ref.at[p], downs.at[i], f_send.at[i], f_recv.at[i], {"feat": p})
+        for i, p in enumerate(peers(f))
+    ]
+    for c in terms:
+        c.start()
 
     @pl.when(place == count - 1)
     def _():
@@ -377,12 +405,28 @@
 
         lax.fori_loop(0, groups, finish, 0)
 
+    stay.wait()
+    for c in terms:
+        c.wait_recv()
+
+    def add_up(i, none):
+        rows = pl.ds(pl.multiple_of(i * 16, 16), 16)
+        total = res_ref[rows, :]
+        for k in range(4):
+            total = total + downs[k, rows, :].astype(f32)
+        final_ref[rows, :] = total.astype(bf16)
+        return none
+
+    lax.fori_loop(0, block // 16, add_up, 0)
+    for c in terms:
+        c.wait_send()
+
 
 def whole_vmem(count):
     return [pl.BlockSpec(memory_space=pltpu.VMEM)] * count
 
 
-def attention_forward(qkv, segc, segr, tables, heads):
+def attention_forward(qkv, segc, segr, tables, cot_own, heads):
     groups, block, _ = qkv.shape
     count = lax.axis_size("seq")
     states = (groups, heads, STATE, HV)
@@ -394,33 +438,43 @@
             jax.ShapeDtypeStruct((groups, block, heads * HV), f32),
             jax.ShapeDtypeStruct(states, bf16),
             jax.ShapeDtypeStruct(sums, f32),
+            jax.ShapeDtypeStruct((groups,) + cot_own.shape, bf16),
         ),
-        in_specs=whole_vmem(6),
-        out_specs=tuple(whole_vmem(4)),
+        in_specs=whole_vmem(6) + in_place(1),
+        out_specs=tuple(whole_vmem(4) + in_place(1)),
         scratch_shapes=[
             pltpu.VMEM(states, bf16),
             pltpu.VMEM(sums, f32),
             pltpu.VMEM((heads, block, 2 * HV), f32),
             pltpu.SemaphoreType.DMA((2, groups)),
             pltpu.SemaphoreType.DMA((2, groups)),
+            pltpu.SemaphoreType.DMA((3,)),
+            pltpu.SemaphoreType.DMA((3,)),
+            pltpu.SemaphoreType.DMA((1,)),
         ],
         compiler_params=pltpu.CompilerParams(
             collective_id=0, has_side_effects=True, vmem_limit_bytes=40 << 20
         ),
+        cost_estimate=pl.CostEstimate(flops=0, bytes_accessed=1 << 20, transcendentals=0),
         name="attention_forward",
-    )(qkv, segc, segr, *tables)
-
-
-def attention_backward(qkv, segc, segr, tables, att, rden, carry, csum, ga, heads):
+    )(qkv, segc, segr, *tables, cot_own)
+
+
+def attention_backward(
+    qkv, segc, segr, tables, att, rden, carry, csum, ga, down, residual, heads
+):
     groups, block, wide = qkv.shape
     count = lax.axis_size("seq")
     states = (groups, heads, STATE, HV)
     sums = (groups, 8, LANES)
     return pl.pallas_call(
         functools.partial(backward_kernel, count, heads),
-        out_shape=jax.ShapeDtypeStruct((groups, block, wide), bf16),
-        in_specs=whole_vmem(11),
-        out_specs=whole_vmem(1)[0],
+        out_shape=(
+            jax.ShapeDtypeStruct((groups, block, wide), bf16),
+            jax.ShapeDtypeStruct(residual.shape, bf16),
+        ),
+        in_specs=whole_vmem(11) + in_place(1) + whole_vmem(1),
+        out_specs=tuple(whole_vmem(2)),
         scratch_shapes=[
             pltpu.VMEM((groups, heads, block, 2 * HV), bf16),
             pltpu.VMEM(states, bf16),
@@ -429,14 +483,307 @@
             pltpu.VMEM(sums, f32),
             pltpu.VMEM((block, heads * FDIM), f32),
             pltpu.VMEM((heads, block, HV), f32),
+            pltpu.VMEM((groups,) + residual.shape, bf16),
             pltpu.SemaphoreType.DMA((2, groups)),
             pltpu.SemaphoreType.DMA((2, groups)),
+            pltpu.SemaphoreType.DMA((3,)),
+            pltpu.SemaphoreType.DMA((3,)),
+            pltpu.SemaphoreType.DMA((1,)),
         ],
         compiler_params=pltpu.CompilerParams(
             collective_id=1, has_side_effects=True, vmem_limit_bytes=48 << 20
         ),
+        cost_estimate=pl.CostEstimate(flops=0, bytes_accessed=1 << 20, transcendentals=0),
         name="attention_backward",
-    )(qkv, segc, segr, *tables, att, rden, carry, csum, ga)
+    )(qkv, segc, segr, *tables, att, rden, carry, csum, ga, down, residual)
+
+
+def peers(f):
+    return 2 * (f // 2) + 1 - f % 2, (f + 2) % 4, 3 - f
+
+
+def greet(targets):
+    barrier = pltpu.get_barrier_semaphore()
+    for target in targets:
+        pl.semaphore_signal(barrier, inc=1, device_id=target, device_id_type=MESH)
+    pl.semaphore_wait(barrier, len(targets))
+
+
+def push(src, dst, send_sem, recv_sem, target):
+    return pltpu.make_async_remote_copy(
+        src_ref=src,
+        dst_ref=dst,
+        send_sem=send_sem,
+        recv_sem=recv_sem,
+        device_id=target,
+        device_id_type=MESH,
+    )
+
+
+def square_targets(f):
+    return [{"feat": p} for p in peers(f)]
+
+
+class SquareGather:
+    def __init__(self, slots, f, send_sem, recv_sem):
+        side, above, across = peers(f)
+        half = slots.shape[1] // 2
+        first, second = pl.ds(0, half), pl.ds(half, half)
+
+        def copy(i, slot, rows, to):
+            ref = slots.at[slot, rows]
+            return push(ref, ref, send_sem.at[i], recv_sem.at[i], {"feat": to})
+
+        self.direct = [
+            copy(0, f, first, side),
+            copy(1, f, second, above),
+            copy(2, f, second, side),
+            copy(3, f, first, above),
+        ]
+        self.forward = [copy(4, side, first, above), copy(5, above, second, side)]
+
+    def start(self):
+        for c in self.direct:
+            c.start()
+
+    def relay(self):
+        self.direct[0].wait_recv()
+        self.forward[0].start()
+        self.direct[1].wait_recv()
+        self.forward[1].start()
+
+    def finish(self):
+        for c in (self.direct[2], self.direct[3], self.forward[0], self.forward[1]):
+            c.wait_recv()
+        for c in self.direct + self.forward:
+            c.wait_send()
+
+
+class SquareSum:
+    def __init__(self, part, land, f, send_sem, recv_sem):
+        self.side, self.above, self.across = peers(f)
+        self.f, self.part, self.land = f, part, land
+        self.half = part.shape[1] // 2
+        first, second = pl.ds(0, self.half), pl.ds(self.half, self.half)
+
+        def copy(i, slot, rows, to):
+            return push(
+                part.at[slot, rows], land.at[i], send_sem.at[i], recv_sem.at[i], {"feat": to}
+            )
+
+        self.cross = [copy(0, self.across, first, self.side), copy(1, self.across, second, self.above)]
+        self.near = [copy(2, self.side, first, self.side), copy(3, self.above, second, self.above)]
+        self.late = [copy(4, self.above, first, self.above), copy(5, self.side, second, self.side)]
+
+    def start_cross(self):
+        for c in self.cross:
+            c.start()
+
+    def add_rows(self, slot, base, landed):
+        step = 32
+
+        def one(i, none):
+            rows = pl.ds(pl.multiple_of(base + i * step, step), step)
+            came = self.land[landed, pl.ds(pl.multiple_of(i * step, step), step), :]
+            self.part[slot, rows, :] = (
+                self.part[slot, rows, :].astype(f32) + came.astype(f32)
+            ).astype(bf16)
+            return none
+
+        lax.fori_loop(0, self.half // step, one, 0)
+
+    def start_near(self):
+        for c in self.near:
+            c.start()
+
+    def relay(self):
+        self.cross[0].wait_recv()
+        self.add_rows(self.above, 0, 0)
+        self.late[0].start()
+        self.cross[1].wait_recv()
+        self.add_rows(self.side, self.half, 1)
+        self.late[1].start()
+
+    def arrive(self):
+        for c in self.near + self.late:
+            c.wait_recv()
+
+    def total(self, half, rows):
+        base = half * self.half
+        own = self.part[self.f, pl.ds(pl.multiple_of(base + rows.start, 16), rows.size), :]
+        near = self.land[2 + half, rows, :]
+        late = self.land[4 + half, rows, :]
+        return own.astype(f32) + near.astype(f32) + late.astype(f32)
+
+    def finish(self):
+        for c in self.cross + self.near + self.late:
+            c.wait_send()
+
+
+def opening_kernel(seqs, dps, tok_ref, pack_ref, gain_ref, x_ref, w_ref, g_ref, *sems):
+    x_send, x_recv, a_send, a_recv, z_send, z_recv, d_send, d_recv, local_sem = sems
+    f, s, d = lax.axis_index("feat"), lax.axis_index("seq"), lax.axis_index("dp")
+    near = peers(f)
+    up, down = lax.rem(s + 1, seqs), lax.rem(s + seqs - 1, seqs)
+    others = [lax.rem(d + k, dps) for k in range(1, dps)]
+    own = [
+        pltpu.make_async_copy(tok_ref, x_ref.at[f], local_sem.at[0]),
+        pltpu.make_async_copy(pack_ref.at[f], w_ref.at[f, s, d], local_sem.at[1]),
+        pltpu.make_async_copy(gain_ref, g_ref.at[f, s, d], local_sem.at[2]),
+    ]
+    for c in own:
+        c.start()
+    greet(
+        square_targets(f)
+        + [{"seq": up}, {"seq": down}]
+        + [{"dp": o} for o in others]
+    )
+
+    shares = []
+    for i, p in enumerate(near):
+        shares.append(
+            push(pack_ref.at[p], w_ref.at[f, s, d], a_send.at[0, i], a_recv.at[0, i], {"feat": p})
+        )
+        shares.append(
+            push(gain_ref, g_ref.at[f, s, d], a_send.at[1, i], a_recv.at[1, i], {"feat": p})
+        )
+    for c in shares:
+        c.start()
+    for c in own:
+        c.wait()
+    gather = SquareGather(x_ref, f, x_send, x_recv)
+    gather.start()
+    for c in shares:
+        c.wait_recv()
+
+    def column(src, i, direction, to):
+        return [
+            push(
+                ref.at[:, src, d],
+                ref.at[:, src, d],
+                z_send.at[j, direction, i],
+                z_recv.at[j, direction, i],
+                {"seq": to},
+            )
+            for j, ref in enumerate((w_ref, g_ref))
+        ]
+
+    def sibling(src, i):
+        return [
+            push(
+                ref.at[:, src, d],
+                ref.at[:, src, d],
+                d_send.at[j, k, i],
+                d_recv.at[j, k, i],
+                {"dp": o},
+            )
+            for j, ref in enumerate((w_ref, g_ref))
+            for k, o in enumerate(others)
+        ]
+
+    def start_all(copies):
+        for c in copies:
+            c.start()
+
+    def both_ways(i):
+        @pl.when((s >= i) & (s < seqs - 1))
+        def _():
+            start_all(column(lax.rem(s + seqs - i, seqs), i, 0, up))
+
+        @pl.when((s + i < seqs) & (s > 0))
+        def _():
+            start_all(column(lax.rem(s + i, seqs), i, 1, down))
+
+    both_ways(0)
+    start_all(sibling(s, 0))
+    for i in range(1, seqs):
+        @pl.when(s >= i)
+        def _():
+            for c in column(lax.rem(s + seqs - i, seqs), i - 1, 0, up):
+                c.wait_recv()
+            start_all(sibling(lax.rem(s + seqs - i, seqs), i))
+
+        @pl.when(s + i < seqs)
+        def _():
+            for c in column(lax.rem(s + i, seqs), i - 1, 1, down):
+                c.wait_recv()
+            start_all(sibling(lax.rem(s + i, seqs), seqs - 1 + i))
+
+        if i < seqs - 1:
+            both_ways(i)
+        if i == 1:
+            gather.relay()
+
+    def close(copies):
+        for c in copies:
+            c.wait_recv()
+        for c in copies:
+            c.wait_send()
+
+    close(sibling(s, 0))
+    for i in range(1, seqs):
+
+        @pl.when(s >= i)
+        def _():
+            close(sibling(lax.rem(s + seqs - i, seqs), i))
+
+        @pl.when(s + i < seqs)
+        def _():
+            close(sibling(lax.rem(s + i, seqs), seqs - 1 + i))
+
+    for i in range(seqs - 1):
+
+        @pl.when((s >= i) & (s < seqs - 1))
+        def _():
+            for c in column(lax.rem(s + seqs - i, seqs), i, 0, up):
+                c.wait_send()
+
+        @pl.when((s + i < seqs) & (s > 0))
+        def _():
+            for c in column(lax.rem(s + i, seqs), i, 1, down):
+                c.wait_send()
+
+    for c in shares:
+        c.wait_send()
+    gather.finish()
+
+
+def in_place(count):
+    return [pl.BlockSpec(memory_space=pl.ANY)] * count
+
+
+def opening(own, pack, gain_tile):
+    parts, seqs, dps = (lax.axis_size(a) for a in ALL)
+    block, width = own.shape
+    _, rows_each, wide = pack.shape
+    others = max(dps - 1, 1)
+    dma = pltpu.SemaphoreType.DMA
+    x_all, w_all, g_all = pl.pallas_call(
+        functools.partial(opening_kernel, seqs, dps),
+        out_shape=(
+            jax.ShapeDtypeStruct((parts, block, width), bf16),
+            jax.ShapeDtypeStruct((parts, seqs, dps, rows_each, wide), bf16),
+            jax.ShapeDtypeStruct((parts, seqs, dps) + gain_tile.shape, f32),
+        ),
+        in_specs=in_place(3),
+        out_specs=tuple(in_place(3)),
+        scratch_shapes=[
+            dma((6,)),
+            dma((6,)),
+            dma((2, 3)),
+            dma((2, 3)),
+            dma((2, 2, seqs)),
+            dma((2, 2, seqs)),
+            dma((2, others, 2 * seqs - 1)),
+            dma((2, others, 2 * seqs - 1)),
+            dma((3,)),
+        ],
+        compiler_params=pltpu.CompilerParams(collective_id=2, has_side_effects=True),
+        cost_estimate=pl.CostEstimate(flops=0, bytes_accessed=1 << 20, transcendentals=0),
+        name="opening",
+    )(own, pack, gain_tile)
+    gains = g_all[..., :2, :rows_each].transpose(3, 0, 1, 2, 4).reshape(2, width)
+    return x_all, w_all.reshape(width, wide), gains
 
 
 def inverse_rms(values):
@@ -446,6 +793,284 @@
 def norm_back(grad, unit, inverse, gain):
     scaled = grad * gain
     return (scaled - unit * jnp.mean(scaled * unit, axis=-1, keepdims=True)) * inverse
+
+
+def product_tiles(part, slot, pairs, tile):
+    def one(i, none):
+        cols = pl.ds(pl.multiple_of(i * tile, tile), tile)
+        total = None
+        for rows, weights in pairs:
+            term = dot_nt(rows[slot], weights[cols, :])
+            total = term if total is None else total + term
+        part[slot, :, cols] = total.astype(bf16)
+        return none
+
+    lax.fori_loop(0, part.shape[2] // tile, one, 0)
+
+
+def summed_products(part, land, f, pairs, send_sem, recv_sem):
+    side, above, across = peers(f)
+    ring = SquareSum(part, land, f, send_sem, recv_sem)
+    product_tiles(part, across, pairs, 512)
+    ring.start_cross()
+    product_tiles(part, side, pairs, 512)
+    product_tiles(part, above, pairs, 512)
+    ring.start_near()
+    product_tiles(part, f, pairs, 512)
+    ring.relay()
+    ring.arrive()
+    return ring
+
+
+def by_rows(ring, body, step=16):
+    for half in (0, 1):
+
+        def one(i, none):
+            start = pl.multiple_of(i * step, step)
+            rows = pl.ds(pl.multiple_of(half * ring.half + i * step, step), step)
+            body(rows, ring.total(half, pl.ds(start, step)))
+            return none
+
+        lax.fori_loop(0, ring.half // step, one, 0)
+
+
+def branch_kernel(
+    att_ref, w_ref, tok_ref, gain_ref, rows_ref, res_ref, part, land, s_send, s_recv, g_send, g_recv
+):
+    f = lax.axis_index("feat")
+    greet(square_targets(f))
+    ring = summed_products(part, land, f, [(att_ref, w_ref)], s_send, s_recv)
+
+    def finish_rows(rows, total):
+        residual = tok_ref[rows, :].astype(f32) + total
+        res_ref[rows, :] = residual
+        rows_ref[f, rows, :] = (residual * inverse_rms(residual) * gain_ref[...]).astype(bf16)
+
+    by_rows(ring, finish_rows)
+    gather = SquareGather(rows_ref, f, g_send, g_recv)
+    gather.start()
+    ring.finish()
+    gather.relay()
+    gather.finish()
+
+
+def square_scratch(parts, block, width):
+    dma = pltpu.SemaphoreType.DMA
+    return [
+        pltpu.VMEM((parts, block, width), bf16),
+        pltpu.VMEM((6, block // 2, width), bf16),
+        dma((6,)),
+        dma((6,)),
+    ]
+
+
+def branch_step(att, out_w, own, gain_two):
+    parts, block, _ = att.shape
+    width = own.shape[1]
+    dma = pltpu.SemaphoreType.DMA
+    return pl.pallas_call(
+        branch_kernel,
+        out_shape=(
+            jax.ShapeDtypeStruct((parts, block, width), bf16),
+            jax.ShapeDtypeStruct((block, width), f32),
+        ),
+        in_specs=whole_vmem(4),
+        out_specs=tuple(whole_vmem(2)),
+        scratch_shapes=square_scratch(parts, block, width) + [dma((6,)), dma((6,))],
+        compiler_params=pltpu.CompilerParams(
+            collective_id=3, has_side_effects=True, vmem_limit_bytes=48 << 20
+        ),
+        cost_estimate=pl.CostEstimate(flops=0, bytes_accessed=1 << 20, transcendentals=0),
+        name="branch_step",
+    )(att, out_w, own, gain_two)
+
+
+def rows_back_kernel(
+    gg_ref,
+    gu_ref,
+    wg_ref,
+    wu_ref,
+    res_ref,
+    cot_ref,
+    gain_ref,
+    all_ref,
+    gres_ref,
+    gsum_ref,
+    part,
+    land,
+    s_send,
+    s_recv,
+    g_send,
+    g_recv,
+):
+    f = lax.axis_index("feat")
+    greet(square_targets(f))
+    pairs = [(gg_ref, wg_ref), (gu_ref, wu_ref)]
+    ring = summed_products(part, land, f, pairs, s_send, s_recv)
+    gsum_ref[...] = jnp.zeros_like(gsum_ref)
+
+    def finish_rows(rows, grad):
+        residual = res_ref[rows, :]
+        inverse = inverse_rms(residual)
+        unit = residual * inverse
+        gsum_ref[...] += jnp.sum(grad * unit, axis=0, keepdims=True)
+        grad_res = cot_ref[rows, :].astype(f32) + norm_back(grad, unit, inverse, gain_ref[...])
+        gres_ref[rows, :] = grad_res
+        all_ref[f, rows, :] = grad_res.astype(bf16)
+
+    by_rows(ring, finish_rows)
+    gather = SquareGather(all_ref, f, g_send, g_recv)
+    gather.start()
+    ring.finish()
+    gather.relay()
+    gather.finish()
+
+
+def rows_back(grad_gate, grad_up, gate_w, up_w, residual, cot_own, gain_two):
+    parts, block, _ = grad_gate.shape
+    width = residual.shape[1]
+    dma = pltpu.SemaphoreType.DMA
+    return pl.pallas_call(
+        rows_back_kernel,
+        out_shape=(
+            jax.ShapeDtypeStruct((parts, block, width), bf16),
+            jax.ShapeDtypeStruct((block, width), f32),
+            jax.ShapeDtypeStruct((1, width), f32),
+        ),
+        in_specs=whole_vmem(7),
+        out_specs=tuple(whole_vmem(3)),
+        scratch_shapes=square_scratch(parts, block, width) + [dma((6,)), dma((6,))],
+        compiler_params=pltpu.CompilerParams(
+            collective_id=4, has_side_effects=True, vmem_limit_bytes=56 << 20
+        ),
+        cost_estimate=pl.CostEstimate(flops=0, bytes_accessed=1 << 20, transcendentals=0),
+        name="rows_back",
+    )(grad_gate, grad_up, gate_w, up_w, residual, cot_own, gain_two)
+
+
+def closing_kernel(
+    seqs,
+    dps,
+    dqkv_ref,
+    w_ref,
+    tok_ref,
+    gres_ref,
+    gain_ref,
+    gsum_two_ref,
+    x_ref,
+    tile_ref,
+    part,
+    land,
+    s_send,
+    s_recv,
+    gsum,
+    cut,
+    came,
+    mid,
+    tail,
+    c_send,
+    c_recv,
+    d_send,
+    d_recv,
+):
+    f, s, d = lax.axis_index("feat"), lax.axis_index("seq"), lax.axis_index("dp")
+    parts = 4
+    others = [lax.rem(d + k, dps) for k in range(1, dps)]
+    circle = [
+        (lax.rem(f + i, parts), lax.rem(s + j, seqs))
+        for i in range(parts)
+        for j in range(seqs)
+        if i or j
+    ]
+    greet(
+        [{"feat": a, "seq": b} for a, b in circle] + [{"dp": o} for o in others]
+    )
+    ring = summed_products(part, land, f, [(dqkv_ref, w_ref)], s_send, s_recv)
+    gsum[...] = jnp.zeros_like(gsum)
+
+    def finish_rows(rows, grad):
+        values = tok_ref[rows, :].astype(f32)
+        inverse = inverse_rms(values)
+        unit = values * inverse
+        gsum[...] += jnp.sum(grad * unit, axis=0, keepdims=True)
+        x_ref[rows, :] = gres_ref[rows, :] + norm_back(grad, unit, inverse, gain_ref[...])
+
+    by_rows(ring, finish_rows)
+    ring.finish()
+
+    lanes = gsum.shape[1] // (parts * seqs)
+    cut[...] = jnp.zeros_like(cut)
+    for k in range(parts * seqs):
+        cut[k, 0:1, :] = gsum[:, k * lanes : (k + 1) * lanes]
+        cut[k, 1:2, :] = gsum_two_ref[:, k * lanes : (k + 1) * lanes]
+    place = f * seqs + s
+    sends = []
+    for i, (a, b) in enumerate(circle):
+        sends.append(
+            push(
+                cut.at[a * seqs + b],
+                came.at[i],
+                c_send.at[i],
+                c_recv.at[i],
+                {"feat": a, "seq": b},
+            )
+        )
+    for c in sends:
+        c.start()
+    total = cut[place]
+    for c in sends:
+        c.wait_recv()
+    for i in range(len(circle)):
+        total = total + came[i]
+    mid[...] = total
+    last = [
+        push(mid, tail.at[k], d_send.at[k], d_recv.at[k], {"dp": o})
+        for k, o in enumerate(others)
+    ]
+    for c in last:
+        c.start()
+    for c in last:
+        c.wait_recv()
+    for k in range(len(others)):
+        total = total + tail[k]
+    tile_ref[...] = total
+    for c in sends + last:
+        c.wait_send()
+
+
+def closing(dqkv, qkv_w, own, grad_residual, gain_one, gain_two_sum):
+    parts, seqs, dps = (lax.axis_size(a) for a in ALL)
+    block, width = own.shape
+    others = max(dps - 1, 1)
+    lanes = width // (parts * seqs)
+    circle = parts * seqs - 1
+    dma = pltpu.SemaphoreType.DMA
+    return pl.pallas_call(
+        functools.partial(closing_kernel, seqs, dps),
+        out_shape=(
+            jax.ShapeDtypeStruct((block, width), f32),
+            jax.ShapeDtypeStruct((8, lanes), f32),
+        ),
+        in_specs=whole_vmem(6),
+        out_specs=tuple(whole_vmem(2)),
+        scratch_shapes=square_scratch(parts, block, width)
+        + [
+            pltpu.VMEM((1, width), f32),
+            pltpu.VMEM((parts * seqs, 8, lanes), f32),
+            pltpu.VMEM((circle, 8, lanes), f32),
+            pltpu.VMEM((8, lanes), f32),
+            pltpu.VMEM((others, 8, lanes), f32),
+            dma((circle,)),
+            dma((circle,)),
+            dma((others,)),
+            dma((others,)),
+        ],
+        compiler_params=pltpu.CompilerParams(
+            collective_id=5, has_side_effects=True, vmem_limit_bytes=48 << 20
+        ),
+        cost_estimate=pl.CostEstimate(flops=0, bytes_accessed=1 << 20, transcendentals=0),
+        name="closing",
+    )(dqkv, qkv_w, own, grad_residual, gain_one, gain_two_sum)
 
 
 def local(
@@ -478,96 +1103,96 @@
         axis=2,
     )
     pack_width = pack.shape[2]
-    pack = lax.all_to_all(pack, "feat", 0, 0, tiled=True)
-    pack = lax.all_gather(pack, ("seq", "dp"), axis=1, tiled=True)
-    attn_w = pack.reshape(width, pack_width)
+    gain_tile = jnp.zeros((8, HV), f32)
+    gain_tile = gain_tile.at[0, :rows_each].set(norm1_gain.astype(f32))
+    gain_tile = gain_tile.at[1, :rows_each].set(norm2_gain.astype(f32))
+    gate_w = lax.all_gather(w_gate, ("seq", "dp"), axis=0, tiled=True)
+    up_w = lax.all_gather(w_up, ("seq", "dp"), axis=0, tiled=True)
+    x_all, attn_w, gains = opening(own, pack, gain_tile)
     qkv_width = pack_width - heads * HV
     qkv_w, out_w = attn_w[:, :qkv_width], attn_w[:, qkv_width:]
-    gains = lax.all_gather(jnp.stack([norm1_gain, norm2_gain]), ALL, axis=1, tiled=True).astype(f32)
-    gain_one, gain_two = gains[0], gains[1]
-
-    x_all = lax.all_gather(own, "feat", axis=0, tiled=True)
-    gate_w = lax.all_gather(w_gate, ("seq", "dp"), axis=0, tiled=True)
-    up_w = lax.all_gather(w_up, ("seq", "dp"), axis=0, tiled=True)
-    down_w = lax.all_gather(w_down.T, ("seq", "dp"), axis=0, tiled=True)
-    cot_all = lax.all_gather(cot_own, "feat", axis=0, tiled=True)
-
-    x_wide = x_all.astype(f32)
+    gain_one, gain_two = gains[0:1], gains[1:2]
+
+    x_wide = x_all.astype(f32).reshape(rows_total, width)
     normed = (x_wide * inverse_rms(x_wide) * gain_one).astype(bf16)
     qkv = dot(normed, qkv_w).astype(bf16).reshape(parts, block, qkv_width)
+    qkv, w_down = lax.optimization_barrier((qkv, w_down))
+    down_w = lax.all_gather(w_down.T, ("seq", "dp"), axis=0, tiled=True)
     segment = segments.reshape(parts, block).astype(f32)
     segc, segr = segment[:, :, None], segment[:, None, :]
     tables = feature_tables(heads)
-    att, rden, carry, csum = attention_forward(qkv, segc, segr, tables, heads)
-    att_rows = att.reshape(rows_total, heads * HV)
-    branch = lax.psum_scatter(
-        dot_nt(att_rows, out_w).astype(bf16), "feat", scatter_dimension=0, tiled=True
-    )
-    inputs = own.astype(f32)
-    residual = inputs + branch.astype(f32)
-    inverse_two = inverse_rms(residual)
-    unit_two = residual * inverse_two
-    rows_all = lax.all_gather((unit_two * gain_two).astype(bf16), "feat", axis=0, tiled=True)
+    att, rden, carry, csum, cot_all = attention_forward(qkv, segc, segr, tables, cot_own, heads)
+    cot_all = cot_all.reshape(rows_total, width)
+    rows_all, residual = branch_step(att, out_w, own, gain_two)
+    rows_all = rows_all.reshape(rows_total, width)
 
     gate_out = dot(rows_all, gate_w)
     up_out = dot(rows_all, up_w)
     sig = jax.nn.sigmoid(gate_out)
     silu = gate_out * sig
     mixed = (silu * up_out).astype(bf16)
-    down_own = lax.psum_scatter(
-        dot_nt(mixed, down_w).astype(bf16), "feat", scatter_dimension=0, tiled=True
-    )
-    output = (residual + down_own.astype(f32)).astype(bf16).reshape(tokens.shape)
-    grad_mixed = dot(cot_all, down_w)
+    mixed, cot_late = lax.optimization_barrier((mixed, cot_all))
+    down = dot_nt(mixed, down_w).astype(bf16).reshape(parts, block, width)
+    grad_mixed = dot(cot_late, down_w)
     grad_gate = (grad_mixed * up_out * sig * (1.0 + gate_out * (1.0 - sig))).astype(bf16)
     grad_up = (grad_mixed * silu).astype(bf16)
-    row_grads = dot_nt(grad_gate, gate_w) + dot_nt(grad_up, up_w)
-    grad_normed_two = lax.psum_scatter(
-        row_grads.astype(bf16), "feat", scatter_dimension=0, tiled=True
-    ).astype(f32)
 
     def summed(term):
-        return lax.psum_scatter(
-            term.astype(bf16), ("seq", "dp"), scatter_dimension=0, tiled=True
-        ).astype(f32)
-
-    grad_w_down = summed(dot_tn(cot_all, mixed)).T
-    grad_w_gate = summed(dot_tn(rows_all, grad_gate))
-    grad_w_up = summed(dot_tn(rows_all, grad_up))
-
-    gain_two_part = jnp.sum(grad_normed_two * unit_two, axis=0)
-    grad_residual = cot_own.astype(f32) + norm_back(grad_normed_two, unit_two, inverse_two, gain_two)
-    branch_all = lax.all_gather(grad_residual.astype(bf16), "feat", axis=0, tiled=True)
+        return lax.psum_scatter(term, ("seq", "dp"), scatter_dimension=0, tiled=True)
+
+    down_term = dot_tn(cot_all, mixed).astype(bf16)
+    gate_term = dot_tn(rows_all, grad_gate).astype(bf16)
+    up_term = dot_tn(rows_all, grad_up).astype(bf16)
+    grad_gate, grad_up, gate_term, up_term = lax.optimization_barrier(
+        (grad_gate, grad_up, gate_term, up_term)
+    )
+    down_sum, gate_sum, up_sum = summed(down_term), summed(gate_term), summed(up_term)
+
+    by_device = (parts, block, -1)
+    branch_all, grad_residual, gain_two_sum = rows_back(
+        grad_gate.reshape(by_device),
+        grad_up.reshape(by_device),
+        gate_w,
+        up_w,
+        residual,
+        cot_own,
+        gain_two,
+    )
+    branch_all = branch_all.reshape(rows_total, width)
     ga = dot(branch_all, out_w).reshape(parts, block, heads * HV)
-    dqkv = attention_backward(qkv, segc, segr, tables, att, rden, carry, csum, ga, heads)
+    dqkv, output = attention_backward(
+        qkv, segc, segr, tables, att, rden, carry, csum, ga, down, residual, heads
+    )
+    x_grad, gain_grads = closing(dqkv, qkv_w, own, grad_residual, gain_one, gain_two_sum)
     dqkv = dqkv.reshape(rows_total, qkv_width)
-    grad_normed_one = lax.psum_scatter(
-        dot_nt(dqkv, qkv_w).astype(bf16), "feat", scatter_dimension=0, tiled=True
-    ).astype(f32)
-    inverse_one = inverse_rms(inputs)
-    unit_one = inputs * inverse_one
-    x_grad = grad_residual + norm_back(grad_normed_one, unit_one, inverse_one, gain_one)
-    gain_one_part = jnp.sum(grad_normed_one * unit_one, axis=0)
-
-    attn_grads = jnp.concatenate([dot_tn(normed, dqkv), dot_tn(branch_all, att_rows)], axis=1)
-    attn_grads = attn_grads.astype(bf16).reshape(parts, width // parts, pack_width)
-    attn_grads = lax.psum_scatter(attn_grads, ("seq", "dp"), scatter_dimension=1, tiled=True)
-    attn_grads = lax.all_to_all(attn_grads, "feat", 0, 0, tiled=True).astype(f32)
-
-    def from_share(first, per):
-        piece = attn_grads[:, :, first : first + heads * per]
+
+    def shared(grads):
+        grads = grads.astype(bf16).reshape(parts, -1, rows_each, grads.shape[1])
+        grads = grads.transpose(1, 0, 2, 3).reshape(width, -1)
+        grads = lax.psum_scatter(grads, ("seq", "dp"), scatter_dimension=0, tiled=True)
+        grads = grads.reshape(parts, rows_each, -1)
+        return lax.all_to_all(grads, "feat", 0, 0, tiled=True).astype(f32)
+
+    def from_share(grads, first, per):
+        piece = grads[:, :, first : first + heads * per]
         return piece.transpose(1, 0, 2).reshape(rows_each, HEADS * per)
 
-    start_value = 2 * heads * FDIM
-    query_grad = from_share(0, FDIM)
-    key_grad = from_share(heads * FDIM, FDIM)
-    value_grad = from_share(start_value, HV)
-    out_grad = from_share(start_value + heads * HV, HV).T
-    gain_grads = lax.psum_scatter(
-        jnp.stack([gain_one_part, gain_two_part]), ALL, scatter_dimension=1, tiled=True
+    out_term = dot_tn(branch_all, att.reshape(rows_total, heads * HV))
+    qkv_term = dot_tn(normed, dqkv)
+    out_term, qkv_term, down_sum, gate_sum, up_sum = lax.optimization_barrier(
+        (out_term, qkv_term, down_sum, gate_sum, up_sum)
+    )
+    out_grads, qkv_grads = shared(out_term), shared(qkv_term)
+    query_grad = from_share(qkv_grads, 0, FDIM)
+    key_grad = from_share(qkv_grads, heads * FDIM, FDIM)
+    value_grad = from_share(qkv_grads, 2 * heads * FDIM, HV)
+    out_grad = from_share(out_grads, 0, HV).T
+    gain_each = gain_grads.shape[1] // lax.axis_size("dp")
+    gain_grads = lax.dynamic_slice_in_dim(
+        gain_grads, lax.axis_index("dp") * gain_each, gain_each, axis=1
     )
     return (
-        output,
+        output.reshape(tokens.shape),
         x_grad.reshape(tokens.shape),
         gain_grads[0],
         gain_grads[1],
@@ -575,9 +1200,9 @@
         key_grad,
         value_grad,
         out_grad,
-        grad_w_gate,
-        grad_w_up,
-        grad_w_down,
+        gate_sum.astype(f32),
+        up_sum.astype(f32),
+        down_sum.T.astype(f32),
     )
 
 

time: 1200 us -> 696 us (0.58)
  waiting for transfers between devices: 817 us -> 13.9 us
  Pallas kernels: 84.9 us -> 498 us
  blocking collectives: 59.7 us -> 0 us
  matrix products: 133 us -> 97 us
  other arithmetic: 36.5 us -> 11.1 us
    pallas_call x0 -> x4, Pallas kernels: none -> 351 us  [the longest x1 140 us: opening(): pl.pallas_call(functools.partial(opening_kernel, seqs, dps), out_shape=(j...]
    reduce_scatter x8 -> x5, waiting for transfers between devices: 354 us -> 6.41 us  [the longest x2 6.4 us: shared(): lax.psum_scatter(grads, ('seq', 'dp'), scatter_dimension=0, tiled=True)]
    all_gather x5 -> x0, waiting for transfers between devices: 161 us -> none  [the longest x1 53.8 us: local(): lax.all_gather((unit_two * gain_two).astype(bf16), 'feat', axis=0, tiled=...]
    unnamed x18 -> x8, waiting for transfers between devices: 135 us -> 1.98 us
    all_gather x1, waiting for transfers between devices: 62.5 us -> 0.02 us  [local(): down_w = lax.all_gather(w_down.T, ('seq', 'dp'), axis=0, tiled=True)]
    all_gather x1, waiting for transfers between devices: 55.2 us -> 0.01 us  [local(): up_w = lax.all_gather(w_up, ('seq', 'dp'), axis=0, tiled=True)]
    all_gather x1, waiting for transfers between devices: 50.4 us -> 0.01 us  [local(): gate_w = lax.all_gather(w_gate, ('seq', 'dp'), axis=0, tiled=True)]
    all_gather x1 -> x0, blocking collectives: 40 us -> none  [local(): lax.all_gather(jnp.stack([norm1_gain, norm2_gain]), ALL, axis=1, tiled=True)]
  transfers between devices with their start and end apart: 18 -> 10, of which waited for: 15 -> 2; matrix products, arithmetic and copies ran while one was open for 12% -> 19% of each run, Pallas kernels for 6% -> 72%
where the time goes in v2:
time: 696 us; the launch traced here: 689 us
  Pallas kernels  498 us (72%)
  matrix products  97 us (14%)
  local copies, waits for them, and re-layouts  46 us (7%)
  between operations  15 us (2%)
  waiting for transfers between devices  13.9 us (2%)
  other arithmetic  11.1 us (2%)
  starting transfers between devices  7.76 us (1%)
    pallas_call x1, Pallas kernels, opening(): pl.pallas_call(functools.partial(opening_kernel, seqs, dps), out_shape=(j...  140 us
    pallas_call x1, Pallas kernels, attention_backward(): pl.pallas_call(functools.partial(backward_kernel, count, heads), out_shap...  93.2 us
    pallas_call x1, Pallas kernels, rows_back(): pl.pallas_call(rows_back_kernel, out_shape=(jax.ShapeDtypeStruct((parts,...  85.6 us
    pallas_call x1, Pallas kernels, branch_step(): pl.pallas_call(branch_kernel, out_shape=(jax.ShapeDtypeStruct((parts, blo...  78.1 us
    pallas_call x1, Pallas kernels, attention_forward(): pl.pallas_call(functools.partial(forward_kernel, count, heads), out_shape...  53.5 us
    dot_general x5, matrix products, dot(): lax.dot_general(a, b, (((1,), (0,)), ((), ())), preferred_element_type=f32)  50 us
    pallas_call x1, Pallas kernels, closing(): pl.pallas_call(functools.partial(closing_kernel, seqs, dps), out_shape=(j...  48 us
    dot_general x5, matrix products, dot_tn(): lax.dot_general(a, b, (((0,), (0,)), ((), ())), preferred_element_type=f32)  35.8 us
  transfers between devices with their start and end apart: 10, of which 2 were waited for; matrix products, arithmetic and copies ran while one was open for 19% of the time, Pallas kernels for 72%

profile of v2, /device:TPU:0, one launch (start us, length us, event | category | flops | bytes accessed | tf_op | source)
XLA Modules:
  0.0 689.0 jit_solution(11045595438506188394)
XLA Ops:
  10.5 1.1 bitcast_bitcast_fusion
  11.6 1.0 concatenate.7.pack_ref
  13.3 139.7 %opening.1 = (bf16[4,256,2048]{2,1,0:T(8,128)(2,1)}, bf16[4,4,2,64,1152]{4,3,2,1,0:T(8,128)(2,1)}, f32[4,4,2,8,128]{4,3,2,1,0:T(8,128)}) custom-call(bf16[256,2048]{1,0:T(8,128)(2,1)} %bitcast.101, bf16[4,64,1152]{2,1,0:T(8,128)(2,1)} %concatenate.7.pack_ref, f32[8,128]{1,0:T(8,128)} %copy-done.31), custom_call_target="tpu_custom_call" | custom-call | bytes 1048576 | tf_op jit(solution)/shard_map/opening/pallas_call | solution.py:761
  153.1 0.9 slice_bitcast_fusion.3
  154.8 3.2 multiply_reduce_fusion
  158.3 1.0 fusion.1
  159.3 1.3 copy-done.24
  160.7 3.4 convolution_convert_fusion.4
  164.2 3.1 slice.85.w_ref
  167.7 1.2 copy-done.4
  168.9 0.9 copy-done.10
  171.4 53.5 %attention_forward.1 = (bf16[4,256,512]{2,1,0:T(8,128)(2,1)S(1)}, f32[4,256,512]{2,1,0:T(8,128)S(1)}, bf16[4,4,160,128]{3,2,1,0:T(8,128)(2,1)S(1)}, f32[4,8,256]{2,1,0:T(8,128)S(1)}, bf16[4,256,2048]{2,1,0:T(8,128)(2,1)S(1)}) custom-call(bf16[4,256,640]{2,1,0:T(8,128)(2,1)S(1)} %bitcast.104, f32[4,256,1]{2,1,0:T(8,128)S(1)} %copy.47.segc_ref, ...), custom_call_target="tpu_custom_call" | custom-call | bytes 1048576 | tf_op jit(solution)/shard_map/attention_forward/pallas_call | solution.py:434
  224.9 1.3 copy-done.5
  226.8 1.9 copy-done.20
  228.7 78.1 %branch_step.1 = (bf16[4,256,2048]{2,1,0:T(8,128)(2,1)}, f32[256,2048]{1,0:T(8,128)S(1)}) custom-call(bf16[4,256,512]{2,1,0:T(8,128)(2,1)S(1)} %get-tuple-element.69.att_ref, bf16[2048,512]{1,0:T(8,128)(2,1)} %slice.85.w_ref, bf16[256,2048]{1,0:T(8,128)(2,1)S(1)} %bitcast.102, f32[1,2048]{1,0:T(1,128)S(1)} %slice.76.gain_ref), custom_call_target="tpu_custom_call" | custom-call | bytes 1048576 | tf_op jit(solution)/shard_map/branch_step/pallas_call | solution.py:871
  306.9 1.3 copy-done.1
  308.2 1.0 copy-done.2
  309.2 11.7 %fusion.14 = f32[1024,1408]{1,0:T(8,128)} fusion(bf16[1024,2048]{1,0:T(8,128)(2,1)} %bitcast.133, bf16[2048,1408]{1,0:T(8,128)(2,1)} %all-gather.4.cloned.1.call-done.wg_ref), kind=kOutput, calls=%fused_computation.46 | convolution fusion | flops 5905580032 | bytes 15728640 | tf_op jit(solution)/shard_map/dot_general | solution.py:24
  320.9 12.8 %multiply_convert_fusion.3 = (bf16[1024,1408]{1,0:T(8,128)(2,1)S(1)}, f32[1024,1408]{1,0:T(8,128)}) fusion(f32[1024,1408]{1,0:T(8,128)} %fusion.14, bf16[1024,2048]{1,0:T(8,128)(2,1)} %bitcast.134, bf16[2048,1408]{1,0:T(8,128)(2,1)} %all-gather.6.cloned.1.call-done.wu_ref), kind=kOutput, calls=%fused_computation.10 | convolution fusion | flops 5914230784 | bytes 24379392 | tf_op jit(solution)/shard_map/dot_general | solution.py:24
  333.7 1.6 copy-done.37
  335.3 8.7 %convolution_convert_fusion = bf16[2048,1408]{1,0:T(8,128)(2,1)} fusion(bf16[1024,2048]{1,0:T(8,128)(2,1)S(1)} %bitcast.111, bf16[1024,1408]{1,0:T(8,128)(2,1)S(1)} %get-tuple-element.81), kind=kOutput, calls=%fused_computation.5 | convolution fusion | flops 5908463616 | bytes 12845056 | tf_op jit(solution)/shard_map/dot_general | solution.py:32
  344.2 15.4 %multiply_convert_fusion.1 = (bf16[1024,1408]{1,0:T(8,128)(2,1)}, bf16[1024,1408]{1,0:T(8,128)(2,1)S(1)}) fusion(f32[1024,1408]{1,0:T(8,128)} %fusion.14, f32[1024,1408]{1,0:T(8,128)} %get-tuple-element.142, bf16[1024,2048]{1,0:T(8,128)(2,1)} %bitcast.110, bf16[2048,1408]{0,1:T(8,128)(2,1)} %all-gather.8.cloned.1.call-done), kind=kOutput, calls=%fused_computation.8 | convolution fusion | flops 5924323328 | bytes 27262976 | tf_op jit(solution)/shard_map/dot_general | solution.py:24
  359.6 1.5 copy-done.25
  361.1 8.5 %convolution_convert_fusion.2 = bf16[2048,1408]{1,0:T(8,128)(2,1)} fusion(bf16[1024,2048]{1,0:T(8,128)(2,1)S(1)} %bitcast.136, bf16[1024,1408]{1,0:T(8,128)(2,1)S(1)} %get-tuple-element.77), kind=kOutput, calls=%fused_computation.7 | convolution fusion | flops 5908463616 | bytes 12845056 | tf_op jit(solution)/shard_map/dot_general | solution.py:32
  369.7 11.0 %convolution_convert_fusion.1 = bf16[2048,1408]{1,0:T(8,128)(2,1)} fusion(bf16[1024,2048]{1,0:T(8,128)(2,1)} %bitcast.135, bf16[1024,1408]{1,0:T(8,128)(2,1)} %get-tuple-element.78), kind=kOutput, calls=%fused_computation.6 | convolution fusion | flops 5908463616 | bytes 12845056 | tf_op jit(solution)/shard_map/dot_general | solution.py:32
  381.5 85.6 %rows_back.1 = (bf16[4,256,2048]{2,1,0:T(8,128)(2,1)}, f32[256,2048]{1,0:T(8,128)}, f32[1,2048]{1,0:T(1,128)}) custom-call(bf16[4,256,1408]{2,1,0:T(8,128)(2,1)} %bitcast.120, bf16[4,256,1408]{2,1,0:T(8,128)(2,1)} %bitcast.119, bf16[2048,1408]{1,0:T(8,128)(2,1)} %all-gather.4.cloned.1.call-done.wg_ref, ...), custom_call_target="tpu_custom_call" | custom-call | bytes 1048576 | tf_op jit(solution)/shard_map/rows_back/pallas_call | solution.py:933
  467.1 6.7 fusion.8.ga_ref
  473.8 11.2 %convolution_convert_fusion.3 = bf16[1024,2048]{1,0:T(8,128)(2,1)} fusion(bf16[1024,1408]{1,0:T(8,128)(2,1)S(1)} %copy-done.38, bf16[2048,1408]{0,1:T(8,128)(2,1)} %all-gather.8.cloned.1.call-done), kind=kOutput, calls=%fused_computation.17 | convolution fusion | flops 5907677184 | bytes 12845056 | tf_op jit(solution)/shard_map/dot_general | solution.py:28
  485.1 93.2 %attention_backward.1 = (bf16[4,256,640]{2,1,0:T(8,128)(2,1)S(1)}, bf16[256,2048]{1,0:T(8,128)(2,1)S(1)}) custom-call(bf16[4,256,640]{2,1,0:T(8,128)(2,1)S(1)} %bitcast.105, f32[4,256,1]{2,1,0:T(8,128)S(1)} %copy.47.segc_ref, f32[4,1,256]{2,1,0:T(1,128)S(1)} %get-tuple-element.139.segr_ref, bf16[4,64,256]{2,1,0:T(8,128)(2,1)S(1)} %copy-done.11, ...), custom_call_target="tpu_custom_call" | custom-call | bytes 1048576 | tf_op jit(solution)/shard_map/attention_backward/pallas_call | solution.py:470
  578.4 2.5 convolution_bitcast_fusion
  581.4 5.2 fusion.7
  586.6 1.5 copy.54
  588.2 3.5 copy.50
  591.7 3.5 slice.84.w_ref
  595.3 1.3 copy-done.7
  596.6 48.0 %closing.1 = (f32[256,2048]{1,0:T(8,128)S(1)}, f32[8,128]{1,0:T(8,128)S(1)}) custom-call(bf16[4,256,640]{2,1,0:T(8,128)(2,1)S(1)} %copy-done.7, bf16[2048,640]{1,0:T(8,128)(2,1)} %slice.84.w_ref, bf16[256,2048]{1,0:T(8,128)(2,1)S(1)} %bitcast.103, f32[256,2048]{1,0:T(8,128)} %get-tuple-element.84.gres_ref, f32[1,2048]{1,0:T(1,128)S(1)} %slice.77.gain_ref, ...), custom_call_target="tpu_custom_call" | custom-call | bytes 1048576 | tf_op jit(solution)/shard_map/closing/pallas_call | solution.py:1048
  644.8 3.5 all-to-all-start.1
  648.8 5.5 all-to-all-done.1
  654.3 6.4 reduce-scatter.12.cloned.1.call-done
  660.7 3.5 all-to-all-start
  664.2 2.3 convert_bitcast_fusion
  666.5 2.3 convert_element_type.87
  668.8 1.2 convert_element_type.88
  670.0 3.0 copy.56
  673.0 1.0 convert_bitcast_fusion.1
  677.6 1.9 copy.61
  679.5 1.0 copy.71
  680.4 1.3 copy.72
  (116 shorter events, 13.7 us)
Async XLA Ops:
  7.2 5.4 copy-start.33
  7.2 5.4 copy-start.36
  7.2 302.0 %all-gather.4.cloned.1.call-start = ((), (), s32[]{:S(2)}) async-start(), calls=%async_computation.7 | async-start | bytes 6488064 | tf_op jit(solution)/shard_map/all_gather | solution.py:1109
  7.9 313.0 %all-gather.6.cloned.1.call-start = ((), (), s32[]{:S(2)}) async-start(), calls=%async_computation.8 | async-start | bytes 6488064 | tf_op jit(solution)/shard_map/all_gather | solution.py:1110
  8.7 335.5 %all-gather.8.cloned.1.call-start = ((), (), s32[]{:S(2)}) async-start(), calls=%async_computation.9 | async-start | bytes 6488064 | tf_op jit(solution)/shard_map/all_gather | solution.py:1120
  154.8 4.6 copy-start.29
  154.8 3.5 copy-start.22
  158.3 2.4 copy-start.24
  164.1 3.2 copy-start.32
  164.1 64.6 %copy-start = (bf16[1,1,256,2048]{3,2,1,0:T(8,128)(2,1)S(1)}, bf16[1,1,256,2048]{3,2,1,0:T(8,128)(2,1)}, u32[]{:S(2)}) copy-start(bf16[1,1,256,2048]{3,2,1,0:T(8,128)(2,1)} %param.19) | copy-start | bytes 3145732
  164.2 422.5 %reduce-scatter.6.cloned.1.call-start = ((), (), s32[]{:S(2)}) async-start(), calls=%async_computation.10 | async-start | bytes 6488064 | tf_op jit(solution)/shard_map/reduce_scatter | solution.py:1141
  167.6 153.2 %copy-start.14 = (f32[1,2048]{1,0:T(1,128)}, f32[1,2048]{1,0:T(1,128)S(1)}, u32[]{:S(2)}) copy-start(f32[1,2048]{1,0:T(1,128)S(1)} %slice.76.gain_ref) | copy-start | bytes 24580
  167.7 1.2 copy-start.4
  168.9 0.9 copy-start.10
  169.8 0.9 copy-start.12
  170.7 0.7 copy-start.15
  224.9 1.3 copy-start.5
  226.2 0.6 copy-start.17
  226.8 1.9 copy-start.20
  306.9 1.3 copy-start.1
  308.2 1.0 copy-start.2
  320.9 14.4 %copy-start.21 = (bf16[4,256,2048]{2,1,0:T(8,128)(2,1)S(1)}, bf16[4,256,2048]{2,1,0:T(8,128)(2,1)}, u32[]{:S(2)}) copy-start(bf16[4,256,2048]{2,1,0:T(8,128)(2,1)} %copy-done.20) | copy-start | bytes 12582916
  333.7 1.6 copy-start.37
  344.0 242.7 %reduce-scatter.8.cloned.1.call-start = ((), (), s32[]{:S(2)}) async-start(), calls=%async_computation.11 | async-start | bytes 6488064 | tf_op jit(solution)/shard_map/reduce_scatter | solution.py:1141
  344.2 16.9 %copy-start.34 = (bf16[4,256,2048]{2,1,0:T(8,128)(2,1)S(1)}, bf16[4,256,2048]{2,1,0:T(8,128)(2,1)}, u32[]{:S(2)}) copy-start(bf16[4,256,2048]{2,1,0:T(8,128)(2,1)} %get-tuple-element.73) | copy-start | bytes 12582916
  359.6 1.5 copy-start.25
  380.7 206.0 %reduce-scatter.10.cloned.1.call-start = ((), (), s32[]{:S(2)}) async-start(), calls=%async_computation.12 | async-start | bytes 6488064 | tf_op jit(solution)/shard_map/reduce_scatter | solution.py:1141
  381.2 263.5 %reduce-scatter.14.cloned.1.call-start = ((), (), s32[]{:S(2)}) async-start(), calls=%async_computation.14 | async-start | bytes 2359296 | tf_op jit(solution)/shard_map/reduce_scatter | solution.py:1172
  467.1 6.7 copy-start.38
  473.8 11.3 %copy-start.3 = (bf16[4,256,512]{2,1,0:T(8,128)(2,1)S(1)}, bf16[4,256,512]{2,1,0:T(8,128)(2,1)}, u32[]{:S(2)}) copy-start(bf16[4,256,512]{2,1,0:T(8,128)(2,1)} %copy-done.2) | copy-start | bytes 3145732
  473.8 11.3 %copy-start.11 = (bf16[4,64,256]{2,1,0:T(8,128)(2,1)S(1)}, bf16[4,64,256]{2,1,0:T(8,128)(2,1)}, u32[]{:S(2)}) copy-start(bf16[4,64,256]{2,1,0:T(8,128)(2,1)} %constant.81.clone.left_ref) | copy-start | bytes 393220
  473.8 11.3 %copy-start.13 = (bf16[4,64,256]{2,1,0:T(8,128)(2,1)S(1)}, bf16[4,64,256]{2,1,0:T(8,128)(2,1)}, u32[]{:S(2)}) copy-start(bf16[4,64,256]{2,1,0:T(8,128)(2,1)} %constant.82.clone.right_ref) | copy-start | bytes 393220
  473.8 11.3 %copy-start.16 = (f32[8,256]{1,0:T(8,128)S(1)}, f32[8,256]{1,0:T(8,128)}, u32[]{:S(2)}) copy-start(f32[8,256]{1,0:T(8,128)} %constant.83.clone.rows_ref) | copy-start | bytes 24580
  473.8 11.3 %copy-start.18 = (f32[4,8,256]{2,1,0:T(8,128)S(1)}, f32[4,8,256]{2,1,0:T(8,128)}, u32[]{:S(2)}) copy-start(f32[4,8,256]{2,1,0:T(8,128)} %copy-done.17) | copy-start | bytes 98308
  485.1 93.2 %copy-start.35 = (bf16[4,256,2048]{2,1,0:T(8,128)(2,1)S(1)}, bf16[4,256,2048]{2,1,0:T(8,128)(2,1)}, u32[]{:S(2)}) copy-start(bf16[4,256,2048]{2,1,0:T(8,128)(2,1)} %get-tuple-element.80) | copy-start | bytes 12582916
  578.4 2.5 copy-start.8
  578.4 2.5 copy-start.6
  578.4 3.0 copy-start.23
  578.4 3.0 copy-start.30
  588.1 72.6 %reduce-scatter.12.cloned.1.call-start = ((), (), s32[]{:S(2)}) async-start(), calls=%async_computation.13 | async-start | bytes 2949120 | tf_op jit(solution)/shard_map/reduce_scatter | solution.py:1172
  591.7 3.5 copy-start.28
  591.7 3.6 copy-start.19
  595.3 1.3 copy-start.7
  644.7 24.2 %copy-start.27 = (bf16[256,1408]{1,0:T(8,128)(2,1)S(1)}, bf16[256,1408]{1,0:T(8,128)(2,1)}, u32[]{:S(2)}) copy-start(bf16[256,1408]{1,0:T(8,128)(2,1)} %reduce-scatter.10.cloned.1.call-done) | copy-start | bytes 2162692
  644.8 9.5 %all-to-all-start.1 = ((bf16[4,64,512]{2,1,0:T(8,128)(2,1)}), bf16[4,64,512]{2,1,0:T(8,128)(2,1)S(1)}, u32[]{:S(2)}, u32[]{:S(2)}) async-start(bf16[4,64,512]{2,1,0:T(8,128)(2,1)} %bitcast.127), calls=%async_computation.6 | async-start | bytes 524288 | tf_op jit(solution)/shard_map/all_to_all | solution.py:1174
  654.3 14.5 %copy-start.26 = (bf16[4,64,512]{2,1,0:T(8,128)(2,1)}, bf16[4,64,512]{2,1,0:T(8,128)(2,1)S(1)}, u32[]{:S(2)}) copy-start(bf16[4,64,512]{2,1,0:T(8,128)(2,1)S(1)} %all-to-all-done.1) | copy-start | bytes 786436
  660.7 14.2 %all-to-all-start = ((bf16[4,64,640]{2,1,0:T(8,128)(2,1)}), bf16[4,64,640]{2,1,0:T(8,128)(2,1)S(1)}, u32[]{:S(2)}, u32[]{:S(2)}) async-start(bf16[4,64,640]{2,1,0:T(8,128)(2,1)} %bitcast.126), calls=%async_computation.4 | async-start | bytes 655360 | tf_op jit(solution)/shard_map/all_to_all | solution.py:1174
  670.0 9.4 %copy-start.9 = (bf16[256,2048]{1,0:T(8,128)(2,1)S(1)}, bf16[256,2048]{1,0:T(8,128)(2,1)}, u32[]{:S(2)}) copy-start(bf16[256,2048]{1,0:T(8,128)(2,1)} %copy-done.8) | copy-start | bytes 3145732
  (1 other events, 0.6 us)
Sparse Core Ops, SparseCore 0:
  9.7 70.9 all-gather.3
  82.3 77.5 all-gather.5
  164.3 72.3 all-gather.7
  344.1 87.8 reduce-scatter.5
  434.2 63.2 reduce-scatter.7
  499.6 77.9 reduce-scatter.9
  588.3 32.9 reduce-scatter.13
  623.6 37.0 reduce-scatter.11

commit v3 on v2

--- a/solution.py
+++ b/solution.py
@@ -90,6 +90,7 @@
 
 def forward_kernel(
     count,
+    dps,
     heads,
     qkv_ref,
     segc_ref,
@@ -98,11 +99,13 @@
     right_ref,
     rows_ref,
     cot_ref,
+    share_ref,
     att_ref,
     rden_ref,
     carry_ref,
     csum_ref,
     cots_ref,
+    wout_ref,
     send_state,
     send_sum,
     part,
@@ -110,9 +113,15 @@
     recv_sem,
     f_send,
     f_recv,
+    a_send,
+    a_recv,
+    z_send,
+    z_recv,
+    d_send,
+    d_recv,
     local_sem,
 ):
-    place, f = lax.axis_index("seq"), lax.axis_index("feat")
+    place, f, d = lax.axis_index("seq"), lax.axis_index("feat"), lax.axis_index("dp")
     groups, block = qkv_ref.shape[0], qkv_ref.shape[1]
     width = heads * FDIM
     tables = (left_ref, right_ref, rows_ref)
@@ -135,16 +144,35 @@
         for copy in hop(g):
             copy.start()
 
-    chain = [lax.rem(place + 1, count), lax.rem(place + count - 1, count)]
-    greet([{"seq": c} for c in chain] + square_targets(f))
-    stay = pltpu.make_async_copy(cot_ref, cots_ref.at[f], local_sem.at[0])
-    stay.start()
-    cots = [
-        push(cot_ref, cots_ref.at[f], f_send.at[i], f_recv.at[i], {"feat": p})
+    columns = [lax.rem(place + k, count) for k in range(1, count)]
+    others = [lax.rem(d + k, dps) for k in range(1, dps)]
+    stay = [
+        pltpu.make_async_copy(cot_ref, cots_ref.at[f], local_sem.at[0]),
+        pltpu.make_async_copy(share_ref.at[f], wout_ref.at[f, place, d], local_sem.at[1]),
+    ]
+    for c in stay:
+        c.start()
+    greet(
+        square_targets(f) + [{"seq": c} for c in columns] + [{"dp": o} for o in others]
+    )
+    shares = [
+        push(share_ref.at[p], wout_ref.at[f, place, d], a_send.at[i], a_recv.at[i], {"feat": p})
         for i, p in enumerate(peers(f))
     ]
-    for c in cots:
+    for c in shares:
         c.start()
+    gather = SquareGather(cots_ref, f, f_send, f_recv, cot_ref)
+
+    def to_column(k):
+        ref = wout_ref.at[:, place, d]
+        return push(ref, ref, z_send.at[k - 1], z_recv.at[k - 1], {"seq": columns[k - 1]})
+
+    def to_sibling(k):
+        ref = wout_ref.at[:, lax.rem(place + count - k, count), d]
+        return [
+            push(ref, ref, d_send.at[o, k], d_recv.at[o, k], {"dp": other})
+            for o, other in enumerate(others)
+        ]
 
     @pl.when(place == 0)
     def _():
@@ -171,6 +199,32 @@
         return none
 
     lax.fori_loop(0, groups, summarize, 0)
+    gather.start()
+    for c in stay:
+        c.wait()
+    for c in shares:
+        c.wait_recv()
+    for k in range(1, count):
+        to_column(k).start()
+    for c in to_sibling(0):
+        c.start()
+
+    def join(g, none):
+        for copy in hop(g):
+            copy.wait_recv()
+        segr = segr_ref[g]
+        mark = csum_ref[g, heads : heads + 1, 0:1]
+        head, tail = segr[:, 0:1], segr[:, block - 1 : block]
+        whole = ((head == tail) & (head == mark)).astype(f32)
+        for h in range(heads):
+            send_state[g, h] = (
+                send_state[g, h].astype(f32) + whole * carry_ref[g, h].astype(f32)
+            ).astype(bf16)
+            send_sum[g, h : h + 1, :] = (
+                send_sum[g, h : h + 1, :] + whole * csum_ref[g, h : h + 1, :]
+            )
+        send(g)
+        return none
 
     def attend(g, none):
         segc, segr = segc_ref[g], segr_ref[g]
@@ -182,33 +236,35 @@
             c = dot_nt(query, key)
             kernel = jnp.where(allowed, 1.0 + c * (0.25 + c * 0.03125), 0.0).astype(bf16)
             wide = jnp.concatenate([value, jnp.ones_like(value)], axis=1)
-            part[h] = dot(kernel, wide)
-
-        @pl.when(place > 0)
+            part[g, h] = dot(kernel, wide)
+
+        @pl.when((place > 0) & (place < count - 1) & (g == place - 1))
+        def _():
+            lax.fori_loop(0, groups, join, 0)
+
+        return none
+
+    lax.fori_loop(0, groups, attend, 0)
+    for k in range(1, count):
+        to_column(k).wait_recv()
+        for c in to_sibling(k):
+            c.start()
+    gather.relay()
+
+    def carry_on(g, none):
+        segc = segc_ref[g]
+
+        @pl.when(place == count - 1)
         def _():
             for copy in hop(g):
                 copy.wait_recv()
 
         mark = csum_ref[g, heads : heads + 1, 0:1]
-        head, tail = segr[:, 0:1], segr[:, block - 1 : block]
-        whole = ((head == tail) & (head == mark)).astype(f32)
-
-        @pl.when((place > 0) & (place < count - 1))
-        def _():
-            for h in range(heads):
-                send_state[g, h] = (
-                    send_state[g, h].astype(f32) + whole * carry_ref[g, h].astype(f32)
-                ).astype(bf16)
-                send_sum[g, h : h + 1, :] = (
-                    send_sum[g, h : h + 1, :] + whole * csum_ref[g, h : h + 1, :]
-                )
-            send(g)
-
         carried = (segc == mark).astype(f32)
         for h in range(heads):
             phi = features(qkv_ref[g, :, 0:width], h, *tables) * carried
             state = padded_state(carry_ref[g, h])
-            both = part[h]
+            both = part[g, h]
             numer = both[:, :HV] + dot(phi.astype(bf16), state)
             denom = both[:, HV:] + jnp.sum(
                 phi * csum_ref[g, h : h + 1, :], axis=1, keepdims=True
@@ -218,7 +274,7 @@
             rden_ref[g, :, h * HV : (h + 1) * HV] = inverse
         return none
 
-    lax.fori_loop(0, groups, attend, 0)
+    lax.fori_loop(0, groups, carry_on, 0)
 
     @pl.when(place < count - 1)
     def _():
@@ -229,11 +285,15 @@
 
         lax.fori_loop(0, groups, finish, 0)
 
-    for c in cots:
-        c.wait_recv()
-    for c in cots:
+    for k in range(count):
+        for c in to_sibling(k):
+            c.wait_recv()
+            c.wait_send()
+    for k in range(1, count):
+        to_column(k).wait_send()
+    for c in shares:
         c.wait_send()
-    stay.wait()
+    gather.finish()
 
 
 def backward_kernel(
@@ -261,7 +321,8 @@
     recv_sum,
     dkey,
     dvalue,
-    downs,
+    terms,
+    land,
     send_sem,
     recv_sem,
     f_send,
@@ -293,14 +354,9 @@
 
     chain = [lax.rem(place + 1, count), lax.rem(place + count - 1, count)]
     greet([{"seq": c} for c in chain] + square_targets(f))
-    stay = pltpu.make_async_copy(down_ref.at[f], downs.at[3], local_sem.at[0])
-    stay.start()
-    terms = [
-        push(down_ref.at[p], downs.at[i], f_send.at[i], f_recv.at[i], {"feat": p})
-        for i, p in enumerate(peers(f))
-    ]
-    for c in terms:
-        c.start()
+    fill = pltpu.make_async_copy(down_ref, terms, local_sem.at[0])
+    fill.start()
+    ring = SquareSum(terms, land, f, f_send, f_recv)
 
     @pl.when(place == count - 1)
     def _():
@@ -333,6 +389,26 @@
         return none
 
     lax.fori_loop(0, groups, summarize, 0)
+    fill.wait()
+    ring.start_cross()
+    ring.start_near()
+
+    def join(g, none):
+        for copy in hop(g):
+            copy.wait_recv()
+        segr = segr_ref[g]
+        mark = recv_sum[g, heads : heads + 1, 0:1]
+        head, tail = segr[:, 0:1], segr[:, block - 1 : block]
+        whole = ((head == tail) & (head == mark)).astype(f32)
+        for h in range(heads):
+            send_state[g, h] = (
+                send_state[g, h].astype(f32) + whole * recv_state[g, h].astype(f32)
+            ).astype(bf16)
+            send_sum[g, h : h + 1, :] = (
+                send_sum[g, h : h + 1, :] + whole * recv_sum[g, h : h + 1, :]
+            )
+        send(g)
+        return none
 
     def pull(g, none):
         segc, segr = segc_ref[g], segr_ref[g]
@@ -341,7 +417,7 @@
         key_all = qkv_ref[g, :, width : 2 * width]
         carried = (segc == csum_ref[g, heads : heads + 1, 0:1]).astype(f32)
         dquery = jnp.zeros((block, width), f32)
-        dkey[...] = jnp.zeros_like(dkey)
+        dkey_sum = jnp.zeros((block, width), f32)
         for h in range(heads):
             query, key = only_head(query_all, h), only_head(key_all, h)
             value = qkv_ref[g, :, 2 * width + h * HV : 2 * width + (h + 1) * HV]
@@ -351,8 +427,8 @@
             kernel = jnp.where(allowed, 1.0 + c * (0.25 + c * 0.03125), 0.0).astype(bf16)
             grad = jnp.where(allowed, dot_nt(both, wide), 0.0)
             grad_c = (grad * (0.25 + c * 0.0625)).astype(bf16)
-            dvalue[h] = dot_tn(kernel, both[:, :HV])
-            dkey[...] += dot_tn(grad_c, query)
+            dvalue[g, h] = dot_tn(kernel, both[:, :HV])
+            dkey_sum = dkey_sum + dot_tn(grad_c, query)
             dquery = dquery + dot(grad_c, key)
             state = padded_state(carry_ref[g, h])
             gphi = dot_nt(both[:, :HV], state) + both[:, HV : HV + 1].astype(f32) * csum_ref[
@@ -360,41 +436,41 @@
             ]
             dquery = dquery + pull_features(gphi * carried, query_all, h, *tables)
         out_ref[g, :, 0:width] = dquery.astype(bf16)
-
-        @pl.when(place < count - 1)
+        dkey[g] = dkey_sum
+
+        @pl.when((place > 0) & (place < count - 1) & (g == count - 2 - place))
+        def _():
+            lax.fori_loop(0, groups, join, 0)
+
+        return none
+
+    lax.fori_loop(0, groups, pull, 0)
+    ring.relay()
+
+    def carry_back(g, none):
+        segc = segc_ref[g]
+        key_all = qkv_ref[g, :, width : 2 * width]
+
+        @pl.when(place == 0)
         def _():
             for copy in hop(g):
                 copy.wait_recv()
 
         mark = recv_sum[g, heads : heads + 1, 0:1]
-        head, tail = segr[:, 0:1], segr[:, block - 1 : block]
-        whole = ((head == tail) & (head == mark)).astype(f32)
-
-        @pl.when((place > 0) & (place < count - 1))
-        def _():
-            for h in range(heads):
-                send_state[g, h] = (
-                    send_state[g, h].astype(f32) + whole * recv_state[g, h].astype(f32)
-                ).astype(bf16)
-                send_sum[g, h : h + 1, :] = (
-                    send_sum[g, h : h + 1, :] + whole * recv_sum[g, h : h + 1, :]
-                )
-            send(g)
-
         later = (segc == mark).astype(f32)
-        total = dkey[...]
+        total = dkey[g]
         for h in range(heads):
             value = qkv_ref[g, :, 2 * width + h * HV : 2 * width + (h + 1) * HV]
             state = padded_state(recv_state[g, h])
             phi = (features(key_all, h, *tables) * later).astype(bf16)
-            dv = dvalue[h] + dot(phi, state)
+            dv = dvalue[g, h] + dot(phi, state)
             out_ref[g, :, 2 * width + h * HV : 2 * width + (h + 1) * HV] = dv.astype(bf16)
             gphi = (dot_nt(value, state) + recv_sum[g, h : h + 1, :]) * later
             total = total + pull_features(gphi, key_all, h, *tables)
         out_ref[g, :, width : 2 * width] = total.astype(bf16)
         return none
 
-    lax.fori_loop(0, groups, pull, 0)
+    lax.fori_loop(0, groups, carry_back, 0)
 
     @pl.when(place > 0)
     def _():
@@ -405,59 +481,61 @@
 
         lax.fori_loop(0, groups, finish, 0)
 
-    stay.wait()
-    for c in terms:
-        c.wait_recv()
-
-    def add_up(i, none):
-        rows = pl.ds(pl.multiple_of(i * 16, 16), 16)
-        total = res_ref[rows, :]
-        for k in range(4):
-            total = total + downs[k, rows, :].astype(f32)
-        final_ref[rows, :] = total.astype(bf16)
-        return none
-
-    lax.fori_loop(0, block // 16, add_up, 0)
-    for c in terms:
-        c.wait_send()
+    ring.arrive()
+
+    def add_up(rows, total):
+        final_ref[rows, :] = (res_ref[rows, :] + total).astype(bf16)
+
+    by_rows(ring, add_up)
+    ring.finish()
 
 
 def whole_vmem(count):
     return [pl.BlockSpec(memory_space=pltpu.VMEM)] * count
 
 
-def attention_forward(qkv, segc, segr, tables, cot_own, heads):
+def attention_forward(qkv, segc, segr, tables, cot_own, out_share, heads):
     groups, block, _ = qkv.shape
-    count = lax.axis_size("seq")
+    count, dps = lax.axis_size("seq"), lax.axis_size("dp")
+    others = max(dps - 1, 1)
+    parts, rows_each, wide = out_share.shape
+    dma = pltpu.SemaphoreType.DMA
     states = (groups, heads, STATE, HV)
     sums = (groups, 8, LANES)
     return pl.pallas_call(
-        functools.partial(forward_kernel, count, heads),
+        functools.partial(forward_kernel, count, dps, heads),
         out_shape=(
             jax.ShapeDtypeStruct((groups, block, heads * HV), bf16),
             jax.ShapeDtypeStruct((groups, block, heads * HV), f32),
             jax.ShapeDtypeStruct(states, bf16),
             jax.ShapeDtypeStruct(sums, f32),
             jax.ShapeDtypeStruct((groups,) + cot_own.shape, bf16),
+            jax.ShapeDtypeStruct((parts, count, dps, rows_each, wide), bf16),
         ),
-        in_specs=whole_vmem(6) + in_place(1),
-        out_specs=tuple(whole_vmem(4) + in_place(1)),
+        in_specs=whole_vmem(6) + in_place(2),
+        out_specs=tuple(whole_vmem(4) + in_place(2)),
         scratch_shapes=[
             pltpu.VMEM(states, bf16),
             pltpu.VMEM(sums, f32),
-            pltpu.VMEM((heads, block, 2 * HV), f32),
-            pltpu.SemaphoreType.DMA((2, groups)),
-            pltpu.SemaphoreType.DMA((2, groups)),
-            pltpu.SemaphoreType.DMA((3,)),
-            pltpu.SemaphoreType.DMA((3,)),
-            pltpu.SemaphoreType.DMA((1,)),
+            pltpu.VMEM((groups, heads, block, 2 * HV), f32),
+            dma((2, groups)),
+            dma((2, groups)),
+            dma((6,)),
+            dma((6,)),
+            dma((3,)),
+            dma((3,)),
+            dma((count - 1,)),
+            dma((count - 1,)),
+            dma((others, count)),
+            dma((others, count)),
+            dma((2,)),
         ],
         compiler_params=pltpu.CompilerParams(
             collective_id=0, has_side_effects=True, vmem_limit_bytes=40 << 20
         ),
         cost_estimate=pl.CostEstimate(flops=0, bytes_accessed=1 << 20, transcendentals=0),
         name="attention_forward",
-    )(qkv, segc, segr, *tables, cot_own)
+    )(qkv, segc, segr, *tables, cot_own, out_share)
 
 
 def attention_backward(
@@ -481,13 +559,14 @@
             pltpu.VMEM(sums, f32),
             pltpu.VMEM(states, bf16),
             pltpu.VMEM(sums, f32),
-            pltpu.VMEM((block, heads * FDIM), f32),
-            pltpu.VMEM((heads, block, HV), f32),
+            pltpu.VMEM((groups, block, heads * FDIM), f32),
+            pltpu.VMEM((groups, heads, block, HV), f32),
             pltpu.VMEM((groups,) + residual.shape, bf16),
+            pltpu.VMEM((6, block // 2, residual.shape[1]), bf16),
             pltpu.SemaphoreType.DMA((2, groups)),
             pltpu.SemaphoreType.DMA((2, groups)),
-            pltpu.SemaphoreType.DMA((3,)),
-            pltpu.SemaphoreType.DMA((3,)),
+            pltpu.SemaphoreType.DMA((6,)),
+            pltpu.SemaphoreType.DMA((6,)),
             pltpu.SemaphoreType.DMA((1,)),
         ],
         compiler_params=pltpu.CompilerParams(
@@ -525,14 +604,15 @@
 
 
 class SquareGather:
-    def __init__(self, slots, f, send_sem, recv_sem):
+    def __init__(self, slots, f, send_sem, recv_sem, own=None):
         side, above, across = peers(f)
         half = slots.shape[1] // 2
         first, second = pl.ds(0, half), pl.ds(half, half)
 
         def copy(i, slot, rows, to):
             ref = slots.at[slot, rows]
-            return push(ref, ref, send_sem.at[i], recv_sem.at[i], {"feat": to})
+            src = ref if own is None or i > 3 else own.at[rows]
+            return push(src, ref, send_sem.at[i], recv_sem.at[i], {"feat": to})
 
         self.direct = [
             copy(0, f, first, side),
@@ -552,11 +632,22 @@
         self.direct[1].wait_recv()
         self.forward[1].start()
 
-    def finish(self):
-        for c in (self.direct[2], self.direct[3], self.forward[0], self.forward[1]):
+    def near(self):
+        self.direct[2].wait_recv()
+        self.direct[3].wait_recv()
+
+    def far(self):
+        for c in self.forward:
             c.wait_recv()
+
+    def sent(self):
         for c in self.direct + self.forward:
             c.wait_send()
+
+    def finish(self):
+        self.near()
+        self.far()
+        self.sent()
 
 
 class SquareSum:
@@ -620,131 +711,132 @@
             c.wait_send()
 
 
-def opening_kernel(seqs, dps, tok_ref, pack_ref, gain_ref, x_ref, w_ref, g_ref, *sems):
-    x_send, x_recv, a_send, a_recv, z_send, z_recv, d_send, d_recv, local_sem = sems
+def opening_kernel(
+    seqs,
+    dps,
+    tok_ref,
+    query_ref,
+    key_ref,
+    value_ref,
+    one_ref,
+    two_ref,
+    x_ref,
+    w_ref,
+    g_ref,
+    pack,
+    tile,
+    x_send,
+    x_recv,
+    a_send,
+    a_recv,
+    z_send,
+    z_recv,
+    d_send,
+    d_recv,
+    local_sem,
+):
     f, s, d = lax.axis_index("feat"), lax.axis_index("seq"), lax.axis_index("dp")
+    parts, rows_each = pack.shape[0], pack.shape[1]
     near = peers(f)
-    up, down = lax.rem(s + 1, seqs), lax.rem(s + seqs - 1, seqs)
+    columns = [lax.rem(s + k, seqs) for k in range(1, seqs)]
     others = [lax.rem(d + k, dps) for k in range(1, dps)]
+    stay = pltpu.make_async_copy(tok_ref, x_ref.at[f], local_sem.at[0])
+    stay.start()
+    greet(
+        square_targets(f) + [{"seq": c} for c in columns] + [{"dp": o} for o in others]
+    )
+    gather = SquareGather(x_ref, f, x_send, x_recv, tok_ref)
+    gather.start()
+
+    first = 0
+    for ref in (query_ref, key_ref, value_ref):
+        each = ref.shape[1] // parts
+        for p in range(parts):
+            pack[p, :, first : first + each] = ref[:, p * each : (p + 1) * each]
+        first += each
+    tile[...] = jnp.zeros_like(tile)
+    tile[0:1, :rows_each] = one_ref[...].astype(f32)
+    tile[1:2, :rows_each] = two_ref[...].astype(f32)
+    outs = (w_ref, g_ref)
     own = [
-        pltpu.make_async_copy(tok_ref, x_ref.at[f], local_sem.at[0]),
-        pltpu.make_async_copy(pack_ref.at[f], w_ref.at[f, s, d], local_sem.at[1]),
-        pltpu.make_async_copy(gain_ref, g_ref.at[f, s, d], local_sem.at[2]),
+        pltpu.make_async_copy(pack.at[f], w_ref.at[f, s, d], local_sem.at[1]),
+        pltpu.make_async_copy(tile, g_ref.at[f, s, d], local_sem.at[2]),
     ]
     for c in own:
         c.start()
-    greet(
-        square_targets(f)
-        + [{"seq": up}, {"seq": down}]
-        + [{"dp": o} for o in others]
-    )
-
-    shares = []
-    for i, p in enumerate(near):
-        shares.append(
-            push(pack_ref.at[p], w_ref.at[f, s, d], a_send.at[0, i], a_recv.at[0, i], {"feat": p})
-        )
-        shares.append(
-            push(gain_ref, g_ref.at[f, s, d], a_send.at[1, i], a_recv.at[1, i], {"feat": p})
-        )
-    for c in shares:
-        c.start()
+    shares = [
+        [
+            push(pack.at[p], w_ref.at[f, s, d], a_send.at[0, i], a_recv.at[0, i], {"feat": p}),
+            push(tile, g_ref.at[f, s, d], a_send.at[1, i], a_recv.at[1, i], {"feat": p}),
+        ]
+        for i, p in enumerate(near)
+    ]
+    for pair in shares:
+        for c in pair:
+            c.start()
     for c in own:
         c.wait()
-    gather = SquareGather(x_ref, f, x_send, x_recv)
-    gather.start()
-    for c in shares:
-        c.wait_recv()
-
-    def column(src, i, direction, to):
+
+    chunks = (f,) + near
+
+    def to_column(n, k):
         return [
             push(
-                ref.at[:, src, d],
-                ref.at[:, src, d],
-                z_send.at[j, direction, i],
-                z_recv.at[j, direction, i],
-                {"seq": to},
+                ref.at[chunks[n], s, d],
+                ref.at[chunks[n], s, d],
+                z_send.at[j, k - 1, n],
+                z_recv.at[j, k - 1, n],
+                {"seq": columns[k - 1]},
             )
-            for j, ref in enumerate((w_ref, g_ref))
+            for j, ref in enumerate(outs)
         ]
 
-    def sibling(src, i):
+    def to_sibling(n, k):
+        back = lax.rem(s + seqs - k, seqs)
         return [
             push(
-                ref.at[:, src, d],
-                ref.at[:, src, d],
-                d_send.at[j, k, i],
-                d_recv.at[j, k, i],
-                {"dp": o},
+                ref.at[chunks[n], back, d],
+                ref.at[chunks[n], back, d],
+                d_send.at[j, o, k, n],
+                d_recv.at[j, o, k, n],
+                {"dp": other},
             )
-            for j, ref in enumerate((w_ref, g_ref))
-            for k, o in enumerate(others)
+            for j, ref in enumerate(outs)
+            for o, other in enumerate(others)
         ]
 
     def start_all(copies):
         for c in copies:
             c.start()
 
-    def both_ways(i):
-        @pl.when((s >= i) & (s < seqs - 1))
-        def _():
-            start_all(column(lax.rem(s + seqs - i, seqs), i, 0, up))
-
-        @pl.when((s + i < seqs) & (s > 0))
-        def _():
-            start_all(column(lax.rem(s + i, seqs), i, 1, down))
-
-    both_ways(0)
-    start_all(sibling(s, 0))
-    for i in range(1, seqs):
-        @pl.when(s >= i)
-        def _():
-            for c in column(lax.rem(s + seqs - i, seqs), i - 1, 0, up):
+    for n in range(parts):
+        if n:
+            for c in shares[n - 1]:
                 c.wait_recv()
-            start_all(sibling(lax.rem(s + seqs - i, seqs), i))
-
-        @pl.when(s + i < seqs)
-        def _():
-            for c in column(lax.rem(s + i, seqs), i - 1, 1, down):
+        for k in range(1, seqs):
+            start_all(to_column(n, k))
+        start_all(to_sibling(n, 0))
+    for n in range(parts):
+        for k in range(1, seqs):
+            for c in to_column(n, k):
                 c.wait_recv()
-            start_all(sibling(lax.rem(s + i, seqs), seqs - 1 + i))
-
-        if i < seqs - 1:
-            both_ways(i)
-        if i == 1:
-            gather.relay()
-
-    def close(copies):
-        for c in copies:
-            c.wait_recv()
-        for c in copies:
+            start_all(to_sibling(n, k))
+    gather.relay()
+    for n in range(parts):
+        for k in range(seqs):
+            for c in to_sibling(n, k):
+                c.wait_recv()
+    for n in range(parts):
+        for k in range(seqs):
+            for c in to_sibling(n, k):
+                c.wait_send()
+        for k in range(1, seqs):
+            for c in to_column(n, k):
+                c.wait_send()
+    for pair in shares:
+        for c in pair:
             c.wait_send()
-
-    close(sibling(s, 0))
-    for i in range(1, seqs):
-
-        @pl.when(s >= i)
-        def _():
-            close(sibling(lax.rem(s + seqs - i, seqs), i))
-
-        @pl.when(s + i < seqs)
-        def _():
-            close(sibling(lax.rem(s + i, seqs), seqs - 1 + i))
-
-    for i in range(seqs - 1):
-
-        @pl.when((s >= i) & (s < seqs - 1))
-        def _():
-            for c in column(lax.rem(s + seqs - i, seqs), i, 0, up):
-                c.wait_send()
-
-        @pl.when((s + i < seqs) & (s > 0))
-        def _():
-            for c in column(lax.rem(s + i, seqs), i, 1, down):
-                c.wait_send()
-
-    for c in shares:
-        c.wait_send()
+    stay.wait()
     gather.finish()
 
 
@@ -752,10 +844,11 @@
     return [pl.BlockSpec(memory_space=pl.ANY)] * count
 
 
-def opening(own, pack, gain_tile):
+def opening(own, w_query, w_key, w_value, gain_one, gain_two):
     parts, seqs, dps = (lax.axis_size(a) for a in ALL)
     block, width = own.shape
-    _, rows_each, wide = pack.shape
+    rows_each = w_query.shape[0]
+    wide = (w_query.shape[1] + w_key.shape[1] + w_value.shape[1]) // parts
     others = max(dps - 1, 1)
     dma = pltpu.SemaphoreType.DMA
     x_all, w_all, g_all = pl.pallas_call(
@@ -763,25 +856,27 @@
         out_shape=(
             jax.ShapeDtypeStruct((parts, block, width), bf16),
             jax.ShapeDtypeStruct((parts, seqs, dps, rows_each, wide), bf16),
-            jax.ShapeDtypeStruct((parts, seqs, dps) + gain_tile.shape, f32),
+            jax.ShapeDtypeStruct((parts, seqs, dps, 8, HV), f32),
         ),
-        in_specs=in_place(3),
+        in_specs=in_place(1) + whole_vmem(5),
         out_specs=tuple(in_place(3)),
         scratch_shapes=[
+            pltpu.VMEM((parts, rows_each, wide), bf16),
+            pltpu.VMEM((8, HV), f32),
             dma((6,)),
             dma((6,)),
             dma((2, 3)),
             dma((2, 3)),
-            dma((2, 2, seqs)),
-            dma((2, 2, seqs)),
-            dma((2, others, 2 * seqs - 1)),
-            dma((2, others, 2 * seqs - 1)),
+            dma((2, seqs - 1, parts)),
+            dma((2, seqs - 1, parts)),
+            dma((2, others, seqs, parts)),
+            dma((2, others, seqs, parts)),
             dma((3,)),
         ],
         compiler_params=pltpu.CompilerParams(collective_id=2, has_side_effects=True),
         cost_estimate=pl.CostEstimate(flops=0, bytes_accessed=1 << 20, transcendentals=0),
         name="opening",
-    )(own, pack, gain_tile)
+    )(own, w_query, w_key, w_value, gain_one, gain_two)
     gains = g_all[..., :2, :rows_each].transpose(3, 0, 1, 2, 4).reshape(2, width)
     return x_all, w_all.reshape(width, wide), gains
 
@@ -808,7 +903,7 @@
     lax.fori_loop(0, part.shape[2] // tile, one, 0)
 
 
-def summed_products(part, land, f, pairs, send_sem, recv_sem):
+def summed_products(part, land, f, pairs, send_sem, recv_sem, beside=None):
     side, above, across = peers(f)
     ring = SquareSum(part, land, f, send_sem, recv_sem)
     product_tiles(part, across, pairs, 512)
@@ -817,6 +912,8 @@
     product_tiles(part, above, pairs, 512)
     ring.start_near()
     product_tiles(part, f, pairs, 512)
+    if beside is not None:
+        beside()
     ring.relay()
     ring.arrive()
     return ring
@@ -893,20 +990,42 @@
     res_ref,
     cot_ref,
     gain_ref,
+    mixed_hbm,
+    wd_hbm,
+    wo_hbm,
     all_ref,
     gres_ref,
     gsum_ref,
+    down_ref,
+    ga_ref,
     part,
     land,
+    mixed,
+    wd,
+    wo,
     s_send,
     s_recv,
     g_send,
     g_recv,
+    local_sem,
 ):
     f = lax.axis_index("feat")
+    fills = [
+        pltpu.make_async_copy(src, dst, local_sem.at[i])
+        for i, (src, dst) in enumerate(((mixed_hbm, mixed), (wd_hbm, wd), (wo_hbm, wo)))
+    ]
+    for c in fills:
+        c.start()
     greet(square_targets(f))
     pairs = [(gg_ref, wg_ref), (gu_ref, wu_ref)]
-    ring = summed_products(part, land, f, pairs, s_send, s_recv)
+
+    def down_products():
+        for c in fills:
+            c.wait()
+        for p in range(part.shape[0]):
+            product_tiles(down_ref, p, [(mixed, wd)], 512)
+
+    ring = summed_products(part, land, f, pairs, s_send, s_recv, down_products)
     gsum_ref[...] = jnp.zeros_like(gsum_ref)
 
     def finish_rows(rows, grad):
@@ -922,12 +1041,25 @@
     gather = SquareGather(all_ref, f, g_send, g_recv)
     gather.start()
     ring.finish()
+    side, above, across = peers(f)
+
+    def attended_grad(slot):
+        ga_ref[slot] = dot(all_ref[slot], wo[...])
+
+    attended_grad(f)
     gather.relay()
-    gather.finish()
-
-
-def rows_back(grad_gate, grad_up, gate_w, up_w, residual, cot_own, gain_two):
-    parts, block, _ = grad_gate.shape
+    gather.near()
+    attended_grad(side)
+    attended_grad(above)
+    gather.far()
+    attended_grad(across)
+    gather.sent()
+
+
+def rows_back(
+    grad_gate, grad_up, gate_w, up_w, residual, cot_own, gain_two, mixed, down_w, out_w
+):
+    parts, block, hidden = grad_gate.shape
     width = residual.shape[1]
     dma = pltpu.SemaphoreType.DMA
     return pl.pallas_call(
@@ -936,16 +1068,25 @@
             jax.ShapeDtypeStruct((parts, block, width), bf16),
             jax.ShapeDtypeStruct((block, width), f32),
             jax.ShapeDtypeStruct((1, width), f32),
+            jax.ShapeDtypeStruct((parts, block, width), bf16),
+            jax.ShapeDtypeStruct((parts, block, out_w.shape[1]), f32),
         ),
-        in_specs=whole_vmem(7),
-        out_specs=tuple(whole_vmem(3)),
-        scratch_shapes=square_scratch(parts, block, width) + [dma((6,)), dma((6,))],
+        in_specs=whole_vmem(7) + in_place(3),
+        out_specs=tuple(whole_vmem(5)),
+        scratch_shapes=square_scratch(parts, block, width)[:2]
+        + [
+            pltpu.VMEM((parts, block, hidden), bf16),
+            pltpu.VMEM((width, hidden), bf16),
+            pltpu.VMEM(out_w.shape, bf16),
+        ]
+        + [dma((6,))] * 4
+        + [dma((3,))],
         compiler_params=pltpu.CompilerParams(
-            collective_id=4, has_side_effects=True, vmem_limit_bytes=56 << 20
+            collective_id=4, has_side_effects=True, vmem_limit_bytes=60 << 20
         ),
         cost_estimate=pl.CostEstimate(flops=0, bytes_accessed=1 << 20, transcendentals=0),
         name="rows_back",
-    )(grad_gate, grad_up, gate_w, up_w, residual, cot_own, gain_two)
+    )(grad_gate, grad_up, gate_w, up_w, residual, cot_own, gain_two, mixed, down_w, out_w)
 
 
 def closing_kernel(
@@ -1095,22 +1236,13 @@
     own = tokens.reshape(block, width)
     cot_own = cotangent.reshape(block, width)
 
-    def by_share(w, per):
-        return w.reshape(rows_each, parts, heads * per).transpose(1, 0, 2)
-
-    pack = jnp.concatenate(
-        [by_share(w_query, FDIM), by_share(w_key, FDIM), by_share(w_value, HV), by_share(w_out.T, HV)],
-        axis=2,
-    )
-    pack_width = pack.shape[2]
-    gain_tile = jnp.zeros((8, HV), f32)
-    gain_tile = gain_tile.at[0, :rows_each].set(norm1_gain.astype(f32))
-    gain_tile = gain_tile.at[1, :rows_each].set(norm2_gain.astype(f32))
+    out_share = w_out.T.reshape(rows_each, parts, heads * HV).transpose(1, 0, 2)
     gate_w = lax.all_gather(w_gate, ("seq", "dp"), axis=0, tiled=True)
     up_w = lax.all_gather(w_up, ("seq", "dp"), axis=0, tiled=True)
-    x_all, attn_w, gains = opening(own, pack, gain_tile)
-    qkv_width = pack_width - heads * HV
-    qkv_w, out_w = attn_w[:, :qkv_width], attn_w[:, qkv_width:]
+    x_all, qkv_w, gains = opening(
+        own, w_query, w_key, w_value, norm1_gain[None], norm2_gain[None]
+    )
+    qkv_width = qkv_w.shape[1]
     gain_one, gain_two = gains[0:1], gains[1:2]
 
     x_wide = x_all.astype(f32).reshape(rows_total, width)
@@ -1121,7 +1253,10 @@
     segment = segments.reshape(parts, block).astype(f32)
     segc, segr = segment[:, :, None], segment[:, None, :]
     tables = feature_tables(heads)
-    att, rden, carry, csum, cot_all = attention_forward(qkv, segc, segr, tables, cot_own, heads)
+    att, rden, carry, csum, cot_all, out_w = attention_forward(
+        qkv, segc, segr, tables, cot_own, out_share, heads
+    )
+    out_w = out_w.reshape(width, heads * HV)
     cot_all = cot_all.reshape(rows_total, width)
     rows_all, residual = branch_step(att, out_w, own, gain_two)
     rows_all = rows_all.reshape(rows_total, width)
@@ -1132,7 +1267,6 @@
     silu = gate_out * sig
     mixed = (silu * up_out).astype(bf16)
     mixed, cot_late = lax.optimization_barrier((mixed, cot_all))
-    down = dot_nt(mixed, down_w).astype(bf16).reshape(parts, block, width)
     grad_mixed = dot(cot_late, down_w)
     grad_gate = (grad_mixed * up_out * sig * (1.0 + gate_out * (1.0 - sig))).astype(bf16)
     grad_up = (grad_mixed * silu).astype(bf16)
@@ -1149,7 +1283,7 @@
     down_sum, gate_sum, up_sum = summed(down_term), summed(gate_term), summed(up_term)
 
     by_device = (parts, block, -1)
-    branch_all, grad_residual, gain_two_sum = rows_back(
+    branch_all, grad_residual, gain_two_sum, down, ga = rows_back(
         grad_gate.reshape(by_device),
         grad_up.reshape(by_device),
         gate_w,
@@ -1157,9 +1291,11 @@
         residual,
         cot_own,
         gain_two,
+        mixed.reshape(by_device),
+        down_w,
+        out_w,
     )
     branch_all = branch_all.reshape(rows_total, width)
-    ga = dot(branch_all, out_w).reshape(parts, block, heads * HV)
     dqkv, output = attention_backward(
         qkv, segc, segr, tables, att, rden, carry, csum, ga, down, residual, heads
     )

time: 696 us -> 671 us (0.964)
  waiting for transfers between devices: 13.9 us -> 66.8 us
  Pallas kernels: 498 us -> 447 us
  matrix products: 97 us -> 81.4 us
  local copies, waits for them, and re-layouts: 46 us -> 34.6 us
    reduce_scatter x3, waiting for transfers between devices: 0.01 us -> 50.6 us  [summed(): lax.psum_scatter(term, ('seq', 'dp'), scatter_dimension=0, tiled=True)]
    pallas_call x1, Pallas kernels: 140 us -> 89.8 us  [opening(): pl.pallas_call(functools.partial(opening_kernel, seqs, dps), out_shape=(j...]
    pallas_call x1, Pallas kernels: 93.2 us -> 70.5 us  [attention_backward(): pl.pallas_call(functools.partial(backward_kernel, count, heads), out_shap...]
    pallas_call x1, Pallas kernels: 53.5 us -> 69 us  [attention_forward(): pl.pallas_call(functools.partial(forward_kernel, count, dps, heads), out_...]
    dot_general x1 -> x0, matrix products: 11.2 us -> none  [dot_nt(): lax.dot_general(a, b, (((1,), (1,)), ((), ())), preferred_element_type=f32)]
    dot_general x5 -> x4, matrix products: 50 us -> 43.4 us  [dot(): lax.dot_general(a, b, (((1,), (0,)), ((), ())), preferred_element_type=f32)]
    unnamed x83 -> x76, local copies, waits for them, and re-layouts: 23.4 us -> 21.2 us
  transfers between devices with their start and end apart: 10 -> 10, of which waited for: 2 -> 3; matrix products, arithmetic and copies ran while one was open for 19% -> 11% of each run, Pallas kernels for 72% -> 67%
where the time goes in v3:
time: 671 us; the launch traced here: 663 us
  Pallas kernels  447 us (67%)
  matrix products  81.4 us (12%)
  waiting for transfers between devices  66.8 us (10%)
  local copies, waits for them, and re-layouts  34.6 us (5%)
  between operations  14.8 us (2%)
  other arithmetic  11.2 us (2%)
  starting transfers between devices  7.4 us (1%)
    pallas_call x1, Pallas kernels, opening(): pl.pallas_call(functools.partial(opening_kernel, seqs, dps), out_shape=(j...  89.8 us
    pallas_call x1, Pallas kernels, rows_back(): pl.pallas_call(rows_back_kernel, out_shape=(jax.ShapeDtypeStruct((parts,...  87.5 us
    pallas_call x1, Pallas kernels, branch_step(): pl.pallas_call(branch_kernel, out_shape=(jax.ShapeDtypeStruct((parts, blo...  78.6 us
    pallas_call x1, Pallas kernels, attention_backward(): pl.pallas_call(functools.partial(backward_kernel, count, heads), out_shap...  70.5 us
    pallas_call x1, Pallas kernels, attention_forward(): pl.pallas_call(functools.partial(forward_kernel, count, dps, heads), out_...  69 us
    pallas_call x1, Pallas kernels, closing(): pl.pallas_call(functools.partial(closing_kernel, seqs, dps), out_shape=(j...  51.6 us
    reduce_scatter x3, waiting for transfers between devices, summed(): lax.psum_scatter(term, ('seq', 'dp'), scatter_dimension=0, tiled=True)  50.6 us
    dot_general x4, matrix products, dot(): lax.dot_general(a, b, (((1,), (0,)), ((), ())), preferred_element_type=f32)  43.4 us
  transfers between devices with their start and end apart: 10, of which 3 were waited for; matrix products, arithmetic and copies ran while one was open for 11% of the time, Pallas kernels for 67%

profile of v3, /device:TPU:0, one launch (start us, length us, event | category | flops | bytes accessed | tf_op | source)
XLA Modules:
  0.0 663.4 jit_solution(134470336410377958)
XLA Ops:
  8.7 89.8 %opening.1 = (bf16[4,256,2048]{2,1,0:T(8,128)(2,1)}, bf16[4,4,2,64,640]{4,3,2,1,0:T(8,128)(2,1)}, f32[4,4,2,8,128]{4,3,2,1,0:T(8,128)}) custom-call(bf16[256,2048]{1,0:T(8,128)(2,1)} %bitcast.81, bf16[64,256]{1,0:T(8,128)(2,1)} %query_ref.1, bf16[64,256]{1,0:T(8,128)(2,1)} %key_ref.1, bf16[64,2048]{1,0:T(8,128)(2,1)} %value_ref.1, bf16[1,64]{1,0:T(2,128)(2,1)} %bitcast.112, ...), custom_call_target="tpu_custom_call" | custom-call | bytes 1048576 | tf_op jit(solution)/shard_map/opening/pallas_call | solution.py:854
  98.5 0.9 slice_bitcast_fusion.3
  100.1 3.3 fusion
  103.9 1.0 fusion.2
  105.0 1.5 copy-done.28
  106.5 3.4 convolution_convert_fusion.3
  110.0 2.3 copy.43
  112.8 1.2 copy-done.5
  114.0 69.0 %attention_forward.1 = (bf16[4,256,512]{2,1,0:T(8,128)(2,1)S(1)}, f32[4,256,512]{2,1,0:T(8,128)S(1)}, bf16[4,4,160,128]{3,2,1,0:T(8,128)(2,1)S(1)}, f32[4,8,256]...) custom-call(bf16[4,256,640]{2,1,0:T(8,128)(2,1)S(1)} %bitcast.86, ...), custom_call_target="tpu_custom_call" | custom-call | bytes 1048576 | tf_op jit(solution)/shard_map/attention_forward/pallas_call | solution.py:505
  183.0 1.3 copy-done.2
  184.4 1.3 copy-done.6
  185.7 0.8 copy-done.11
  186.5 2.0 copy-done.23
  188.5 78.6 %branch_step.1 = (bf16[4,256,2048]{2,1,0:T(8,128)(2,1)}, f32[256,2048]{1,0:T(8,128)S(1)}) custom-call(bf16[4,256,512]{2,1,0:T(8,128)(2,1)S(1)} %get-tuple-element.48.att_ref, bf16[2048,512]{1,0:T(8,128)(2,1)} %bitcast.84, bf16[256,2048]{1,0:T(8,128)(2,1)S(1)} %bitcast.82, f32[1,2048]{1,0:T(1,128)S(1)} %slice.33.gain_ref), custom_call_target="tpu_custom_call" | custom-call | bytes 1048576 | tf_op jit(solution)/shard_map/branch_step/pallas_call | solution.py:968
  267.1 1.3 copy-done.1
  268.5 1.0 copy-done.3
  269.5 11.7 %fusion.5 = f32[1024,1408]{1,0:T(8,128)} fusion(bf16[1024,2048]{1,0:T(8,128)(2,1)} %bitcast.114, bf16[2048,1408]{1,0:T(8,128)(2,1)} %all-gather.4.cloned.1.call-done.wg_ref), kind=kOutput, calls=%fused_computation.31 | convolution fusion | flops 5905580032 | bytes 15728640 | tf_op jit(solution)/shard_map/dot_general | solution.py:24
  281.2 13.1 %multiply_convert_fusion.2 = (bf16[1024,1408]{1,0:T(8,128)(2,1)}, f32[1024,1408]{1,0:T(8,128)}) fusion(f32[1024,1408]{1,0:T(8,128)} %fusion.5, bf16[1024,2048]{1,0:T(8,128)(2,1)} %bitcast.115, bf16[2048,1408]{1,0:T(8,128)(2,1)} %all-gather.6.cloned.1.call-done.wu_ref), kind=kOutput, calls=%fused_computation.10 | convolution fusion | flops 5914230784 | bytes 24379392 | tf_op jit(solution)/shard_map/dot_general | solution.py:24
  294.3 15.2 %multiply_convert_fusion = (bf16[1024,1408]{1,0:T(8,128)(2,1)S(1)}, bf16[1024,1408]{1,0:T(8,128)(2,1)}) fusion(f32[1024,1408]{1,0:T(8,128)} %fusion.5, f32[1024,1408]{1,0:T(8,128)} %get-tuple-element.122, bf16[1024,2048]{1,0:T(8,128)(2,1)} %bitcast.93, bf16[2048,1408]{1,0:T(8,128)(2,1)} %all-gather.8.cloned.1.call-done.wd_hbm), kind=kOutput, calls=%fused_computation.8 | convolution fusion | flops 5924323328 | bytes 27262976 | tf_op jit(solution)/shard_map/dot_general | solution.py:24
  309.5 1.5 copy-done.27
  311.0 8.7 %convolution_convert_fusion.1 = bf16[2048,1408]{1,0:T(8,128)(2,1)} fusion(bf16[1024,2048]{1,0:T(8,128)(2,1)S(1)} %bitcast.117, bf16[1024,1408]{1,0:T(8,128)(2,1)S(1)} %get-tuple-element.58), kind=kOutput, calls=%fused_computation.6 | convolution fusion | flops 5908463616 | bytes 12845056 | tf_op jit(solution)/shard_map/dot_general | solution.py:32
  319.7 11.1 %convolution_convert_fusion.2 = bf16[2048,1408]{1,0:T(8,128)(2,1)} fusion(bf16[1024,2048]{1,0:T(8,128)(2,1)} %bitcast.116, bf16[1024,1408]{1,0:T(8,128)(2,1)} %get-tuple-element.57), kind=kOutput, calls=%fused_computation.7 | convolution fusion | flops 5908463616 | bytes 12845056 | tf_op jit(solution)/shard_map/dot_general | solution.py:32
  331.5 11.0 %convolution_convert_fusion = bf16[2048,1408]{1,0:T(8,128)(2,1)} fusion(bf16[1024,2048]{1,0:T(8,128)(2,1)} %bitcast.94, bf16[1024,1408]{1,0:T(8,128)(2,1)} %get-tuple-element.60), kind=kOutput, calls=%fused_computation.5 | convolution fusion | flops 5908463616 | bytes 12845056 | tf_op jit(solution)/shard_map/dot_general | solution.py:32
  342.6 87.5 %rows_back.1 = (bf16[4,256,2048]{2,1,0:T(8,128)(2,1)}, f32[256,2048]{1,0:T(8,128)}, f32[1,2048]{1,0:T(1,128)}, bf16[4,256,2048]{2,1,0:T(8,128)(2,1)}, f32[4,256,512]{2,1,0:T(8,128)}) custom-call(bf16[4,256,1408]{2,1,0:T(8,128)(2,1)} %bitcast.101, bf16[4,256,1408]{2,1,0:T(8,128)(2,1)} %bitcast.100, bf16[2048,1408]{1,0:T(8,128)(2,1)} %all-gather.4.cloned.1.call-done.wg_ref, ...), custom_call_target="tpu_custom_call" | custom-call | bytes 1048576 | tf_op jit(solution)/shard_map/rows_back/pallas_call | solution.py:1065
  430.2 1.2 copy-done.4
  431.4 70.5 %attention_backward.1 = (bf16[4,256,640]{2,1,0:T(8,128)(2,1)S(1)}, bf16[256,2048]{1,0:T(8,128)(2,1)S(1)}) custom-call(bf16[4,256,640]{2,1,0:T(8,128)(2,1)S(1)} %bitcast.87, f32[4,256,1]{2,1,0:T(8,128)S(1)} %copy.44.segc_ref, f32[4,1,256]{2,1,0:T(1,128)S(1)} %get-tuple-element.119.segr_ref, bf16[4,64,256]{2,1,0:T(8,128)(2,1)S(1)} %copy-done.16, ...), custom_call_target="tpu_custom_call" | custom-call | bytes 1048576 | tf_op jit(solution)/shard_map/attention_backward/pallas_call | solution.py:548
  502.0 2.4 convolution_bitcast_fusion.1
  505.0 4.9 convolution_bitcast_fusion
  509.9 50.6 %reduce-scatter.6.cloned.1.call-done = bf16[256,1408]{1,0:T(8,128)(2,1)} async-done(((bf16[2048,1408]{1,0:T(8,128)(2,1)}), bf16[256,1408]{1,0:T(8,128)(2,1)}) %reduce-scatter.6.cloned.1.call-update) | async-done | bytes 720912 | tf_op jit(solution)/shard_map/reduce_scatter | solution.py:1275
  560.5 1.5 copy.51
  562.1 3.5 copy.47
  565.7 1.3 copy-done.8
  567.0 51.6 %closing.1 = (f32[256,2048]{1,0:T(8,128)S(1)}, f32[8,128]{1,0:T(8,128)S(1)}) custom-call(bf16[4,256,640]{2,1,0:T(8,128)(2,1)S(1)} %copy-done.8, bf16[2048,640]{1,0:T(8,128)(2,1)} %bitcast.102, bf16[256,2048]{1,0:T(8,128)(2,1)S(1)} %bitcast.83, f32[256,2048]{1,0:T(8,128)} %get-tuple-element.65.gres_ref, f32[1,2048]{1,0:T(1,128)S(1)} %slice.34.gain_ref, ...), custom_call_target="tpu_custom_call" | custom-call | bytes 1048576 | tf_op jit(solution)/shard_map/closing/pallas_call | solution.py:1189
  618.7 3.5 all-to-all-start.1
  622.8 5.5 all-to-all-done.1
  628.3 8.8 %reduce-scatter.12.cloned.1.call-done = bf16[256,640]{1,0:T(8,128)(2,1)} async-done(((bf16[2048,640]{1,0:T(8,128)(2,1)}), bf16[256,640]{1,0:T(8,128)(2,1)}) %reduce-scatter.12.cloned.1.call-update) | async-done | bytes 327696 | tf_op jit(solution)/shard_map/reduce_scatter | solution.py:1308
  637.0 3.5 all-to-all-start
  640.6 2.3 convert_bitcast_fusion
  642.9 2.3 convert_element_type.82
  645.2 1.2 convert_element_type.83
  646.4 3.0 copy.53
  649.4 1.0 convert_bitcast_fusion.1
  650.4 0.8 copy.58
  651.4 0.8 copy.57
  652.4 0.8 reshape.162
  653.2 0.8 reshape.161
  654.0 1.0 copy.63
  655.0 1.3 copy.64
  (99 shorter events, 5.7 us)
Async XLA Ops:
  7.2 262.3 %all-gather.4.cloned.1.call-start = ((), (), s32[]{:S(2)}) async-start(), calls=%async_computation.7 | async-start | bytes 6488064 | tf_op jit(solution)/shard_map/all_gather | solution.py:1240
  7.9 273.3 %all-gather.6.cloned.1.call-start = ((), (), s32[]{:S(2)}) async-start(), calls=%async_computation.8 | async-start | bytes 6488064 | tf_op jit(solution)/shard_map/all_gather | solution.py:1241
  8.7 285.6 %all-gather.8.cloned.1.call-start = ((), (), s32[]{:S(2)}) async-start(), calls=%async_computation.9 | async-start | bytes 6488064 | tf_op jit(solution)/shard_map/all_gather | solution.py:1252
  100.1 3.8 copy-start.24
  103.9 2.6 copy-start.28
  105.0 5.0 copy-start.25
  106.5 5.9 copy-start.31
  106.5 5.9 copy-start.33
  106.5 6.3 copy-start.13
  106.5 6.3 copy-start.15
  106.5 6.3 copy-start.18
  110.0 78.5 %copy-start = (bf16[1,1,256,2048]{3,2,1,0:T(8,128)(2,1)S(1)}, bf16[1,1,256,2048]{3,2,1,0:T(8,128)(2,1)}, u32[]{:S(2)}) copy-start(bf16[1,1,256,2048]{3,2,1,0:T(8,128)(2,1)} %param.15) | copy-start | bytes 3145732
  112.3 397.6 %reduce-scatter.8.cloned.1.call-start = ((), (), s32[]{:S(2)}) async-start(), calls=%async_computation.11 | async-start | bytes 6488064 | tf_op jit(solution)/shard_map/reduce_scatter | solution.py:1275
  112.8 168.4 %copy-start.17 = (f32[1,2048]{1,0:T(1,128)}, f32[1,2048]{1,0:T(1,128)S(1)}, u32[]{:S(2)}) copy-start(f32[1,2048]{1,0:T(1,128)S(1)} %slice.33.gain_ref) | copy-start | bytes 24580
  112.8 1.2 copy-start.5
  183.0 1.3 copy-start.2
  184.4 1.3 copy-start.6
  185.7 0.8 copy-start.11
  186.5 2.0 copy-start.23
  188.5 92.7 %copy-start.20 = (f32[4,8,256]{2,1,0:T(8,128)}, f32[4,8,256]{2,1,0:T(8,128)S(1)}, u32[]{:S(2)}) copy-start(f32[4,8,256]{2,1,0:T(8,128)S(1)} %get-tuple-element.51.csum_ref) | copy-start | bytes 98308
  267.1 1.3 copy-start.1
  268.5 1.0 copy-start.3
  294.3 16.7 %copy-start.35 = (bf16[4,256,2048]{2,1,0:T(8,128)(2,1)S(1)}, bf16[4,256,2048]{2,1,0:T(8,128)(2,1)}, u32[]{:S(2)}) copy-start(bf16[4,256,2048]{2,1,0:T(8,128)(2,1)} %get-tuple-element.53) | copy-start | bytes 12582916
  309.5 1.5 copy-start.27
  330.9 179.1 %reduce-scatter.10.cloned.1.call-start = ((), (), s32[]{:S(2)}) async-start(), calls=%async_computation.12 | async-start | bytes 6488064 | tf_op jit(solution)/shard_map/reduce_scatter | solution.py:1275
  331.4 229.0 %reduce-scatter.6.cloned.1.call-start = ((), (), s32[]{:S(2)}) async-start(), calls=%async_computation.10 | async-start | bytes 6488064 | tf_op jit(solution)/shard_map/reduce_scatter | solution.py:1275
  342.5 276.2 %reduce-scatter.14.cloned.1.call-start = ((), (), s32[]{:S(2)}) async-start(), calls=%async_computation.14 | async-start | bytes 2359296 | tf_op jit(solution)/shard_map/reduce_scatter | solution.py:1308
  342.5 87.6 %copy-start.12 = (bf16[4,4,160,128]{3,2,1,0:T(8,128)(2,1)S(1)}, bf16[4,4,160,128]{3,2,1,0:T(8,128)(2,1)}, u32[]{:S(2)}) copy-start(bf16[4,4,160,128]{3,2,1,0:T(8,128)(2,1)} %copy-done.11) | copy-start | bytes 1966084
  342.5 87.6 %copy-start.14 = (bf16[4,64,256]{2,1,0:T(8,128)(2,1)S(1)}, bf16[4,64,256]{2,1,0:T(8,128)(2,1)}, u32[]{:S(2)}) copy-start(bf16[4,64,256]{2,1,0:T(8,128)(2,1)} %constant.26.clone.right_ref) | copy-start | bytes 393220
  342.6 87.6 %copy-start.16 = (bf16[4,64,256]{2,1,0:T(8,128)(2,1)S(1)}, bf16[4,64,256]{2,1,0:T(8,128)(2,1)}, u32[]{:S(2)}) copy-start(bf16[4,64,256]{2,1,0:T(8,128)(2,1)} %constant.25.clone.left_ref) | copy-start | bytes 393220
  342.6 87.6 %copy-start.19 = (f32[8,256]{1,0:T(8,128)S(1)}, f32[8,256]{1,0:T(8,128)}, u32[]{:S(2)}) copy-start(f32[8,256]{1,0:T(8,128)} %constant.27.clone.rows_ref) | copy-start | bytes 24580
  342.6 87.6 %copy-start.21 = (f32[4,8,256]{2,1,0:T(8,128)S(1)}, f32[4,8,256]{2,1,0:T(8,128)}, u32[]{:S(2)}) copy-start(f32[4,8,256]{2,1,0:T(8,128)} %copy-done.20) | copy-start | bytes 98308
  430.2 1.2 copy-start.4
  431.4 70.6 %copy-start.34 = (bf16[4,256,2048]{2,1,0:T(8,128)(2,1)S(1)}, bf16[4,256,2048]{2,1,0:T(8,128)(2,1)}, u32[]{:S(2)}) copy-start(bf16[4,256,2048]{2,1,0:T(8,128)(2,1)} %get-tuple-element.69) | copy-start | bytes 12582916
  502.0 2.4 copy-start.9
  502.0 2.4 copy-start.7
  502.0 3.0 copy-start.26
  562.0 3.6 copy-start.32
  562.0 3.7 copy-start.22
  562.0 75.0 %reduce-scatter.12.cloned.1.call-start = ((), (), s32[]{:S(2)}) async-start(), calls=%async_computation.13 | async-start | bytes 2949120 | tf_op jit(solution)/shard_map/reduce_scatter | solution.py:1308
  565.7 1.3 copy-start.8
  618.6 26.6 %copy-start.30 = (bf16[256,1408]{1,0:T(8,128)(2,1)S(1)}, bf16[256,1408]{1,0:T(8,128)(2,1)}, u32[]{:S(2)}) copy-start(bf16[256,1408]{1,0:T(8,128)(2,1)} %reduce-scatter.10.cloned.1.call-done) | copy-start | bytes 2162692
  618.7 9.5 %all-to-all-start.1 = ((bf16[4,64,512]{2,1,0:T(8,128)(2,1)}), bf16[4,64,512]{2,1,0:T(8,128)(2,1)S(1)}, u32[]{:S(2)}, u32[]{:S(2)}) async-start(bf16[4,64,512]{2,1,0:T(8,128)(2,1)} %bitcast.110), calls=%async_computation.6 | async-start | bytes 524288 | tf_op jit(solution)/shard_map/all_to_all | solution.py:1310
  628.3 16.9 %copy-start.29 = (bf16[4,64,512]{2,1,0:T(8,128)(2,1)}, bf16[4,64,512]{2,1,0:T(8,128)(2,1)S(1)}, u32[]{:S(2)}) copy-start(bf16[4,64,512]{2,1,0:T(8,128)(2,1)S(1)} %all-to-all-done.1) | copy-start | bytes 786436
  637.0 14.2 %all-to-all-start = ((bf16[4,64,640]{2,1,0:T(8,128)(2,1)}), bf16[4,64,640]{2,1,0:T(8,128)(2,1)S(1)}, u32[]{:S(2)}, u32[]{:S(2)}) async-start(bf16[4,64,640]{2,1,0:T(8,128)(2,1)} %bitcast.108), calls=%async_computation.4 | async-start | bytes 655360 | tf_op jit(solution)/shard_map/all_to_all | solution.py:1310
  646.4 7.6 %copy-start.10 = (bf16[256,2048]{1,0:T(8,128)(2,1)S(1)}, bf16[256,2048]{1,0:T(8,128)(2,1)}, u32[]{:S(2)}) copy-start(bf16[256,2048]{1,0:T(8,128)(2,1)} %copy-done.9) | copy-start | bytes 3145732
Sparse Core Ops, SparseCore 0:
  9.7 85.5 all-gather.3
  96.8 83.3 all-gather.5
  182.5 63.6 all-gather.7
  331.0 84.1 reduce-scatter.7
  417.3 77.9 reduce-scatter.9
  497.5 62.9 reduce-scatter.5
  563.4 34.1 reduce-scatter.13
  599.9 37.1 reduce-scatter.11

commit v4 on v3

--- a/solution.py
+++ b/solution.py
@@ -245,10 +245,6 @@
         return none
 
     lax.fori_loop(0, groups, attend, 0)
-    for k in range(1, count):
-        to_column(k).wait_recv()
-        for c in to_sibling(k):
-            c.start()
     gather.relay()
 
     def carry_on(g, none):
@@ -285,6 +281,10 @@
 
         lax.fori_loop(0, groups, finish, 0)
 
+    for k in range(1, count):
+        to_column(k).wait_recv()
+        for c in to_sibling(k):
+            c.start()
     for k in range(count):
         for c in to_sibling(k):
             c.wait_recv()
@@ -298,6 +298,7 @@
 
 def backward_kernel(
     count,
+    dps,
     heads,
     qkv_ref,
     segc_ref,
@@ -312,8 +313,10 @@
     ga_ref,
     down_ref,
     res_ref,
+    oterm_ref,
     out_ref,
     final_ref,
+    ograd_ref,
     gn,
     send_state,
     send_sum,
@@ -328,8 +331,9 @@
     f_send,
     f_recv,
     local_sem,
+    *sum_scratch,
 ):
-    place, f = lax.axis_index("seq"), lax.axis_index("feat")
+    place, f, d = lax.axis_index("seq"), lax.axis_index("feat"), lax.axis_index("dp")
     groups, block = qkv_ref.shape[0], qkv_ref.shape[1]
     width = heads * FDIM
     tables = (left_ref, right_ref, rows_ref)
@@ -352,8 +356,13 @@
         for copy in hop(g):
             copy.start()
 
-    chain = [lax.rem(place + 1, count), lax.rem(place + count - 1, count)]
-    greet([{"seq": c} for c in chain] + square_targets(f))
+    columns = [lax.rem(place + k, count) for k in range(1, count)]
+    others = [lax.rem(d + k, dps) for k in range(1, dps)]
+    greet(
+        square_targets(f) + [{"seq": c} for c in columns] + [{"dp": o} for o in others]
+    )
+    rows_sum = row_sum(oterm_ref, sum_scratch, f, place, d, count, dps)
+    rows_sum.start()
     fill = pltpu.make_async_copy(down_ref, terms, local_sem.at[0])
     fill.start()
     ring = SquareSum(terms, land, f, f_send, f_recv)
@@ -392,6 +401,7 @@
     fill.wait()
     ring.start_cross()
     ring.start_near()
+    rows_sum.over_seq()
 
     def join(g, none):
         for copy in hop(g):
@@ -446,6 +456,7 @@
 
     lax.fori_loop(0, groups, pull, 0)
     ring.relay()
+    rows_sum.over_feat()
 
     def carry_back(g, none):
         segc = segc_ref[g]
@@ -488,6 +499,11 @@
 
     by_rows(ring, add_up)
     ring.finish()
+    rows_sum.arrive()
+    wide = heads * HV
+    for p in range(rows_sum.parts):
+        ograd_ref[:, p * wide : (p + 1) * wide] = rows_sum.shares[p].astype(f32)
+    rows_sum.finish()
 
 
 def whole_vmem(count):
@@ -539,20 +555,22 @@
 
 
 def attention_backward(
-    qkv, segc, segr, tables, att, rden, carry, csum, ga, down, residual, heads
+    qkv, segc, segr, tables, att, rden, carry, csum, ga, down, residual, out_term, heads
 ):
     groups, block, wide = qkv.shape
-    count = lax.axis_size("seq")
+    count, dps = lax.axis_size("seq"), lax.axis_size("dp")
+    rows_each = out_term.shape[3]
     states = (groups, heads, STATE, HV)
     sums = (groups, 8, LANES)
     return pl.pallas_call(
-        functools.partial(backward_kernel, count, heads),
+        functools.partial(backward_kernel, count, dps, heads),
         out_shape=(
             jax.ShapeDtypeStruct((groups, block, wide), bf16),
             jax.ShapeDtypeStruct(residual.shape, bf16),
+            jax.ShapeDtypeStruct((rows_each, HEADS * HV), f32),
         ),
-        in_specs=whole_vmem(11) + in_place(1) + whole_vmem(1),
-        out_specs=tuple(whole_vmem(2)),
+        in_specs=whole_vmem(11) + in_place(1) + whole_vmem(2),
+        out_specs=tuple(whole_vmem(3)),
         scratch_shapes=[
             pltpu.VMEM((groups, heads, block, 2 * HV), bf16),
             pltpu.VMEM(states, bf16),
@@ -568,13 +586,14 @@
             pltpu.SemaphoreType.DMA((6,)),
             pltpu.SemaphoreType.DMA((6,)),
             pltpu.SemaphoreType.DMA((1,)),
-        ],
+        ]
+        + row_sum_scratch(out_term.shape),
         compiler_params=pltpu.CompilerParams(
             collective_id=1, has_side_effects=True, vmem_limit_bytes=48 << 20
         ),
         cost_estimate=pl.CostEstimate(flops=0, bytes_accessed=1 << 20, transcendentals=0),
         name="attention_backward",
-    )(qkv, segc, segr, *tables, att, rden, carry, csum, ga, down, residual)
+    )(qkv, segc, segr, *tables, att, rden, carry, csum, ga, down, residual, out_term)
 
 
 def peers(f):
@@ -709,6 +728,96 @@
     def finish(self):
         for c in self.cross + self.near + self.late:
             c.wait_send()
+
+
+class RowSum:
+    def __init__(self, term, acc, shares, lands, sems, f, s, d, seqs, dps):
+        self.term, self.acc, self.shares, self.lands = term, acc, shares, lands
+        self.f, self.s, self.d = f, s, d
+        self.parts, self.seqs = term.shape[0], seqs
+        columns = [lax.rem(s + k, seqs) for k in range(1, seqs)]
+        others = [lax.rem(d + k, dps) for k in range(1, dps)]
+        d_send, d_recv, z_send, z_recv, a_send, a_recv = sems
+        self.one = [
+            push(term.at[:, :, o], lands[0].at[k], d_send.at[k], d_recv.at[k], {"dp": o})
+            for k, o in enumerate(others)
+        ]
+        self.two = [
+            push(acc.at[c], lands[1].at[k], z_send.at[k], z_recv.at[k], {"seq": c})
+            for k, c in enumerate(columns)
+        ]
+        self.three = [
+            push(lands[2].at[p], shares.at[f], a_send.at[i], a_recv.at[i], {"feat": p})
+            for i, p in enumerate(peers(f))
+        ]
+
+    def start(self):
+        for c in self.one:
+            c.start()
+
+    def over_seq(self):
+        for c in self.one:
+            c.wait_recv()
+
+        def one(i, none):
+            p, c = i // self.seqs, lax.rem(i, self.seqs)
+            total = self.term[p, c, self.d].astype(f32)
+            for k in range(len(self.one)):
+                total = total + self.lands[0][k, p, c].astype(f32)
+            self.acc[c, p] = total.astype(bf16)
+            return none
+
+        lax.fori_loop(0, self.parts * self.seqs, one, 0)
+        for c in self.two:
+            c.start()
+
+    def over_feat(self):
+        for c in self.two:
+            c.wait_recv()
+
+        def one(p, none):
+            total = self.acc[self.s, p].astype(f32)
+            for k in range(len(self.two)):
+                total = total + self.lands[1][k, p].astype(f32)
+            self.lands[2][p] = total.astype(bf16)
+            return none
+
+        lax.fori_loop(0, self.parts, one, 0)
+        self.shares[self.f] = self.lands[2][self.f]
+        for c in self.three:
+            c.start()
+
+    def arrive(self):
+        for c in self.three:
+            c.wait_recv()
+
+    def finish(self):
+        for c in self.one + self.two + self.three:
+            c.wait_send()
+
+
+def row_sum_scratch(shape):
+    parts, seqs, dps, rows, wide = shape
+    others = max(dps - 1, 1)
+    dma = pltpu.SemaphoreType.DMA
+    return [
+        pltpu.VMEM((parts, rows, wide), bf16),
+        pltpu.VMEM((seqs, parts, rows, wide), bf16),
+        pltpu.VMEM((others, parts, seqs, rows, wide), bf16),
+        pltpu.VMEM((seqs - 1, parts, rows, wide), bf16),
+        pltpu.VMEM((parts, rows, wide), bf16),
+        dma((others,)),
+        dma((others,)),
+        dma((seqs - 1,)),
+        dma((seqs - 1,)),
+        dma((3,)),
+        dma((3,)),
+    ]
+
+
+def row_sum(term, scratch, f, s, d, seqs, dps):
+    shares, acc = scratch[:2]
+    return RowSum(term, acc, shares, scratch[2:5], scratch[5:], f, s, d, seqs, dps)
 
 
 def opening_kernel(
@@ -1098,8 +1207,12 @@
     gres_ref,
     gain_ref,
     gsum_two_ref,
+    term_ref,
     x_ref,
     tile_ref,
+    query_ref,
+    key_ref,
+    value_ref,
     part,
     land,
     s_send,
@@ -1113,6 +1226,7 @@
     c_recv,
     d_send,
     d_recv,
+    *sum_scratch,
 ):
     f, s, d = lax.axis_index("feat"), lax.axis_index("seq"), lax.axis_index("dp")
     parts = 4
@@ -1126,7 +1240,11 @@
     greet(
         [{"feat": a, "seq": b} for a, b in circle] + [{"dp": o} for o in others]
     )
-    ring = summed_products(part, land, f, [(dqkv_ref, w_ref)], s_send, s_recv)
+    rows_sum = row_sum(term_ref, sum_scratch, f, s, d, seqs, dps)
+    rows_sum.start()
+    ring = summed_products(
+        part, land, f, [(dqkv_ref, w_ref)], s_send, s_recv, rows_sum.over_seq
+    )
     gsum[...] = jnp.zeros_like(gsum)
 
     def finish_rows(rows, grad):
@@ -1137,6 +1255,7 @@
         x_ref[rows, :] = gres_ref[rows, :] + norm_back(grad, unit, inverse, gain_ref[...])
 
     by_rows(ring, finish_rows)
+    rows_sum.over_feat()
     ring.finish()
 
     lanes = gsum.shape[1] // (parts * seqs)
@@ -1175,25 +1294,38 @@
     for k in range(len(others)):
         total = total + tail[k]
     tile_ref[...] = total
+    rows_sum.arrive()
+    first = 0
+    for ref in (query_ref, key_ref, value_ref):
+        each = ref.shape[1] // parts
+        for p in range(parts):
+            piece = rows_sum.shares[p, :, first : first + each]
+            ref[:, p * each : (p + 1) * each] = piece.astype(f32)
+        first += each
+    rows_sum.finish()
     for c in sends + last:
         c.wait_send()
 
 
-def closing(dqkv, qkv_w, own, grad_residual, gain_one, gain_two_sum):
+def closing(dqkv, qkv_w, own, grad_residual, gain_one, gain_two_sum, qkv_term):
     parts, seqs, dps = (lax.axis_size(a) for a in ALL)
     block, width = own.shape
     others = max(dps - 1, 1)
     lanes = width // (parts * seqs)
     circle = parts * seqs - 1
+    rows_each = qkv_term.shape[3]
     dma = pltpu.SemaphoreType.DMA
     return pl.pallas_call(
         functools.partial(closing_kernel, seqs, dps),
         out_shape=(
             jax.ShapeDtypeStruct((block, width), f32),
             jax.ShapeDtypeStruct((8, lanes), f32),
+            jax.ShapeDtypeStruct((rows_each, HEADS * FDIM), f32),
+            jax.ShapeDtypeStruct((rows_each, HEADS * FDIM), f32),
+            jax.ShapeDtypeStruct((rows_each, HEADS * HV), f32),
         ),
-        in_specs=whole_vmem(6),
-        out_specs=tuple(whole_vmem(2)),
+        in_specs=whole_vmem(7),
+        out_specs=tuple(whole_vmem(5)),
         scratch_shapes=square_scratch(parts, block, width)
         + [
             pltpu.VMEM((1, width), f32),
@@ -1205,13 +1337,14 @@
             dma((circle,)),
             dma((others,)),
             dma((others,)),
-        ],
+        ]
+        + row_sum_scratch(qkv_term.shape),
         compiler_params=pltpu.CompilerParams(
             collective_id=5, has_side_effects=True, vmem_limit_bytes=48 << 20
         ),
         cost_estimate=pl.CostEstimate(flops=0, bytes_accessed=1 << 20, transcendentals=0),
         name="closing",
-    )(dqkv, qkv_w, own, grad_residual, gain_one, gain_two_sum)
+    )(dqkv, qkv_w, own, grad_residual, gain_one, gain_two_sum, qkv_term)
 
 
 def local(
@@ -1237,12 +1370,13 @@
     cot_own = cotangent.reshape(block, width)
 
     out_share = w_out.T.reshape(rows_each, parts, heads * HV).transpose(1, 0, 2)
+    x_all, qkv_w, gains = opening(
+        own, w_query, w_key, w_value, norm1_gain[None], norm2_gain[None]
+    )
+    qkv_width = qkv_w.shape[1]
+    x_all, w_gate, w_up = lax.optimization_barrier((x_all, w_gate, w_up))
     gate_w = lax.all_gather(w_gate, ("seq", "dp"), axis=0, tiled=True)
     up_w = lax.all_gather(w_up, ("seq", "dp"), axis=0, tiled=True)
-    x_all, qkv_w, gains = opening(
-        own, w_query, w_key, w_value, norm1_gain[None], norm2_gain[None]
-    )
-    qkv_width = qkv_w.shape[1]
     gain_one, gain_two = gains[0:1], gains[1:2]
 
     x_wide = x_all.astype(f32).reshape(rows_total, width)
@@ -1266,7 +1400,8 @@
     sig = jax.nn.sigmoid(gate_out)
     silu = gate_out * sig
     mixed = (silu * up_out).astype(bf16)
-    mixed, cot_late = lax.optimization_barrier((mixed, cot_all))
+    down_term = dot_tn(cot_all, mixed).astype(bf16)
+    mixed, cot_late, down_term = lax.optimization_barrier((mixed, cot_all, down_term))
     grad_mixed = dot(cot_late, down_w)
     grad_gate = (grad_mixed * up_out * sig * (1.0 + gate_out * (1.0 - sig))).astype(bf16)
     grad_up = (grad_mixed * silu).astype(bf16)
@@ -1274,7 +1409,6 @@
     def summed(term):
         return lax.psum_scatter(term, ("seq", "dp"), scatter_dimension=0, tiled=True)
 
-    down_term = dot_tn(cot_all, mixed).astype(bf16)
     gate_term = dot_tn(rows_all, grad_gate).astype(bf16)
     up_term = dot_tn(rows_all, grad_up).astype(bf16)
     grad_gate, grad_up, gate_term, up_term = lax.optimization_barrier(
@@ -1296,33 +1430,27 @@
         out_w,
     )
     branch_all = branch_all.reshape(rows_total, width)
-    dqkv, output = attention_backward(
-        qkv, segc, segr, tables, att, rden, carry, csum, ga, down, residual, heads
-    )
-    x_grad, gain_grads = closing(dqkv, qkv_w, own, grad_residual, gain_one, gain_two_sum)
-    dqkv = dqkv.reshape(rows_total, qkv_width)
-
-    def shared(grads):
-        grads = grads.astype(bf16).reshape(parts, -1, rows_each, grads.shape[1])
-        grads = grads.transpose(1, 0, 2, 3).reshape(width, -1)
-        grads = lax.psum_scatter(grads, ("seq", "dp"), scatter_dimension=0, tiled=True)
-        grads = grads.reshape(parts, rows_each, -1)
-        return lax.all_to_all(grads, "feat", 0, 0, tiled=True).astype(f32)
-
-    def from_share(grads, first, per):
-        piece = grads[:, :, first : first + heads * per]
-        return piece.transpose(1, 0, 2).reshape(rows_each, HEADS * per)
-
-    out_term = dot_tn(branch_all, att.reshape(rows_total, heads * HV))
-    qkv_term = dot_tn(normed, dqkv)
-    out_term, qkv_term, down_sum, gate_sum, up_sum = lax.optimization_barrier(
-        (out_term, qkv_term, down_sum, gate_sum, up_sum)
-    )
-    out_grads, qkv_grads = shared(out_term), shared(qkv_term)
-    query_grad = from_share(qkv_grads, 0, FDIM)
-    key_grad = from_share(qkv_grads, heads * FDIM, FDIM)
-    value_grad = from_share(qkv_grads, 2 * heads * FDIM, HV)
-    out_grad = from_share(out_grads, 0, HV).T
+    by_row = (parts, lax.axis_size("seq"), lax.axis_size("dp"), rows_each, -1)
+    out_term = dot_tn(branch_all, att.reshape(rows_total, heads * HV)).astype(bf16)
+    dqkv, output, out_grad = attention_backward(
+        qkv,
+        segc,
+        segr,
+        tables,
+        att,
+        rden,
+        carry,
+        csum,
+        ga,
+        down,
+        residual,
+        out_term.reshape(by_row),
+        heads,
+    )
+    qkv_term = dot_tn(normed, dqkv.reshape(rows_total, qkv_width)).astype(bf16)
+    x_grad, gain_grads, query_grad, key_grad, value_grad = closing(
+        dqkv, qkv_w, own, grad_residual, gain_one, gain_two_sum, qkv_term.reshape(by_row)
+    )
     gain_each = gain_grads.shape[1] // lax.axis_size("dp")
     gain_grads = lax.dynamic_slice_in_dim(
         gain_grads, lax.axis_index("dp") * gain_each, gain_each, axis=1
@@ -1335,7 +1463,7 @@
         query_grad,
         key_grad,
         value_grad,
-        out_grad,
+        out_grad.T,
         gate_sum.astype(f32),
         up_sum.astype(f32),
         down_sum.T.astype(f32),

time: 671 us -> 622 us (0.927)
  waiting for transfers between devices: 66.8 us -> 14.4 us
  Pallas kernels: 447 us -> 465 us
  local copies, waits for them, and re-layouts: 34.6 us -> 27 us
  starting transfers between devices: 7.4 us -> 0.63 us
    reduce_scatter x3, waiting for transfers between devices: 50.6 us -> 0.01 us  [summed(): lax.psum_scatter(term, ('seq', 'dp'), scatter_dimension=0, tiled=True)]
    pallas_call x1, Pallas kernels: 70.5 us -> 109 us  [attention_backward(): pl.pallas_call(functools.partial(backward_kernel, count, dps, heads), out...]
    pallas_call x1, Pallas kernels: 89.8 us -> 67.6 us  [opening(): pl.pallas_call(functools.partial(opening_kernel, seqs, dps), out_shape=(j...]
    all_gather x1, waiting for transfers between devices: 0.01 us -> 13.3 us  [local(): down_w = lax.all_gather(w_down.T, ('seq', 'dp'), axis=0, tiled=True)]
    reduce_scatter x2 -> x0, waiting for transfers between devices: 8.78 us -> none  [shared(): lax.psum_scatter(grads, ('seq', 'dp'), scatter_dimension=0, tiled=True)]
    reshape x5 -> x0, local copies, waits for them, and re-layouts: 7.38 us -> none  [the longest x2 5.01 us: shared(): grads = grads.astype(bf16).reshape(parts, -1, rows_each, grads.shape[1])]
    all_to_all x2 -> x0, starting transfers between devices: 7.08 us -> none  [shared(): return lax.all_to_all(grads, 'feat', 0, 0, tiled=True).astype(f32)]
    unnamed x76 -> x71, local copies, waits for them, and re-layouts: 21.2 us -> 22.1 us
  transfers between devices with their start and end apart: 10 -> 6, of which waited for: 3 -> 1; matrix products, arithmetic and copies ran while one was open for 11% -> 16% of each run, Pallas kernels for 67% -> 65%
where the time goes in v4:
time: 622 us; the launch traced here: 615 us
  Pallas kernels  465 us (75%)
  matrix products  82.3 us (13%)
  local copies, waits for them, and re-layouts  27 us (4%)
  between operations  14.9 us (2%)
  waiting for transfers between devices  14.4 us (2%)
  other arithmetic  11.3 us (2%)
    pallas_call x1, Pallas kernels, attention_backward(): pl.pallas_call(functools.partial(backward_kernel, count, dps, heads), out...  109 us
    pallas_call x1, Pallas kernels, rows_back(): pl.pallas_call(rows_back_kernel, out_shape=(jax.ShapeDtypeStruct((parts,...  93.7 us
    pallas_call x1, Pallas kernels, branch_step(): pl.pallas_call(branch_kernel, out_shape=(jax.ShapeDtypeStruct((parts, blo...  72.2 us
    pallas_call x1, Pallas kernels, attention_forward(): pl.pallas_call(functools.partial(forward_kernel, count, dps, heads), out_...  68.6 us
    pallas_call x1, Pallas kernels, opening(): pl.pallas_call(functools.partial(opening_kernel, seqs, dps), out_shape=(j...  67.6 us
    pallas_call x1, Pallas kernels, closing(): pl.pallas_call(functools.partial(closing_kernel, seqs, dps), out_shape=(j...  54.2 us
    dot_general x4, matrix products, dot(): lax.dot_general(a, b, (((1,), (0,)), ((), ())), preferred_element_type=f32)  43.2 us
    dot_general x5, matrix products, dot_tn(): lax.dot_general(a, b, (((0,), (0,)), ((), ())), preferred_element_type=f32)  39.1 us
  transfers between devices with their start and end apart: 6, of which 1 were waited for; matrix products, arithmetic and copies ran while one was open for 16% of the time, Pallas kernels for 65%

profile of v4, /device:TPU:0, one launch (start us, length us, event | category | flops | bytes accessed | tf_op | source)
XLA Modules:
  0.0 615.3 jit_solution(3659018543650581250)
XLA Ops:
  7.2 67.6 %opening.1 = (bf16[4,256,2048]{2,1,0:T(8,128)(2,1)}, bf16[4,4,2,64,640]{4,3,2,1,0:T(8,128)(2,1)}, f32[4,4,2,8,128]{4,3,2,1,0:T(8,128)}) custom-call(bf16[256,2048]{1,0:T(8,128)(2,1)} %bitcast.60, bf16[64,256]{1,0:T(8,128)(2,1)} %query_ref.1, bf16[64,256]{1,0:T(8,128)(2,1)} %key_ref.1, bf16[64,2048]{1,0:T(8,128)(2,1)} %value_ref.1, bf16[1,64]{1,0:T(2,128)(2,1)} %bitcast.86, ...), custom_call_target="tpu_custom_call" | custom-call | bytes 1048576 | tf_op jit(solution)/shard_map/opening/pallas_call | solution.py:963
  74.9 0.7 all-gather.6.cloned.1.call-update
  75.6 0.9 slice_bitcast_fusion
  76.7 3.2 fusion
  80.0 0.2 copy-done.23
  80.2 1.0 fusion.2
  81.2 0.8 copy-done.28
  82.1 3.4 convolution_convert_fusion.3
  85.5 2.7 copy.34
  88.4 0.2 copy.36.segc_ref
  88.8 1.3 copy-done.4
  90.0 68.6 %attention_forward.1 = (bf16[4,256,512]{2,1,0:T(8,128)(2,1)S(1)}, f32[4,256,512]{2,1,0:T(8,128)S(1)}, bf16[4,4,160,128]{3,2,1,0:T(8,128)(2,1)S(1)}, f32[4,8,256]...) custom-call(bf16[4,256,640]{2,1,0:T(8,128)(2,1)S(1)} %bitcast.65, ...), custom_call_target="tpu_custom_call" | custom-call | bytes 1048576 | tf_op jit(solution)/shard_map/attention_forward/pallas_call | solution.py:521
  158.6 1.3 copy-done.1
  159.9 1.3 copy-done.7
  161.2 0.8 copy-done.10
  162.1 2.1 copy-done.21
  164.1 72.2 %branch_step.1 = (bf16[4,256,2048]{2,1,0:T(8,128)(2,1)}, f32[256,2048]{1,0:T(8,128)S(1)}) custom-call(bf16[4,256,512]{2,1,0:T(8,128)(2,1)S(1)} %get-tuple-element.52.att_ref, bf16[2048,512]{1,0:T(8,128)(2,1)} %bitcast.63, bf16[256,2048]{1,0:T(8,128)(2,1)S(1)} %bitcast.61, f32[1,2048]{1,0:T(1,128)S(1)} %slice.24.gain_ref), custom_call_target="tpu_custom_call" | custom-call | bytes 1048576 | tf_op jit(solution)/shard_map/branch_step/pallas_call | solution.py:1077
  236.3 1.3 copy-done.2
  237.7 1.0 copy-done.5
  238.7 11.7 %fusion.5 = f32[1024,1408]{1,0:T(8,128)} fusion(bf16[1024,2048]{1,0:T(8,128)(2,1)} %bitcast.88, bf16[2048,1408]{1,0:T(8,128)(2,1)} %all-gather.4.cloned.1.call-done.wg_ref), kind=kOutput, calls=%fused_computation.27 | convolution fusion | flops 5905580032 | bytes 15728640 | tf_op jit(solution)/shard_map/dot_general | solution.py:24
  250.4 12.9 %multiply_convert_fusion.2 = (bf16[1024,1408]{1,0:T(8,128)(2,1)S(1)}, f32[1024,1408]{1,0:T(8,128)}) fusion(f32[1024,1408]{1,0:T(8,128)} %fusion.5, bf16[1024,2048]{1,0:T(8,128)(2,1)} %bitcast.89, bf16[2048,1408]{1,0:T(8,128)(2,1)} %all-gather.6.cloned.1.call-done.wu_ref), kind=kOutput, calls=%fused_computation.10 | convolution fusion | flops 5914230784 | bytes 24379392 | tf_op jit(solution)/shard_map/dot_general | solution.py:24
  263.3 1.6 copy-done.26
  264.8 8.6 %convolution_convert_fusion.2 = bf16[2048,1408]{1,0:T(8,128)(2,1)} fusion(bf16[1024,2048]{1,0:T(8,128)(2,1)S(1)} %bitcast.74, bf16[1024,1408]{1,0:T(8,128)(2,1)S(1)} %get-tuple-element.66), kind=kOutput, calls=%fused_computation.7 | convolution fusion | flops 5908463616 | bytes 12845056 | tf_op jit(solution)/shard_map/dot_general | solution.py:32
  273.5 0.2 reduce-scatter.6.cloned.1.call-start
  273.7 13.3 %all-gather.8.cloned.1.call-done.wd_hbm = bf16[2048,1408]{1,0:T(8,128)(2,1)} async-done(((bf16[256,1408]{1,0:T(8,128)(2,1)}), bf16[2048,1408]{1,0:T(8,128)(2,1)}) %all-gather.8.cloned.1.call-update) | async-done | bytes 5767184 | tf_op jit(solution)/shard_map/all_gather | solution.py:1386
  287.1 15.1 %multiply_convert_fusion = (bf16[1024,1408]{1,0:T(8,128)(2,1)S(1)}, bf16[1024,1408]{1,0:T(8,128)(2,1)}) fusion(f32[1024,1408]{1,0:T(8,128)} %fusion.5, f32[1024,1408]{1,0:T(8,128)} %get-tuple-element.115, bf16[1024,2048]{1,0:T(8,128)(2,1)} %bitcast.73, bf16[2048,1408]{1,0:T(8,128)(2,1)} %all-gather.8.cloned.1.call-done.wd_hbm), kind=kOutput, calls=%fused_computation.8 | convolution fusion | flops 5924323328 | bytes 27262976 | tf_op jit(solution)/shard_map/dot_general | solution.py:24
  302.2 1.5 copy-done.27
  303.8 8.6 %convolution_convert_fusion = bf16[2048,1408]{1,0:T(8,128)(2,1)} fusion(bf16[1024,2048]{1,0:T(8,128)(2,1)S(1)} %bitcast.91, bf16[1024,1408]{1,0:T(8,128)(2,1)S(1)} %get-tuple-element.64), kind=kOutput, calls=%fused_computation.5 | convolution fusion | flops 5908463616 | bytes 12845056 | tf_op jit(solution)/shard_map/dot_general | solution.py:32
  312.4 11.0 %convolution_convert_fusion.1 = bf16[2048,1408]{1,0:T(8,128)(2,1)} fusion(bf16[1024,2048]{1,0:T(8,128)(2,1)} %bitcast.90, bf16[1024,1408]{1,0:T(8,128)(2,1)} %get-tuple-element.63), kind=kOutput, calls=%fused_computation.6 | convolution fusion | flops 5908463616 | bytes 12845056 | tf_op jit(solution)/shard_map/dot_general | solution.py:32
  323.4 0.3 reduce-scatter.4.cloned.1.call-start
  323.6 0.3 reduce-scatter.4.cloned.1.call-update
  324.0 93.7 %rows_back.1 = (bf16[4,256,2048]{2,1,0:T(8,128)(2,1)}, f32[256,2048]{1,0:T(8,128)}, f32[1,2048]{1,0:T(1,128)}, bf16[4,256,2048]{2,1,0:T(8,128)(2,1)}, f32[4,256,512]{2,1,0:T(8,128)}) custom-call(bf16[4,256,1408]{2,1,0:T(8,128)(2,1)} %bitcast.79, bf16[4,256,1408]{2,1,0:T(8,128)(2,1)} %bitcast.78, bf16[2048,1408]{1,0:T(8,128)(2,1)} %all-gather.4.cloned.1.call-done.wg_ref, ...), custom_call_target="tpu_custom_call" | custom-call | bytes 1048576 | tf_op jit(solution)/shard_map/rows_back/pallas_call | solution.py:1174
  417.7 6.0 bitcast_convert_fusion.1
  423.8 108.6 %attention_backward.1 = (bf16[4,256,640]{2,1,0:T(8,128)(2,1)S(1)}, bf16[256,2048]{1,0:T(8,128)(2,1)S(1)}, f32[64,2048]{1,0:T(8,128)S(1)}) custom-call(bf16[4,256,640]{2,1,0:T(8,128)(2,1)} %bitcast.66, f32[4,256,1]{2,1,0:T(8,128)S(1)} %copy.36.segc_ref, f32[4,1,256]{2,1,0:T(1,128)S(1)} %get-tuple-element.112.segr_ref, bf16[4,64,256]{2,1,0:T(8,128)(2,1)S(1)} %copy-done.13, ...), custom_call_target="tpu_custom_call" | custom-call | bytes 1048576 | tf_op jit(solution)/shard_map/attention_backward/pallas_call | solution.py:565
  532.4 4.9 bitcast_convert_fusion
  537.3 54.2 %closing.1 = (f32[256,2048]{1,0:T(8,128)S(1)}, f32[8,128]{1,0:T(8,128)S(1)}, f32[64,256]{1,0:T(8,128)S(1)}, f32[64,256]{1,0:T(8,128)S(1)}, f32[64,2048]{1,0:T(8,128)S(1)}) custom-call(bf16[4,256,640]{2,1,0:T(8,128)(2,1)S(1)} %get-tuple-element.71.dqkv_ref, bf16[2048,640]{1,0:T(8,128)(2,1)} %bitcast.80, bf16[256,2048]{1,0:T(8,128)(2,1)S(1)} %bitcast.62, ...), custom_call_target="tpu_custom_call" | custom-call | bytes 1048576 | tf_op jit(solution)/shard_map/closing/pallas_call | solution.py:1318
  591.5 0.8 copy-done.16
  592.4 0.5 slice_bitcast_fusion.1
  592.9 2.4 convert_bitcast_fusion
  595.3 2.9 copy.38
  598.2 2.3 convert_element_type.78
  600.5 2.4 convert_element_type.77
  602.8 1.0 copy.50
  603.8 1.3 copy.51
  605.1 0.6 copy.52
  605.8 0.6 copy.53
  606.4 0.8 copy.54
  607.2 0.8 copy.55
  (73 shorter events, 0.8 us)
Async XLA Ops:
  7.2 231.5 %all-gather.4.cloned.1.call-start = ((), (), s32[]{:S(2)}) async-start(), calls=%async_computation.3 | async-start | bytes 6488064 | tf_op jit(solution)/shard_map/all_gather | solution.py:1378
  74.8 175.5 %all-gather.6.cloned.1.call-start = ((), (), s32[]{:S(2)}) async-start(), calls=%async_computation.4 | async-start | bytes 6488064 | tf_op jit(solution)/shard_map/all_gather | solution.py:1379
  75.6 211.5 %all-gather.8.cloned.1.call-start = ((), (), s32[]{:S(2)}) async-start(), calls=%async_computation.5 | async-start | bytes 6488064 | tf_op jit(solution)/shard_map/all_gather | solution.py:1386
  76.7 3.4 copy-start.23
  80.2 1.8 copy-start.28
  81.2 4.3 copy-start.24
  82.0 6.3 %copy-start.29 = (bf16[2048,64]{0,1:T(8,128)(2,1)S(1)}, bf16[2048,64]{0,1:T(8,128)(2,1)}, u32[]{:S(2)}) copy-start(bf16[2048,64]{0,1:T(8,128)(2,1)} %param.22) | copy-start | bytes 786436
  82.0 6.3 %copy-start.30 = (s32[4,1,256]{2,1,0:T(1,128)S(1)}, s32[4,1,256]{2,1,0:T(1,128)}, u32[]{:S(2)}) copy-start(s32[4,1,256]{2,1,0:T(1,128)} %param.16) | copy-start | bytes 12292
  82.0 6.7 %copy-start.12 = (bf16[4,64,256]{2,1,0:T(8,128)(2,1)S(1)}, bf16[4,64,256]{2,1,0:T(8,128)(2,1)}, u32[]{:S(2)}) copy-start(bf16[4,64,256]{2,1,0:T(8,128)(2,1)} %constant.26.clone.right_ref) | copy-start | bytes 393220
  82.0 6.7 %copy-start.13 = (bf16[4,64,256]{2,1,0:T(8,128)(2,1)S(1)}, bf16[4,64,256]{2,1,0:T(8,128)(2,1)}, u32[]{:S(2)}) copy-start(bf16[4,64,256]{2,1,0:T(8,128)(2,1)} %constant.25.clone.left_ref) | copy-start | bytes 393220
  82.1 6.7 %copy-start.19 = (f32[8,256]{1,0:T(8,128)S(1)}, f32[8,256]{1,0:T(8,128)}, u32[]{:S(2)}) copy-start(f32[8,256]{1,0:T(8,128)} %constant.27.clone.rows_ref) | copy-start | bytes 24580
  85.5 150.8 %copy-start.3 = (bf16[1024,640]{1,0:T(8,128)(2,1)}, bf16[1024,640]{1,0:T(8,128)(2,1)S(1)}, u32[]{:S(2)}) copy-start(bf16[1024,640]{1,0:T(8,128)(2,1)S(1)} %convolution_convert_fusion.3) | copy-start | bytes 3932164
  85.5 78.6 %copy-start = (bf16[1,1,256,2048]{3,2,1,0:T(8,128)(2,1)S(1)}, bf16[1,1,256,2048]{3,2,1,0:T(8,128)(2,1)}, u32[]{:S(2)}) copy-start(bf16[1,1,256,2048]{3,2,1,0:T(8,128)(2,1)} %param.15) | copy-start | bytes 3145732
  88.3 504.6 %reduce-scatter.8.cloned.1.call-start = ((), (), s32[]{:S(2)}) async-start(), calls=%async_computation.8 | async-start | bytes 6488064 | tf_op jit(solution)/shard_map/reduce_scatter | solution.py:1410
  88.7 161.7 %copy-start.18 = (f32[1,2048]{1,0:T(1,128)}, f32[1,2048]{1,0:T(1,128)S(1)}, u32[]{:S(2)}) copy-start(f32[1,2048]{1,0:T(1,128)S(1)} %slice.24.gain_ref) | copy-start | bytes 24580
  88.8 1.3 copy-start.4
  158.6 1.3 copy-start.1
  159.9 1.3 copy-start.7
  161.2 0.8 copy-start.10
  162.1 2.1 copy-start.21
  236.3 1.4 copy-start.2
  237.7 1.0 copy-start.5
  250.4 14.4 %copy-start.22 = (bf16[4,256,2048]{2,1,0:T(8,128)(2,1)S(1)}, bf16[4,256,2048]{2,1,0:T(8,128)(2,1)}, u32[]{:S(2)}) copy-start(bf16[4,256,2048]{2,1,0:T(8,128)(2,1)} %copy-done.21) | copy-start | bytes 12582916
  263.3 1.6 copy-start.26
  273.5 324.7 %reduce-scatter.6.cloned.1.call-start = ((), (), s32[]{:S(2)}) async-start(), calls=%async_computation.7 | async-start | bytes 6488064 | tf_op jit(solution)/shard_map/reduce_scatter | solution.py:1410
  287.1 16.7 %copy-start.31 = (bf16[4,256,2048]{2,1,0:T(8,128)(2,1)S(1)}, bf16[4,256,2048]{2,1,0:T(8,128)(2,1)}, u32[]{:S(2)}) copy-start(bf16[4,256,2048]{2,1,0:T(8,128)(2,1)} %get-tuple-element.57) | copy-start | bytes 12582916
  302.2 1.5 copy-start.27
  323.4 277.1 %reduce-scatter.4.cloned.1.call-start = ((), (), s32[]{:S(2)}) async-start(), calls=%async_computation.6 | async-start | bytes 6488064 | tf_op jit(solution)/shard_map/reduce_scatter | solution.py:1410
  324.0 93.7 %copy-start.6 = (bf16[4,256,512]{2,1,0:T(8,128)(2,1)S(1)}, bf16[4,256,512]{2,1,0:T(8,128)(2,1)}, u32[]{:S(2)}) copy-start(bf16[4,256,512]{2,1,0:T(8,128)(2,1)} %copy-done.5) | copy-start | bytes 3145732
  417.7 6.1 copy-start.11
  423.8 108.6 %copy-start.25 = (bf16[4,256,2048]{2,1,0:T(8,128)(2,1)S(1)}, bf16[4,256,2048]{2,1,0:T(8,128)(2,1)}, u32[]{:S(2)}) copy-start(bf16[4,256,2048]{2,1,0:T(8,128)(2,1)} %copy-done.24) | copy-start | bytes 12582916
  532.4 4.9 copy-start.8
  532.4 4.9 copy-start.14
  532.4 4.9 copy-start.20
  591.5 0.8 copy-start.16
  592.9 10.0 %copy-start.9 = (bf16[256,2048]{1,0:T(8,128)(2,1)S(1)}, bf16[256,2048]{1,0:T(8,128)(2,1)}, u32[]{:S(2)}) copy-start(bf16[256,2048]{1,0:T(8,128)(2,1)} %copy-done.8) | copy-start | bytes 3145732
  600.5 5.9 copy-start.17
  602.8 4.4 copy-start.15
Sparse Core Ops, SparseCore 0:
  75.0 86.7 all-gather.3
  163.4 62.1 all-gather.5
  227.9 59.1 all-gather.7
  289.2 77.7 reduce-scatter.7
  369.1 63.2 reduce-scatter.5
  434.6 94.5 reduce-scatter.3

commit v5 on v4

--- a/solution.py
+++ b/solution.py
@@ -90,7 +90,6 @@
 
 def forward_kernel(
     count,
-    dps,
     heads,
     qkv_ref,
     segc_ref,
@@ -99,13 +98,11 @@
     right_ref,
     rows_ref,
     cot_ref,
-    share_ref,
     att_ref,
     rden_ref,
     carry_ref,
     csum_ref,
     cots_ref,
-    wout_ref,
     send_state,
     send_sum,
     part,
@@ -113,15 +110,9 @@
     recv_sem,
     f_send,
     f_recv,
-    a_send,
-    a_recv,
-    z_send,
-    z_recv,
-    d_send,
-    d_recv,
     local_sem,
 ):
-    place, f, d = lax.axis_index("seq"), lax.axis_index("feat"), lax.axis_index("dp")
+    place, f = lax.axis_index("seq"), lax.axis_index("feat")
     groups, block = qkv_ref.shape[0], qkv_ref.shape[1]
     width = heads * FDIM
     tables = (left_ref, right_ref, rows_ref)
@@ -144,35 +135,12 @@
         for copy in hop(g):
             copy.start()
 
-    columns = [lax.rem(place + k, count) for k in range(1, count)]
-    others = [lax.rem(d + k, dps) for k in range(1, dps)]
-    stay = [
-        pltpu.make_async_copy(cot_ref, cots_ref.at[f], local_sem.at[0]),
-        pltpu.make_async_copy(share_ref.at[f], wout_ref.at[f, place, d], local_sem.at[1]),
-    ]
-    for c in stay:
-        c.start()
-    greet(
-        square_targets(f) + [{"seq": c} for c in columns] + [{"dp": o} for o in others]
-    )
-    shares = [
-        push(share_ref.at[p], wout_ref.at[f, place, d], a_send.at[i], a_recv.at[i], {"feat": p})
-        for i, p in enumerate(peers(f))
-    ]
-    for c in shares:
-        c.start()
+    chain = [lax.rem(place + 1, count), lax.rem(place + count - 1, count)]
+    stay = pltpu.make_async_copy(cot_ref, cots_ref.at[f], local_sem.at[0])
+    stay.start()
+    greet(square_targets(f) + [{"seq": c} for c in chain])
     gather = SquareGather(cots_ref, f, f_send, f_recv, cot_ref)
-
-    def to_column(k):
-        ref = wout_ref.at[:, place, d]
-        return push(ref, ref, z_send.at[k - 1], z_recv.at[k - 1], {"seq": columns[k - 1]})
-
-    def to_sibling(k):
-        ref = wout_ref.at[:, lax.rem(place + count - k, count), d]
-        return [
-            push(ref, ref, d_send.at[o, k], d_recv.at[o, k], {"dp": other})
-            for o, other in enumerate(others)
-        ]
+    gather.start()
 
     @pl.when(place == 0)
     def _():
@@ -199,16 +167,6 @@
         return none
 
     lax.fori_loop(0, groups, summarize, 0)
-    gather.start()
-    for c in stay:
-        c.wait()
-    for c in shares:
-        c.wait_recv()
-    for k in range(1, count):
-        to_column(k).start()
-    for c in to_sibling(0):
-        c.start()
-
     def join(g, none):
         for copy in hop(g):
             copy.wait_recv()
@@ -281,24 +239,12 @@
 
         lax.fori_loop(0, groups, finish, 0)
 
-    for k in range(1, count):
-        to_column(k).wait_recv()
-        for c in to_sibling(k):
-            c.start()
-    for k in range(count):
-        for c in to_sibling(k):
-            c.wait_recv()
-            c.wait_send()
-    for k in range(1, count):
-        to_column(k).wait_send()
-    for c in shares:
-        c.wait_send()
+    stay.wait()
     gather.finish()
 
 
 def backward_kernel(
     count,
-    dps,
     heads,
     qkv_ref,
     segc_ref,
@@ -313,10 +259,8 @@
     ga_ref,
     down_ref,
     res_ref,
-    oterm_ref,
     out_ref,
     final_ref,
-    ograd_ref,
     gn,
     send_state,
     send_sum,
@@ -331,9 +275,8 @@
     f_send,
     f_recv,
     local_sem,
-    *sum_scratch,
 ):
-    place, f, d = lax.axis_index("seq"), lax.axis_index("feat"), lax.axis_index("dp")
+    place, f = lax.axis_index("seq"), lax.axis_index("feat")
     groups, block = qkv_ref.shape[0], qkv_ref.shape[1]
     width = heads * FDIM
     tables = (left_ref, right_ref, rows_ref)
@@ -356,13 +299,8 @@
         for copy in hop(g):
             copy.start()
 
-    columns = [lax.rem(place + k, count) for k in range(1, count)]
-    others = [lax.rem(d + k, dps) for k in range(1, dps)]
-    greet(
-        square_targets(f) + [{"seq": c} for c in columns] + [{"dp": o} for o in others]
-    )
-    rows_sum = row_sum(oterm_ref, sum_scratch, f, place, d, count, dps)
-    rows_sum.start()
+    chain = [lax.rem(place + 1, count), lax.rem(place + count - 1, count)]
+    greet(square_targets(f) + [{"seq": c} for c in chain])
     fill = pltpu.make_async_copy(down_ref, terms, local_sem.at[0])
     fill.start()
     ring = SquareSum(terms, land, f, f_send, f_recv)
@@ -401,7 +339,6 @@
     fill.wait()
     ring.start_cross()
     ring.start_near()
-    rows_sum.over_seq()
 
     def join(g, none):
         for copy in hop(g):
@@ -456,7 +393,6 @@
 
     lax.fori_loop(0, groups, pull, 0)
     ring.relay()
-    rows_sum.over_feat()
 
     def carry_back(g, none):
         segc = segc_ref[g]
@@ -499,37 +435,29 @@
 
     by_rows(ring, add_up)
     ring.finish()
-    rows_sum.arrive()
-    wide = heads * HV
-    for p in range(rows_sum.parts):
-        ograd_ref[:, p * wide : (p + 1) * wide] = rows_sum.shares[p].astype(f32)
-    rows_sum.finish()
 
 
 def whole_vmem(count):
     return [pl.BlockSpec(memory_space=pltpu.VMEM)] * count
 
 
-def attention_forward(qkv, segc, segr, tables, cot_own, out_share, heads):
+def attention_forward(qkv, segc, segr, tables, cot_own, heads):
     groups, block, _ = qkv.shape
-    count, dps = lax.axis_size("seq"), lax.axis_size("dp")
-    others = max(dps - 1, 1)
-    parts, rows_each, wide = out_share.shape
+    count = lax.axis_size("seq")
     dma = pltpu.SemaphoreType.DMA
     states = (groups, heads, STATE, HV)
     sums = (groups, 8, LANES)
     return pl.pallas_call(
-        functools.partial(forward_kernel, count, dps, heads),
+        functools.partial(forward_kernel, count, heads),
         out_shape=(
             jax.ShapeDtypeStruct((groups, block, heads * HV), bf16),
             jax.ShapeDtypeStruct((groups, block, heads * HV), f32),
             jax.ShapeDtypeStruct(states, bf16),
             jax.ShapeDtypeStruct(sums, f32),
             jax.ShapeDtypeStruct((groups,) + cot_own.shape, bf16),
-            jax.ShapeDtypeStruct((parts, count, dps, rows_each, wide), bf16),
         ),
-        in_specs=whole_vmem(6) + in_place(2),
-        out_specs=tuple(whole_vmem(4) + in_place(2)),
+        in_specs=whole_vmem(6) + in_place(1),
+        out_specs=tuple(whole_vmem(4) + in_place(1)),
         scratch_shapes=[
             pltpu.VMEM(states, bf16),
             pltpu.VMEM(sums, f32),
@@ -538,39 +466,31 @@
             dma((2, groups)),
             dma((6,)),
             dma((6,)),
-            dma((3,)),
-            dma((3,)),
-            dma((count - 1,)),
-            dma((count - 1,)),
-            dma((others, count)),
-            dma((others, count)),
-            dma((2,)),
+            dma((1,)),
         ],
         compiler_params=pltpu.CompilerParams(
             collective_id=0, has_side_effects=True, vmem_limit_bytes=40 << 20
         ),
         cost_estimate=pl.CostEstimate(flops=0, bytes_accessed=1 << 20, transcendentals=0),
         name="attention_forward",
-    )(qkv, segc, segr, *tables, cot_own, out_share)
+    )(qkv, segc, segr, *tables, cot_own)
 
 
 def attention_backward(
-    qkv, segc, segr, tables, att, rden, carry, csum, ga, down, residual, out_term, heads
+    qkv, segc, segr, tables, att, rden, carry, csum, ga, down, residual, heads
 ):
     groups, block, wide = qkv.shape
-    count, dps = lax.axis_size("seq"), lax.axis_size("dp")
-    rows_each = out_term.shape[3]
+    count = lax.axis_size("seq")
     states = (groups, heads, STATE, HV)
     sums = (groups, 8, LANES)
     return pl.pallas_call(
-        functools.partial(backward_kernel, count, dps, heads),
+        functools.partial(backward_kernel, count, heads),
         out_shape=(
             jax.ShapeDtypeStruct((groups, block, wide), bf16),
             jax.ShapeDtypeStruct(residual.shape, bf16),
-            jax.ShapeDtypeStruct((rows_each, HEADS * HV), f32),
         ),
-        in_specs=whole_vmem(11) + in_place(1) + whole_vmem(2),
-        out_specs=tuple(whole_vmem(3)),
+        in_specs=whole_vmem(11) + in_place(1) + whole_vmem(1),
+        out_specs=tuple(whole_vmem(2)),
         scratch_shapes=[
             pltpu.VMEM((groups, heads, block, 2 * HV), bf16),
             pltpu.VMEM(states, bf16),
@@ -586,14 +506,13 @@
             pltpu.SemaphoreType.DMA((6,)),
             pltpu.SemaphoreType.DMA((6,)),
             pltpu.SemaphoreType.DMA((1,)),
-        ]
-        + row_sum_scratch(out_term.shape),
+        ],
         compiler_params=pltpu.CompilerParams(
             collective_id=1, has_side_effects=True, vmem_limit_bytes=48 << 20
         ),
         cost_estimate=pl.CostEstimate(flops=0, bytes_accessed=1 << 20, transcendentals=0),
         name="attention_backward",
-    )(qkv, segc, segr, *tables, att, rden, carry, csum, ga, down, residual, out_term)
+    )(qkv, segc, segr, *tables, att, rden, carry, csum, ga, down, residual)
 
 
 def peers(f):
@@ -827,12 +746,15 @@
     query_ref,
     key_ref,
     value_ref,
+    out_ref,
     one_ref,
     two_ref,
     x_ref,
     w_ref,
     g_ref,
+    o_ref,
     pack,
+    opack,
     tile,
     x_send,
     x_recv,
@@ -851,12 +773,6 @@
     others = [lax.rem(d + k, dps) for k in range(1, dps)]
     stay = pltpu.make_async_copy(tok_ref, x_ref.at[f], local_sem.at[0])
     stay.start()
-    greet(
-        square_targets(f) + [{"seq": c} for c in columns] + [{"dp": o} for o in others]
-    )
-    gather = SquareGather(x_ref, f, x_send, x_recv, tok_ref)
-    gather.start()
-
     first = 0
     for ref in (query_ref, key_ref, value_ref):
         each = ref.shape[1] // parts
@@ -873,6 +789,9 @@
     ]
     for c in own:
         c.start()
+    greet(
+        square_targets(f) + [{"seq": c} for c in columns] + [{"dp": o} for o in others]
+    )
     shares = [
         [
             push(pack.at[p], w_ref.at[f, s, d], a_send.at[0, i], a_recv.at[0, i], {"feat": p}),
@@ -883,6 +802,19 @@
     for pair in shares:
         for c in pair:
             c.start()
+    gather = SquareGather(x_ref, f, x_send, x_recv, tok_ref)
+    gather.start()
+    each = out_ref.shape[1] // parts
+    for p in range(parts):
+        opack[p] = out_ref[:, p * each : (p + 1) * each]
+    own_out = pltpu.make_async_copy(opack.at[f], o_ref.at[f], local_sem.at[3])
+    own_out.start()
+    out_shares = [
+        push(opack.at[p], o_ref.at[f], a_send.at[2, i], a_recv.at[2, i], {"feat": p})
+        for i, p in enumerate(near)
+    ]
+    for c in out_shares:
+        c.start()
     for c in own:
         c.wait()
 
@@ -946,6 +878,11 @@
         for c in pair:
             c.wait_send()
     stay.wait()
+    own_out.wait()
+    for c in out_shares:
+        c.wait_recv()
+    for c in out_shares:
+        c.wait_send()
     gather.finish()
 
 
@@ -953,41 +890,44 @@
     return [pl.BlockSpec(memory_space=pl.ANY)] * count
 
 
-def opening(own, w_query, w_key, w_value, gain_one, gain_two):
+def opening(own, w_query, w_key, w_value, w_out, gain_one, gain_two):
     parts, seqs, dps = (lax.axis_size(a) for a in ALL)
     block, width = own.shape
     rows_each = w_query.shape[0]
     wide = (w_query.shape[1] + w_key.shape[1] + w_value.shape[1]) // parts
     others = max(dps - 1, 1)
     dma = pltpu.SemaphoreType.DMA
-    x_all, w_all, g_all = pl.pallas_call(
+    out_wide = w_out.shape[1] // parts
+    x_all, w_all, g_all, o_own = pl.pallas_call(
         functools.partial(opening_kernel, seqs, dps),
         out_shape=(
             jax.ShapeDtypeStruct((parts, block, width), bf16),
             jax.ShapeDtypeStruct((parts, seqs, dps, rows_each, wide), bf16),
             jax.ShapeDtypeStruct((parts, seqs, dps, 8, HV), f32),
+            jax.ShapeDtypeStruct((parts, rows_each, out_wide), bf16),
         ),
-        in_specs=in_place(1) + whole_vmem(5),
-        out_specs=tuple(in_place(3)),
+        in_specs=in_place(1) + whole_vmem(6),
+        out_specs=tuple(in_place(4)),
         scratch_shapes=[
             pltpu.VMEM((parts, rows_each, wide), bf16),
+            pltpu.VMEM((parts, rows_each, out_wide), bf16),
             pltpu.VMEM((8, HV), f32),
             dma((6,)),
             dma((6,)),
-            dma((2, 3)),
-            dma((2, 3)),
+            dma((3, 3)),
+            dma((3, 3)),
             dma((2, seqs - 1, parts)),
             dma((2, seqs - 1, parts)),
             dma((2, others, seqs, parts)),
             dma((2, others, seqs, parts)),
-            dma((3,)),
+            dma((4,)),
         ],
         compiler_params=pltpu.CompilerParams(collective_id=2, has_side_effects=True),
         cost_estimate=pl.CostEstimate(flops=0, bytes_accessed=1 << 20, transcendentals=0),
         name="opening",
-    )(own, w_query, w_key, w_value, gain_one, gain_two)
+    )(own, w_query, w_key, w_value, w_out, gain_one, gain_two)
     gains = g_all[..., :2, :rows_each].transpose(3, 0, 1, 2, 4).reshape(2, width)
-    return x_all, w_all.reshape(width, wide), gains
+    return x_all, w_all.reshape(width, wide), gains, o_own
 
 
 def inverse_rms(values):
@@ -999,31 +939,64 @@
     return (scaled - unit * jnp.mean(scaled * unit, axis=-1, keepdims=True)) * inverse
 
 
-def product_tiles(part, slot, pairs, tile):
+class ByShare:
+    def __init__(self, ref):
+        self.ref = ref
+
+    def tile(self, i, size):
+        block = self.ref[:, i]
+        return block.reshape(size, block.shape[2])
+
+
+class ByTiles:
+    def __init__(self, src, ref, sem, tile):
+        self.ref = ref
+        self.fills = [
+            pltpu.make_async_copy(
+                src.at[pl.ds(i * tile, tile)], ref.at[pl.ds(i * tile, tile)], sem.at[i]
+            )
+            for i in range(ref.shape[0] // tile)
+        ]
+
+    def tile(self, i, size):
+        return self.ref[pl.ds(pl.multiple_of(i * size, size), size), :]
+
+
+def product_tiles(part, slot, pairs, tile, first=False):
     def one(i, none):
         cols = pl.ds(pl.multiple_of(i * tile, tile), tile)
         total = None
         for rows, weights in pairs:
-            term = dot_nt(rows[slot], weights[cols, :])
+            if hasattr(weights, "tile"):
+                block = weights.tile(i, tile)
+            else:
+                block = weights[cols, :]
+            term = dot_nt(rows[slot], block)
             total = term if total is None else total + term
         part[slot, :, cols] = total.astype(bf16)
         return none
 
-    lax.fori_loop(0, part.shape[2] // tile, one, 0)
-
-
-def summed_products(part, land, f, pairs, send_sem, recv_sem, beside=None):
+    if first:
+        for i in range(part.shape[2] // tile):
+            for _, weights in pairs:
+                weights.fills[i].wait()
+            one(i, 0)
+    else:
+        lax.fori_loop(0, part.shape[2] // tile, one, 0)
+
+
+def summed_products(part, land, f, pairs, send_sem, recv_sem, beside=None, first=False):
     side, above, across = peers(f)
     ring = SquareSum(part, land, f, send_sem, recv_sem)
-    product_tiles(part, across, pairs, 512)
+    product_tiles(part, across, pairs, 512, first)
     ring.start_cross()
     product_tiles(part, side, pairs, 512)
     product_tiles(part, above, pairs, 512)
     ring.start_near()
     product_tiles(part, f, pairs, 512)
+    ring.relay()
     if beside is not None:
         beside()
-    ring.relay()
     ring.arrive()
     return ring
 
@@ -1045,7 +1018,7 @@
 ):
     f = lax.axis_index("feat")
     greet(square_targets(f))
-    ring = summed_products(part, land, f, [(att_ref, w_ref)], s_send, s_recv)
+    ring = summed_products(part, land, f, [(att_ref, ByShare(w_ref))], s_send, s_recv)
 
     def finish_rows(rows, total):
         residual = tok_ref[rows, :].astype(f32) + total
@@ -1094,8 +1067,8 @@
 def rows_back_kernel(
     gg_ref,
     gu_ref,
-    wg_ref,
-    wu_ref,
+    wg_hbm,
+    wu_hbm,
     res_ref,
     cot_ref,
     gain_ref,
@@ -1109,6 +1082,8 @@
     ga_ref,
     part,
     land,
+    wg,
+    wu,
     mixed,
     wd,
     wo,
@@ -1117,8 +1092,16 @@
     g_send,
     g_recv,
     local_sem,
+    tile_sem,
 ):
     f = lax.axis_index("feat")
+    weights = [
+        ByTiles(src, dst, tile_sem.at[i], 512)
+        for i, (src, dst) in enumerate(((wg_hbm, wg), (wu_hbm, wu)))
+    ]
+    for pair in zip(*(w.fills for w in weights)):
+        for c in pair:
+            c.start()
     fills = [
         pltpu.make_async_copy(src, dst, local_sem.at[i])
         for i, (src, dst) in enumerate(((mixed_hbm, mixed), (wd_hbm, wd), (wo_hbm, wo)))
@@ -1126,7 +1109,7 @@
     for c in fills:
         c.start()
     greet(square_targets(f))
-    pairs = [(gg_ref, wg_ref), (gu_ref, wu_ref)]
+    pairs = [(gg_ref, weights[0]), (gu_ref, weights[1])]
 
     def down_products():
         for c in fills:
@@ -1134,7 +1117,7 @@
         for p in range(part.shape[0]):
             product_tiles(down_ref, p, [(mixed, wd)], 512)
 
-    ring = summed_products(part, land, f, pairs, s_send, s_recv, down_products)
+    ring = summed_products(part, land, f, pairs, s_send, s_recv, down_products, True)
     gsum_ref[...] = jnp.zeros_like(gsum_ref)
 
     def finish_rows(rows, grad):
@@ -1153,7 +1136,13 @@
     side, above, across = peers(f)
 
     def attended_grad(slot):
-        ga_ref[slot] = dot(all_ref[slot], wo[...])
+        blocks = ByShare(wo)
+        size = all_ref.shape[2] // wo.shape[1]
+        total = None
+        for i in range(wo.shape[1]):
+            term = dot(all_ref[slot, :, i * size : (i + 1) * size], blocks.tile(i, size))
+            total = term if total is None else total + term
+        ga_ref[slot] = total
 
     attended_grad(f)
     gather.relay()
@@ -1178,18 +1167,20 @@
             jax.ShapeDtypeStruct((block, width), f32),
             jax.ShapeDtypeStruct((1, width), f32),
             jax.ShapeDtypeStruct((parts, block, width), bf16),
-            jax.ShapeDtypeStruct((parts, block, out_w.shape[1]), f32),
+            jax.ShapeDtypeStruct((parts, block, out_w.shape[3]), f32),
         ),
-        in_specs=whole_vmem(7) + in_place(3),
+        in_specs=whole_vmem(2) + in_place(2) + whole_vmem(3) + in_place(3),
         out_specs=tuple(whole_vmem(5)),
         scratch_shapes=square_scratch(parts, block, width)[:2]
         + [
+            pltpu.VMEM((width, hidden), bf16),
+            pltpu.VMEM((width, hidden), bf16),
             pltpu.VMEM((parts, block, hidden), bf16),
             pltpu.VMEM((width, hidden), bf16),
             pltpu.VMEM(out_w.shape, bf16),
         ]
         + [dma((6,))] * 4
-        + [dma((3,))],
+        + [dma((3,)), dma((2, width // 512))],
         compiler_params=pltpu.CompilerParams(
             collective_id=4, has_side_effects=True, vmem_limit_bytes=60 << 20
         ),
@@ -1208,11 +1199,13 @@
     gain_ref,
     gsum_two_ref,
     term_ref,
+    osum_ref,
     x_ref,
     tile_ref,
     query_ref,
     key_ref,
     value_ref,
+    ograd_ref,
     part,
     land,
     s_send,
@@ -1226,6 +1219,9 @@
     c_recv,
     d_send,
     d_recv,
+    oland,
+    o_send,
+    o_recv,
     *sum_scratch,
 ):
     f, s, d = lax.axis_index("feat"), lax.axis_index("seq"), lax.axis_index("dp")
@@ -1242,6 +1238,12 @@
     )
     rows_sum = row_sum(term_ref, sum_scratch, f, s, d, seqs, dps)
     rows_sum.start()
+    outs = [
+        push(osum_ref.at[p], oland.at[f], o_send.at[i], o_recv.at[i], {"feat": p})
+        for i, p in enumerate(peers(f))
+    ]
+    for c in outs:
+        c.start()
     ring = summed_products(
         part, land, f, [(dqkv_ref, w_ref)], s_send, s_recv, rows_sum.over_seq
     )
@@ -1303,11 +1305,17 @@
             ref[:, p * each : (p + 1) * each] = piece.astype(f32)
         first += each
     rows_sum.finish()
-    for c in sends + last:
+    oland[f] = osum_ref[f]
+    for c in outs:
+        c.wait_recv()
+    each = ograd_ref.shape[1] // parts
+    for p in range(parts):
+        ograd_ref[:, p * each : (p + 1) * each] = oland[p].astype(f32)
+    for c in outs + sends + last:
         c.wait_send()
 
 
-def closing(dqkv, qkv_w, own, grad_residual, gain_one, gain_two_sum, qkv_term):
+def closing(dqkv, qkv_w, own, grad_residual, gain_one, gain_two_sum, qkv_term, out_sum):
     parts, seqs, dps = (lax.axis_size(a) for a in ALL)
     block, width = own.shape
     others = max(dps - 1, 1)
@@ -1323,9 +1331,10 @@
             jax.ShapeDtypeStruct((rows_each, HEADS * FDIM), f32),
             jax.ShapeDtypeStruct((rows_each, HEADS * FDIM), f32),
             jax.ShapeDtypeStruct((rows_each, HEADS * HV), f32),
+            jax.ShapeDtypeStruct((rows_each, HEADS * HV), f32),
         ),
-        in_specs=whole_vmem(7),
-        out_specs=tuple(whole_vmem(5)),
+        in_specs=whole_vmem(8),
+        out_specs=tuple(whole_vmem(6)),
         scratch_shapes=square_scratch(parts, block, width)
         + [
             pltpu.VMEM((1, width), f32),
@@ -1337,6 +1346,9 @@
             dma((circle,)),
             dma((others,)),
             dma((others,)),
+            pltpu.VMEM(out_sum.shape, bf16),
+            dma((3,)),
+            dma((3,)),
         ]
         + row_sum_scratch(qkv_term.shape),
         compiler_params=pltpu.CompilerParams(
@@ -1344,7 +1356,7 @@
         ),
         cost_estimate=pl.CostEstimate(flops=0, bytes_accessed=1 << 20, transcendentals=0),
         name="closing",
-    )(dqkv, qkv_w, own, grad_residual, gain_one, gain_two_sum, qkv_term)
+    )(dqkv, qkv_w, own, grad_residual, gain_one, gain_two_sum, qkv_term, out_sum)
 
 
 def local(
@@ -1369,12 +1381,12 @@
     own = tokens.reshape(block, width)
     cot_own = cotangent.reshape(block, width)
 
-    out_share = w_out.T.reshape(rows_each, parts, heads * HV).transpose(1, 0, 2)
-    x_all, qkv_w, gains = opening(
-        own, w_query, w_key, w_value, norm1_gain[None], norm2_gain[None]
+    x_all, qkv_w, gains, out_share = opening(
+        own, w_query, w_key, w_value, w_out.T, norm1_gain[None], norm2_gain[None]
     )
     qkv_width = qkv_w.shape[1]
     x_all, w_gate, w_up = lax.optimization_barrier((x_all, w_gate, w_up))
+    out_w = lax.all_gather(out_share[None], ("seq", "dp"), axis=0, tiled=True)
     gate_w = lax.all_gather(w_gate, ("seq", "dp"), axis=0, tiled=True)
     up_w = lax.all_gather(w_up, ("seq", "dp"), axis=0, tiled=True)
     gain_one, gain_two = gains[0:1], gains[1:2]
@@ -1387,10 +1399,7 @@
     segment = segments.reshape(parts, block).astype(f32)
     segc, segr = segment[:, :, None], segment[:, None, :]
     tables = feature_tables(heads)
-    att, rden, carry, csum, cot_all, out_w = attention_forward(
-        qkv, segc, segr, tables, cot_own, out_share, heads
-    )
-    out_w = out_w.reshape(width, heads * HV)
+    att, rden, carry, csum, cot_all = attention_forward(qkv, segc, segr, tables, cot_own, heads)
     cot_all = cot_all.reshape(rows_total, width)
     rows_all, residual = branch_step(att, out_w, own, gain_two)
     rows_all = rows_all.reshape(rows_total, width)
@@ -1432,24 +1441,17 @@
     branch_all = branch_all.reshape(rows_total, width)
     by_row = (parts, lax.axis_size("seq"), lax.axis_size("dp"), rows_each, -1)
     out_term = dot_tn(branch_all, att.reshape(rows_total, heads * HV)).astype(bf16)
-    dqkv, output, out_grad = attention_backward(
-        qkv,
-        segc,
-        segr,
-        tables,
-        att,
-        rden,
-        carry,
-        csum,
-        ga,
-        down,
-        residual,
-        out_term.reshape(by_row),
-        heads,
+    out_term = out_term.reshape(parts, -1, rows_each, heads * HV).transpose(1, 0, 2, 3)
+    out_sum = summed(out_term.reshape(width, -1)).reshape(parts, rows_each, -1)
+    dqkv, output = attention_backward(
+        qkv, segc, segr, tables, att, rden, carry, csum, ga, down, residual, heads
     )
-    qkv_term = dot_tn(normed, dqkv.reshape(rows_total, qkv_width)).astype(bf16)
-    x_grad, gain_grads, query_grad, key_grad, value_grad = closing(
-        dqkv, qkv_w, own, grad_residual, gain_one, gain_two_sum, qkv_term.reshape(by_row)
+    dqkv_late, down_sum, gate_sum, up_sum = lax.optimization_barrier(
+        (dqkv, down_sum, gate_sum, up_sum)
+    )
+    qkv_term = dot_tn(normed, dqkv_late.reshape(rows_total, qkv_width)).astype(bf16)
+    x_grad, gain_grads, query_grad, key_grad, value_grad, out_grad = closing(
+        dqkv, qkv_w, own, grad_residual, gain_one, gain_two_sum, qkv_term.reshape(by_row), out_sum
     )
     gain_each = gain_grads.shape[1] // lax.axis_size("dp")
     gain_grads = lax.dynamic_slice_in_dim(

time: 622 us -> 618 us (level)
  Pallas kernels: 465 us -> 383 us
  waiting for transfers between devices: 14.4 us -> 80.7 us
  local copies, waits for them, and re-layouts: 27 us -> 39.8 us
    pallas_call x2, Pallas kernels: 177 us -> 107 us  [the longest x1 68.8 us: attention_backward(): pl.pallas_call(functools.partial(backward_kernel, count, heads), out_shap...]
    reduce_scatter x3 -> x4, waiting for transfers between devices: 0.01 us -> 26.7 us  [summed(): lax.psum_scatter(term, ('seq', 'dp'), scatter_dimension=0, tiled=True)]
    all_gather x1, waiting for transfers between devices: 13.3 us -> 38 us  [local(): down_w = lax.all_gather(w_down.T, ('seq', 'dp'), axis=0, tiled=True)]
    pallas_call x1, Pallas kernels: 67.6 us -> 50.2 us  [opening(): pl.pallas_call(functools.partial(opening_kernel, seqs, dps), out_shape=(j...]
    all_gather x1, waiting for transfers between devices: 0.01 us -> 13.8 us  [local(): up_w = lax.all_gather(w_up, ('seq', 'dp'), axis=0, tiled=True)]
    unnamed x71 -> x91, local copies, waits for them, and re-layouts: 22.1 us -> 33.2 us
  transfers between devices with their start and end apart: 6 -> 8, of which waited for: 1 -> 3; matrix products, arithmetic and copies ran while one was open for 16% -> 15% of each run, Pallas kernels for 65% -> 45%
where the time goes in v5:
time: 618 us; the launch traced here: 611 us
  Pallas kernels  383 us (62%)
  matrix products  84 us (14%)
  waiting for transfers between devices  80.7 us (13%)
  local copies, waits for them, and re-layouts  39.8 us (6%)
  between operations  14.9 us (2%)
  other arithmetic  7.89 us (1%)
    pallas_call x1, Pallas kernels, rows_back(): pl.pallas_call(rows_back_kernel, out_shape=(jax.ShapeDtypeStruct((parts,...  93.3 us
    pallas_call x1, Pallas kernels, branch_step(): pl.pallas_call(branch_kernel, out_shape=(jax.ShapeDtypeStruct((parts, blo...  73.6 us
    pallas_call x1, Pallas kernels, attention_backward(): pl.pallas_call(functools.partial(backward_kernel, count, heads), out_shap...  68.8 us
    pallas_call x1, Pallas kernels, closing(): pl.pallas_call(functools.partial(closing_kernel, seqs, dps), out_shape=(j...  59.4 us
    pallas_call x1, Pallas kernels, opening(): pl.pallas_call(functools.partial(opening_kernel, seqs, dps), out_shape=(j...  50.2 us
    dot_general x4, matrix products, dot(): lax.dot_general(a, b, (((1,), (0,)), ((), ())), preferred_element_type=f32)  43.1 us
    dot_general x5, matrix products, dot_tn(): lax.dot_general(a, b, (((0,), (0,)), ((), ())), preferred_element_type=f32)  40.9 us
    all_gather x1, waiting for transfers between devices, local(): down_w = lax.all_gather(w_down.T, ('seq', 'dp'), axis=0, tiled=True)  38 us
  transfers between devices with their start and end apart: 8, of which 3 were waited for; matrix products, arithmetic and copies ran while one was open for 15% of the time, Pallas kernels for 45%

profile of v5, /device:TPU:0, one launch (start us, length us, event | category | flops | bytes accessed | tf_op | source)
XLA Modules:
  0.0 611.1 jit_solution(7394750138016957743)
XLA Ops:
  7.2 50.2 %opening.1 = (bf16[4,256,2048]{2,1,0:T(8,128)(2,1)}, bf16[4,4,2,64,640]{4,3,2,1,0:T(8,128)(2,1)}, f32[4,4,2,8,128]{4,3,2,1,0:T(8,128)}, bf16[4,64,512]{2,1,0:T(8,128)(2,1)}) custom-call(bf16[256,2048]{1,0:T(8,128)(2,1)} %bitcast.57, bf16[64,256]{1,0:T(8,128)(2,1)} %query_ref.1, bf16[64,256]{1,0:T(8,128)(2,1)} %key_ref.1, bf16[64,2048]{1,0:T(8,128)(2,1)} %value_ref.1, ...), custom_call_target="tpu_custom_call" | custom-call | bytes 1048576 | tf_op jit(solution)/shard_map/opening/pallas_call | solution.py:901
  59.0 0.9 slice_bitcast_fusion
  60.6 3.2 fusion
  64.1 1.0 fusion.2
  65.9 3.4 convolution_convert_fusion.3
  69.4 1.1 copy.34
  71.0 1.3 copy-done.5
  72.2 0.9 copy-done.13
  73.1 0.9 copy-done.15
  74.7 37.8 %attention_forward.1 = (bf16[4,256,512]{2,1,0:T(8,128)(2,1)S(1)}, f32[4,256,512]{2,1,0:T(8,128)S(1)}, bf16[4,4,160,128]{3,2,1,0:T(8,128)(2,1)S(1)}, f32[4,8,256]{2,1,0:T(8,128)S(1)}, bf16[4,256,2048]{2,1,0:T(8,128)(2,1)S(1)}) custom-call(bf16[4,256,640]{2,1,0:T(8,128)(2,1)S(1)} %bitcast.60, f32[4,256,1]{2,1,0:T(8,128)S(1)} %copy.35.segc_ref, ...), custom_call_target="tpu_custom_call" | custom-call | bytes 1048576 | tf_op jit(solution)/shard_map/attention_forward/pallas_call | solution.py:450
  112.6 1.0 copy-done.2
  113.5 1.3 copy-done.6
  115.5 2.1 copy-done.29
  117.5 1.2 copy-done.3
  118.8 73.6 %branch_step.1 = (bf16[4,256,2048]{2,1,0:T(8,128)(2,1)}, f32[256,2048]{1,0:T(8,128)S(1)}) custom-call(bf16[4,256,512]{2,1,0:T(8,128)(2,1)S(1)} %copy-done.3, bf16[8,4,64,512]{3,2,1,0:T(8,128)(2,1)} %bitcast.70, bf16[256,2048]{1,0:T(8,128)(2,1)S(1)} %bitcast.58, f32[1,2048]{1,0:T(1,128)S(1)} %slice.24.gain_ref), custom_call_target="tpu_custom_call" | custom-call | bytes 1048576 | tf_op jit(solution)/shard_map/branch_step/pallas_call | solution.py:1050
  192.4 1.4 copy-done.1
  193.7 11.8 %fusion.5 = f32[1024,1408]{1,0:T(8,128)} fusion(bf16[1024,2048]{1,0:T(8,128)(2,1)} %bitcast.86, bf16[2048,1408]{1,0:T(8,128)(2,1)} %all-gather.6.cloned.1.call-done.wg_hbm), kind=kOutput, calls=%fused_computation.26 | convolution fusion | flops 5905580032 | bytes 15728640 | tf_op jit(solution)/shard_map/dot_general | solution.py:24
  205.5 13.8 %all-gather.8.cloned.1.call-done.wu_hbm = bf16[2048,1408]{1,0:T(8,128)(2,1)} async-done(((bf16[256,1408]{1,0:T(8,128)(2,1)}), bf16[2048,1408]{1,0:T(8,128)(2,1)}) %all-gather.8.cloned.1.call-update) | async-done | bytes 5767184 | tf_op jit(solution)/shard_map/all_gather | solution.py:1391
  219.3 12.7 %multiply_convert_fusion.2 = (bf16[1024,1408]{1,0:T(8,128)(2,1)S(1)}, f32[1024,1408]{1,0:T(8,128)}) fusion(f32[1024,1408]{1,0:T(8,128)} %fusion.5, bf16[1024,2048]{1,0:T(8,128)(2,1)} %bitcast.87, bf16[2048,1408]{1,0:T(8,128)(2,1)} %all-gather.8.cloned.1.call-done.wu_hbm), kind=kOutput, calls=%fused_computation.10 | convolution fusion | flops 5914230784 | bytes 24379392 | tf_op jit(solution)/shard_map/dot_general | solution.py:24
  232.0 1.6 copy-done.33
  233.6 8.6 %convolution_convert_fusion.2 = bf16[2048,1408]{1,0:T(8,128)(2,1)} fusion(bf16[1024,2048]{1,0:T(8,128)(2,1)S(1)} %bitcast.69, bf16[1024,1408]{1,0:T(8,128)(2,1)S(1)} %get-tuple-element.70), kind=kOutput, calls=%fused_computation.7 | convolution fusion | flops 5908463616 | bytes 12845056 | tf_op jit(solution)/shard_map/dot_general | solution.py:32
  242.5 38.0 %all-gather.10.cloned.1.call-done.wd_hbm = bf16[2048,1408]{1,0:T(8,128)(2,1)} async-done(((bf16[256,1408]{1,0:T(8,128)(2,1)}), bf16[2048,1408]{1,0:T(8,128)(2,1)}) %all-gather.10.cloned.1.call-update) | async-done | bytes 5767184 | tf_op jit(solution)/shard_map/all_gather | solution.py:1398
  280.5 15.2 %multiply_convert_fusion = (bf16[1024,1408]{1,0:T(8,128)(2,1)S(1)}, bf16[1024,1408]{1,0:T(8,128)(2,1)}) fusion(f32[1024,1408]{1,0:T(8,128)} %fusion.5, f32[1024,1408]{1,0:T(8,128)} %get-tuple-element.123, bf16[1024,2048]{1,0:T(8,128)(2,1)} %bitcast.68, bf16[2048,1408]{1,0:T(8,128)(2,1)} %all-gather.10.cloned.1.call-done.wd_hbm), kind=kOutput, calls=%fused_computation.8 | convolution fusion | flops 5924323328 | bytes 27262976 | tf_op jit(solution)/shard_map/dot_general | solution.py:24
  295.7 1.5 copy-done.34
  297.2 8.7 %convolution_convert_fusion = bf16[2048,1408]{1,0:T(8,128)(2,1)} fusion(bf16[1024,2048]{1,0:T(8,128)(2,1)S(1)} %bitcast.89, bf16[1024,1408]{1,0:T(8,128)(2,1)S(1)} %get-tuple-element.68), kind=kOutput, calls=%fused_computation.5 | convolution fusion | flops 5908463616 | bytes 12845056 | tf_op jit(solution)/shard_map/dot_general | solution.py:32
  305.9 11.0 %convolution_convert_fusion.1 = bf16[2048,1408]{1,0:T(8,128)(2,1)} fusion(bf16[1024,2048]{1,0:T(8,128)(2,1)} %bitcast.88, bf16[1024,1408]{1,0:T(8,128)(2,1)} %get-tuple-element.67), kind=kOutput, calls=%fused_computation.6 | convolution fusion | flops 5908463616 | bytes 12845056 | tf_op jit(solution)/shard_map/dot_general | solution.py:32
  317.9 93.3 %rows_back.1 = (bf16[4,256,2048]{2,1,0:T(8,128)(2,1)}, f32[256,2048]{1,0:T(8,128)}, f32[1,2048]{1,0:T(1,128)}, bf16[4,256,2048]{2,1,0:T(8,128)(2,1)}, f32[4,256,512]{2,1,0:T(8,128)}) custom-call(bf16[4,256,1408]{2,1,0:T(8,128)(2,1)} %bitcast.77, bf16[4,256,1408]{2,1,0:T(8,128)(2,1)} %bitcast.76, bf16[2048,1408]{1,0:T(8,128)(2,1)} %all-gather.6.cloned.1.call-done.wg_hbm, ...), custom_call_target="tpu_custom_call" | custom-call | bytes 1048576 | tf_op jit(solution)/shard_map/rows_back/pallas_call | solution.py:1163
  411.2 4.9 bitcast_convert_fusion.1
  416.1 1.5 copy.38
  417.7 1.4 slice.25.gain_ref
  419.1 1.2 copy-done.4
  420.3 0.9 copy-done.14
  421.2 0.9 copy-done.16
  422.9 68.8 %attention_backward.1 = (bf16[4,256,640]{2,1,0:T(8,128)(2,1)S(1)}, bf16[256,2048]{1,0:T(8,128)(2,1)S(1)}) custom-call(bf16[4,256,640]{2,1,0:T(8,128)(2,1)S(1)} %bitcast.61, f32[4,256,1]{2,1,0:T(8,128)S(1)} %copy.35.segc_ref, f32[4,1,256]{2,1,0:T(1,128)S(1)} %get-tuple-element.120.segr_ref, bf16[4,64,256]{2,1,0:T(8,128)(2,1)S(1)} %copy-done.16, ...), custom_call_target="tpu_custom_call" | custom-call | bytes 1048576 | tf_op jit(solution)/shard_map/attention_backward/pallas_call | solution.py:486
  491.7 1.0 copy-done.9
  492.8 1.0 copy-done.11
  493.8 7.7 %bitcast_convert_fusion = bf16[2048,640]{1,0:T(8,128)(2,1)} fusion(bf16[4,256,2048]{2,1,0:T(8,128)(2,1)} %copy-done.32, bf16[4,256,640]{2,1,0:T(8,128)(2,1)} %copy-done.9), kind=kOutput, calls=%fused_computation.13 | convolution fusion | flops 2685665280 | bytes 8126464 | tf_op jit(solution)/shard_map/dot_general | solution.py:32
  501.5 26.7 %reduce-scatter.11.cloned.1.call-done = bf16[256,512]{1,0:T(8,128)(2,1)} async-done(((bf16[2048,512]{1,0:T(8,128)(2,1)}), bf16[256,512]{1,0:T(8,128)(2,1)}) %reduce-scatter.11.cloned.1.call-update) | async-done | bytes 262160 | tf_op jit(solution)/shard_map/reduce_scatter | solution.py:1419
  528.2 0.9 copy-done.21
  529.2 59.4 %closing.1 = (f32[256,2048]{1,0:T(8,128)S(1)}, f32[8,128]{1,0:T(8,128)S(1)}, f32[64,256]{1,0:T(8,128)S(1)}, f32[64,256]{1,0:T(8,128)S(1)}, f32[64,2048]{1,0:T(8,128)S(1)}, /*index=5*/f32[64,2048]{1,0:T(8,128)S(1)}) custom-call(bf16[4,256,640]{2,1,0:T(8,128)(2,1)S(1)} %copy-done.10, bf16[2048,640]{1,0:T(8,128)(2,1)} %bitcast.78, ...), custom_call_target="tpu_custom_call" | custom-call | bytes 1048576 | tf_op jit(solution)/shard_map/closing/pallas_call | solution.py:1326
  588.6 1.3 copy-done.7
  589.9 0.8 copy-done.17
  592.1 1.2 convert_element_type.77
  593.3 1.2 convert_element_type.78
  594.5 1.2 convert_bitcast_fusion
  595.7 2.9 copy.39
  598.6 1.0 copy.48
  599.6 1.3 copy.49
  (99 shorter events, 11.3 us)
Async XLA Ops:
  7.2 110.4 %all-gather.12.cloned.1.call-start = ((), (), s32[]{:S(2)}) async-start(), calls=%async_computation.11 | async-start | bytes 2359296 | tf_op jit(solution)/shard_map/all_gather | solution.py:1389
  57.4 136.3 %all-gather.6.cloned.1.call-start = ((), (), s32[]{:S(2)}) async-start(), calls=%async_computation.4 | async-start | bytes 6488064 | tf_op jit(solution)/shard_map/all_gather | solution.py:1390
  58.2 161.1 %all-gather.8.cloned.1.call-start = ((), (), s32[]{:S(2)}) async-start(), calls=%async_computation.5 | async-start | bytes 6488064 | tf_op jit(solution)/shard_map/all_gather | solution.py:1391
  58.9 221.6 %all-gather.10.cloned.1.call-start = ((), (), s32[]{:S(2)}) async-start(), calls=%async_computation.6 | async-start | bytes 6488064 | tf_op jit(solution)/shard_map/all_gather | solution.py:1398
  60.6 3.5 copy-start.31
  64.1 1.8 copy-start.35
  65.1 4.2 copy-start.32
  65.9 3.5 copy-start.36
  65.9 4.7 copy-start.40
  69.4 48.2 %copy-start = (bf16[1,1,256,2048]{3,2,1,0:T(8,128)(2,1)S(1)}, bf16[1,1,256,2048]{3,2,1,0:T(8,128)(2,1)}, u32[]{:S(2)}) copy-start(bf16[1,1,256,2048]{3,2,1,0:T(8,128)(2,1)} %param.15) | copy-start | bytes 3145732
  70.5 423.2 %reduce-scatter.5.cloned.1.call-start = ((), (), s32[]{:S(2)}) async-start(), calls=%async_computation.7 | async-start | bytes 6488064 | tf_op jit(solution)/shard_map/reduce_scatter | solution.py:1419
  70.9 134.6 %copy-start.22 = (f32[1,2048]{1,0:T(1,128)}, f32[1,2048]{1,0:T(1,128)S(1)}, u32[]{:S(2)}) copy-start(f32[1,2048]{1,0:T(1,128)S(1)} %slice.24.gain_ref) | copy-start | bytes 24580
  70.9 1.3 copy-start.5
  72.2 0.9 copy-start.13
  73.1 0.9 copy-start.15
  112.5 1.0 copy-start.2
  113.5 1.3 copy-start.6
  115.5 2.1 copy-start.29
  117.5 1.2 copy-start.3
  192.4 1.4 copy-start.1
  219.3 14.3 %copy-start.30 = (bf16[4,256,2048]{2,1,0:T(8,128)(2,1)S(1)}, bf16[4,256,2048]{2,1,0:T(8,128)(2,1)}, u32[]{:S(2)}) copy-start(bf16[4,256,2048]{2,1,0:T(8,128)(2,1)} %copy-done.29) | copy-start | bytes 12582916
  232.0 1.6 copy-start.33
  242.3 251.5 %reduce-scatter.7.cloned.1.call-start = ((), (), s32[]{:S(2)}) async-start(), calls=%async_computation.8 | async-start | bytes 6488064 | tf_op jit(solution)/shard_map/reduce_scatter | solution.py:1419
  280.5 16.7 %copy-start.41 = (bf16[4,256,2048]{2,1,0:T(8,128)(2,1)S(1)}, bf16[4,256,2048]{2,1,0:T(8,128)(2,1)}, u32[]{:S(2)}) copy-start(bf16[4,256,2048]{2,1,0:T(8,128)(2,1)} %get-tuple-element.61) | copy-start | bytes 12582916
  295.7 1.5 copy-start.34
  316.9 176.8 %reduce-scatter.9.cloned.1.call-start = ((), (), s32[]{:S(2)}) async-start(), calls=%async_computation.9 | async-start | bytes 6488064 | tf_op jit(solution)/shard_map/reduce_scatter | solution.py:1419
  317.6 210.5 %reduce-scatter.11.cloned.1.call-start = ((), (), s32[]{:S(2)}) async-start(), calls=%async_computation.10 | async-start | bytes 2359296 | tf_op jit(solution)/shard_map/reduce_scatter | solution.py:1419
  416.1 3.0 copy-start.24
  419.1 1.2 copy-start.4
  420.3 0.9 copy-start.14
  421.2 0.9 copy-start.16
  422.1 0.8 copy-start.26
  491.7 1.1 copy-start.9
  492.8 1.0 copy-start.11
  493.7 34.5 %copy-start.10 = (bf16[4,256,640]{2,1,0:T(8,128)(2,1)S(1)}, bf16[4,256,640]{2,1,0:T(8,128)(2,1)}, u32[]{:S(2)}) copy-start(bf16[4,256,640]{2,1,0:T(8,128)(2,1)} %copy-done.9) | copy-start | bytes 3932164
  493.7 34.5 %copy-start.27 = (f32[1,2048]{1,0:T(1,128)S(1)}, f32[1,2048]{1,0:T(1,128)}, u32[]{:S(2)}) copy-start(f32[1,2048]{1,0:T(1,128)} %slice.25.gain_ref) | copy-start | bytes 24580
  493.7 34.4 %copy-start.28 = (f32[1,2048]{1,0:T(1,128)S(1)}, f32[1,2048]{1,0:T(1,128)}, u32[]{:S(2)}) copy-start(f32[1,2048]{1,0:T(1,128)} %get-tuple-element.76.gsum_two_ref) | copy-start | bytes 24580
  528.2 1.0 copy-start.21
  529.1 63.0 %copy-start.38 = (bf16[256,1408]{1,0:T(8,128)(2,1)S(1)}, bf16[256,1408]{1,0:T(8,128)(2,1)}, u32[]{:S(2)}) copy-start(bf16[256,1408]{1,0:T(8,128)(2,1)} %reduce-scatter.7.cloned.1.call-done) | copy-start | bytes 2162692
  529.1 64.2 %copy-start.39 = (bf16[256,1408]{1,0:T(8,128)(2,1)S(1)}, bf16[256,1408]{1,0:T(8,128)(2,1)}, u32[]{:S(2)}) copy-start(bf16[256,1408]{1,0:T(8,128)(2,1)} %reduce-scatter.9.cloned.1.call-done) | copy-start | bytes 2162692
  588.6 1.3 copy-start.7
  589.9 0.8 copy-start.17
  590.7 0.8 copy-start.19
  591.5 3.0 copy-start.37
  592.1 6.5 %copy-start.12 = (bf16[256,2048]{1,0:T(8,128)(2,1)S(1)}, bf16[256,2048]{1,0:T(8,128)(2,1)}, u32[]{:S(2)}) copy-start(bf16[256,2048]{1,0:T(8,128)(2,1)} %copy-done.11) | copy-start | bytes 3145732
  593.3 6.3 %copy-start.8 = (f32[256,2048]{1,0:T(8,128)S(1)}, f32[256,2048]{1,0:T(8,128)}, u32[]{:S(2)}) copy-start(f32[256,2048]{1,0:T(8,128)} %copy-done.7) | copy-start | bytes 6291460
  598.6 3.6 copy-start.20
  598.6 4.4 copy-start.18
  (2 other events, 1.3 us)
Sparse Core Ops, SparseCore 0:
  57.6 29.2 all-gather.11
  88.5 63.1 all-gather.5
  153.3 65.9 all-gather.7
  221.4 59.1 all-gather.9
  282.7 63.5 reduce-scatter.4
  348.4 63.2 reduce-scatter.6
  414.0 77.9 reduce-scatter.8
  494.3 33.8 reduce-scatter.10

commit v6 on v5

--- a/solution.py
+++ b/solution.py
@@ -991,10 +991,11 @@
     product_tiles(part, across, pairs, 512, first)
     ring.start_cross()
     product_tiles(part, side, pairs, 512)
+    ring.near[0].start()
     product_tiles(part, above, pairs, 512)
-    ring.start_near()
+    ring.near[1].start()
+    ring.relay()
     product_tiles(part, f, pairs, 512)
-    ring.relay()
     if beside is not None:
         beside()
     ring.arrive()
@@ -1112,12 +1113,10 @@
     pairs = [(gg_ref, weights[0]), (gu_ref, weights[1])]
 
     def down_products():
-        for c in fills:
-            c.wait()
         for p in range(part.shape[0]):
             product_tiles(down_ref, p, [(mixed, wd)], 512)
 
-    ring = summed_products(part, land, f, pairs, s_send, s_recv, down_products, True)
+    ring = summed_products(part, land, f, pairs, s_send, s_recv, first=True)
     gsum_ref[...] = jnp.zeros_like(gsum_ref)
 
     def finish_rows(rows, grad):
@@ -1144,7 +1143,10 @@
             total = term if total is None else total + term
         ga_ref[slot] = total
 
+    for c in fills:
+        c.wait()
     attended_grad(f)
+    down_products()
     gather.relay()
     gather.near()
     attended_grad(side)
@@ -1385,9 +1387,9 @@
         own, w_query, w_key, w_value, w_out.T, norm1_gain[None], norm2_gain[None]
     )
     qkv_width = qkv_w.shape[1]
-    x_all, w_gate, w_up = lax.optimization_barrier((x_all, w_gate, w_up))
+    gate_w = lax.all_gather(w_gate, ("seq", "dp"), axis=0, tiled=True)
+    gate_w, out_share, w_up = lax.optimization_barrier((gate_w, out_share, w_up))
     out_w = lax.all_gather(out_share[None], ("seq", "dp"), axis=0, tiled=True)
-    gate_w = lax.all_gather(w_gate, ("seq", "dp"), axis=0, tiled=True)
     up_w = lax.all_gather(w_up, ("seq", "dp"), axis=0, tiled=True)
     gain_one, gain_two = gains[0:1], gains[1:2]
 
@@ -1446,9 +1448,7 @@
     dqkv, output = attention_backward(
         qkv, segc, segr, tables, att, rden, carry, csum, ga, down, residual, heads
     )
-    dqkv_late, down_sum, gate_sum, up_sum = lax.optimization_barrier(
-        (dqkv, down_sum, gate_sum, up_sum)
-    )
+    dqkv_late, down_sum, gate_sum = lax.optimization_barrier((dqkv, down_sum, gate_sum))
     qkv_term = dot_tn(normed, dqkv_late.reshape(rows_total, qkv_width)).astype(bf16)
     x_grad, gain_grads, query_grad, key_grad, value_grad, out_grad = closing(
         dqkv, qkv_w, own, grad_residual, gain_one, gain_two_sum, qkv_term.reshape(by_row), out_sum

time: 618 us -> 584 us (0.945)
  waiting for transfers between devices: 80.7 us -> 13.1 us
  Pallas kernels: 383 us -> 416 us
    all_gather x1, waiting for transfers between devices: 38 us -> 0.02 us  [local(): down_w = lax.all_gather(w_down.T, ('seq', 'dp'), axis=0, tiled=True)]
    reduce_scatter x4, waiting for transfers between devices: 26.7 us -> 0.01 us  [summed(): lax.psum_scatter(term, ('seq', 'dp'), scatter_dimension=0, tiled=True)]
    pallas_call x1, Pallas kernels: 50.2 us -> 74.9 us  [opening(): pl.pallas_call(functools.partial(opening_kernel, seqs, dps), out_shape=(j...]
    pallas_call x1, Pallas kernels: 59.4 us -> 81.7 us  [closing(): pl.pallas_call(functools.partial(closing_kernel, seqs, dps), out_shape=(j...]
    all_gather x1, waiting for transfers between devices: 13.8 us -> 0.01 us  [local(): up_w = lax.all_gather(w_up, ('seq', 'dp'), axis=0, tiled=True)]
    pallas_call x1, Pallas kernels: 68.8 us -> 55.5 us  [attention_backward(): pl.pallas_call(functools.partial(backward_kernel, count, heads), out_shap...]
    all_gather x1, waiting for transfers between devices: 0.01 us -> 10.9 us  [local(): gate_w = lax.all_gather(w_gate, ('seq', 'dp'), axis=0, tiled=True)]
    unnamed x91 -> x89, local copies, waits for them, and re-layouts: 33.2 us -> 33.2 us
  transfers between devices with their start and end apart: 8 -> 8, of which waited for: 3 -> 1; matrix products, arithmetic and copies ran while one was open for 15% -> 17% of each run, Pallas kernels for 45% -> 72%
where the time goes in v6:
time: 584 us; the launch traced here: 577 us
  Pallas kernels  416 us (71%)
  matrix products  84.1 us (14%)
  local copies, waits for them, and re-layouts  39.7 us (7%)
  between operations  14.9 us (3%)
  waiting for transfers between devices  13.1 us (2%)
  other arithmetic  9.02 us (2%)
    pallas_call x1, Pallas kernels, rows_back(): pl.pallas_call(rows_back_kernel, out_shape=(jax.ShapeDtypeStruct((parts,...  87.8 us
    pallas_call x1, Pallas kernels, closing(): pl.pallas_call(functools.partial(closing_kernel, seqs, dps), out_shape=(j...  81.7 us
    pallas_call x1, Pallas kernels, branch_step(): pl.pallas_call(branch_kernel, out_shape=(jax.ShapeDtypeStruct((parts, blo...  77.8 us
    pallas_call x1, Pallas kernels, opening(): pl.pallas_call(functools.partial(opening_kernel, seqs, dps), out_shape=(j...  74.9 us
    pallas_call x1, Pallas kernels, attention_backward(): pl.pallas_call(functools.partial(backward_kernel, count, heads), out_shap...  55.5 us
    dot_general x4, matrix products, dot(): lax.dot_general(a, b, (((1,), (0,)), ((), ())), preferred_element_type=f32)  43.1 us
    dot_general x5, matrix products, dot_tn(): lax.dot_general(a, b, (((0,), (0,)), ((), ())), preferred_element_type=f32)  41 us
    pallas_call x1, Pallas kernels, attention_forward(): pl.pallas_call(functools.partial(forward_kernel, count, heads), out_shape...  37.8 us
  transfers between devices with their start and end apart: 8, of which 1 were waited for; matrix products, arithmetic and copies ran while one was open for 17% of the time, Pallas kernels for 72%

profile of v6, /device:TPU:0, one launch (start us, length us, event | category | flops | bytes accessed | tf_op | source)
XLA Modules:
  0.0 577.0 jit_solution(16822952147015175865)
XLA Ops:
  8.0 74.9 %opening.1 = (bf16[4,256,2048]{2,1,0:T(8,128)(2,1)}, bf16[4,4,2,64,640]{4,3,2,1,0:T(8,128)(2,1)}, f32[4,4,2,8,128]{4,3,2,1,0:T(8,128)}, bf16[4,64,512]{2,1,0:T(8,128)(2,1)}) custom-call(bf16[256,2048]{1,0:T(8,128)(2,1)} %bitcast.57, bf16[64,256]{1,0:T(8,128)(2,1)} %query_ref.1, bf16[64,256]{1,0:T(8,128)(2,1)} %key_ref.1, bf16[64,2048]{1,0:T(8,128)(2,1)} %value_ref.1, ...), custom_call_target="tpu_custom_call" | custom-call | bytes 1048576 | tf_op jit(solution)/shard_map/opening/pallas_call | solution.py:901
  82.9 10.9 %all-gather.6.cloned.1.call-done.wg_hbm = bf16[2048,1408]{1,0:T(8,128)(2,1)} async-done(((bf16[256,1408]{1,0:T(8,128)(2,1)}), bf16[2048,1408]{1,0:T(8,128)(2,1)}) %all-gather.6.cloned.1.call-update) | async-done | bytes 5767184 | tf_op jit(solution)/shard_map/all_gather | solution.py:1390
  94.6 0.9 slice_bitcast_fusion
  96.3 3.2 fusion
  99.7 1.0 fusion.2
  101.5 3.4 convolution_convert_fusion.3
  105.0 1.1 copy.34
  106.5 1.2 copy-done.5
  107.8 0.9 copy-done.13
  108.7 0.9 copy-done.15
  110.3 37.8 %attention_forward.1 = (bf16[4,256,512]{2,1,0:T(8,128)(2,1)S(1)}, f32[4,256,512]{2,1,0:T(8,128)S(1)}, bf16[4,4,160,128]{3,2,1,0:T(8,128)(2,1)S(1)}, f32[4,8,256]{2,1,0:T(8,128)S(1)}, bf16[4,256,2048]{2,1,0:T(8,128)(2,1)S(1)}) custom-call(bf16[4,256,640]{2,1,0:T(8,128)(2,1)S(1)} %bitcast.60, f32[4,256,1]{2,1,0:T(8,128)S(1)} %copy.35.segc_ref, ...), custom_call_target="tpu_custom_call" | custom-call | bytes 1048576 | tf_op jit(solution)/shard_map/attention_forward/pallas_call | solution.py:450
  148.1 1.0 copy-done.2
  149.1 1.3 copy-done.6
  151.0 2.1 copy-done.29
  153.1 1.2 copy-done.3
  154.3 77.8 %branch_step.1 = (bf16[4,256,2048]{2,1,0:T(8,128)(2,1)}, f32[256,2048]{1,0:T(8,128)S(1)}) custom-call(bf16[4,256,512]{2,1,0:T(8,128)(2,1)S(1)} %copy-done.3, bf16[8,4,64,512]{3,2,1,0:T(8,128)(2,1)} %bitcast.70, bf16[256,2048]{1,0:T(8,128)(2,1)S(1)} %bitcast.58, f32[1,2048]{1,0:T(1,128)S(1)} %slice.24.gain_ref), custom_call_target="tpu_custom_call" | custom-call | bytes 1048576 | tf_op jit(solution)/shard_map/branch_step/pallas_call | solution.py:1051
  232.2 1.4 copy-done.1
  233.5 11.7 %fusion.5 = f32[1024,1408]{1,0:T(8,128)} fusion(bf16[1024,2048]{1,0:T(8,128)(2,1)} %bitcast.86, bf16[2048,1408]{1,0:T(8,128)(2,1)} %all-gather.6.cloned.1.call-done.wg_hbm), kind=kOutput, calls=%fused_computation.26 | convolution fusion | flops 5905580032 | bytes 15728640 | tf_op jit(solution)/shard_map/dot_general | solution.py:24
  245.2 12.8 %multiply_convert_fusion.2 = (bf16[1024,1408]{1,0:T(8,128)(2,1)S(1)}, f32[1024,1408]{1,0:T(8,128)}) fusion(f32[1024,1408]{1,0:T(8,128)} %fusion.5, bf16[1024,2048]{1,0:T(8,128)(2,1)} %bitcast.87, bf16[2048,1408]{1,0:T(8,128)(2,1)} %all-gather.8.cloned.1.call-done.wu_hbm), kind=kOutput, calls=%fused_computation.10 | convolution fusion | flops 5914230784 | bytes 24379392 | tf_op jit(solution)/shard_map/dot_general | solution.py:24
  258.0 1.6 copy-done.33
  259.6 8.7 %convolution_convert_fusion.2 = bf16[2048,1408]{1,0:T(8,128)(2,1)} fusion(bf16[1024,2048]{1,0:T(8,128)(2,1)S(1)} %bitcast.69, bf16[1024,1408]{1,0:T(8,128)(2,1)S(1)} %get-tuple-element.69), kind=kOutput, calls=%fused_computation.7 | convolution fusion | flops 5908463616 | bytes 12845056 | tf_op jit(solution)/shard_map/dot_general | solution.py:32
  268.6 15.2 %multiply_convert_fusion = (bf16[1024,1408]{1,0:T(8,128)(2,1)S(1)}, bf16[1024,1408]{1,0:T(8,128)(2,1)}) fusion(f32[1024,1408]{1,0:T(8,128)} %fusion.5, f32[1024,1408]{1,0:T(8,128)} %get-tuple-element.121, bf16[1024,2048]{1,0:T(8,128)(2,1)} %bitcast.68, bf16[2048,1408]{1,0:T(8,128)(2,1)} %all-gather.10.cloned.1.call-done.wd_hbm), kind=kOutput, calls=%fused_computation.8 | convolution fusion | flops 5924323328 | bytes 27262976 | tf_op jit(solution)/shard_map/dot_general | solution.py:24
  283.8 1.5 copy-done.34
  285.3 8.7 %convolution_convert_fusion = bf16[2048,1408]{1,0:T(8,128)(2,1)} fusion(bf16[1024,2048]{1,0:T(8,128)(2,1)S(1)} %bitcast.89, bf16[1024,1408]{1,0:T(8,128)(2,1)S(1)} %get-tuple-element.67), kind=kOutput, calls=%fused_computation.5 | convolution fusion | flops 5908463616 | bytes 12845056 | tf_op jit(solution)/shard_map/dot_general | solution.py:32
  294.0 11.0 %convolution_convert_fusion.1 = bf16[2048,1408]{1,0:T(8,128)(2,1)} fusion(bf16[1024,2048]{1,0:T(8,128)(2,1)} %bitcast.88, bf16[1024,1408]{1,0:T(8,128)(2,1)} %get-tuple-element.66), kind=kOutput, calls=%fused_computation.6 | convolution fusion | flops 5908463616 | bytes 12845056 | tf_op jit(solution)/shard_map/dot_general | solution.py:32
  305.3 87.8 %rows_back.1 = (bf16[4,256,2048]{2,1,0:T(8,128)(2,1)}, f32[256,2048]{1,0:T(8,128)}, f32[1,2048]{1,0:T(1,128)}, bf16[4,256,2048]{2,1,0:T(8,128)(2,1)}, f32[4,256,512]{2,1,0:T(8,128)}) custom-call(bf16[4,256,1408]{2,1,0:T(8,128)(2,1)} %bitcast.77, bf16[4,256,1408]{2,1,0:T(8,128)(2,1)} %bitcast.76, bf16[2048,1408]{1,0:T(8,128)(2,1)} %all-gather.6.cloned.1.call-done.wg_hbm, ...), custom_call_target="tpu_custom_call" | custom-call | bytes 1048576 | tf_op jit(solution)/shard_map/rows_back/pallas_call | solution.py:1165
  393.1 4.9 bitcast_convert_fusion.1
  398.0 1.5 copy.38
  400.3 1.4 slice.25.gain_ref
  401.7 1.2 copy-done.4
  402.9 0.9 copy-done.14
  403.8 0.9 copy-done.16
  405.5 55.5 %attention_backward.1 = (bf16[4,256,640]{2,1,0:T(8,128)(2,1)S(1)}, bf16[256,2048]{1,0:T(8,128)(2,1)S(1)}) custom-call(bf16[4,256,640]{2,1,0:T(8,128)(2,1)S(1)} %bitcast.61, f32[4,256,1]{2,1,0:T(8,128)S(1)} %copy.35.segc_ref, f32[4,1,256]{2,1,0:T(1,128)S(1)} %get-tuple-element.118.segr_ref, bf16[4,64,256]{2,1,0:T(8,128)(2,1)S(1)} %copy-done.16, ...), custom_call_target="tpu_custom_call" | custom-call | bytes 1048576 | tf_op jit(solution)/shard_map/attention_backward/pallas_call | solution.py:486
  461.0 1.0 copy-done.9
  462.0 1.0 copy-done.11
  463.0 7.7 %bitcast_convert_fusion = bf16[2048,640]{1,0:T(8,128)(2,1)} fusion(bf16[4,256,2048]{2,1,0:T(8,128)(2,1)} %copy-done.32, bf16[4,256,640]{2,1,0:T(8,128)(2,1)} %copy-done.9), kind=kOutput, calls=%fused_computation.13 | convolution fusion | flops 2685665280 | bytes 8126464 | tf_op jit(solution)/shard_map/dot_general | solution.py:32
  470.8 0.9 copy-done.21
  471.7 81.7 %closing.1 = (f32[256,2048]{1,0:T(8,128)S(1)}, f32[8,128]{1,0:T(8,128)S(1)}, f32[64,256]{1,0:T(8,128)S(1)}, f32[64,256]{1,0:T(8,128)S(1)}, f32[64,2048]{1,0:T(8,128)S(1)}, /*index=5*/f32[64,2048]{1,0:T(8,128)S(1)}) custom-call(bf16[4,256,640]{2,1,0:T(8,128)(2,1)S(1)} %copy-done.10, bf16[2048,640]{1,0:T(8,128)(2,1)} %bitcast.78, ...), custom_call_target="tpu_custom_call" | custom-call | bytes 1048576 | tf_op jit(solution)/shard_map/closing/pallas_call | solution.py:1328
  553.4 1.3 copy-done.7
  554.8 0.8 copy-done.17
  556.3 1.2 convert_element_type.77
  557.5 1.2 convert_bitcast_fusion
  558.7 2.9 copy.39
  562.2 2.4 convert_element_type.78
  564.6 1.0 copy.48
  565.6 1.3 copy.49
  568.2 0.8 copy.52
  568.9 0.8 copy.53
  (97 shorter events, 9.7 us)
Async XLA Ops:
  7.2 86.6 %all-gather.6.cloned.1.call-start = ((), (), s32[]{:S(2)}) async-start(), calls=%async_computation.4 | async-start | bytes 6488064 | tf_op jit(solution)/shard_map/all_gather | solution.py:1390
  7.9 145.2 %all-gather.12.cloned.1.call-start = ((), (), s32[]{:S(2)}) async-start(), calls=%async_computation.11 | async-start | bytes 2359296 | tf_op jit(solution)/shard_map/all_gather | solution.py:1392
  93.8 151.4 %all-gather.8.cloned.1.call-start = ((), (), s32[]{:S(2)}) async-start(), calls=%async_computation.5 | async-start | bytes 6488064 | tf_op jit(solution)/shard_map/all_gather | solution.py:1393
  94.6 174.0 %all-gather.10.cloned.1.call-start = ((), (), s32[]{:S(2)}) async-start(), calls=%async_computation.6 | async-start | bytes 6488064 | tf_op jit(solution)/shard_map/all_gather | solution.py:1400
  96.3 3.4 copy-start.31
  99.7 1.8 copy-start.35
  100.7 4.2 copy-start.32
  101.5 3.5 copy-start.36
  101.5 4.7 copy-start.39
  104.9 48.1 %copy-start = (bf16[1,1,256,2048]{3,2,1,0:T(8,128)(2,1)S(1)}, bf16[1,1,256,2048]{3,2,1,0:T(8,128)(2,1)}, u32[]{:S(2)}) copy-start(bf16[1,1,256,2048]{3,2,1,0:T(8,128)(2,1)} %param.15) | copy-start | bytes 3145732
  106.1 356.9 %reduce-scatter.5.cloned.1.call-start = ((), (), s32[]{:S(2)}) async-start(), calls=%async_computation.7 | async-start | bytes 6488064 | tf_op jit(solution)/shard_map/reduce_scatter | solution.py:1421
  106.5 138.7 %copy-start.22 = (f32[1,2048]{1,0:T(1,128)}, f32[1,2048]{1,0:T(1,128)S(1)}, u32[]{:S(2)}) copy-start(f32[1,2048]{1,0:T(1,128)S(1)} %slice.24.gain_ref) | copy-start | bytes 24580
  106.5 1.2 copy-start.5
  107.8 0.9 copy-start.13
  108.7 0.9 copy-start.15
  109.6 0.7 copy-start.23
  148.1 1.0 copy-start.2
  149.1 1.3 copy-start.6
  151.0 2.1 copy-start.29
  153.1 1.2 copy-start.3
  232.2 1.4 copy-start.1
  245.2 14.4 %copy-start.30 = (bf16[4,256,2048]{2,1,0:T(8,128)(2,1)S(1)}, bf16[4,256,2048]{2,1,0:T(8,128)(2,1)}, u32[]{:S(2)}) copy-start(bf16[4,256,2048]{2,1,0:T(8,128)(2,1)} %copy-done.29) | copy-start | bytes 12582916
  258.0 1.6 copy-start.33
  268.3 194.7 %reduce-scatter.7.cloned.1.call-start = ((), (), s32[]{:S(2)}) async-start(), calls=%async_computation.8 | async-start | bytes 6488064 | tf_op jit(solution)/shard_map/reduce_scatter | solution.py:1421
  268.6 16.7 %copy-start.40 = (bf16[4,256,2048]{2,1,0:T(8,128)(2,1)S(1)}, bf16[4,256,2048]{2,1,0:T(8,128)(2,1)}, u32[]{:S(2)}) copy-start(bf16[4,256,2048]{2,1,0:T(8,128)(2,1)} %get-tuple-element.60) | copy-start | bytes 12582916
  283.8 1.5 copy-start.34
  305.0 165.7 %reduce-scatter.9.cloned.1.call-start = ((), (), s32[]{:S(2)}) async-start(), calls=%async_computation.9 | async-start | bytes 2359296 | tf_op jit(solution)/shard_map/reduce_scatter | solution.py:1421
  399.5 2.2 copy-start.24
  399.5 162.7 %reduce-scatter.11.cloned.1.call-start = ((), (), s32[]{:S(2)}) async-start(), calls=%async_computation.10 | async-start | bytes 6488064 | tf_op jit(solution)/shard_map/reduce_scatter | solution.py:1421
  401.7 1.2 copy-start.4
  402.9 0.9 copy-start.14
  403.8 0.9 copy-start.16
  404.7 0.8 copy-start.26
  461.0 1.1 copy-start.9
  462.0 1.0 copy-start.11
  463.0 7.7 %copy-start.10 = (bf16[4,256,640]{2,1,0:T(8,128)(2,1)S(1)}, bf16[4,256,640]{2,1,0:T(8,128)(2,1)}, u32[]{:S(2)}) copy-start(bf16[4,256,640]{2,1,0:T(8,128)(2,1)} %copy-done.9) | copy-start | bytes 3932164
  463.0 7.7 %copy-start.27 = (f32[1,2048]{1,0:T(1,128)S(1)}, f32[1,2048]{1,0:T(1,128)}, u32[]{:S(2)}) copy-start(f32[1,2048]{1,0:T(1,128)} %slice.25.gain_ref) | copy-start | bytes 24580
  463.0 7.7 %copy-start.28 = (f32[1,2048]{1,0:T(1,128)S(1)}, f32[1,2048]{1,0:T(1,128)}, u32[]{:S(2)}) copy-start(f32[1,2048]{1,0:T(1,128)} %get-tuple-element.75.gsum_two_ref) | copy-start | bytes 24580
  470.8 1.0 copy-start.21
  471.7 84.6 %copy-start.38 = (bf16[256,1408]{1,0:T(8,128)(2,1)S(1)}, bf16[256,1408]{1,0:T(8,128)(2,1)}, u32[]{:S(2)}) copy-start(bf16[256,1408]{1,0:T(8,128)(2,1)} %reduce-scatter.7.cloned.1.call-done) | copy-start | bytes 2162692
  471.7 85.8 %copy-start.37 = (bf16[256,1408]{1,0:T(8,128)(2,1)S(1)}, bf16[256,1408]{1,0:T(8,128)(2,1)}, u32[]{:S(2)}) copy-start(bf16[256,1408]{1,0:T(8,128)(2,1)} %reduce-scatter.5.cloned.1.call-done) | copy-start | bytes 2162692
  553.4 1.3 copy-start.7
  554.7 0.8 copy-start.17
  555.5 0.8 copy-start.19
  556.3 8.3 %copy-start.12 = (bf16[256,2048]{1,0:T(8,128)(2,1)S(1)}, bf16[256,2048]{1,0:T(8,128)(2,1)}, u32[]{:S(2)}) copy-start(bf16[256,2048]{1,0:T(8,128)(2,1)} %copy-done.11) | copy-start | bytes 3145732
  557.5 8.0 %copy-start.8 = (f32[256,2048]{1,0:T(8,128)S(1)}, f32[256,2048]{1,0:T(8,128)}, u32[]{:S(2)}) copy-start(f32[256,2048]{1,0:T(8,128)} %copy-done.7) | copy-start | bytes 6291460
  562.2 5.9 %copy-start.20 = (f32[64,2048]{1,0:T(8,128)S(1)}, f32[64,2048]{1,0:T(8,128)}, u32[]{:S(2)}) copy-start(f32[64,2048]{1,0:T(8,128)} %copy-done.19) | copy-start | bytes 1572868
  564.6 4.4 copy-start.18
  (1 other events, 0.6 us)
Sparse Core Ops, SparseCore 0:
  9.7 84.0 all-gather.5
  95.4 29.6 all-gather.11
  126.8 62.5 all-gather.7
  191.5 64.8 all-gather.9
  268.4 74.9 reduce-scatter.4
  345.6 63.2 reduce-scatter.6
  411.2 42.1 reduce-scatter.8
  455.7 80.3 reduce-scatter.10

commit v7 on v6

--- a/solution.py
+++ b/solution.py
@@ -90,6 +90,7 @@
 
 def forward_kernel(
     count,
+    dps,
     heads,
     qkv_ref,
     segc_ref,
@@ -98,11 +99,13 @@
     right_ref,
     rows_ref,
     cot_ref,
+    old_ref,
     att_ref,
     rden_ref,
     carry_ref,
     csum_ref,
     cots_ref,
+    downs_ref,
     send_state,
     send_sum,
     part,
@@ -111,8 +114,12 @@
     f_send,
     f_recv,
     local_sem,
+    h_send,
+    h_recv,
+    b_send,
+    b_recv,
 ):
-    place, f = lax.axis_index("seq"), lax.axis_index("feat")
+    place, f, d = lax.axis_index("seq"), lax.axis_index("feat"), lax.axis_index("dp")
     groups, block = qkv_ref.shape[0], qkv_ref.shape[1]
     width = heads * FDIM
     tables = (left_ref, right_ref, rows_ref)
@@ -138,9 +145,16 @@
     chain = [lax.rem(place + 1, count), lax.rem(place + count - 1, count)]
     stay = pltpu.make_async_copy(cot_ref, cots_ref.at[f], local_sem.at[0])
     stay.start()
-    greet(square_targets(f) + [{"seq": c} for c in chain])
+    greet(
+        square_targets(f)
+        + [{"seq": c} for c in chain]
+        + [{"dp": lax.rem(d + o, dps)} for o in range(1, dps)]
+    )
     gather = SquareGather(cots_ref, f, f_send, f_recv, cot_ref)
     gather.start()
+    line = LineHop(downs_ref, 2, place, d, count, h_send, h_recv)
+    beside = SiblingHop(downs_ref, 1, place, d, count, dps, b_send, b_recv)
+    beside.start()
 
     @pl.when(place == 0)
     def _():
@@ -203,6 +217,7 @@
         return none
 
     lax.fori_loop(0, groups, attend, 0)
+    line.start()
     gather.relay()
 
     def carry_on(g, none):
@@ -241,6 +256,9 @@
 
     stay.wait()
     gather.finish()
+    beside.finish()
+    line.arrive()
+    line.finish()
 
 
 def backward_kernel(
@@ -259,8 +277,11 @@
     ga_ref,
     down_ref,
     res_ref,
+    acc_ref,
+    came_ref,
     out_ref,
     final_ref,
+    next_ref,
     gn,
     send_state,
     send_sum,
@@ -275,6 +296,7 @@
     f_send,
     f_recv,
     local_sem,
+    *line_refs,
 ):
     place, f = lax.axis_index("seq"), lax.axis_index("feat")
     groups, block = qkv_ref.shape[0], qkv_ref.shape[1]
@@ -304,6 +326,8 @@
     fill = pltpu.make_async_copy(down_ref, terms, local_sem.at[0])
     fill.start()
     ring = SquareSum(terms, land, f, f_send, f_recv)
+    line = LineSum(acc_ref, came_ref, next_ref, line_refs[0], line_refs[1], 2, place, count, *line_refs[2:])
+    line.load()
 
     @pl.when(place == count - 1)
     def _():
@@ -392,6 +416,7 @@
         return none
 
     lax.fori_loop(0, groups, pull, 0)
+    line.start()
     ring.relay()
 
     def carry_back(g, none):
@@ -435,29 +460,34 @@
 
     by_rows(ring, add_up)
     ring.finish()
+    line.arrive()
+    line.finish()
 
 
 def whole_vmem(count):
     return [pl.BlockSpec(memory_space=pltpu.VMEM)] * count
 
 
-def attention_forward(qkv, segc, segr, tables, cot_own, heads):
+def attention_forward(qkv, segc, segr, tables, cot_own, downs, heads):
     groups, block, _ = qkv.shape
-    count = lax.axis_size("seq")
+    count, dps = downs.shape[:2]
+    others = max(dps - 1, 1)
     dma = pltpu.SemaphoreType.DMA
     states = (groups, heads, STATE, HV)
     sums = (groups, 8, LANES)
     return pl.pallas_call(
-        functools.partial(forward_kernel, count, heads),
+        functools.partial(forward_kernel, count, dps, heads),
         out_shape=(
             jax.ShapeDtypeStruct((groups, block, heads * HV), bf16),
             jax.ShapeDtypeStruct((groups, block, heads * HV), f32),
             jax.ShapeDtypeStruct(states, bf16),
             jax.ShapeDtypeStruct(sums, f32),
             jax.ShapeDtypeStruct((groups,) + cot_own.shape, bf16),
+            jax.ShapeDtypeStruct(downs.shape, bf16),
         ),
-        in_specs=whole_vmem(6) + in_place(1),
-        out_specs=tuple(whole_vmem(4) + in_place(1)),
+        in_specs=whole_vmem(6) + in_place(2),
+        out_specs=tuple(whole_vmem(4) + in_place(2)),
+        input_output_aliases={7: 5},
         scratch_shapes=[
             pltpu.VMEM(states, bf16),
             pltpu.VMEM(sums, f32),
@@ -467,17 +497,21 @@
             dma((6,)),
             dma((6,)),
             dma((1,)),
+            dma((2,)),
+            dma((2,)),
+            dma((2, others)),
+            dma((2, others)),
         ],
         compiler_params=pltpu.CompilerParams(
             collective_id=0, has_side_effects=True, vmem_limit_bytes=40 << 20
         ),
         cost_estimate=pl.CostEstimate(flops=0, bytes_accessed=1 << 20, transcendentals=0),
         name="attention_forward",
-    )(qkv, segc, segr, *tables, cot_own)
+    )(qkv, segc, segr, *tables, cot_own, downs)
 
 
 def attention_backward(
-    qkv, segc, segr, tables, att, rden, carry, csum, ga, down, residual, heads
+    qkv, segc, segr, tables, att, rden, carry, csum, ga, down, residual, acc, came, heads
 ):
     groups, block, wide = qkv.shape
     count = lax.axis_size("seq")
@@ -488,9 +522,10 @@
         out_shape=(
             jax.ShapeDtypeStruct((groups, block, wide), bf16),
             jax.ShapeDtypeStruct(residual.shape, bf16),
+            jax.ShapeDtypeStruct(came.shape, bf16),
         ),
-        in_specs=whole_vmem(11) + in_place(1) + whole_vmem(1),
-        out_specs=tuple(whole_vmem(2)),
+        in_specs=whole_vmem(11) + in_place(1) + whole_vmem(1) + in_place(2),
+        out_specs=tuple(whole_vmem(2) + in_place(1)),
         scratch_shapes=[
             pltpu.VMEM((groups, heads, block, 2 * HV), bf16),
             pltpu.VMEM(states, bf16),
@@ -506,13 +541,14 @@
             pltpu.SemaphoreType.DMA((6,)),
             pltpu.SemaphoreType.DMA((6,)),
             pltpu.SemaphoreType.DMA((1,)),
-        ],
+        ]
+        + line_scratch(acc.shape[1:]),
         compiler_params=pltpu.CompilerParams(
             collective_id=1, has_side_effects=True, vmem_limit_bytes=48 << 20
         ),
         cost_estimate=pl.CostEstimate(flops=0, bytes_accessed=1 << 20, transcendentals=0),
         name="attention_backward",
-    )(qkv, segc, segr, *tables, att, rden, carry, csum, ga, down, residual)
+    )(qkv, segc, segr, *tables, att, rden, carry, csum, ga, down, residual, acc, came)
 
 
 def peers(f):
@@ -647,6 +683,140 @@
     def finish(self):
         for c in self.cross + self.near + self.late:
             c.wait_send()
+
+
+class LineHop:
+    def __init__(self, ref, k, s, d, seqs, send_sem, recv_sem, own=None):
+        back, ahead = lax.rem(s + seqs - (k - 1), seqs), lax.rem(s + k - 1, seqs)
+        up, down = lax.rem(s + 1, seqs), lax.rem(s + seqs - 1, seqs)
+
+        def copy(i, block, to):
+            src = ref.at[block, d] if own is None else own
+            return push(src, ref.at[block, d], send_sem.at[i], recv_sem.at[i], {"seq": to})
+
+        self.copies = (copy(0, back, up), copy(1, ahead, down))
+        self.sends = ((s >= k - 1) & (s < seqs - 1), (s + k - 1 < seqs) & (s > 0))
+        self.comes = (s >= k, s + k < seqs)
+
+    def start(self):
+        for c, sends in zip(self.copies, self.sends):
+            pl.when(sends)(c.start)
+
+    def arrive(self):
+        for c, comes in zip(self.copies, self.comes):
+            pl.when(comes)(c.wait_recv)
+
+    def finish(self):
+        for c, sends in zip(self.copies, self.sends):
+            pl.when(sends)(c.wait_send)
+
+
+class SiblingHop:
+    def __init__(self, ref, k, s, d, seqs, dps, send_sem, recv_sem, own=None):
+        back, ahead = lax.rem(s + seqs - k, seqs), lax.rem(s + k, seqs)
+        blocks = ((back, s >= k), (ahead, s + k < seqs)) if k else ((s, s >= 0),)
+        self.groups = []
+        for i, (block, there) in enumerate(blocks):
+            copies = []
+            for o in range(1, dps):
+                src = ref.at[block, d] if own is None else own
+                copies.append(
+                    push(
+                        src,
+                        ref.at[block, d],
+                        send_sem.at[i, o - 1],
+                        recv_sem.at[i, o - 1],
+                        {"dp": lax.rem(d + o, dps)},
+                    )
+                )
+            self.groups.append((there, copies))
+
+    def each(self, act):
+        for there, copies in self.groups:
+
+            @pl.when(there)
+            def _():
+                for c in copies:
+                    act(c)
+
+    def start(self):
+        self.each(lambda c: c.start())
+
+    def finish(self):
+        self.each(lambda c: c.wait_recv())
+        self.each(lambda c: c.wait_send())
+
+
+def add_block(into, more):
+    def one(i, none):
+        rows = pl.ds(pl.multiple_of(i * 32, 32), 32)
+        into[rows, :] = (into[rows, :].astype(f32) + more[rows, :].astype(f32)).astype(into.dtype)
+        return none
+
+    lax.fori_loop(0, into.shape[0] // 32, one, 0)
+
+
+class LineSum:
+    def __init__(self, acc, came, to, room, more, t, s, seqs, send_sem, recv_sem, local_sem):
+        self.room, self.more, self.t, self.s, self.seqs = room, more, t, s, seqs
+        up, down = lax.rem(s + 1, seqs), lax.rem(s + seqs - 1, seqs)
+        blocks = (lax.rem(s + seqs - t, seqs), lax.rem(s + t, seqs))
+        self.sends = (s < t, s > seqs - 1 - t)
+        self.added = tuple(
+            sends & here
+            for sends, here in zip(self.sends, (s > 0, s < seqs - 1))
+        )
+        self.loads = [
+            pltpu.make_async_copy(acc.at[b], room.at[i], local_sem.at[i])
+            for i, b in enumerate(blocks)
+        ]
+        if t > 1:
+            self.extra = [
+                pltpu.make_async_copy(came.at[i], more.at[i], local_sem.at[2 + i])
+                for i in range(2)
+            ]
+        self.copies = [
+            push(room.at[i], to.at[i], send_sem.at[i], recv_sem.at[i], {"seq": p})
+            for i, p in enumerate((up, down))
+        ]
+        self.comes = ((s > 0) & (s - 1 < t), (s < seqs - 1) & (s + 1 > seqs - 1 - t))
+
+    def load(self):
+        for i in range(2):
+            pl.when(self.sends[i])(self.loads[i].start)
+            if self.t > 1:
+                pl.when(self.added[i])(self.extra[i].start)
+
+    def start(self):
+        for i in range(2):
+            pl.when(self.sends[i])(self.loads[i].wait)
+            if self.t > 1:
+
+                @pl.when(self.added[i])
+                def _():
+                    self.extra[i].wait()
+                    add_block(self.room.at[i], self.more.at[i])
+
+            pl.when(self.sends[i])(self.copies[i].start)
+
+    def arrive(self):
+        for i in range(2):
+            pl.when(self.comes[i])(self.copies[i].wait_recv)
+
+    def finish(self):
+        for i in range(2):
+            pl.when(self.sends[i])(self.copies[i].wait_send)
+
+
+def line_scratch(shape):
+    dma = pltpu.SemaphoreType.DMA
+    return [
+        pltpu.VMEM((2,) + shape, bf16),
+        pltpu.VMEM((2,) + shape, bf16),
+        dma((2,)),
+        dma((2,)),
+        dma((4,)),
+    ]
 
 
 class RowSum:
@@ -749,10 +919,12 @@
     out_ref,
     one_ref,
     two_ref,
+    down_ref,
     x_ref,
     w_ref,
     g_ref,
     o_ref,
+    downs_ref,
     pack,
     opack,
     tile,
@@ -765,6 +937,10 @@
     d_send,
     d_recv,
     local_sem,
+    h_send,
+    h_recv,
+    b_send,
+    b_recv,
 ):
     f, s, d = lax.axis_index("feat"), lax.axis_index("seq"), lax.axis_index("dp")
     parts, rows_each = pack.shape[0], pack.shape[1]
@@ -857,6 +1033,12 @@
         for k in range(1, seqs):
             start_all(to_column(n, k))
         start_all(to_sibling(n, 0))
+    hop = LineHop(downs_ref, 1, s, d, seqs, h_send, h_recv, down_ref)
+    beside = SiblingHop(downs_ref, 0, s, d, seqs, dps, b_send, b_recv, down_ref)
+    own_down = pltpu.make_async_copy(down_ref, downs_ref.at[s, d], local_sem.at[4])
+    own_down.start()
+    hop.start()
+    beside.start()
     for n in range(parts):
         for k in range(1, seqs):
             for c in to_column(n, k):
@@ -878,6 +1060,10 @@
         for c in pair:
             c.wait_send()
     stay.wait()
+    own_down.wait()
+    hop.arrive()
+    hop.finish()
+    beside.finish()
     own_out.wait()
     for c in out_shares:
         c.wait_recv()
@@ -890,7 +1076,7 @@
     return [pl.BlockSpec(memory_space=pl.ANY)] * count
 
 
-def opening(own, w_query, w_key, w_value, w_out, gain_one, gain_two):
+def opening(own, w_query, w_key, w_value, w_out, gain_one, gain_two, w_down):
     parts, seqs, dps = (lax.axis_size(a) for a in ALL)
     block, width = own.shape
     rows_each = w_query.shape[0]
@@ -898,16 +1084,17 @@
     others = max(dps - 1, 1)
     dma = pltpu.SemaphoreType.DMA
     out_wide = w_out.shape[1] // parts
-    x_all, w_all, g_all, o_own = pl.pallas_call(
+    x_all, w_all, g_all, o_own, downs = pl.pallas_call(
         functools.partial(opening_kernel, seqs, dps),
         out_shape=(
             jax.ShapeDtypeStruct((parts, block, width), bf16),
             jax.ShapeDtypeStruct((parts, seqs, dps, rows_each, wide), bf16),
             jax.ShapeDtypeStruct((parts, seqs, dps, 8, HV), f32),
             jax.ShapeDtypeStruct((parts, rows_each, out_wide), bf16),
+            jax.ShapeDtypeStruct((seqs, dps) + w_down.shape, bf16),
         ),
-        in_specs=in_place(1) + whole_vmem(6),
-        out_specs=tuple(in_place(4)),
+        in_specs=in_place(1) + whole_vmem(6) + in_place(1),
+        out_specs=tuple(in_place(5)),
         scratch_shapes=[
             pltpu.VMEM((parts, rows_each, wide), bf16),
             pltpu.VMEM((parts, rows_each, out_wide), bf16),
@@ -920,14 +1107,18 @@
             dma((2, seqs - 1, parts)),
             dma((2, others, seqs, parts)),
             dma((2, others, seqs, parts)),
-            dma((4,)),
+            dma((5,)),
+            dma((2,)),
+            dma((2,)),
+            dma((1, others)),
+            dma((1, others)),
         ],
         compiler_params=pltpu.CompilerParams(collective_id=2, has_side_effects=True),
         cost_estimate=pl.CostEstimate(flops=0, bytes_accessed=1 << 20, transcendentals=0),
         name="opening",
-    )(own, w_query, w_key, w_value, w_out, gain_one, gain_two)
+    )(own, w_query, w_key, w_value, w_out, gain_one, gain_two, w_down)
     gains = g_all[..., :2, :rows_each].transpose(3, 0, 1, 2, 4).reshape(2, width)
-    return x_all, w_all.reshape(width, wide), gains, o_own
+    return x_all, w_all.reshape(width, wide), gains, o_own, downs
 
 
 def inverse_rms(values):
@@ -1015,10 +1206,39 @@
 
 
 def branch_kernel(
-    att_ref, w_ref, tok_ref, gain_ref, rows_ref, res_ref, part, land, s_send, s_recv, g_send, g_recv
+    att_ref,
+    w_ref,
+    tok_ref,
+    gain_ref,
+    old_ref,
+    rows_ref,
+    res_ref,
+    downs_ref,
+    part,
+    land,
+    s_send,
+    s_recv,
+    g_send,
+    g_recv,
+    h_send,
+    h_recv,
+    b_send,
+    b_recv,
+    e_send,
+    e_recv,
 ):
-    f = lax.axis_index("feat")
-    greet(square_targets(f))
+    f, s, d = lax.axis_index("feat"), lax.axis_index("seq"), lax.axis_index("dp")
+    seqs, dps = downs_ref.shape[:2]
+    greet(
+        square_targets(f)
+        + [{"seq": lax.rem(s + 1, seqs)}, {"seq": lax.rem(s + seqs - 1, seqs)}]
+        + [{"dp": lax.rem(d + o, dps)} for o in range(1, dps)]
+    )
+    line = LineHop(downs_ref, 3, s, d, seqs, h_send, h_recv)
+    beside = SiblingHop(downs_ref, 2, s, d, seqs, dps, b_send, b_recv)
+    after = SiblingHop(downs_ref, 3, s, d, seqs, dps, e_send, e_recv)
+    line.start()
+    beside.start()
     ring = summed_products(part, land, f, [(att_ref, ByShare(w_ref))], s_send, s_recv)
 
     def finish_rows(rows, total):
@@ -1030,8 +1250,13 @@
     gather = SquareGather(rows_ref, f, g_send, g_recv)
     gather.start()
     ring.finish()
+    line.arrive()
+    after.start()
     gather.relay()
     gather.finish()
+    beside.finish()
+    after.finish()
+    line.finish()
 
 
 def square_scratch(parts, block, width):
@@ -1044,8 +1269,9 @@
     ]
 
 
-def branch_step(att, out_w, own, gain_two):
+def branch_step(att, out_w, own, gain_two, downs):
     parts, block, _ = att.shape
+    others = max(downs.shape[1] - 1, 1)
     width = own.shape[1]
     dma = pltpu.SemaphoreType.DMA
     return pl.pallas_call(
@@ -1053,16 +1279,20 @@
         out_shape=(
             jax.ShapeDtypeStruct((parts, block, width), bf16),
             jax.ShapeDtypeStruct((block, width), f32),
+            jax.ShapeDtypeStruct(downs.shape, bf16),
         ),
-        in_specs=whole_vmem(4),
-        out_specs=tuple(whole_vmem(2)),
-        scratch_shapes=square_scratch(parts, block, width) + [dma((6,)), dma((6,))],
+        in_specs=whole_vmem(4) + in_place(1),
+        out_specs=tuple(whole_vmem(2) + in_place(1)),
+        input_output_aliases={4: 2},
+        scratch_shapes=square_scratch(parts, block, width)
+        + [dma((6,)), dma((6,)), dma((2,)), dma((2,))]
+        + [dma((2, others))] * 4,
         compiler_params=pltpu.CompilerParams(
             collective_id=3, has_side_effects=True, vmem_limit_bytes=48 << 20
         ),
         cost_estimate=pl.CostEstimate(flops=0, bytes_accessed=1 << 20, transcendentals=0),
         name="branch_step",
-    )(att, out_w, own, gain_two)
+    )(att, out_w, own, gain_two, downs)
 
 
 def rows_back_kernel(
@@ -1076,11 +1306,13 @@
     mixed_hbm,
     wd_hbm,
     wo_hbm,
+    acc_ref,
     all_ref,
     gres_ref,
     gsum_ref,
     down_ref,
     ga_ref,
+    next_ref,
     part,
     land,
     wg,
@@ -1094,8 +1326,10 @@
     g_recv,
     local_sem,
     tile_sem,
+    *line_refs,
 ):
-    f = lax.axis_index("feat")
+    f, s = lax.axis_index("feat"), lax.axis_index("seq")
+    seqs = acc_ref.shape[0]
     weights = [
         ByTiles(src, dst, tile_sem.at[i], 512)
         for i, (src, dst) in enumerate(((wg_hbm, wg), (wu_hbm, wu)))
@@ -1109,7 +1343,13 @@
     ]
     for c in fills:
         c.start()
-    greet(square_targets(f))
+    line = LineSum(acc_ref, None, next_ref, line_refs[0], None, 1, s, seqs, *line_refs[1:])
+    line.load()
+    greet(
+        square_targets(f)
+        + [{"seq": lax.rem(s + 1, seqs)}, {"seq": lax.rem(s + seqs - 1, seqs)}]
+    )
+    line.start()
     pairs = [(gg_ref, weights[0]), (gu_ref, weights[1])]
 
     def down_products():
@@ -1154,10 +1394,12 @@
     gather.far()
     attended_grad(across)
     gather.sent()
+    line.arrive()
+    line.finish()
 
 
 def rows_back(
-    grad_gate, grad_up, gate_w, up_w, residual, cot_own, gain_two, mixed, down_w, out_w
+    grad_gate, grad_up, gate_w, up_w, residual, cot_own, gain_two, mixed, down_w, out_w, acc
 ):
     parts, block, hidden = grad_gate.shape
     width = residual.shape[1]
@@ -1170,9 +1412,10 @@
             jax.ShapeDtypeStruct((1, width), f32),
             jax.ShapeDtypeStruct((parts, block, width), bf16),
             jax.ShapeDtypeStruct((parts, block, out_w.shape[3]), f32),
+            jax.ShapeDtypeStruct((2,) + acc.shape[1:], bf16),
         ),
-        in_specs=whole_vmem(2) + in_place(2) + whole_vmem(3) + in_place(3),
-        out_specs=tuple(whole_vmem(5)),
+        in_specs=whole_vmem(2) + in_place(2) + whole_vmem(3) + in_place(4),
+        out_specs=tuple(whole_vmem(5) + in_place(1)),
         scratch_shapes=square_scratch(parts, block, width)[:2]
         + [
             pltpu.VMEM((width, hidden), bf16),
@@ -1182,13 +1425,14 @@
             pltpu.VMEM(out_w.shape, bf16),
         ]
         + [dma((6,))] * 4
-        + [dma((3,)), dma((2, width // 512))],
+        + [dma((3,)), dma((2, width // 512))]
+        + line_scratch(acc.shape[1:])[1:],
         compiler_params=pltpu.CompilerParams(
             collective_id=4, has_side_effects=True, vmem_limit_bytes=60 << 20
         ),
         cost_estimate=pl.CostEstimate(flops=0, bytes_accessed=1 << 20, transcendentals=0),
         name="rows_back",
-    )(grad_gate, grad_up, gate_w, up_w, residual, cot_own, gain_two, mixed, down_w, out_w)
+    )(grad_gate, grad_up, gate_w, up_w, residual, cot_own, gain_two, mixed, down_w, out_w, acc)
 
 
 def closing_kernel(
@@ -1202,12 +1446,15 @@
     gsum_two_ref,
     term_ref,
     osum_ref,
+    acc_ref,
+    came_ref,
     x_ref,
     tile_ref,
     query_ref,
     key_ref,
     value_ref,
     ograd_ref,
+    dgrad_ref,
     part,
     land,
     s_send,
@@ -1224,8 +1471,12 @@
     oland,
     o_send,
     o_recv,
-    *sum_scratch,
+    last_ref,
+    mine,
+    mine_sem,
+    *more_refs,
 ):
+    line_refs, sum_scratch = more_refs[:5], more_refs[5:]
     f, s, d = lax.axis_index("feat"), lax.axis_index("seq"), lax.axis_index("dp")
     parts = 4
     others = [lax.rem(d + k, dps) for k in range(1, dps)]
@@ -1238,6 +1489,10 @@
     greet(
         [{"feat": a, "seq": b} for a, b in circle] + [{"dp": o} for o in others]
     )
+    line = LineSum(acc_ref, came_ref, last_ref, line_refs[0], line_refs[1], 3, s, seqs, *line_refs[2:])
+    line.load()
+    own_block = pltpu.make_async_copy(acc_ref.at[s], mine, mine_sem.at[0])
+    own_block.start()
     rows_sum = row_sum(term_ref, sum_scratch, f, s, d, seqs, dps)
     rows_sum.start()
     outs = [
@@ -1249,6 +1504,7 @@
     ring = summed_products(
         part, land, f, [(dqkv_ref, w_ref)], s_send, s_recv, rows_sum.over_seq
     )
+    line.start()
     gsum[...] = jnp.zeros_like(gsum)
 
     def finish_rows(rows, grad):
@@ -1313,11 +1569,27 @@
     each = ograd_ref.shape[1] // parts
     for p in range(parts):
         ograd_ref[:, p * each : (p + 1) * each] = oland[p].astype(f32)
+    own_block.wait()
+    line.arrive()
+
+    def widen(i, none):
+        rows = pl.ds(pl.multiple_of(i * 32, 32), 32)
+        dgrad_ref[rows, :] = mine[rows, :].astype(f32)
+        return none
+
+    lax.fori_loop(0, mine.shape[0] // 32, widen, 0)
+    for i in range(2):
+
+        @pl.when(line.comes[i])
+        def _():
+            add_block(dgrad_ref, last_ref.at[i])
+
+    line.finish()
     for c in outs + sends + last:
         c.wait_send()
 
 
-def closing(dqkv, qkv_w, own, grad_residual, gain_one, gain_two_sum, qkv_term, out_sum):
+def closing(dqkv, qkv_w, own, grad_residual, gain_one, gain_two_sum, qkv_term, out_sum, acc, came):
     parts, seqs, dps = (lax.axis_size(a) for a in ALL)
     block, width = own.shape
     others = max(dps - 1, 1)
@@ -1334,9 +1606,10 @@
             jax.ShapeDtypeStruct((rows_each, HEADS * FDIM), f32),
             jax.ShapeDtypeStruct((rows_each, HEADS * HV), f32),
             jax.ShapeDtypeStruct((rows_each, HEADS * HV), f32),
+            jax.ShapeDtypeStruct(acc.shape[1:], f32),
         ),
-        in_specs=whole_vmem(8),
-        out_specs=tuple(whole_vmem(6)),
+        in_specs=whole_vmem(8) + in_place(2),
+        out_specs=tuple(whole_vmem(7)),
         scratch_shapes=square_scratch(parts, block, width)
         + [
             pltpu.VMEM((1, width), f32),
@@ -1351,14 +1624,18 @@
             pltpu.VMEM(out_sum.shape, bf16),
             dma((3,)),
             dma((3,)),
+            pltpu.VMEM(came.shape, bf16),
+            pltpu.VMEM(acc.shape[1:], bf16),
+            dma((1,)),
         ]
+        + line_scratch(acc.shape[1:])
         + row_sum_scratch(qkv_term.shape),
         compiler_params=pltpu.CompilerParams(
             collective_id=5, has_side_effects=True, vmem_limit_bytes=48 << 20
         ),
         cost_estimate=pl.CostEstimate(flops=0, bytes_accessed=1 << 20, transcendentals=0),
         name="closing",
-    )(dqkv, qkv_w, own, grad_residual, gain_one, gain_two_sum, qkv_term, out_sum)
+    )(dqkv, qkv_w, own, grad_residual, gain_one, gain_two_sum, qkv_term, out_sum, acc, came)
 
 
 def local(
@@ -1383,27 +1660,28 @@
     own = tokens.reshape(block, width)
     cot_own = cotangent.reshape(block, width)
 
-    x_all, qkv_w, gains, out_share = opening(
-        own, w_query, w_key, w_value, w_out.T, norm1_gain[None], norm2_gain[None]
+    x_all, qkv_w, gains, out_share, downs = opening(
+        own, w_query, w_key, w_value, w_out.T, norm1_gain[None], norm2_gain[None], w_down.T
     )
     qkv_width = qkv_w.shape[1]
+    x_all, w_gate, w_up = lax.optimization_barrier((x_all, w_gate, w_up))
+    out_w = lax.all_gather(out_share[None], ("seq", "dp"), axis=0, tiled=True)
     gate_w = lax.all_gather(w_gate, ("seq", "dp"), axis=0, tiled=True)
-    gate_w, out_share, w_up = lax.optimization_barrier((gate_w, out_share, w_up))
-    out_w = lax.all_gather(out_share[None], ("seq", "dp"), axis=0, tiled=True)
     up_w = lax.all_gather(w_up, ("seq", "dp"), axis=0, tiled=True)
     gain_one, gain_two = gains[0:1], gains[1:2]
 
     x_wide = x_all.astype(f32).reshape(rows_total, width)
     normed = (x_wide * inverse_rms(x_wide) * gain_one).astype(bf16)
     qkv = dot(normed, qkv_w).astype(bf16).reshape(parts, block, qkv_width)
-    qkv, w_down = lax.optimization_barrier((qkv, w_down))
-    down_w = lax.all_gather(w_down.T, ("seq", "dp"), axis=0, tiled=True)
     segment = segments.reshape(parts, block).astype(f32)
     segc, segr = segment[:, :, None], segment[:, None, :]
     tables = feature_tables(heads)
-    att, rden, carry, csum, cot_all = attention_forward(qkv, segc, segr, tables, cot_own, heads)
+    att, rden, carry, csum, cot_all, downs = attention_forward(
+        qkv, segc, segr, tables, cot_own, downs, heads
+    )
     cot_all = cot_all.reshape(rows_total, width)
-    rows_all, residual = branch_step(att, out_w, own, gain_two)
+    rows_all, residual, downs = branch_step(att, out_w, own, gain_two, downs)
+    down_w = downs.reshape(width, -1)
     rows_all = rows_all.reshape(rows_total, width)
 
     gate_out = dot(rows_all, gate_w)
@@ -1425,10 +1703,14 @@
     grad_gate, grad_up, gate_term, up_term = lax.optimization_barrier(
         (grad_gate, grad_up, gate_term, up_term)
     )
-    down_sum, gate_sum, up_sum = summed(down_term), summed(gate_term), summed(up_term)
+    seqs = lax.axis_size("seq")
+    down_acc = lax.psum_scatter(
+        down_term.reshape(seqs, width // seqs, -1), "dp", scatter_dimension=1, tiled=True
+    )
+    gate_sum, up_sum = summed(gate_term), summed(up_term)
 
     by_device = (parts, block, -1)
-    branch_all, grad_residual, gain_two_sum, down, ga = rows_back(
+    branch_all, grad_residual, gain_two_sum, down, ga, came = rows_back(
         grad_gate.reshape(by_device),
         grad_up.reshape(by_device),
         gate_w,
@@ -1439,19 +1721,42 @@
         mixed.reshape(by_device),
         down_w,
         out_w,
+        down_acc,
     )
     branch_all = branch_all.reshape(rows_total, width)
     by_row = (parts, lax.axis_size("seq"), lax.axis_size("dp"), rows_each, -1)
     out_term = dot_tn(branch_all, att.reshape(rows_total, heads * HV)).astype(bf16)
     out_term = out_term.reshape(parts, -1, rows_each, heads * HV).transpose(1, 0, 2, 3)
     out_sum = summed(out_term.reshape(width, -1)).reshape(parts, rows_each, -1)
-    dqkv, output = attention_backward(
-        qkv, segc, segr, tables, att, rden, carry, csum, ga, down, residual, heads
+    dqkv, output, came = attention_backward(
+        qkv,
+        segc,
+        segr,
+        tables,
+        att,
+        rden,
+        carry,
+        csum,
+        ga,
+        down,
+        residual,
+        down_acc,
+        came,
+        heads,
     )
-    dqkv_late, down_sum, gate_sum = lax.optimization_barrier((dqkv, down_sum, gate_sum))
+    dqkv_late, gate_sum, up_sum = lax.optimization_barrier((dqkv, gate_sum, up_sum))
     qkv_term = dot_tn(normed, dqkv_late.reshape(rows_total, qkv_width)).astype(bf16)
-    x_grad, gain_grads, query_grad, key_grad, value_grad, out_grad = closing(
-        dqkv, qkv_w, own, grad_residual, gain_one, gain_two_sum, qkv_term.reshape(by_row), out_sum
+    x_grad, gain_grads, query_grad, key_grad, value_grad, out_grad, down_grad = closing(
+        dqkv,
+        qkv_w,
+        own,
+        grad_residual,
+        gain_one,
+        gain_two_sum,
+        qkv_term.reshape(by_row),
+        out_sum,
+        down_acc,
+        came,
     )
     gain_each = gain_grads.shape[1] // lax.axis_size("dp")
     gain_grads = lax.dynamic_slice_in_dim(
@@ -1468,7 +1773,7 @@
         out_grad.T,
         gate_sum.astype(f32),
         up_sum.astype(f32),
-        down_sum.T.astype(f32),
+        down_grad.T,
     )
 
 

time: 584 us -> 651 us (1.11)
  Pallas kernels: 416 us -> 461 us
  waiting for transfers between devices: 13.1 us -> 37.2 us
    pallas_call x1, Pallas kernels: 37.8 us -> 74.2 us  [attention_forward(): pl.pallas_call(functools.partial(forward_kernel, count, dps, heads), out_...]
    reduce_scatter x4 -> x3, waiting for transfers between devices: 0.01 us -> 35.2 us  [summed(): lax.psum_scatter(term, ('seq', 'dp'), scatter_dimension=0, tiled=True)]
    pallas_call x1, Pallas kernels: 74.9 us -> 57.2 us  [opening(): pl.pallas_call(functools.partial(opening_kernel, seqs, dps), out_shape=(j...]
    pallas_call x1, Pallas kernels: 77.8 us -> 95.5 us  [branch_step(): pl.pallas_call(branch_kernel, out_shape=(jax.ShapeDtypeStruct((parts, blo...]
    all_gather x1, waiting for transfers between devices: 10.9 us -> 0.01 us  [local(): gate_w = lax.all_gather(w_gate, ('seq', 'dp'), axis=0, tiled=True)]
    pallas_call x1, Pallas kernels: 87.8 us -> 98.3 us  [rows_back(): pl.pallas_call(rows_back_kernel, out_shape=(jax.ShapeDtypeStruct((parts,...]
    pallas_call x1, Pallas kernels: 81.7 us -> 73.4 us  [closing(): pl.pallas_call(functools.partial(closing_kernel, seqs, dps), out_shape=(j...]
    pallas_call x1, Pallas kernels: 55.5 us -> 62.3 us  [attention_backward(): pl.pallas_call(functools.partial(backward_kernel, count, heads), out_shap...]
  transfers between devices with their start and end apart: 8 -> 7, of which waited for: 1 -> 2; matrix products, arithmetic and copies ran while one was open for 17% -> 12% of each run, Pallas kernels for 72% -> 51%
where the time goes in v7:
time: 651 us; the launch traced here: 643 us
  Pallas kernels  461 us (71%)
  matrix products  83.4 us (13%)
  local copies, waits for them, and re-layouts  37.2 us (6%)
  waiting for transfers between devices  37.2 us (6%)
  between operations  14.8 us (2%)
  other arithmetic  8.88 us (1%)
    pallas_call x1, Pallas kernels, rows_back(): pl.pallas_call(rows_back_kernel, out_shape=(jax.ShapeDtypeStruct((parts,...  98.3 us
    pallas_call x1, Pallas kernels, branch_step(): pl.pallas_call(branch_kernel, out_shape=(jax.ShapeDtypeStruct((parts, blo...  95.5 us
    pallas_call x1, Pallas kernels, attention_forward(): pl.pallas_call(functools.partial(forward_kernel, count, dps, heads), out_...  74.2 us
    pallas_call x1, Pallas kernels, closing(): pl.pallas_call(functools.partial(closing_kernel, seqs, dps), out_shape=(j...  73.4 us
    pallas_call x1, Pallas kernels, attention_backward(): pl.pallas_call(functools.partial(backward_kernel, count, heads), out_shap...  62.3 us
    pallas_call x1, Pallas kernels, opening(): pl.pallas_call(functools.partial(opening_kernel, seqs, dps), out_shape=(j...  57.2 us
    dot_general x4, matrix products, dot(): lax.dot_general(a, b, (((1,), (0,)), ((), ())), preferred_element_type=f32)  43 us
    dot_general x5, matrix products, dot_tn(): lax.dot_general(a, b, (((0,), (0,)), ((), ())), preferred_element_type=f32)  40.3 us
  transfers between devices with their start and end apart: 7, of which 2 were waited for; matrix products, arithmetic and copies ran while one was open for 12% of the time, Pallas kernels for 51%

profile of v7, /device:TPU:0, one launch (start us, length us, event | category | flops | bytes accessed | tf_op | source)
XLA Modules:
  0.0 642.9 jit_solution(5818873102397926700)
XLA Ops:
  7.2 2.2 copy.35
  9.5 57.2 %opening.1 = (bf16[4,256,2048]{2,1,0:T(8,128)(2,1)}, bf16[4,4,2,64,640]{4,3,2,1,0:T(8,128)(2,1)}, f32[4,4,2,8,128]{4,3,2,1,0:T(8,128)}, bf16[4,64,512]{2,1,0:T(8,128)(2,1)}, bf16[4,2,256,1408]{3,2,1,0:T(8,128)(2,1)}) custom-call(bf16[256,2048]{1,0:T(8,128)(2,1)} %bitcast.58, bf16[64,256]{1,0:T(8,128)(2,1)} %query_ref.1, bf16[64,256]{1,0:T(8,128)(2,1)} %key_ref.1, ...), custom_call_target="tpu_custom_call" | custom-call | bytes 1048576 | tf_op jit(solution)/shard_map/opening/pallas_call | solution.py:1087
  66.7 0.7 all-gather.5.cloned.1.call-update
  67.5 0.7 all-gather.7.cloned.1.call-update
  68.5 0.9 slice_bitcast_fusion
  69.4 0.7 slice_reduce_fusion
  70.2 3.2 fusion
  73.7 1.0 fusion.2
  74.7 0.7 copy-done.33
  75.4 3.4 convolution_convert_fusion.3
  78.9 74.2 %attention_forward.1 = (bf16[4,256,512]{2,1,0:T(8,128)(2,1)S(1)}, f32[4,256,512]{2,1,0:T(8,128)S(1)}, bf16[4,4,160,128]{3,2,1,0:T(8,128)(2,1)S(1)}, f32[4,8,256]...) custom-call(bf16[4,256,640]{2,1,0:T(8,128)(2,1)S(1)} %bitcast.61, ...), custom_call_target="tpu_custom_call", output_to_operand_aliasing={{5}: (7, {})} | custom-call | bytes 1048576 | tf_op jit(solution)/shard_map/attention_forward/pallas_call | solution.py:478
  153.1 1.0 copy-done.3
  154.1 1.3 copy-done.6
  156.0 2.1 copy-done.27
  158.1 1.2 copy-done.4
  159.3 95.5 %branch_step.1 = (bf16[4,256,2048]{2,1,0:T(8,128)(2,1)}, f32[256,2048]{1,0:T(8,128)S(1)}, bf16[4,2,256,1408]{3,2,1,0:T(8,128)(2,1)}) custom-call(bf16[4,256,512]{2,1,0:T(8,128)(2,1)S(1)} %copy-done.4, bf16[8,4,64,512]{3,2,1,0:T(8,128)(2,1)} %bitcast.73, bf16[256,2048]{1,0:T(8,128)(2,1)S(1)} %bitcast.59, ...), custom_call_target="tpu_custom_call", output_to_operand_aliasing={{2}: (4, {})} | custom-call | bytes 1048576 | tf_op jit(solution)/shard_map/branch_step/pallas_call | solution.py:1277
  254.9 1.3 copy-done.1
  256.2 11.7 %fusion.5 = f32[1024,1408]{1,0:T(8,128)} fusion(bf16[1024,2048]{1,0:T(8,128)(2,1)} %bitcast.91, bf16[2048,1408]{1,0:T(8,128)(2,1)} %all-gather.5.cloned.1.call-done.wg_hbm), kind=kOutput, calls=%fused_computation.25 | convolution fusion | flops 5905580032 | bytes 15728640 | tf_op jit(solution)/shard_map/dot_general | solution.py:24
  267.8 12.8 %multiply_convert_fusion.2 = (bf16[1024,1408]{1,0:T(8,128)(2,1)S(1)}, f32[1024,1408]{1,0:T(8,128)}) fusion(f32[1024,1408]{1,0:T(8,128)} %fusion.5, bf16[1024,2048]{1,0:T(8,128)(2,1)} %bitcast.92, bf16[2048,1408]{1,0:T(8,128)(2,1)} %all-gather.7.cloned.1.call-done.wu_hbm), kind=kOutput, calls=%fused_computation.10 | convolution fusion | flops 5914230784 | bytes 24379392 | tf_op jit(solution)/shard_map/dot_general | solution.py:24
  280.6 8.7 %convolution_convert_fusion.2 = bf16[2048,1408]{1,0:T(8,128)(2,1)} fusion(bf16[1024,2048]{1,0:T(8,128)(2,1)S(1)} %bitcast.70, bf16[1024,1408]{1,0:T(8,128)(2,1)S(1)} %get-tuple-element.74), kind=kOutput, calls=%fused_computation.7 | convolution fusion | flops 5908463616 | bytes 12845056 | tf_op jit(solution)/shard_map/dot_general | solution.py:32
  289.6 15.2 %multiply_convert_fusion = (bf16[1024,1408]{1,0:T(8,128)(2,1)S(1)}, bf16[1024,1408]{1,0:T(8,128)(2,1)}) fusion(f32[1024,1408]{1,0:T(8,128)} %fusion.5, f32[1024,1408]{1,0:T(8,128)} %get-tuple-element.129, bf16[1024,2048]{1,0:T(8,128)(2,1)} %bitcast.69, bf16[2048,1408]{1,0:T(8,128)(2,1)} %bitcast.71), kind=kOutput, calls=%fused_computation.8 | convolution fusion | flops 5924323328 | bytes 27262976 | tf_op jit(solution)/shard_map/dot_general | solution.py:24
  304.7 1.8 copy-done.32
  306.6 8.6 %convolution_convert_fusion = bf16[2048,1408]{1,0:T(8,128)(2,1)} fusion(bf16[1024,2048]{1,0:T(8,128)(2,1)S(1)} %bitcast.94, bf16[1024,1408]{1,0:T(8,128)(2,1)S(1)} %get-tuple-element.72), kind=kOutput, calls=%fused_computation.5 | convolution fusion | flops 5908463616 | bytes 12845056 | tf_op jit(solution)/shard_map/dot_general | solution.py:32
  315.2 11.0 %convolution_convert_fusion.1 = bf16[2048,1408]{1,0:T(8,128)(2,1)} fusion(bf16[1024,2048]{1,0:T(8,128)(2,1)} %bitcast.93, bf16[1024,1408]{1,0:T(8,128)(2,1)} %get-tuple-element.71), kind=kOutput, calls=%fused_computation.6 | convolution fusion | flops 5908463616 | bytes 12845056 | tf_op jit(solution)/shard_map/dot_general | solution.py:32
  327.1 98.3 %rows_back.1 = (bf16[4,256,2048]{2,1,0:T(8,128)(2,1)}, f32[256,2048]{1,0:T(8,128)}, f32[1,2048]{1,0:T(1,128)}, bf16[4,256,2048]{2,1,0:T(8,128)(2,1)}, f32[4,256,...) custom-call(bf16[4,256,1408]{2,1,0:T(8,128)(2,1)} %bitcast.81, bf16[4,256,1408]{2,1,0:T(8,128)(2,1)} %bitcast.80, ...), custom_call_target="tpu_custom_call" | custom-call | bytes 1048576 | tf_op jit(solution)/shard_map/rows_back/pallas_call | solution.py:1407
  425.4 4.9 bitcast_convert_fusion.1
  430.3 1.5 copy.40
  431.8 1.4 slice.25.gain_ref
  433.2 1.2 copy-done.5
  434.4 0.9 copy-done.12
  435.4 0.9 copy-done.14
  436.3 0.8 copy-done.22
  437.0 62.3 %attention_backward.1 = (bf16[4,256,640]{2,1,0:T(8,128)(2,1)S(1)}, bf16[256,2048]{1,0:T(8,128)(2,1)S(1)}, bf16[2,256,1408]{2,1,0:T(8,128)(2,1)}) custom-call(bf16[4,256,640]{2,1,0:T(8,128)(2,1)S(1)} %bitcast.62, f32[4,256,1]{2,1,0:T(8,128)S(1)} %copy.37.segc_ref, f32[4,1,256]{2,1,0:T(1,128)S(1)} %get-tuple-element.126.segr_ref, ...), custom_call_target="tpu_custom_call" | custom-call | bytes 1048576 | tf_op jit(solution)/shard_map/attention_backward/pallas_call | solution.py:520
  499.3 1.0 copy-done.7
  500.4 1.0 copy-done.10
  501.3 10.0 %reduce-scatter.9.cloned.1.call-done = bf16[256,1408]{1,0:T(8,128)(2,1)} async-done(((bf16[2048,1408]{1,0:T(8,128)(2,1)}), bf16[256,1408]{1,0:T(8,128)(2,1)}) %reduce-scatter.9.cloned.1.call-update) | async-done | bytes 720912 | tf_op jit(solution)/shard_map/reduce_scatter | solution.py:1699
  511.3 2.3 convert_element_type.71
  513.6 2.3 convert_element_type.72
  515.9 7.2 %bitcast_convert_fusion = bf16[2048,640]{1,0:T(8,128)(2,1)} fusion(bf16[4,256,2048]{2,1,0:T(8,128)(2,1)} %copy-done.30, bf16[4,256,640]{2,1,0:T(8,128)(2,1)S(1)} %copy-done.8), kind=kOutput, calls=%fused_computation.13 | convolution fusion | flops 2685665280 | bytes 8126464 | tf_op jit(solution)/shard_map/dot_general | solution.py:32
  523.1 25.2 %reduce-scatter.11.cloned.1.call-done = bf16[256,512]{1,0:T(8,128)(2,1)} async-done(((bf16[2048,512]{1,0:T(8,128)(2,1)}), bf16[256,512]{1,0:T(8,128)(2,1)}) %reduce-scatter.11.cloned.1.call-update) | async-done | bytes 262160 | tf_op jit(solution)/shard_map/reduce_scatter | solution.py:1699
  548.3 1.3 copy-done.9
  549.6 0.9 copy-done.15
  550.6 73.4 %closing.1 = (f32[256,2048]{1,0:T(8,128)}, f32[8,128]{1,0:T(8,128)S(1)}, f32[64,256]{1,0:T(8,128)S(1)}, f32[64,256]{1,0:T(8,128)S(1)}, f32[64,2048]{1,0:T(8,128)...) custom-call(bf16[4,256,640]{2,1,0:T(8,128)(2,1)S(1)} %copy-done.9, bf16[2048,640]{1,0:T(8,128)(2,1)} %bitcast.82, ...), custom_call_target="tpu_custom_call" | custom-call | bytes 1048576 | tf_op jit(solution)/shard_map/closing/pallas_call | solution.py:1600
  625.8 1.5 copy.41
  627.4 2.3 copy.52
  629.7 3.1 copy.53
  634.1 0.8 copy.56
  634.9 0.8 copy.57
  (83 shorter events, 5.7 us)
Async XLA Ops:
  7.2 61.0 %copy-start.34 = (s32[4,1,256]{2,1,0:T(1,128)S(1)}, s32[4,1,256]{2,1,0:T(1,128)}, u32[]{:S(2)}) copy-start(s32[4,1,256]{2,1,0:T(1,128)} %param.16) | copy-start | bytes 12292
  7.2 150.9 %all-gather.9.cloned.1.call-start = ((), (), s32[]{:S(2)}) async-start(), calls=%async_computation.10 | async-start | bytes 2359296 | tf_op jit(solution)/shard_map/all_gather | solution.py:1668
  66.7 189.5 %all-gather.5.cloned.1.call-start = ((), (), s32[]{:S(2)}) async-start(), calls=%async_computation.4 | async-start | bytes 6488064 | tf_op jit(solution)/shard_map/all_gather | solution.py:1669
  67.4 200.4 %all-gather.7.cloned.1.call-start = ((), (), s32[]{:S(2)}) async-start(), calls=%async_computation.5 | async-start | bytes 6488064 | tf_op jit(solution)/shard_map/all_gather | solution.py:1670
  68.2 258.9 %reduce-scatter.5.cloned.1.call-start = ((), (), s32[]{:S(2)}) async-start(), calls=%async_computation.6 | async-start | bytes 8650752 | tf_op jit(solution)/shard_map/reduce_scatter | solution.py:1707
  70.1 87.9 %copy-start.16 = (f32[1,2048]{1,0:T(1,128)}, f32[1,2048]{1,0:T(1,128)S(1)}, u32[]{:S(2)}) copy-start(f32[1,2048]{1,0:T(1,128)S(1)} %slice.24.gain_ref) | copy-start | bytes 24580
  70.2 3.4 copy-start.29
  73.7 1.7 copy-start.33
  74.7 4.1 copy-start.30
  75.4 3.4 copy-start.2
  75.4 3.4 copy-start.11
  75.4 3.5 copy-start.13
  75.4 3.5 copy-start.23
  78.9 79.2 %copy-start = (bf16[1,1,256,2048]{3,2,1,0:T(8,128)(2,1)S(1)}, bf16[1,1,256,2048]{3,2,1,0:T(8,128)(2,1)}, u32[]{:S(2)}) copy-start(bf16[1,1,256,2048]{3,2,1,0:T(8,128)(2,1)} %param.15) | copy-start | bytes 3145732
  153.1 1.0 copy-start.3
  154.0 1.3 copy-start.6
  155.4 0.6 copy-start.21
  156.0 2.1 copy-start.27
  158.1 1.2 copy-start.4
  254.8 1.3 copy-start.1
  267.8 12.8 %copy-start.28 = (bf16[4,256,2048]{2,1,0:T(8,128)(2,1)S(1)}, bf16[4,256,2048]{2,1,0:T(8,128)(2,1)}, u32[]{:S(2)}) copy-start(bf16[4,256,2048]{2,1,0:T(8,128)(2,1)} %copy-done.27) | copy-start | bytes 12582916
  280.6 8.7 %copy-start.31 = (bf16[1024,1408]{1,0:T(8,128)(2,1)}, bf16[1024,1408]{1,0:T(8,128)(2,1)S(1)}, u32[]{:S(2)}) copy-start(bf16[1024,1408]{1,0:T(8,128)(2,1)S(1)} %get-tuple-element.74) | copy-start | bytes 8650756
  289.3 212.0 %reduce-scatter.7.cloned.1.call-start = ((), (), s32[]{:S(2)}) async-start(), calls=%async_computation.7 | async-start | bytes 6488064 | tf_op jit(solution)/shard_map/reduce_scatter | solution.py:1699
  289.5 17.0 %copy-start.35 = (bf16[4,256,2048]{2,1,0:T(8,128)(2,1)S(1)}, bf16[4,256,2048]{2,1,0:T(8,128)(2,1)}, u32[]{:S(2)}) copy-start(bf16[4,256,2048]{2,1,0:T(8,128)(2,1)} %get-tuple-element.65) | copy-start | bytes 12582916
  304.7 1.9 copy-start.32
  326.2 185.0 %reduce-scatter.9.cloned.1.call-start = ((), (), s32[]{:S(2)}) async-start(), calls=%async_computation.8 | async-start | bytes 6488064 | tf_op jit(solution)/shard_map/reduce_scatter | solution.py:1699
  326.8 221.5 %reduce-scatter.11.cloned.1.call-start = ((), (), s32[]{:S(2)}) async-start(), calls=%async_computation.9 | async-start | bytes 2359296 | tf_op jit(solution)/shard_map/reduce_scatter | solution.py:1699
  430.2 2.9 copy-start.24
  433.2 1.3 copy-start.5
  434.4 0.9 copy-start.12
  435.4 0.9 copy-start.14
  436.3 0.8 copy-start.22
  499.3 1.1 copy-start.7
  500.3 1.0 copy-start.10
  501.3 14.6 %copy-start.8 = (bf16[4,256,640]{2,1,0:T(8,128)(2,1)S(1)}, bf16[4,256,640]{2,1,0:T(8,128)(2,1)}, u32[]{:S(2)}) copy-start(bf16[4,256,640]{2,1,0:T(8,128)(2,1)} %copy-done.7) | copy-start | bytes 3932164
  515.9 32.4 %copy-start.25 = (f32[1,2048]{1,0:T(1,128)S(1)}, f32[1,2048]{1,0:T(1,128)}, u32[]{:S(2)}) copy-start(f32[1,2048]{1,0:T(1,128)} %slice.25.gain_ref) | copy-start | bytes 24580
  515.9 32.4 %copy-start.26 = (f32[1,2048]{1,0:T(1,128)S(1)}, f32[1,2048]{1,0:T(1,128)}, u32[]{:S(2)}) copy-start(f32[1,2048]{1,0:T(1,128)} %get-tuple-element.82.gsum_two_ref) | copy-start | bytes 24580
  548.3 1.3 copy-start.9
  549.6 0.9 copy-start.15
  624.0 0.6 copy-start.17
  624.6 0.6 copy-start.19
  625.8 7.0 %copy-start.20 = (f32[64,256]{1,0:T(8,128)S(1)}, f32[64,256]{1,0:T(8,128)}, u32[]{:S(2)}) copy-start(f32[64,256]{1,0:T(8,128)} %copy-done.19) | copy-start | bytes 196612
  625.8 7.6 %copy-start.18 = (f32[64,256]{1,0:T(8,128)S(1)}, f32[64,256]{1,0:T(8,128)}, u32[]{:S(2)}) copy-start(f32[64,256]{1,0:T(8,128)} %copy-done.17) | copy-start | bytes 196612
Sparse Core Ops, SparseCore 0:
  66.8 36.2 all-gather.8
  104.8 77.3 all-gather.4
  183.8 64.4 all-gather.6
  289.4 24.0 reduce-scatter.4
  326.4 90.2 reduce-scatter.6
  418.9 92.3 reduce-scatter.8
  513.7 34.5 reduce-scatter.10

commit v8 on v6

--- a/solution.py
+++ b/solution.py
@@ -98,11 +98,15 @@
     right_ref,
     rows_ref,
     cot_ref,
+    att_hbm,
+    rden_hbm,
+    carry_hbm,
+    csum_hbm,
+    cots_ref,
     att_ref,
     rden_ref,
     carry_ref,
     csum_ref,
-    cots_ref,
     send_state,
     send_sum,
     part,
@@ -111,11 +115,21 @@
     f_send,
     f_recv,
     local_sem,
+    store_sem,
 ):
     place, f = lax.axis_index("seq"), lax.axis_index("feat")
     groups, block = qkv_ref.shape[0], qkv_ref.shape[1]
     width = heads * FDIM
     tables = (left_ref, right_ref, rows_ref)
+
+    def stores(g):
+        pairs = (
+            (att_ref, att_hbm),
+            (rden_ref, rden_hbm),
+            (carry_ref, carry_hbm),
+            (csum_ref, csum_hbm),
+        )
+        return Loads([(a.at[g], b.at[g]) for a, b in pairs], store_sem.at[g])
 
     def hop(g):
         target = {"seq": lax.rem(place + 1, count)}
@@ -226,6 +240,7 @@
             inverse = 1.0 / denom
             att_ref[g, :, h * HV : (h + 1) * HV] = (numer * inverse).astype(bf16)
             rden_ref[g, :, h * HV : (h + 1) * HV] = inverse
+        stores(g).start()
         return none
 
     lax.fori_loop(0, groups, carry_on, 0)
@@ -242,25 +257,38 @@
     stay.wait()
     gather.finish()
 
+    def stored(g, none):
+        stores(g).wait()
+        return none
+
+    lax.fori_loop(0, groups, stored, 0)
+
 
 def backward_kernel(
     count,
     heads,
-    qkv_ref,
+    qkv_hbm,
     segc_ref,
     segr_ref,
     left_ref,
     right_ref,
     rows_ref,
+    att_hbm,
+    rden_hbm,
+    carry_hbm,
+    csum_ref,
+    ga_hbm,
+    down_ref,
+    res_hbm,
+    out_hbm,
+    final_ref,
+    qkv_ref,
     att_ref,
     rden_ref,
     carry_ref,
-    csum_ref,
     ga_ref,
-    down_ref,
     res_ref,
     out_ref,
-    final_ref,
     gn,
     send_state,
     send_sum,
@@ -275,8 +303,21 @@
     f_send,
     f_recv,
     local_sem,
+    load_sem,
+    store_sem,
 ):
     place, f = lax.axis_index("seq"), lax.axis_index("feat")
+    loads = Loads(
+        (
+            (qkv_hbm, qkv_ref),
+            (ga_hbm, ga_ref),
+            (rden_hbm, rden_ref),
+            (att_hbm, att_ref),
+            (carry_hbm, carry_ref),
+            (res_hbm, res_ref),
+        ),
+        load_sem,
+    ).start()
     groups, block = qkv_ref.shape[0], qkv_ref.shape[1]
     width = heads * FDIM
     tables = (left_ref, right_ref, rows_ref)
@@ -304,6 +345,11 @@
     fill = pltpu.make_async_copy(down_ref, terms, local_sem.at[0])
     fill.start()
     ring = SquareSum(terms, land, f, f_send, f_recv)
+    loads.wait()
+
+    def store(g):
+        return pltpu.make_async_copy(out_ref.at[g], out_hbm.at[g], store_sem.at[g])
+
 
     @pl.when(place == count - 1)
     def _():
@@ -415,6 +461,7 @@
             gphi = (dot_nt(value, state) + recv_sum[g, h : h + 1, :]) * later
             total = total + pull_features(gphi, key_all, h, *tables)
         out_ref[g, :, width : 2 * width] = total.astype(bf16)
+        store(g).start()
         return none
 
     lax.fori_loop(0, groups, carry_back, 0)
@@ -435,6 +482,12 @@
 
     by_rows(ring, add_up)
     ring.finish()
+
+    def stored(g, none):
+        store(g).wait()
+        return none
+
+    lax.fori_loop(0, groups, stored, 0)
 
 
 def whole_vmem(count):
@@ -457,8 +510,12 @@
             jax.ShapeDtypeStruct((groups,) + cot_own.shape, bf16),
         ),
         in_specs=whole_vmem(6) + in_place(1),
-        out_specs=tuple(whole_vmem(4) + in_place(1)),
+        out_specs=tuple(in_place(5)),
         scratch_shapes=[
+            pltpu.VMEM((groups, block, heads * HV), bf16),
+            pltpu.VMEM((groups, block, heads * HV), f32),
+            pltpu.VMEM(states, bf16),
+            pltpu.VMEM(sums, f32),
             pltpu.VMEM(states, bf16),
             pltpu.VMEM(sums, f32),
             pltpu.VMEM((groups, heads, block, 2 * HV), f32),
@@ -467,9 +524,10 @@
             dma((6,)),
             dma((6,)),
             dma((1,)),
+            dma((groups, 4)),
         ],
         compiler_params=pltpu.CompilerParams(
-            collective_id=0, has_side_effects=True, vmem_limit_bytes=40 << 20
+            collective_id=0, has_side_effects=True, vmem_limit_bytes=60 << 20
         ),
         cost_estimate=pl.CostEstimate(flops=0, bytes_accessed=1 << 20, transcendentals=0),
         name="attention_forward",
@@ -489,9 +547,15 @@
             jax.ShapeDtypeStruct((groups, block, wide), bf16),
             jax.ShapeDtypeStruct(residual.shape, bf16),
         ),
-        in_specs=whole_vmem(11) + in_place(1) + whole_vmem(1),
-        out_specs=tuple(whole_vmem(2)),
-        scratch_shapes=[
+        in_specs=in_place(1)
+        + whole_vmem(5)
+        + in_place(3)
+        + whole_vmem(1)
+        + in_place(3),
+        out_specs=tuple(in_place(1) + whole_vmem(1)),
+        scratch_shapes=vmem_like(qkv, att, rden, carry, ga, residual)
+        + [
+            pltpu.VMEM((groups, block, wide), bf16),
             pltpu.VMEM((groups, heads, block, 2 * HV), bf16),
             pltpu.VMEM(states, bf16),
             pltpu.VMEM(sums, f32),
@@ -506,9 +570,11 @@
             pltpu.SemaphoreType.DMA((6,)),
             pltpu.SemaphoreType.DMA((6,)),
             pltpu.SemaphoreType.DMA((1,)),
+            pltpu.SemaphoreType.DMA((6,)),
+            pltpu.SemaphoreType.DMA((groups,)),
         ],
         compiler_params=pltpu.CompilerParams(
-            collective_id=1, has_side_effects=True, vmem_limit_bytes=48 << 20
+            collective_id=1, has_side_effects=True, vmem_limit_bytes=60 << 20
         ),
         cost_estimate=pl.CostEstimate(flops=0, bytes_accessed=1 << 20, transcendentals=0),
         name="attention_backward",
@@ -541,11 +607,29 @@
     return [{"feat": p} for p in peers(f)]
 
 
+class Loads:
+    def __init__(self, pairs, sem):
+        self.copies = [pltpu.make_async_copy(a, b, sem.at[i]) for i, (a, b) in enumerate(pairs)]
+
+    def start(self):
+        for c in self.copies:
+            c.start()
+        return self
+
+    def wait(self):
+        for c in self.copies:
+            c.wait()
+
+
+def vmem_like(*arrays):
+    return [pltpu.VMEM(a.shape, a.dtype) for a in arrays]
+
+
 class SquareGather:
-    def __init__(self, slots, f, send_sem, recv_sem, own=None):
+    def __init__(self, slots, f, send_sem, recv_sem, own=None, base=0, rows=None):
         side, above, across = peers(f)
-        half = slots.shape[1] // 2
-        first, second = pl.ds(0, half), pl.ds(half, half)
+        half = (slots.shape[1] if rows is None else rows) // 2
+        first, second = pl.ds(base, half), pl.ds(base + half, half)
 
         def copy(i, slot, rows, to):
             ref = slots.at[slot, rows]
@@ -589,11 +673,11 @@
 
 
 class SquareSum:
-    def __init__(self, part, land, f, send_sem, recv_sem):
+    def __init__(self, part, land, f, send_sem, recv_sem, base=0, rows=None):
         self.side, self.above, self.across = peers(f)
-        self.f, self.part, self.land = f, part, land
-        self.half = part.shape[1] // 2
-        first, second = pl.ds(0, self.half), pl.ds(self.half, self.half)
+        self.f, self.part, self.land, self.base = f, part, land, base
+        self.half = (part.shape[1] if rows is None else rows) // 2
+        first, second = pl.ds(base, self.half), pl.ds(base + self.half, self.half)
 
         def copy(i, slot, rows, to):
             return push(
@@ -609,7 +693,7 @@
             c.start()
 
     def add_rows(self, slot, base, landed):
-        step = 32
+        step = 16
 
         def one(i, none):
             rows = pl.ds(pl.multiple_of(base + i * step, step), step)
@@ -627,10 +711,10 @@
 
     def relay(self):
         self.cross[0].wait_recv()
-        self.add_rows(self.above, 0, 0)
+        self.add_rows(self.above, self.base, 0)
         self.late[0].start()
         self.cross[1].wait_recv()
-        self.add_rows(self.side, self.half, 1)
+        self.add_rows(self.side, self.base + self.half, 1)
         self.late[1].start()
 
     def arrive(self):
@@ -638,7 +722,7 @@
             c.wait_recv()
 
     def total(self, half, rows):
-        base = half * self.half
+        base = self.base + half * self.half
         own = self.part[self.f, pl.ds(pl.multiple_of(base + rows.start, 16), rows.size), :]
         near = self.land[2 + half, rows, :]
         late = self.land[4 + half, rows, :]
@@ -887,7 +971,7 @@
 
 
 def in_place(count):
-    return [pl.BlockSpec(memory_space=pl.ANY)] * count
+    return [pl.BlockSpec(memory_space=pltpu.HBM)] * count
 
 
 def opening(own, w_query, w_key, w_value, w_out, gain_one, gain_two):
@@ -922,7 +1006,7 @@
             dma((2, others, seqs, parts)),
             dma((4,)),
         ],
-        compiler_params=pltpu.CompilerParams(collective_id=2, has_side_effects=True),
+        compiler_params=pltpu.CompilerParams(collective_id=2, has_side_effects=True, vmem_limit_bytes=60 << 20),
         cost_estimate=pl.CostEstimate(flops=0, bytes_accessed=1 << 20, transcendentals=0),
         name="opening",
     )(own, w_query, w_key, w_value, w_out, gain_one, gain_two)
@@ -985,21 +1069,46 @@
         lax.fori_loop(0, part.shape[2] // tile, one, 0)
 
 
-def summed_products(part, land, f, pairs, send_sem, recv_sem, beside=None, first=False):
+def summed_products(part, land, f, pairs, send_sem, recv_sem, chunks=1, beside=None, first=False):
     side, above, across = peers(f)
-    ring = SquareSum(part, land, f, send_sem, recv_sem)
+    rows = part.shape[1] // chunks
+    rings = [
+        SquareSum(
+            part, land.at[c], f, send_sem.at[c], recv_sem.at[c], base=c * rows, rows=rows
+        )
+        for c in range(chunks)
+    ]
     product_tiles(part, across, pairs, 512, first)
-    ring.start_cross()
-    product_tiles(part, side, pairs, 512)
-    ring.near[0].start()
-    product_tiles(part, above, pairs, 512)
-    ring.near[1].start()
-    ring.relay()
-    product_tiles(part, f, pairs, 512)
+    for ring in rings:
+        ring.start_cross()
     if beside is not None:
         beside()
-    ring.arrive()
-    return ring
+    product_tiles(part, side, pairs, 512)
+    for ring in rings:
+        ring.near[0].start()
+    product_tiles(part, above, pairs, 512)
+    for ring in rings:
+        ring.near[1].start()
+    rings[0].relay()
+    product_tiles(part, f, pairs, 512)
+    for ring in rings[1:]:
+        ring.relay()
+    return rings
+
+
+def sum_then_gather(rings, finish_rows, slots, f, send_sem, recv_sem):
+    gathers = []
+    for c, ring in enumerate(rings):
+        ring.arrive()
+        by_rows(ring, finish_rows)
+        gather = SquareGather(
+            slots, f, send_sem.at[c], recv_sem.at[c], base=ring.base, rows=2 * ring.half
+        )
+        gather.start()
+        gathers.append(gather)
+    for ring in rings:
+        ring.finish()
+    return gathers
 
 
 def by_rows(ring, body, step=16):
@@ -1007,7 +1116,9 @@
 
         def one(i, none):
             start = pl.multiple_of(i * step, step)
-            rows = pl.ds(pl.multiple_of(half * ring.half + i * step, step), step)
+            rows = pl.ds(
+                pl.multiple_of(ring.base + half * ring.half + i * step, step), step
+            )
             body(rows, ring.total(half, pl.ds(start, step)))
             return none
 
@@ -1015,32 +1126,75 @@
 
 
 def branch_kernel(
-    att_ref, w_ref, tok_ref, gain_ref, rows_ref, res_ref, part, land, s_send, s_recv, g_send, g_recv
+    att_hbm,
+    w_hbm,
+    tok_hbm,
+    gain_ref,
+    rows_hbm,
+    res_hbm,
+    rows_ref,
+    res_ref,
+    att_ref,
+    w_ref,
+    tok_ref,
+    part,
+    land,
+    s_send,
+    s_recv,
+    g_send,
+    g_recv,
+    load_sem,
+    store_sem,
 ):
     f = lax.axis_index("feat")
+    loads = Loads(((att_hbm, att_ref), (w_hbm, w_ref), (tok_hbm, tok_ref)), load_sem).start()
     greet(square_targets(f))
-    ring = summed_products(part, land, f, [(att_ref, ByShare(w_ref))], s_send, s_recv)
+    loads.wait()
+    rings = summed_products(
+        part, land, f, [(att_ref, ByShare(w_ref))], s_send, s_recv, land.shape[0]
+    )
 
     def finish_rows(rows, total):
         residual = tok_ref[rows, :].astype(f32) + total
         res_ref[rows, :] = residual
         rows_ref[f, rows, :] = (residual * inverse_rms(residual) * gain_ref[...]).astype(bf16)
 
-    by_rows(ring, finish_rows)
-    gather = SquareGather(rows_ref, f, g_send, g_recv)
-    gather.start()
-    ring.finish()
-    gather.relay()
-    gather.finish()
-
-
-def square_scratch(parts, block, width):
+    gathers = sum_then_gather(rings, finish_rows, rows_ref, f, g_send, g_recv)
+    stores = [pltpu.make_async_copy(res_ref, res_hbm, store_sem.at[0])]
+    stores[0].start()
+
+    def store(slot):
+        c = pltpu.make_async_copy(rows_ref.at[slot], rows_hbm.at[slot], store_sem.at[len(stores)])
+        c.start()
+        stores.append(c)
+
+    side, above, across = peers(f)
+    store(f)
+    for gather in gathers:
+        gather.relay()
+    for gather in gathers:
+        gather.near()
+    store(side)
+    store(above)
+    for gather in gathers:
+        gather.far()
+    store(across)
+    for gather in gathers:
+        gather.sent()
+    for c in stores:
+        c.wait()
+
+
+CHUNKS = 2
+
+
+def square_scratch(parts, block, width, chunks=CHUNKS):
     dma = pltpu.SemaphoreType.DMA
     return [
         pltpu.VMEM((parts, block, width), bf16),
-        pltpu.VMEM((6, block // 2, width), bf16),
-        dma((6,)),
-        dma((6,)),
+        pltpu.VMEM((chunks, 6, block // 2 // chunks, width), bf16),
+        dma((chunks, 6)),
+        dma((chunks, 6)),
     ]
 
 
@@ -1054,11 +1208,14 @@
             jax.ShapeDtypeStruct((parts, block, width), bf16),
             jax.ShapeDtypeStruct((block, width), f32),
         ),
-        in_specs=whole_vmem(4),
-        out_specs=tuple(whole_vmem(2)),
-        scratch_shapes=square_scratch(parts, block, width) + [dma((6,)), dma((6,))],
+        in_specs=in_place(3) + whole_vmem(1),
+        out_specs=tuple(in_place(2)),
+        scratch_shapes=[pltpu.VMEM((parts, block, width), bf16), pltpu.VMEM((block, width), f32)]
+        + vmem_like(att, out_w, own)
+        + square_scratch(parts, block, width)
+        + [dma((CHUNKS, 6)), dma((CHUNKS, 6)), dma((3,)), dma((1 + parts,))],
         compiler_params=pltpu.CompilerParams(
-            collective_id=3, has_side_effects=True, vmem_limit_bytes=48 << 20
+            collective_id=3, has_side_effects=True, vmem_limit_bytes=60 << 20
         ),
         cost_estimate=pl.CostEstimate(flops=0, bytes_accessed=1 << 20, transcendentals=0),
         name="branch_step",
@@ -1066,21 +1223,29 @@
 
 
 def rows_back_kernel(
-    gg_ref,
-    gu_ref,
+    gg_hbm,
+    gu_hbm,
     wg_hbm,
     wu_hbm,
-    res_ref,
-    cot_ref,
+    res_hbm,
+    cot_hbm,
     gain_ref,
     mixed_hbm,
     wd_hbm,
     wo_hbm,
+    all_hbm,
+    gres_hbm,
+    gsum_ref,
+    down_hbm,
+    ga_hbm,
     all_ref,
     gres_ref,
-    gsum_ref,
     down_ref,
     ga_ref,
+    gg_ref,
+    gu_ref,
+    res_ref,
+    cot_ref,
     part,
     land,
     wg,
@@ -1094,8 +1259,11 @@
     g_recv,
     local_sem,
     tile_sem,
+    load_sem,
+    store_sem,
 ):
     f = lax.axis_index("feat")
+    rows_in = Loads(((gg_hbm, gg_ref), (gu_hbm, gu_ref)), load_sem).start()
     weights = [
         ByTiles(src, dst, tile_sem.at[i], 512)
         for i, (src, dst) in enumerate(((wg_hbm, wg), (wu_hbm, wu)))
@@ -1107,17 +1275,20 @@
         pltpu.make_async_copy(src, dst, local_sem.at[i])
         for i, (src, dst) in enumerate(((mixed_hbm, mixed), (wd_hbm, wd), (wo_hbm, wo)))
     ]
+    late_in = Loads(((res_hbm, res_ref), (cot_hbm, cot_ref)), load_sem.at[pl.ds(2, 2)]).start()
     for c in fills:
         c.start()
     greet(square_targets(f))
+    rows_in.wait()
     pairs = [(gg_ref, weights[0]), (gu_ref, weights[1])]
 
-    def down_products():
-        for p in range(part.shape[0]):
+    def down_products(slots):
+        for p in slots:
             product_tiles(down_ref, p, [(mixed, wd)], 512)
 
-    ring = summed_products(part, land, f, pairs, s_send, s_recv, first=True)
+    rings = summed_products(part, land, f, pairs, s_send, s_recv, land.shape[0], first=True)
     gsum_ref[...] = jnp.zeros_like(gsum_ref)
+    late_in.wait()
 
     def finish_rows(rows, grad):
         residual = res_ref[rows, :]
@@ -1128,10 +1299,7 @@
         gres_ref[rows, :] = grad_res
         all_ref[f, rows, :] = grad_res.astype(bf16)
 
-    by_rows(ring, finish_rows)
-    gather = SquareGather(all_ref, f, g_send, g_recv)
-    gather.start()
-    ring.finish()
+    gathers = sum_then_gather(rings, finish_rows, all_ref, f, g_send, g_recv)
     side, above, across = peers(f)
 
     def attended_grad(slot):
@@ -1142,18 +1310,36 @@
             term = dot(all_ref[slot, :, i * size : (i + 1) * size], blocks.tile(i, size))
             total = term if total is None else total + term
         ga_ref[slot] = total
-
+        store(ga_ref.at[slot], ga_hbm.at[slot])
+        store(all_ref.at[slot], all_hbm.at[slot])
+
+    stores = []
+
+    def store(src, dst):
+        c = pltpu.make_async_copy(src, dst, store_sem.at[len(stores)])
+        c.start()
+        stores.append(c)
+
+    store(gres_ref, gres_hbm)
     for c in fills:
         c.wait()
     attended_grad(f)
-    down_products()
-    gather.relay()
-    gather.near()
+    down_products(range(2))
+    for gather in gathers:
+        gather.relay()
+    down_products(range(2, part.shape[0]))
+    store(down_ref, down_hbm)
+    for gather in gathers:
+        gather.near()
     attended_grad(side)
     attended_grad(above)
-    gather.far()
+    for gather in gathers:
+        gather.far()
     attended_grad(across)
-    gather.sent()
+    for gather in gathers:
+        gather.sent()
+    for c in stores:
+        c.wait()
 
 
 def rows_back(
@@ -1171,9 +1357,16 @@
             jax.ShapeDtypeStruct((parts, block, width), bf16),
             jax.ShapeDtypeStruct((parts, block, out_w.shape[3]), f32),
         ),
-        in_specs=whole_vmem(2) + in_place(2) + whole_vmem(3) + in_place(3),
-        out_specs=tuple(whole_vmem(5)),
-        scratch_shapes=square_scratch(parts, block, width)[:2]
+        in_specs=in_place(6) + whole_vmem(1) + in_place(3),
+        out_specs=tuple(in_place(2) + whole_vmem(1) + in_place(2)),
+        scratch_shapes=[
+            pltpu.VMEM((parts, block, width), bf16),
+            pltpu.VMEM((block, width), f32),
+            pltpu.VMEM((parts, block, width), bf16),
+            pltpu.VMEM((parts, block, out_w.shape[3]), f32),
+        ]
+        + vmem_like(grad_gate, grad_up, residual, cot_own)
+        + square_scratch(parts, block, width)[:2]
         + [
             pltpu.VMEM((width, hidden), bf16),
             pltpu.VMEM((width, hidden), bf16),
@@ -1181,8 +1374,8 @@
             pltpu.VMEM((width, hidden), bf16),
             pltpu.VMEM(out_w.shape, bf16),
         ]
-        + [dma((6,))] * 4
-        + [dma((3,)), dma((2, width // 512))],
+        + [dma((CHUNKS, 6))] * 4
+        + [dma((3,)), dma((2, width // 512)), dma((4,)), dma((2 * parts + 2,))],
         compiler_params=pltpu.CompilerParams(
             collective_id=4, has_side_effects=True, vmem_limit_bytes=60 << 20
         ),
@@ -1194,14 +1387,14 @@
 def closing_kernel(
     seqs,
     dps,
-    dqkv_ref,
-    w_ref,
-    tok_ref,
-    gres_ref,
+    dqkv_hbm,
+    w_hbm,
+    tok_hbm,
+    gres_hbm,
     gain_ref,
     gsum_two_ref,
-    term_ref,
-    osum_ref,
+    term_hbm,
+    oterm_hbm,
     x_ref,
     tile_ref,
     query_ref,
@@ -1221,11 +1414,27 @@
     c_recv,
     d_send,
     d_recv,
-    oland,
-    o_send,
-    o_recv,
+    dqkv_ref,
+    w_ref,
+    tok_ref,
+    gres_ref,
+    term_ref,
+    oterm_ref,
+    load_sem,
     *sum_scratch,
 ):
+    loads = Loads(
+        (
+            (oterm_hbm, oterm_ref),
+            (term_hbm, term_ref),
+            (dqkv_hbm, dqkv_ref),
+            (w_hbm, w_ref),
+            (tok_hbm, tok_ref),
+            (gres_hbm, gres_ref),
+        ),
+        load_sem,
+    ).start()
+    half = len(sum_scratch) // 2
     f, s, d = lax.axis_index("feat"), lax.axis_index("seq"), lax.axis_index("dp")
     parts = 4
     others = [lax.rem(d + k, dps) for k in range(1, dps)]
@@ -1238,16 +1447,18 @@
     greet(
         [{"feat": a, "seq": b} for a, b in circle] + [{"dp": o} for o in others]
     )
-    rows_sum = row_sum(term_ref, sum_scratch, f, s, d, seqs, dps)
+    loads.wait()
+    rows_sum = row_sum(term_ref, sum_scratch[:half], f, s, d, seqs, dps)
+    out_sum = row_sum(oterm_ref, sum_scratch[half:], f, s, d, seqs, dps)
+    out_sum.start()
     rows_sum.start()
-    outs = [
-        push(osum_ref.at[p], oland.at[f], o_send.at[i], o_recv.at[i], {"feat": p})
-        for i, p in enumerate(peers(f))
-    ]
-    for c in outs:
-        c.start()
-    ring = summed_products(
-        part, land, f, [(dqkv_ref, w_ref)], s_send, s_recv, rows_sum.over_seq
+
+    def over_seq():
+        out_sum.over_seq()
+        rows_sum.over_seq()
+
+    rings = summed_products(
+        part, land, f, [(dqkv_ref, w_ref)], s_send, s_recv, land.shape[0], over_seq
     )
     gsum[...] = jnp.zeros_like(gsum)
 
@@ -1258,9 +1469,13 @@
         gsum[...] += jnp.sum(grad * unit, axis=0, keepdims=True)
         x_ref[rows, :] = gres_ref[rows, :] + norm_back(grad, unit, inverse, gain_ref[...])
 
-    by_rows(ring, finish_rows)
+    for ring in rings:
+        ring.arrive()
+        by_rows(ring, finish_rows)
+    out_sum.over_feat()
     rows_sum.over_feat()
-    ring.finish()
+    for ring in rings:
+        ring.finish()
 
     lanes = gsum.shape[1] // (parts * seqs)
     cut[...] = jnp.zeros_like(cut)
@@ -1307,17 +1522,16 @@
             ref[:, p * each : (p + 1) * each] = piece.astype(f32)
         first += each
     rows_sum.finish()
-    oland[f] = osum_ref[f]
-    for c in outs:
-        c.wait_recv()
+    out_sum.arrive()
     each = ograd_ref.shape[1] // parts
     for p in range(parts):
-        ograd_ref[:, p * each : (p + 1) * each] = oland[p].astype(f32)
-    for c in outs + sends + last:
+        ograd_ref[:, p * each : (p + 1) * each] = out_sum.shares[p].astype(f32)
+    out_sum.finish()
+    for c in sends + last:
         c.wait_send()
 
 
-def closing(dqkv, qkv_w, own, grad_residual, gain_one, gain_two_sum, qkv_term, out_sum):
+def closing(dqkv, qkv_w, own, grad_residual, gain_one, gain_two_sum, qkv_term, out_term):
     parts, seqs, dps = (lax.axis_size(a) for a in ALL)
     block, width = own.shape
     others = max(dps - 1, 1)
@@ -1335,7 +1549,7 @@
             jax.ShapeDtypeStruct((rows_each, HEADS * HV), f32),
             jax.ShapeDtypeStruct((rows_each, HEADS * HV), f32),
         ),
-        in_specs=whole_vmem(8),
+        in_specs=in_place(4) + whole_vmem(2) + in_place(2),
         out_specs=tuple(whole_vmem(6)),
         scratch_shapes=square_scratch(parts, block, width)
         + [
@@ -1348,17 +1562,17 @@
             dma((circle,)),
             dma((others,)),
             dma((others,)),
-            pltpu.VMEM(out_sum.shape, bf16),
-            dma((3,)),
-            dma((3,)),
         ]
-        + row_sum_scratch(qkv_term.shape),
+        + vmem_like(dqkv, qkv_w, own, grad_residual, qkv_term, out_term)
+        + [dma((6,))]
+        + row_sum_scratch(qkv_term.shape)
+        + row_sum_scratch(out_term.shape),
         compiler_params=pltpu.CompilerParams(
-            collective_id=5, has_side_effects=True, vmem_limit_bytes=48 << 20
+            collective_id=5, has_side_effects=True, vmem_limit_bytes=60 << 20
         ),
         cost_estimate=pl.CostEstimate(flops=0, bytes_accessed=1 << 20, transcendentals=0),
         name="closing",
-    )(dqkv, qkv_w, own, grad_residual, gain_one, gain_two_sum, qkv_term, out_sum)
+    )(dqkv, qkv_w, own, grad_residual, gain_one, gain_two_sum, qkv_term, out_term)
 
 
 def local(
@@ -1388,15 +1602,16 @@
     )
     qkv_width = qkv_w.shape[1]
     gate_w = lax.all_gather(w_gate, ("seq", "dp"), axis=0, tiled=True)
-    gate_w, out_share, w_up = lax.optimization_barrier((gate_w, out_share, w_up))
-    out_w = lax.all_gather(out_share[None], ("seq", "dp"), axis=0, tiled=True)
-    up_w = lax.all_gather(w_up, ("seq", "dp"), axis=0, tiled=True)
     gain_one, gain_two = gains[0:1], gains[1:2]
 
     x_wide = x_all.astype(f32).reshape(rows_total, width)
     normed = (x_wide * inverse_rms(x_wide) * gain_one).astype(bf16)
     qkv = dot(normed, qkv_w).astype(bf16).reshape(parts, block, qkv_width)
-    qkv, w_down = lax.optimization_barrier((qkv, w_down))
+    qkv, gate_w, out_share, w_up, w_down = lax.optimization_barrier(
+        (qkv, gate_w, out_share, w_up, w_down)
+    )
+    out_w = lax.all_gather(out_share[None], ("seq", "dp"), axis=0, tiled=True)
+    up_w = lax.all_gather(w_up, ("seq", "dp"), axis=0, tiled=True)
     down_w = lax.all_gather(w_down.T, ("seq", "dp"), axis=0, tiled=True)
     segment = segments.reshape(parts, block).astype(f32)
     segc, segr = segment[:, :, None], segment[:, None, :]
@@ -1443,15 +1658,13 @@
     branch_all = branch_all.reshape(rows_total, width)
     by_row = (parts, lax.axis_size("seq"), lax.axis_size("dp"), rows_each, -1)
     out_term = dot_tn(branch_all, att.reshape(rows_total, heads * HV)).astype(bf16)
-    out_term = out_term.reshape(parts, -1, rows_each, heads * HV).transpose(1, 0, 2, 3)
-    out_sum = summed(out_term.reshape(width, -1)).reshape(parts, rows_each, -1)
     dqkv, output = attention_backward(
         qkv, segc, segr, tables, att, rden, carry, csum, ga, down, residual, heads
     )
-    dqkv_late, down_sum, gate_sum = lax.optimization_barrier((dqkv, down_sum, gate_sum))
+    dqkv_late, down_sum = lax.optimization_barrier((dqkv, down_sum))
     qkv_term = dot_tn(normed, dqkv_late.reshape(rows_total, qkv_width)).astype(bf16)
     x_grad, gain_grads, query_grad, key_grad, value_grad, out_grad = closing(
-        dqkv, qkv_w, own, grad_residual, gain_one, gain_two_sum, qkv_term.reshape(by_row), out_sum
+        dqkv, qkv_w, own, grad_residual, gain_one, gain_two_sum, qkv_term.reshape(by_row), out_term.reshape(by_row)
     )
     gain_each = gain_grads.shape[1] // lax.axis_size("dp")
     gain_grads = lax.dynamic_slice_in_dim(

time: 584 us -> 555 us (0.950)
  local copies, waits for them, and re-layouts: 39.7 us -> 14.2 us
  Pallas kernels: 416 us -> 406 us
    unnamed x89 -> x45, local copies, waits for them, and re-layouts: 33.2 us -> 8.93 us
    all_gather x1, waiting for transfers between devices: 0.02 us -> 14.8 us  [local(): down_w = lax.all_gather(w_down.T, ('seq', 'dp'), axis=0, tiled=True)]
    all_gather x1, waiting for transfers between devices: 10.9 us -> 0.01 us  [local(): gate_w = lax.all_gather(w_gate, ('seq', 'dp'), axis=0, tiled=True)]
    pallas_call x1, Pallas kernels: 81.7 us -> 73 us  [closing(): pl.pallas_call(functools.partial(closing_kernel, seqs, dps), out_shape=(j...]
  transfers between devices with their start and end apart: 8 -> 7, of which waited for: 1 -> 1; matrix products, arithmetic and copies ran while one was open for 17% -> 18% of each run, Pallas kernels for 72% -> 74%
where the time goes in v8:
time: 555 us; the launch traced here: 548 us
  Pallas kernels  406 us (73%)
  matrix products  85.9 us (15%)
  waiting for transfers between devices  16.8 us (3%)
  between operations  14.8 us (3%)
  local copies, waits for them, and re-layouts  14.2 us (3%)
  other arithmetic  9.78 us (2%)
    pallas_call x1, Pallas kernels, rows_back(): pl.pallas_call(rows_back_kernel, out_shape=(jax.ShapeDtypeStruct((parts,...  84.1 us
    pallas_call x1, Pallas kernels, opening(): pl.pallas_call(functools.partial(opening_kernel, seqs, dps), out_shape=(j...  74.9 us
    pallas_call x1, Pallas kernels, closing(): pl.pallas_call(functools.partial(closing_kernel, seqs, dps), out_shape=(j...  73 us
    pallas_call x1, Pallas kernels, branch_step(): pl.pallas_call(branch_kernel, out_shape=(jax.ShapeDtypeStruct((parts, blo...  72.2 us
    pallas_call x1, Pallas kernels, attention_backward(): pl.pallas_call(functools.partial(backward_kernel, count, heads), out_shap...  61 us
    dot_general x4, matrix products, dot(): lax.dot_general(a, b, (((1,), (0,)), ((), ())), preferred_element_type=f32)  44.3 us
    dot_general x5, matrix products, dot_tn(): lax.dot_general(a, b, (((0,), (0,)), ((), ())), preferred_element_type=f32)  41.7 us
    pallas_call x1, Pallas kernels, attention_forward(): pl.pallas_call(functools.partial(forward_kernel, count, heads), out_shape...  41 us
  transfers between devices with their start and end apart: 7, of which 1 were waited for; matrix products, arithmetic and copies ran while one was open for 18% of the time, Pallas kernels for 74%

profile of v8, /device:TPU:0, one launch (start us, length us, event | category | flops | bytes accessed | tf_op | source)
XLA Modules:
  0.0 548.3 jit_solution(8686533461874554946)
XLA Ops:
  7.2 0.7 all-gather.6.cloned.1.call-update
  7.9 0.0 all-gather.12.cloned.1.call-start
  8.0 74.9 %opening.1 = (bf16[4,256,2048]{2,1,0:T(8,128)(2,1)}, bf16[4,4,2,64,640]{4,3,2,1,0:T(8,128)(2,1)}, f32[4,4,2,8,128]{4,3,2,1,0:T(8,128)}, bf16[4,64,512]{2,1,0:T(8,128)(2,1)}) custom-call(bf16[256,2048]{1,0:T(8,128)(2,1)} %bitcast.53, bf16[64,256]{1,0:T(8,128)(2,1)} %query_ref.1, bf16[64,256]{1,0:T(8,128)(2,1)} %key_ref.1, bf16[64,2048]{1,0:T(8,128)(2,1)} %value_ref.1, ...), custom_call_target="tpu_custom_call" | custom-call | bytes 1048576 | tf_op jit(solution)/shard_map/opening/pallas_call | solution.py:985
  82.9 0.9 slice_bitcast_fusion
  83.8 0.1 slice_reduce_fusion
  83.9 0.1 mul.53
  84.0 3.3 fusion
  87.3 0.2 copy-done
  87.5 1.0 fusion.2
  88.5 2.0 copy-done.2
  90.5 4.5 convolution_convert_fusion.3
  95.1 0.7 all-gather.8.cloned.1.call-update
  95.8 0.0 all-gather.10.cloned.1.call-start
  95.8 1.1 copy.33
  97.0 0.0 reduce-scatter.4.cloned.1.call-start
  97.0 0.6 fusion.4
  97.6 1.0 copy.34.segc_ref
  98.7 0.7 slice.24.gain_ref
  99.4 41.0 %attention_forward.1 = (bf16[4,256,512]{2,1,0:T(8,128)(2,1)}, f32[4,256,512]{2,1,0:T(8,128)}, bf16[4,4,160,128]{3,2,1,0:T(8,128)(2,1)}, f32[4,8,256]{2,1,0:T(8,128)}, bf16[4,256,2048]{2,1,0:T(8,128)(2,1)}) custom-call(bf16[4,256,640]{2,1,0:T(8,128)(2,1)} %bitcast.58, f32[4,256,1]{2,1,0:T(8,128)} %copy.34.segc_ref, f32[4,1,256]{2,1,0:T(1,128)} %get-tuple-element.116.segr_ref, ...), custom_call_target="tpu_custom_call" | custom-call | bytes 1048576 | tf_op jit(solution)/shard_map/attention_forward/pallas_call | solution.py:503
  140.4 72.2 %branch_step.1 = (bf16[4,256,2048]{2,1,0:T(8,128)(2,1)}, f32[256,2048]{1,0:T(8,128)}) custom-call(bf16[4,256,512]{2,1,0:T(8,128)(2,1)} %get-tuple-element.54.att_hbm, bf16[8,4,64,512]{3,2,1,0:T(8,128)(2,1)} %bitcast.56, bf16[256,2048]{1,0:T(8,128)(2,1)} %bitcast.54, f32[1,2048]{1,0:T(1,128)} %slice.24.gain_ref), custom_call_target="tpu_custom_call" | custom-call | bytes 1048576 | tf_op jit(solution)/shard_map/branch_step/pallas_call | solution.py:1205
  212.6 11.8 %fusion.5 = f32[1024,1408]{1,0:T(8,128)} fusion(bf16[1024,2048]{1,0:T(8,128)(2,1)} %bitcast.80, bf16[2048,1408]{1,0:T(8,128)(2,1)} %all-gather.6.cloned.1.call-done.wg_hbm), kind=kOutput, calls=%fused_computation.26 | convolution fusion | flops 5905580032 | bytes 15728640 | tf_op jit(solution)/shard_map/dot_general | solution.py:24
  224.4 12.9 %multiply_convert_fusion.2 = (bf16[1024,1408]{1,0:T(8,128)(2,1)S(1)}, f32[1024,1408]{1,0:T(8,128)}) fusion(f32[1024,1408]{1,0:T(8,128)} %fusion.5, bf16[1024,2048]{1,0:T(8,128)(2,1)} %bitcast.81, bf16[2048,1408]{1,0:T(8,128)(2,1)} %all-gather.8.cloned.1.call-done.wu_hbm), kind=kOutput, calls=%fused_computation.10 | convolution fusion | flops 5914230784 | bytes 24379392 | tf_op jit(solution)/shard_map/dot_general | solution.py:24
  237.3 8.7 %convolution_convert_fusion.2 = bf16[2048,1408]{1,0:T(8,128)(2,1)} fusion(bf16[1024,2048]{1,0:T(8,128)(2,1)S(1)} %bitcast.79, bf16[1024,1408]{1,0:T(8,128)(2,1)S(1)} %get-tuple-element.68), kind=kOutput, calls=%fused_computation.7 | convolution fusion | flops 5908463616 | bytes 12845056 | tf_op jit(solution)/shard_map/dot_general | solution.py:32
  246.0 0.2 reduce-scatter.8.cloned.1.call-start
  246.2 14.8 %all-gather.10.cloned.1.call-done.wd_hbm = bf16[2048,1408]{1,0:T(8,128)(2,1)} async-done(((bf16[256,1408]{1,0:T(8,128)(2,1)}), bf16[2048,1408]{1,0:T(8,128)(2,1)}) %all-gather.10.cloned.1.call-update) | async-done | bytes 5767184 | tf_op jit(solution)/shard_map/all_gather | solution.py:1615
  261.0 15.2 %multiply_convert_fusion = (bf16[1024,1408]{1,0:T(8,128)(2,1)S(1)}, bf16[1024,1408]{1,0:T(8,128)(2,1)}) fusion(f32[1024,1408]{1,0:T(8,128)} %fusion.5, f32[1024,1408]{1,0:T(8,128)} %get-tuple-element.119, bf16[1024,2048]{1,0:T(8,128)(2,1)} %bitcast.78, bf16[2048,1408]{1,0:T(8,128)(2,1)} %all-gather.10.cloned.1.call-done.wd_hbm), kind=kOutput, calls=%fused_computation.8 | convolution fusion | flops 5924323328 | bytes 27262976 | tf_op jit(solution)/shard_map/dot_general | solution.py:24
  276.2 8.6 %convolution_convert_fusion = bf16[2048,1408]{1,0:T(8,128)(2,1)} fusion(bf16[1024,2048]{1,0:T(8,128)(2,1)S(1)} %bitcast.83, bf16[1024,1408]{1,0:T(8,128)(2,1)S(1)} %get-tuple-element.66), kind=kOutput, calls=%fused_computation.5 | convolution fusion | flops 5908463616 | bytes 12845056 | tf_op jit(solution)/shard_map/dot_general | solution.py:32
  284.8 11.1 %convolution_convert_fusion.1 = bf16[2048,1408]{1,0:T(8,128)(2,1)} fusion(bf16[1024,2048]{1,0:T(8,128)(2,1)} %bitcast.82, bf16[1024,1408]{1,0:T(8,128)(2,1)} %get-tuple-element.65), kind=kOutput, calls=%fused_computation.6 | convolution fusion | flops 5908463616 | bytes 12845056 | tf_op jit(solution)/shard_map/dot_general | solution.py:32
  295.9 0.3 reduce-scatter.6.cloned.1.call-start
  296.2 0.5 reduce-scatter.6.cloned.1.call-update
  296.7 0.7 slice.25.gain_ref
  297.4 84.1 %rows_back.1 = (bf16[4,256,2048]{2,1,0:T(8,128)(2,1)}, f32[256,2048]{1,0:T(8,128)}, f32[1,2048]{1,0:T(1,128)}, bf16[4,256,2048]{2,1,0:T(8,128)(2,1)}, f32[4,256,512]{2,1,0:T(8,128)}) custom-call(bf16[4,256,1408]{2,1,0:T(8,128)(2,1)} %bitcast.66, bf16[4,256,1408]{2,1,0:T(8,128)(2,1)} %bitcast.65, bf16[2048,1408]{1,0:T(8,128)(2,1)} %all-gather.6.cloned.1.call-done.wg_hbm, ...), custom_call_target="tpu_custom_call" | custom-call | bytes 1048576 | tf_op jit(solution)/shard_map/rows_back/pallas_call | solution.py:1351
  381.5 61.0 %attention_backward.1 = (bf16[4,256,640]{2,1,0:T(8,128)(2,1)}, bf16[256,2048]{1,0:T(8,128)(2,1)}) custom-call(bf16[4,256,640]{2,1,0:T(8,128)(2,1)} %bitcast.59, f32[4,256,1]{2,1,0:T(8,128)} %copy.34.segc_ref, f32[4,1,256]{2,1,0:T(1,128)} %get-tuple-element.116.segr_ref, bf16[4,64,256]{2,1,0:T(8,128)(2,1)} %constant.25.clone.left_ref, ...), custom_call_target="tpu_custom_call" | custom-call | bytes 1048576 | tf_op jit(solution)/shard_map/attention_backward/pallas_call | solution.py:544
  442.5 6.1 %bitcast_convert_fusion.1 = bf16[2048,512]{1,0:T(8,128)(2,1)} fusion(bf16[4,256,2048]{2,1,0:T(8,128)(2,1)} %get-tuple-element.77, bf16[4,256,512]{2,1,0:T(8,128)(2,1)S(1)} %copy-done.1), kind=kOutput, calls=%fused_computation.14 | convolution fusion | flops 2148532224 | bytes 7340032 | tf_op jit(solution)/shard_map/dot_general | solution.py:32
  448.6 7.2 %bitcast_convert_fusion = bf16[2048,640]{1,0:T(8,128)(2,1)} fusion(bf16[4,256,2048]{2,1,0:T(8,128)(2,1)} %copy-done.2, bf16[4,256,640]{2,1,0:T(8,128)(2,1)S(1)} %copy-done.7), kind=kOutput, calls=%fused_computation.13 | convolution fusion | flops 2685665280 | bytes 8126464 | tf_op jit(solution)/shard_map/dot_general | solution.py:32
  455.9 73.0 %closing.1 = (f32[256,2048]{1,0:T(8,128)}, f32[8,128]{1,0:T(8,128)}, f32[64,256]{1,0:T(8,128)}, f32[64,256]{1,0:T(8,128)}, f32[64,2048]{1,0:T(8,128)}, /*index=5*/f32[64,2048]{1,0:T(8,128)}) custom-call(bf16[4,256,640]{2,1,0:T(8,128)(2,1)} %get-tuple-element.76.dqkv_hbm, bf16[2048,640]{1,0:T(8,128)(2,1)} %bitcast.67, bf16[256,2048]{1,0:T(8,128)(2,1)} %bitcast.55, ...), custom_call_target="tpu_custom_call" | custom-call | bytes 1048576 | tf_op jit(solution)/shard_map/closing/pallas_call | solution.py:1542
  528.9 0.1 convert_bitcast_fusion
  529.0 1.5 copy.37
  530.5 2.4 convert_element_type.78
  532.9 0.1 constant_dynamic-slice_fusion
  533.0 0.5 slice_bitcast_fusion.1
  533.5 2.4 convert_element_type.77
  535.9 1.0 copy.46
  536.9 1.3 copy.47
  538.2 0.6 copy.48
  538.8 0.6 copy.49
  539.5 0.8 copy.50
  540.3 0.8 copy.51
  (49 shorter events, 0.2 us)
Async XLA Ops:
  7.2 87.8 %all-gather.6.cloned.1.call-start = ((), (), s32[]{:S(2)}) async-start(), calls=%async_computation.3 | async-start | bytes 6488064 | tf_op jit(solution)/shard_map/all_gather | solution.py:1604
  7.9 132.5 %all-gather.12.cloned.1.call-start = ((), (), s32[]{:S(2)}) async-start(), calls=%async_computation.9 | async-start | bytes 2359296 | tf_op jit(solution)/shard_map/all_gather | solution.py:1613
  84.0 3.5 copy-start
  87.5 3.0 copy-start.5
  88.5 2.0 copy-start.2
  90.5 5.3 copy-start.9
  90.5 6.5 %copy-start.15 = (s32[4,1,256]{2,1,0:T(1,128)S(1)}, s32[4,1,256]{2,1,0:T(1,128)}, u32[]{:S(2)}) copy-start(s32[4,1,256]{2,1,0:T(1,128)} %param.16) | copy-start | bytes 12292
  95.0 129.4 %all-gather.8.cloned.1.call-start = ((), (), s32[]{:S(2)}) async-start(), calls=%async_computation.4 | async-start | bytes 6488064 | tf_op jit(solution)/shard_map/all_gather | solution.py:1614
  95.8 165.3 %all-gather.10.cloned.1.call-start = ((), (), s32[]{:S(2)}) async-start(), calls=%async_computation.5 | async-start | bytes 6488064 | tf_op jit(solution)/shard_map/all_gather | solution.py:1615
  97.0 351.6 %reduce-scatter.4.cloned.1.call-start = ((), (), s32[]{:S(2)}) async-start(), calls=%async_computation.6 | async-start | bytes 6488064 | tf_op jit(solution)/shard_map/reduce_scatter | solution.py:1636
  224.4 12.9 %copy-start.17 = (bf16[4,256,2048]{2,1,0:T(8,128)(2,1)S(1)}, bf16[4,256,2048]{2,1,0:T(8,128)(2,1)}, u32[]{:S(2)}) copy-start(bf16[4,256,2048]{2,1,0:T(8,128)(2,1)} %get-tuple-element.62) | copy-start | bytes 12582916
  237.3 8.7 %copy-start.3 = (bf16[1024,1408]{1,0:T(8,128)(2,1)}, bf16[1024,1408]{1,0:T(8,128)(2,1)S(1)}, u32[]{:S(2)}) copy-start(bf16[1024,1408]{1,0:T(8,128)(2,1)S(1)} %get-tuple-element.68) | copy-start | bytes 8650756
  246.0 284.6 %reduce-scatter.8.cloned.1.call-start = ((), (), s32[]{:S(2)}) async-start(), calls=%async_computation.8 | async-start | bytes 6488064 | tf_op jit(solution)/shard_map/reduce_scatter | solution.py:1636
  261.0 15.2 %copy-start.18 = (bf16[4,256,2048]{2,1,0:T(8,128)(2,1)S(1)}, bf16[4,256,2048]{2,1,0:T(8,128)(2,1)}, u32[]{:S(2)}) copy-start(bf16[4,256,2048]{2,1,0:T(8,128)(2,1)} %get-tuple-element.59) | copy-start | bytes 12582916
  276.2 8.6 %copy-start.4 = (bf16[1024,1408]{1,0:T(8,128)(2,1)}, bf16[1024,1408]{1,0:T(8,128)(2,1)S(1)}, u32[]{:S(2)}) copy-start(bf16[1024,1408]{1,0:T(8,128)(2,1)S(1)} %get-tuple-element.66) | copy-start | bytes 8650756
  295.9 237.6 %reduce-scatter.6.cloned.1.call-start = ((), (), s32[]{:S(2)}) async-start(), calls=%async_computation.7 | async-start | bytes 6488064 | tf_op jit(solution)/shard_map/reduce_scatter | solution.py:1636
  381.5 61.0 %copy-start.1 = (bf16[4,256,512]{2,1,0:T(8,128)(2,1)S(1)}, bf16[4,256,512]{2,1,0:T(8,128)(2,1)}, u32[]{:S(2)}) copy-start(bf16[4,256,512]{2,1,0:T(8,128)(2,1)} %get-tuple-element.54.att_hbm) | copy-start | bytes 3145732
  442.5 6.1 %copy-start.7 = (bf16[4,256,640]{2,1,0:T(8,128)(2,1)S(1)}, bf16[4,256,640]{2,1,0:T(8,128)(2,1)}, u32[]{:S(2)}) copy-start(bf16[4,256,640]{2,1,0:T(8,128)(2,1)} %get-tuple-element.76.dqkv_hbm) | copy-start | bytes 3932164
  455.9 73.0 %copy-start.10 = (bf16[256,1408]{1,0:T(8,128)(2,1)S(1)}, bf16[256,1408]{1,0:T(8,128)(2,1)}, u32[]{:S(2)}) copy-start(bf16[256,1408]{1,0:T(8,128)(2,1)} %reduce-scatter.4.cloned.1.call-done) | copy-start | bytes 2162692
  528.9 4.1 copy-start.16
  529.0 7.9 %copy-start.6 = (f32[256,2048]{1,0:T(8,128)S(1)}, f32[256,2048]{1,0:T(8,128)}, u32[]{:S(2)}) copy-start(f32[256,2048]{1,0:T(8,128)} %get-tuple-element.78) | copy-start | bytes 6291460
  530.5 5.4 copy-start.8
  533.5 4.7 copy-start.14
  533.5 5.3 copy-start.13
  533.5 5.9 %copy-start.12 = (f32[64,2048]{1,0:T(8,128)S(1)}, f32[64,2048]{1,0:T(8,128)}, u32[]{:S(2)}) copy-start(f32[64,2048]{1,0:T(8,128)} %get-tuple-element.137) | copy-start | bytes 1572868
  535.9 4.4 copy-start.11
Sparse Core Ops, SparseCore 0:
  9.7 84.0 all-gather.5
  95.4 39.3 all-gather.11
  136.5 63.3 all-gather.7
  201.9 59.1 all-gather.9
  263.2 63.5 reduce-scatter.3
  328.9 64.1 reduce-scatter.7
  395.4 79.1 reduce-scatter.5

commit v9 on v8

--- a/solution.py
+++ b/solution.py
@@ -280,14 +280,17 @@
     ga_hbm,
     down_ref,
     res_hbm,
+    branch_hbm,
     out_hbm,
     final_ref,
+    acc_hbm,
     qkv_ref,
     att_ref,
     rden_ref,
     carry_ref,
     ga_ref,
     res_ref,
+    branch_ref,
     out_ref,
     gn,
     send_state,
@@ -305,8 +308,14 @@
     local_sem,
     load_sem,
     store_sem,
+    term_ref,
+    acc_ref,
+    sib_land,
+    sib_send,
+    sib_recv,
 ):
-    place, f = lax.axis_index("seq"), lax.axis_index("feat")
+    place, f, d = lax.axis_index("seq"), lax.axis_index("feat"), lax.axis_index("dp")
+    dps = term_ref.shape[2]
     loads = Loads(
         (
             (qkv_hbm, qkv_ref),
@@ -318,6 +327,7 @@
         ),
         load_sem,
     ).start()
+    late = Loads(((branch_hbm, branch_ref),), load_sem.at[pl.ds(6, 1)]).start()
     groups, block = qkv_ref.shape[0], qkv_ref.shape[1]
     width = heads * FDIM
     tables = (left_ref, right_ref, rows_ref)
@@ -341,7 +351,11 @@
             copy.start()
 
     chain = [lax.rem(place + 1, count), lax.rem(place + count - 1, count)]
-    greet(square_targets(f) + [{"seq": c} for c in chain])
+    greet(
+        square_targets(f)
+        + [{"seq": c} for c in chain]
+        + [{"dp": lax.rem(d + o, dps)} for o in range(1, dps)]
+    )
     fill = pltpu.make_async_copy(down_ref, terms, local_sem.at[0])
     fill.start()
     ring = SquareSum(terms, land, f, f_send, f_recv)
@@ -439,6 +453,10 @@
 
     lax.fori_loop(0, groups, pull, 0)
     ring.relay()
+    late.wait()
+    term_tiles(term_ref, branch_ref, att_ref)
+    sibling = SiblingSum(term_ref, acc_ref, sib_land, (sib_send, sib_recv), d, dps)
+    sibling.start()
 
     def carry_back(g, none):
         segc = segc_ref[g]
@@ -482,12 +500,32 @@
 
     by_rows(ring, add_up)
     ring.finish()
+    sibling.add()
+    keep = pltpu.make_async_copy(acc_ref, acc_hbm, store_sem.at[groups])
+    keep.start()
 
     def stored(g, none):
         store(g).wait()
         return none
 
     lax.fori_loop(0, groups, stored, 0)
+    sibling.finish()
+    keep.wait()
+
+
+def term_tiles(term, left, right):
+    parts, *shape = term.shape
+    tile = left.shape[2] // parts
+
+    def one(i, none):
+        cols = pl.ds(pl.multiple_of(i * tile, tile), tile)
+        total = dot_tn(left[0, :, cols], right[0])
+        for g in range(1, left.shape[0]):
+            total = total + dot_tn(left[g, :, cols], right[g])
+        term[i] = total.astype(bf16).reshape(shape)
+        return none
+
+    lax.fori_loop(0, parts, one, 0)
 
 
 def whole_vmem(count):
@@ -535,10 +573,13 @@
 
 
 def attention_backward(
-    qkv, segc, segr, tables, att, rden, carry, csum, ga, down, residual, heads
+    qkv, segc, segr, tables, att, rden, carry, csum, ga, down, residual, branch, heads
 ):
     groups, block, wide = qkv.shape
     count = lax.axis_size("seq")
+    parts, dps = lax.axis_size("feat"), lax.axis_size("dp")
+    rows_each = branch.shape[2] // (parts * count * dps)
+    by_row = (parts, count, dps, rows_each, heads * HV)
     states = (groups, heads, STATE, HV)
     sums = (groups, 8, LANES)
     return pl.pallas_call(
@@ -546,14 +587,15 @@
         out_shape=(
             jax.ShapeDtypeStruct((groups, block, wide), bf16),
             jax.ShapeDtypeStruct(residual.shape, bf16),
+            jax.ShapeDtypeStruct((count, by_row[0]) + by_row[3:], bf16),
         ),
         in_specs=in_place(1)
         + whole_vmem(5)
         + in_place(3)
         + whole_vmem(1)
-        + in_place(3),
-        out_specs=tuple(in_place(1) + whole_vmem(1)),
-        scratch_shapes=vmem_like(qkv, att, rden, carry, ga, residual)
+        + in_place(4),
+        out_specs=tuple(in_place(1) + whole_vmem(1) + in_place(1)),
+        scratch_shapes=vmem_like(qkv, att, rden, carry, ga, residual, branch)
         + [
             pltpu.VMEM((groups, block, wide), bf16),
             pltpu.VMEM((groups, heads, block, 2 * HV), bf16),
@@ -570,15 +612,16 @@
             pltpu.SemaphoreType.DMA((6,)),
             pltpu.SemaphoreType.DMA((6,)),
             pltpu.SemaphoreType.DMA((1,)),
-            pltpu.SemaphoreType.DMA((6,)),
-            pltpu.SemaphoreType.DMA((groups,)),
-        ],
+            pltpu.SemaphoreType.DMA((7,)),
+            pltpu.SemaphoreType.DMA((groups + 1,)),
+        ]
+        + sibling_scratch(by_row),
         compiler_params=pltpu.CompilerParams(
             collective_id=1, has_side_effects=True, vmem_limit_bytes=60 << 20
         ),
         cost_estimate=pl.CostEstimate(flops=0, bytes_accessed=1 << 20, transcendentals=0),
         name="attention_backward",
-    )(qkv, segc, segr, *tables, att, rden, carry, csum, ga, down, residual)
+    )(qkv, segc, segr, *tables, att, rden, carry, csum, ga, down, residual, branch)
 
 
 def peers(f):
@@ -733,44 +776,56 @@
             c.wait_send()
 
 
-class RowSum:
-    def __init__(self, term, acc, shares, lands, sems, f, s, d, seqs, dps):
-        self.term, self.acc, self.shares, self.lands = term, acc, shares, lands
-        self.f, self.s, self.d = f, s, d
-        self.parts, self.seqs = term.shape[0], seqs
-        columns = [lax.rem(s + k, seqs) for k in range(1, seqs)]
+class SiblingSum:
+    def __init__(self, term, acc, land, sems, d, dps):
+        self.term, self.acc, self.land, self.d = term, acc, land, d
         others = [lax.rem(d + k, dps) for k in range(1, dps)]
-        d_send, d_recv, z_send, z_recv, a_send, a_recv = sems
-        self.one = [
-            push(term.at[:, :, o], lands[0].at[k], d_send.at[k], d_recv.at[k], {"dp": o})
+        self.copies = [
+            push(term.at[:, :, o], land.at[k], sems[0].at[k], sems[1].at[k], {"dp": o})
             for k, o in enumerate(others)
         ]
+
+    def start(self):
+        for c in self.copies:
+            c.start()
+
+    def add(self):
+        for c in self.copies:
+            c.wait_recv()
+        seqs, parts = self.acc.shape[:2]
+
+        def one(i, none):
+            p, c = i // seqs, lax.rem(i, seqs)
+            total = self.term[p, c, self.d].astype(f32)
+            for k in range(len(self.copies)):
+                total = total + self.land[k, p, c].astype(f32)
+            self.acc[c, p] = total.astype(bf16)
+            return none
+
+        lax.fori_loop(0, parts * seqs, one, 0)
+
+    def finish(self):
+        for c in self.copies:
+            c.wait_send()
+
+
+class RowSum:
+    def __init__(self, acc, shares, land, total, sems, f, s):
+        self.acc, self.shares, self.land, self.total = acc, shares, land, total
+        self.f, self.s = f, s
+        seqs, self.parts = acc.shape[:2]
+        columns = [lax.rem(s + k, seqs) for k in range(1, seqs)]
+        z_send, z_recv, a_send, a_recv = sems
         self.two = [
-            push(acc.at[c], lands[1].at[k], z_send.at[k], z_recv.at[k], {"seq": c})
+            push(acc.at[c], land.at[k], z_send.at[k], z_recv.at[k], {"seq": c})
             for k, c in enumerate(columns)
         ]
         self.three = [
-            push(lands[2].at[p], shares.at[f], a_send.at[i], a_recv.at[i], {"feat": p})
+            push(total.at[p], shares.at[f], a_send.at[i], a_recv.at[i], {"feat": p})
             for i, p in enumerate(peers(f))
         ]
 
     def start(self):
-        for c in self.one:
-            c.start()
-
-    def over_seq(self):
-        for c in self.one:
-            c.wait_recv()
-
-        def one(i, none):
-            p, c = i // self.seqs, lax.rem(i, self.seqs)
-            total = self.term[p, c, self.d].astype(f32)
-            for k in range(len(self.one)):
-                total = total + self.lands[0][k, p, c].astype(f32)
-            self.acc[c, p] = total.astype(bf16)
-            return none
-
-        lax.fori_loop(0, self.parts * self.seqs, one, 0)
         for c in self.two:
             c.start()
 
@@ -781,12 +836,12 @@
         def one(p, none):
             total = self.acc[self.s, p].astype(f32)
             for k in range(len(self.two)):
-                total = total + self.lands[1][k, p].astype(f32)
-            self.lands[2][p] = total.astype(bf16)
+                total = total + self.land[k, p].astype(f32)
+            self.total[p] = total.astype(bf16)
             return none
 
         lax.fori_loop(0, self.parts, one, 0)
-        self.shares[self.f] = self.lands[2][self.f]
+        self.shares[self.f] = self.total[self.f]
         for c in self.three:
             c.start()
 
@@ -795,32 +850,35 @@
             c.wait_recv()
 
     def finish(self):
-        for c in self.one + self.two + self.three:
+        for c in self.two + self.three:
             c.wait_send()
 
 
-def row_sum_scratch(shape):
+def sibling_scratch(shape):
     parts, seqs, dps, rows, wide = shape
     others = max(dps - 1, 1)
     dma = pltpu.SemaphoreType.DMA
     return [
-        pltpu.VMEM((parts, rows, wide), bf16),
+        pltpu.VMEM(shape, bf16),
         pltpu.VMEM((seqs, parts, rows, wide), bf16),
         pltpu.VMEM((others, parts, seqs, rows, wide), bf16),
+        dma((others,)),
+        dma((others,)),
+    ]
+
+
+def row_sum_scratch(shape):
+    seqs, parts, rows, wide = shape
+    dma = pltpu.SemaphoreType.DMA
+    return [
+        pltpu.VMEM((parts, rows, wide), bf16),
         pltpu.VMEM((seqs - 1, parts, rows, wide), bf16),
         pltpu.VMEM((parts, rows, wide), bf16),
-        dma((others,)),
-        dma((others,)),
         dma((seqs - 1,)),
         dma((seqs - 1,)),
         dma((3,)),
         dma((3,)),
     ]
-
-
-def row_sum(term, scratch, f, s, d, seqs, dps):
-    shares, acc = scratch[:2]
-    return RowSum(term, acc, shares, scratch[2:5], scratch[5:], f, s, d, seqs, dps)
 
 
 def opening_kernel(
@@ -1069,7 +1127,7 @@
         lax.fori_loop(0, part.shape[2] // tile, one, 0)
 
 
-def summed_products(part, land, f, pairs, send_sem, recv_sem, chunks=1, beside=None, first=False):
+def summed_products(part, land, f, pairs, send_sem, recv_sem, chunks=1, beside=(), first=False):
     side, above, across = peers(f)
     rows = part.shape[1] // chunks
     rings = [
@@ -1081,16 +1139,18 @@
     product_tiles(part, across, pairs, 512, first)
     for ring in rings:
         ring.start_cross()
-    if beside is not None:
-        beside()
+    beside = iter(beside)
+    next(beside, int)()
     product_tiles(part, side, pairs, 512)
     for ring in rings:
         ring.near[0].start()
     product_tiles(part, above, pairs, 512)
     for ring in rings:
         ring.near[1].start()
+    next(beside, int)()
     rings[0].relay()
     product_tiles(part, f, pairs, 512)
+    next(beside, int)()
     for ring in rings[1:]:
         ring.relay()
     return rings
@@ -1223,8 +1283,7 @@
 
 
 def rows_back_kernel(
-    gg_hbm,
-    gu_hbm,
+    grads_hbm,
     wg_hbm,
     wu_hbm,
     res_hbm,
@@ -1263,7 +1322,7 @@
     store_sem,
 ):
     f = lax.axis_index("feat")
-    rows_in = Loads(((gg_hbm, gg_ref), (gu_hbm, gu_ref)), load_sem).start()
+    rows_in = Loads(((grads_hbm.at[0], gg_ref), (grads_hbm.at[1], gu_ref)), load_sem).start()
     weights = [
         ByTiles(src, dst, tile_sem.at[i], 512)
         for i, (src, dst) in enumerate(((wg_hbm, wg), (wu_hbm, wu)))
@@ -1343,9 +1402,9 @@
 
 
 def rows_back(
-    grad_gate, grad_up, gate_w, up_w, residual, cot_own, gain_two, mixed, down_w, out_w
+    grads, gate_w, up_w, residual, cot_own, gain_two, mixed, down_w, out_w
 ):
-    parts, block, hidden = grad_gate.shape
+    _, parts, block, hidden = grads.shape
     width = residual.shape[1]
     dma = pltpu.SemaphoreType.DMA
     return pl.pallas_call(
@@ -1357,7 +1416,7 @@
             jax.ShapeDtypeStruct((parts, block, width), bf16),
             jax.ShapeDtypeStruct((parts, block, out_w.shape[3]), f32),
         ),
-        in_specs=in_place(6) + whole_vmem(1) + in_place(3),
+        in_specs=in_place(5) + whole_vmem(1) + in_place(3),
         out_specs=tuple(in_place(2) + whole_vmem(1) + in_place(2)),
         scratch_shapes=[
             pltpu.VMEM((parts, block, width), bf16),
@@ -1365,7 +1424,8 @@
             pltpu.VMEM((parts, block, width), bf16),
             pltpu.VMEM((parts, block, out_w.shape[3]), f32),
         ]
-        + vmem_like(grad_gate, grad_up, residual, cot_own)
+        + [pltpu.VMEM((parts, block, hidden), bf16)] * 2
+        + vmem_like(residual, cot_own)
         + square_scratch(parts, block, width)[:2]
         + [
             pltpu.VMEM((width, hidden), bf16),
@@ -1381,7 +1441,7 @@
         ),
         cost_estimate=pl.CostEstimate(flops=0, bytes_accessed=1 << 20, transcendentals=0),
         name="rows_back",
-    )(grad_gate, grad_up, gate_w, up_w, residual, cot_own, gain_two, mixed, down_w, out_w)
+    )(grads, gate_w, up_w, residual, cot_own, gain_two, mixed, down_w, out_w)
 
 
 def closing_kernel(
@@ -1393,8 +1453,9 @@
     gres_hbm,
     gain_ref,
     gsum_two_ref,
-    term_hbm,
-    oterm_hbm,
+    normed_hbm,
+    oacc_hbm,
+    down_hbm,
     x_ref,
     tile_ref,
     query_ref,
@@ -1418,16 +1479,22 @@
     w_ref,
     tok_ref,
     gres_ref,
+    normed_ref,
+    oacc_ref,
+    load_sem,
+    first_sem,
     term_ref,
-    oterm_ref,
-    load_sem,
+    acc_ref,
+    sib_land,
+    sib_send,
+    sib_recv,
     *sum_scratch,
 ):
+    begin = Loads(((oacc_hbm, oacc_ref),), first_sem).start()
     loads = Loads(
         (
-            (oterm_hbm, oterm_ref),
-            (term_hbm, term_ref),
             (dqkv_hbm, dqkv_ref),
+            (normed_hbm, normed_ref),
             (w_hbm, w_ref),
             (tok_hbm, tok_ref),
             (gres_hbm, gres_ref),
@@ -1447,18 +1514,21 @@
     greet(
         [{"feat": a, "seq": b} for a, b in circle] + [{"dp": o} for o in others]
     )
+    begin.wait()
+    rows_sum = RowSum(acc_ref, *sum_scratch[:3], sum_scratch[3:half], f, s)
+    out_sum = RowSum(oacc_ref, *sum_scratch[half : half + 3], sum_scratch[half + 3 :], f, s)
+    out_sum.start()
     loads.wait()
-    rows_sum = row_sum(term_ref, sum_scratch[:half], f, s, d, seqs, dps)
-    out_sum = row_sum(oterm_ref, sum_scratch[half:], f, s, d, seqs, dps)
-    out_sum.start()
-    rows_sum.start()
+    term_tiles(term_ref, normed_ref, dqkv_ref)
+    sibling = SiblingSum(term_ref, acc_ref, sib_land, (sib_send, sib_recv), d, dps)
+    sibling.start()
 
     def over_seq():
-        out_sum.over_seq()
-        rows_sum.over_seq()
+        sibling.add()
+        rows_sum.start()
 
     rings = summed_products(
-        part, land, f, [(dqkv_ref, w_ref)], s_send, s_recv, land.shape[0], over_seq
+        part, land, f, [(dqkv_ref, w_ref)], s_send, s_recv, land.shape[0], (over_seq,)
     )
     gsum[...] = jnp.zeros_like(gsum)
 
@@ -1472,8 +1542,6 @@
     for ring in rings:
         ring.arrive()
         by_rows(ring, finish_rows)
-    out_sum.over_feat()
-    rows_sum.over_feat()
     for ring in rings:
         ring.finish()
 
@@ -1513,6 +1581,8 @@
     for k in range(len(others)):
         total = total + tail[k]
     tile_ref[...] = total
+    out_sum.over_feat()
+    rows_sum.over_feat()
     rows_sum.arrive()
     first = 0
     for ref in (query_ref, key_ref, value_ref):
@@ -1522,6 +1592,7 @@
             ref[:, p * each : (p + 1) * each] = piece.astype(f32)
         first += each
     rows_sum.finish()
+    sibling.finish()
     out_sum.arrive()
     each = ograd_ref.shape[1] // parts
     for p in range(parts):
@@ -1531,13 +1602,15 @@
         c.wait_send()
 
 
-def closing(dqkv, qkv_w, own, grad_residual, gain_one, gain_two_sum, qkv_term, out_term):
+def closing(dqkv, qkv_w, own, grad_residual, gain_one, gain_two_sum, normed, out_acc, down_grad):
     parts, seqs, dps = (lax.axis_size(a) for a in ALL)
     block, width = own.shape
     others = max(dps - 1, 1)
     lanes = width // (parts * seqs)
     circle = parts * seqs - 1
-    rows_each = qkv_term.shape[3]
+    rows_each = out_acc.shape[2]
+    by_row = (parts, seqs, dps, rows_each, dqkv.shape[2])
+    acc_shape = out_acc.shape[:3] + dqkv.shape[2:]
     dma = pltpu.SemaphoreType.DMA
     return pl.pallas_call(
         functools.partial(closing_kernel, seqs, dps),
@@ -1549,7 +1622,7 @@
             jax.ShapeDtypeStruct((rows_each, HEADS * HV), f32),
             jax.ShapeDtypeStruct((rows_each, HEADS * HV), f32),
         ),
-        in_specs=in_place(4) + whole_vmem(2) + in_place(2),
+        in_specs=in_place(4) + whole_vmem(2) + in_place(3),
         out_specs=tuple(whole_vmem(6)),
         scratch_shapes=square_scratch(parts, block, width)
         + [
@@ -1563,16 +1636,17 @@
             dma((others,)),
             dma((others,)),
         ]
-        + vmem_like(dqkv, qkv_w, own, grad_residual, qkv_term, out_term)
-        + [dma((6,))]
-        + row_sum_scratch(qkv_term.shape)
-        + row_sum_scratch(out_term.shape),
+        + vmem_like(dqkv, qkv_w, own, grad_residual, normed, out_acc)
+        + [dma((5,)), dma((1,))]
+        + sibling_scratch(by_row)
+        + row_sum_scratch(acc_shape)
+        + row_sum_scratch(out_acc.shape),
         compiler_params=pltpu.CompilerParams(
             collective_id=5, has_side_effects=True, vmem_limit_bytes=60 << 20
         ),
         cost_estimate=pl.CostEstimate(flops=0, bytes_accessed=1 << 20, transcendentals=0),
         name="closing",
-    )(dqkv, qkv_w, own, grad_residual, gain_one, gain_two_sum, qkv_term, out_term)
+    )(dqkv, qkv_w, own, grad_residual, gain_one, gain_two_sum, normed, out_acc, down_grad)
 
 
 def local(
@@ -1629,23 +1703,20 @@
     down_term = dot_tn(cot_all, mixed).astype(bf16)
     mixed, cot_late, down_term = lax.optimization_barrier((mixed, cot_all, down_term))
     grad_mixed = dot(cot_late, down_w)
-    grad_gate = (grad_mixed * up_out * sig * (1.0 + gate_out * (1.0 - sig))).astype(bf16)
-    grad_up = (grad_mixed * silu).astype(bf16)
-
-    def summed(term):
-        return lax.psum_scatter(term, ("seq", "dp"), scatter_dimension=0, tiled=True)
-
-    gate_term = dot_tn(rows_all, grad_gate).astype(bf16)
-    up_term = dot_tn(rows_all, grad_up).astype(bf16)
-    grad_gate, grad_up, gate_term, up_term = lax.optimization_barrier(
-        (grad_gate, grad_up, gate_term, up_term)
-    )
-    down_sum, gate_sum, up_sum = summed(down_term), summed(gate_term), summed(up_term)
+    grads = jnp.stack(
+        [grad_mixed * up_out * sig * (1.0 + gate_out * (1.0 - sig)), grad_mixed * silu]
+    ).astype(bf16)
+
+    def summed(term, dim):
+        return lax.psum_scatter(term, ("seq", "dp"), scatter_dimension=dim, tiled=True)
+
+    both_term = jnp.einsum("xtf,td->xfd", grads, rows_all, preferred_element_type=f32).astype(bf16)
+    grads, both_term = lax.optimization_barrier((grads, both_term))
+    down_sum, both_sum = summed(down_term, 0), summed(both_term, 2)
 
     by_device = (parts, block, -1)
     branch_all, grad_residual, gain_two_sum, down, ga = rows_back(
-        grad_gate.reshape(by_device),
-        grad_up.reshape(by_device),
+        grads.reshape((2,) + by_device),
         gate_w,
         up_w,
         residual,
@@ -1655,16 +1726,32 @@
         down_w,
         out_w,
     )
-    branch_all = branch_all.reshape(rows_total, width)
-    by_row = (parts, lax.axis_size("seq"), lax.axis_size("dp"), rows_each, -1)
-    out_term = dot_tn(branch_all, att.reshape(rows_total, heads * HV)).astype(bf16)
-    dqkv, output = attention_backward(
-        qkv, segc, segr, tables, att, rden, carry, csum, ga, down, residual, heads
+    dqkv, output, out_acc = attention_backward(
+        qkv,
+        segc,
+        segr,
+        tables,
+        att,
+        rden,
+        carry,
+        csum,
+        ga,
+        down,
+        residual,
+        branch_all,
+        heads,
     )
-    dqkv_late, down_sum = lax.optimization_barrier((dqkv, down_sum))
-    qkv_term = dot_tn(normed, dqkv_late.reshape(rows_total, qkv_width)).astype(bf16)
+    down_grad = down_sum.T.astype(f32)
     x_grad, gain_grads, query_grad, key_grad, value_grad, out_grad = closing(
-        dqkv, qkv_w, own, grad_residual, gain_one, gain_two_sum, qkv_term.reshape(by_row), out_term.reshape(by_row)
+        dqkv,
+        qkv_w,
+        own,
+        grad_residual,
+        gain_one,
+        gain_two_sum,
+        normed.reshape(parts, block, width),
+        out_acc,
+        down_grad,
     )
     gain_each = gain_grads.shape[1] // lax.axis_size("dp")
     gain_grads = lax.dynamic_slice_in_dim(
@@ -1679,9 +1766,9 @@
         key_grad,
         value_grad,
         out_grad.T,
-        gate_sum.astype(f32),
-        up_sum.astype(f32),
-        down_sum.T.astype(f32),
+        both_sum[0].T.astype(f32),
+        both_sum[1].T.astype(f32),
+        down_grad,
     )
 
 

time: 555 us -> 551 us (level)
  matrix products: 85.9 us -> 66.7 us
  Pallas kernels: 406 us -> 415 us
    dot_general x5 -> x1, matrix products: 41.7 us -> 8.16 us  [dot_tn(): lax.dot_general(a, b, (((0,), (0,)), ((), ())), preferred_element_type=f32)]
    dot_general x0 -> x1, matrix products: none -> 15.3 us  [local(): jnp.einsum('xtf,td->xfd', grads, rows_all, preferred_element_type=f32)]
    pallas_call x1, Pallas kernels: 61 us -> 72 us  [attention_backward(): pl.pallas_call(functools.partial(backward_kernel, count, heads), out_shap...]
    unnamed x45 -> x34, local copies, waits for them, and re-layouts: 8.93 us -> 12.4 us
  transfers between devices with their start and end apart: 7 -> 6, of which waited for: 1 -> 1; matrix products, arithmetic and copies ran while one was open for 18% -> 15% of each run, Pallas kernels for 74% -> 76%
where the time goes in v9:
time: 551 us; the launch traced here: 544 us
  Pallas kernels  415 us (75%)
  matrix products  66.7 us (12%)
  local copies, waits for them, and re-layouts  18.3 us (3%)
  waiting for transfers between devices  17 us (3%)
  between operations  14.8 us (3%)
  other arithmetic  12.1 us (2%)
    pallas_call x1, Pallas kernels, rows_back(): pl.pallas_call(rows_back_kernel, out_shape=(jax.ShapeDtypeStruct((parts,...  84.2 us
    pallas_call x1, Pallas kernels, opening(): pl.pallas_call(functools.partial(opening_kernel, seqs, dps), out_shape=(j...  74.9 us
    pallas_call x1, Pallas kernels, branch_step(): pl.pallas_call(branch_kernel, out_shape=(jax.ShapeDtypeStruct((parts, blo...  72.2 us
    pallas_call x1, Pallas kernels, attention_backward(): pl.pallas_call(functools.partial(backward_kernel, count, heads), out_shap...  72 us
    pallas_call x1, Pallas kernels, closing(): pl.pallas_call(functools.partial(closing_kernel, seqs, dps), out_shape=(j...  70.6 us
    dot_general x4, matrix products, dot(): lax.dot_general(a, b, (((1,), (0,)), ((), ())), preferred_element_type=f32)  43.3 us
    pallas_call x1, Pallas kernels, attention_forward(): pl.pallas_call(functools.partial(forward_kernel, count, heads), out_shape...  41 us
    all_gather x1, waiting for transfers between devices, local(): down_w = lax.all_gather(w_down.T, ('seq', 'dp'), axis=0, tiled=True)  15.5 us
  transfers between devices with their start and end apart: 6, of which 1 were waited for; matrix products, arithmetic and copies ran while one was open for 15% of the time, Pallas kernels for 76%

profile of v9, /device:TPU:0, one launch (start us, length us, event | category | flops | bytes accessed | tf_op | source)
XLA Modules:
  0.0 544.2 jit_solution(4095942046530436866)
XLA Ops:
  7.2 0.0 all-gather.6.cloned.1.call-start
  7.2 0.7 all-gather.6.cloned.1.call-update
  7.9 0.0 all-gather.12.cloned.1.call-start
  8.0 74.9 %opening.1 = (bf16[4,256,2048]{2,1,0:T(8,128)(2,1)}, bf16[4,4,2,64,640]{4,3,2,1,0:T(8,128)(2,1)}, f32[4,4,2,8,128]{4,3,2,1,0:T(8,128)}, bf16[4,64,512]{2,1,0:T(8,128)(2,1)}) custom-call(bf16[256,2048]{1,0:T(8,128)(2,1)} %bitcast.61, bf16[64,256]{1,0:T(8,128)(2,1)} %query_ref.1, bf16[64,256]{1,0:T(8,128)(2,1)} %key_ref.1, bf16[64,2048]{1,0:T(8,128)(2,1)} %value_ref.1, ...), custom_call_target="tpu_custom_call" | custom-call | bytes 1048576 | tf_op jit(solution)/shard_map/opening/pallas_call | solution.py:1043
  82.9 0.9 slice_bitcast_fusion.2
  83.8 0.1 slice_reduce_fusion
  83.9 0.1 mul.53
  84.0 3.3 fusion
  87.3 0.2 copy-done
  87.5 1.0 fusion.2.normed_hbm
  88.5 2.0 copy-done.1
  90.5 4.5 convolution_convert_fusion.2
  95.0 0.0 all-gather.8.cloned.1.call-start
  95.1 0.7 all-gather.8.cloned.1.call-update
  95.8 0.0 all-gather.10.cloned.1.call-start
  95.8 1.1 copy.35
  97.0 0.0 reduce-scatter.3.cloned.1.call-start
  97.0 0.6 fusion.6
  97.6 1.0 copy.37.segc_ref
  98.7 0.7 slice.30.gain_ref
  99.3 41.0 %attention_forward.1 = (bf16[4,256,512]{2,1,0:T(8,128)(2,1)}, f32[4,256,512]{2,1,0:T(8,128)}, bf16[4,4,160,128]{3,2,1,0:T(8,128)(2,1)}, f32[4,8,256]{2,1,0:T(8,128)}, bf16[4,256,2048]{2,1,0:T(8,128)(2,1)}) custom-call(bf16[4,256,640]{2,1,0:T(8,128)(2,1)} %bitcast.66, f32[4,256,1]{2,1,0:T(8,128)} %copy.37.segc_ref, f32[4,1,256]{2,1,0:T(1,128)} %get-tuple-element.112.segr_ref, ...), custom_call_target="tpu_custom_call" | custom-call | bytes 1048576 | tf_op jit(solution)/shard_map/attention_forward/pallas_call | solution.py:541
  140.4 0.0 all-gather.12.cloned.1.call-done
  140.4 72.2 %branch_step.1 = (bf16[4,256,2048]{2,1,0:T(8,128)(2,1)}, f32[256,2048]{1,0:T(8,128)}) custom-call(bf16[4,256,512]{2,1,0:T(8,128)(2,1)} %get-tuple-element.51.att_hbm, bf16[8,4,64,512]{3,2,1,0:T(8,128)(2,1)} %bitcast.64, bf16[256,2048]{1,0:T(8,128)(2,1)} %bitcast.62, f32[1,2048]{1,0:T(1,128)} %slice.30.gain_ref), custom_call_target="tpu_custom_call" | custom-call | bytes 1048576 | tf_op jit(solution)/shard_map/branch_step/pallas_call | solution.py:1265
  212.6 11.8 %fusion.7 = f32[1024,1408]{1,0:T(8,128)} fusion(bf16[1024,2048]{1,0:T(8,128)(2,1)} %bitcast.83, bf16[2048,1408]{1,0:T(8,128)(2,1)} %all-gather.6.cloned.1.call-done.wg_hbm), kind=kOutput, calls=%fused_computation.30 | convolution fusion | flops 5905580032 | bytes 15728640 | tf_op jit(solution)/shard_map/dot_general | solution.py:24
  224.4 12.9 %multiply_convert_fusion.2 = (bf16[1024,1408]{1,0:T(8,128)(2,1)S(1)}, f32[1024,1408]{1,0:T(8,128)}) fusion(f32[1024,1408]{1,0:T(8,128)} %fusion.7, bf16[1024,2048]{1,0:T(8,128)(2,1)} %bitcast.84, bf16[2048,1408]{1,0:T(8,128)(2,1)} %all-gather.8.cloned.1.call-done.wu_hbm), kind=kOutput, calls=%fused_computation.10 | convolution fusion | flops 5914230784 | bytes 24379392 | tf_op jit(solution)/shard_map/dot_general | solution.py:24
  237.3 8.2 %convolution_convert_fusion.1 = bf16[2048,1408]{0,1:T(8,128)(2,1)} fusion(bf16[1024,2048]{1,0:T(8,128)(2,1)S(1)} %bitcast.82, bf16[1024,1408]{1,0:T(8,128)(2,1)S(1)} %get-tuple-element.64), kind=kOutput, calls=%fused_computation.6 | convolution fusion | flops 5908463616 | bytes 12845056 | tf_op jit(solution)/shard_map/dot_general | solution.py:32
  245.5 0.0 reduce-scatter.5.cloned.1.call-start
  245.5 15.5 %all-gather.10.cloned.1.call-done.wd_hbm = bf16[2048,1408]{1,0:T(8,128)(2,1)} async-done(((bf16[256,1408]{1,0:T(8,128)(2,1)}), bf16[2048,1408]{1,0:T(8,128)(2,1)}) %all-gather.10.cloned.1.call-update) | async-done | bytes 5767184 | tf_op jit(solution)/shard_map/all_gather | solution.py:1689
  261.1 14.1 %fusion.5 = (bf16[1,1024,1408]{2,1,0:T(8,128)(2,1)S(1)}, bf16[1,1024,1408]{2,1,0:T(8,128)(2,1)S(1)}) fusion(f32[1024,1408]{1,0:T(8,128)} %fusion.7, f32[1024,1408]{1,0:T(8,128)} %get-tuple-element.115, bf16[1024,2048]{1,0:T(8,128)(2,1)} %bitcast.81, bf16[2048,1408]{1,0:T(8,128)(2,1)} %all-gather.10.cloned.1.call-done.wd_hbm), kind=kOutput, calls=%fused_computation.14 | convolution fusion | flops 5924323328 | bytes 27262976 | tf_op jit(solution)/shard_map/dot_general | solution.py:24
  275.2 3.4 pad_maximum_fusion
  278.6 0.5 copy-done.12
  279.1 15.3 %convolution_convert_fusion = bf16[2,1408,2048]{2,1,0:T(8,128)(2,1)} fusion(bf16[1024,2048,1]{1,0,2:T(8,128)(2,1)S(1)} %bitcast.85, bf16[1,1024,1408]{2,1,0:T(8,128)(2,1)S(1)} %get-tuple-element.106, bf16[1,1024,1408]{2,1,0:T(8,128)(2,1)S(1)} %get-tuple-element.105), kind=kOutput, calls=%fused_computation | convolution fusion | flops 11819810816 | bytes 21495808 | tf_op jit(solution)/shard_map/xtf,td->xfd/dot_general | solution.py:1713
  294.4 0.7 slice.31.gain_ref
  295.1 84.2 %rows_back.1 = (bf16[4,256,2048]{2,1,0:T(8,128)(2,1)}, f32[256,2048]{1,0:T(8,128)}, f32[1,2048]{1,0:T(1,128)}, bf16[4,256,2048]{2,1,0:T(8,128)(2,1)}, f32[4,256,512]{2,1,0:T(8,128)}) custom-call(bf16[2,4,256,1408]{3,2,1,0:T(8,128)(2,1)} %bitcast.59, bf16[2048,1408]{1,0:T(8,128)(2,1)} %all-gather.6.cloned.1.call-done.wg_hbm, ...), custom_call_target="tpu_custom_call" | custom-call | bytes 1048576 | tf_op jit(solution)/shard_map/rows_back/pallas_call | solution.py:1410
  379.4 72.0 %attention_backward.1 = (bf16[4,256,640]{2,1,0:T(8,128)(2,1)}, bf16[256,2048]{1,0:T(8,128)(2,1)}, bf16[4,4,64,512]{3,2,1,0:T(8,128)(2,1)}) custom-call(bf16[4,256,640]{2,1,0:T(8,128)(2,1)} %bitcast.67, f32[4,256,1]{2,1,0:T(8,128)} %copy.37.segc_ref, f32[4,1,256]{2,1,0:T(1,128)} %get-tuple-element.112.segr_ref, bf16[4,64,256]{2,1,0:T(8,128)(2,1)} %constant.25.clone.left_ref, ...), custom_call_target="tpu_custom_call" | custom-call | bytes 1048576 | tf_op jit(solution)/shard_map/attention_backward/pallas_call | solution.py:585
  451.4 2.3 convert_bitcast_fusion.2.down_hbm
  453.7 70.6 %closing.1 = (f32[256,2048]{1,0:T(8,128)}, f32[8,128]{1,0:T(8,128)}, f32[64,256]{1,0:T(8,128)}, f32[64,256]{1,0:T(8,128)}, f32[64,2048]{1,0:T(8,128)}, /*index=5*/f32[64,2048]{1,0:T(8,128)}) custom-call(bf16[4,256,640]{2,1,0:T(8,128)(2,1)} %get-tuple-element.69.dqkv_hbm, bf16[2048,640]{1,0:T(8,128)(2,1)} %bitcast.72, bf16[256,2048]{1,0:T(8,128)(2,1)} %bitcast.63, ...), custom_call_target="tpu_custom_call" | custom-call | bytes 1048576 | tf_op jit(solution)/shard_map/closing/pallas_call | solution.py:1615
  524.3 0.8 constant_dynamic-slice_fusion
  525.1 0.5 slice_bitcast_fusion.3
  525.6 1.5 convert_bitcast_fusion
  527.2 1.5 copy.39
  528.7 1.5 copy.38
  530.3 2.4 copy.48
  532.7 1.3 copy.49
  534.0 0.6 copy.50
  534.6 0.6 copy.51
  535.3 0.8 copy.52
  536.1 0.8 copy.53
  (32 shorter events, 0.1 us)
Async XLA Ops:
  7.2 87.8 %all-gather.6.cloned.1.call-start = ((), (), s32[]{:S(2)}) async-start(), calls=%async_computation.2 | async-start | bytes 6488064 | tf_op jit(solution)/shard_map/all_gather | solution.py:1678
  7.9 132.5 %all-gather.12.cloned.1.call-start = ((), (), s32[]{:S(2)}) async-start(), calls=%async_computation.7 | async-start | bytes 2359296 | tf_op jit(solution)/shard_map/all_gather | solution.py:1687
  84.0 3.5 copy-start
  87.5 3.0 copy-start.3
  88.5 2.0 copy-start.1
  90.5 5.3 copy-start.5
  90.5 6.5 %copy-start.10 = (s32[4,1,256]{2,1,0:T(1,128)S(1)}, s32[4,1,256]{2,1,0:T(1,128)}, u32[]{:S(2)}) copy-start(s32[4,1,256]{2,1,0:T(1,128)} %param.16) | copy-start | bytes 12292
  95.0 129.4 %all-gather.8.cloned.1.call-start = ((), (), s32[]{:S(2)}) async-start(), calls=%async_computation.3 | async-start | bytes 6488064 | tf_op jit(solution)/shard_map/all_gather | solution.py:1688
  95.8 165.3 %all-gather.10.cloned.1.call-start = ((), (), s32[]{:S(2)}) async-start(), calls=%async_computation.4 | async-start | bytes 6488064 | tf_op jit(solution)/shard_map/all_gather | solution.py:1689
  97.0 354.4 %reduce-scatter.3.cloned.1.call-start = ((), (), s32[]{:S(2)}) async-start(), calls=%async_computation.5 | async-start | bytes 6488064 | tf_op jit(solution)/shard_map/reduce_scatter | solution.py:1711
  224.4 12.9 %copy-start.11 = (bf16[4,256,2048]{2,1,0:T(8,128)(2,1)S(1)}, bf16[4,256,2048]{2,1,0:T(8,128)(2,1)}, u32[]{:S(2)}) copy-start(bf16[4,256,2048]{2,1,0:T(8,128)(2,1)} %get-tuple-element.59) | copy-start | bytes 12582916
  237.3 8.2 %copy-start.2 = (bf16[1024,1408]{1,0:T(8,128)(2,1)}, bf16[1024,1408]{1,0:T(8,128)(2,1)S(1)}, u32[]{:S(2)}) copy-start(bf16[1024,1408]{1,0:T(8,128)(2,1)S(1)} %get-tuple-element.64) | copy-start | bytes 8650756
  245.5 280.1 %reduce-scatter.5.cloned.1.call-start = ((), (), s32[]{:S(2)}) async-start(), calls=%async_computation.6 | async-start | bytes 12976128 | tf_op jit(solution)/shard_map/reduce_scatter | solution.py:1711
  275.2 3.9 copy-start.12
  528.7 4.0 copy-start.4
  530.3 3.7 copy-start.9
  530.3 4.4 copy-start.8
  530.3 5.0 copy-start.7
  530.3 5.8 %copy-start.6 = (f32[64,2048]{1,0:T(8,128)S(1)}, f32[64,2048]{1,0:T(8,128)}, u32[]{:S(2)}) copy-start(f32[64,2048]{1,0:T(8,128)} %get-tuple-element.79) | copy-start | bytes 1572868
Sparse Core Ops, SparseCore 0:
  9.7 84.0 all-gather.5
  95.4 39.3 all-gather.11
  136.5 63.3 all-gather.7
  201.9 59.1 all-gather.9
  263.2 63.5 reduce-scatter.2
  328.9 132.9 reduce-scatter.4

commit v10 on v9

--- a/solution.py
+++ b/solution.py
@@ -813,34 +813,55 @@
     def __init__(self, acc, shares, land, total, sems, f, s):
         self.acc, self.shares, self.land, self.total = acc, shares, land, total
         self.f, self.s = f, s
-        seqs, self.parts = acc.shape[:2]
-        columns = [lax.rem(s + k, seqs) for k in range(1, seqs)]
+        self.seqs, self.parts = seqs, parts = acc.shape[:2]
+        to = (lax.rem(s + 1, seqs), lax.rem(s + seqs - 1, seqs))
         z_send, z_recv, a_send, a_recv = sems
-        self.two = [
-            push(acc.at[c], land.at[k], z_send.at[k], z_recv.at[k], {"seq": c})
-            for k, c in enumerate(columns)
-        ]
+        self.blocks, self.sends, self.comes, self.two = [], [], [], []
+        for t in range(1, seqs):
+            blocks = (lax.rem(s + seqs - t, seqs), lax.rem(s + t, seqs))
+            self.blocks.append(blocks)
+            self.sends.append((s < t, s > seqs - 1 - t))
+            self.comes.append(((s > 0) & (s - 1 < t), (s < seqs - 1) & (s + 1 > seqs - 1 - t)))
+            self.two.append(
+                [
+                    push(
+                        acc.at[blocks[i]],
+                        land.at[t - 1, i],
+                        z_send.at[t - 1, i],
+                        z_recv.at[t - 1, i],
+                        {"seq": to[i]},
+                    )
+                    for i in range(2)
+                ]
+            )
         self.three = [
             push(total.at[p], shares.at[f], a_send.at[i], a_recv.at[i], {"feat": p})
             for i, p in enumerate(peers(f))
         ]
 
-    def start(self):
-        for c in self.two:
-            c.start()
+    def add(self, into, t, i):
+        @pl.when(self.comes[t - 1][i])
+        def _():
+            self.two[t - 1][i].wait_recv()
+
+            def one(p, none):
+                into[p] = (
+                    into[p].astype(f32) + self.land[t - 1, i, p].astype(f32)
+                ).astype(bf16)
+                return none
+
+            lax.fori_loop(0, self.parts, one, 0)
+
+    def step(self, t):
+        for i in range(2):
+            if t > 1:
+                self.add(self.acc.at[self.blocks[t - 1][i]], t - 1, i)
+            pl.when(self.sends[t - 1][i])(self.two[t - 1][i].start)
 
     def over_feat(self):
-        for c in self.two:
-            c.wait_recv()
-
-        def one(p, none):
-            total = self.acc[self.s, p].astype(f32)
-            for k in range(len(self.two)):
-                total = total + self.land[k, p].astype(f32)
-            self.total[p] = total.astype(bf16)
-            return none
-
-        lax.fori_loop(0, self.parts, one, 0)
+        self.total[...] = self.acc[self.s]
+        for i in range(2):
+            self.add(self.total, self.seqs - 1, i)
         self.shares[self.f] = self.total[self.f]
         for c in self.three:
             c.start()
@@ -850,7 +871,10 @@
             c.wait_recv()
 
     def finish(self):
-        for c in self.two + self.three:
+        for sends, copies in zip(self.sends, self.two):
+            for i in range(2):
+                pl.when(sends[i])(copies[i].wait_send)
+        for c in self.three:
             c.wait_send()
 
 
@@ -872,10 +896,10 @@
     dma = pltpu.SemaphoreType.DMA
     return [
         pltpu.VMEM((parts, rows, wide), bf16),
-        pltpu.VMEM((seqs - 1, parts, rows, wide), bf16),
+        pltpu.VMEM((seqs - 1, 2, parts, rows, wide), bf16),
         pltpu.VMEM((parts, rows, wide), bf16),
-        dma((seqs - 1,)),
-        dma((seqs - 1,)),
+        dma((seqs - 1, 2)),
+        dma((seqs - 1, 2)),
         dma((3,)),
         dma((3,)),
     ]
@@ -1517,19 +1541,24 @@
     begin.wait()
     rows_sum = RowSum(acc_ref, *sum_scratch[:3], sum_scratch[3:half], f, s)
     out_sum = RowSum(oacc_ref, *sum_scratch[half : half + 3], sum_scratch[half + 3 :], f, s)
-    out_sum.start()
+    out_sum.step(1)
     loads.wait()
     term_tiles(term_ref, normed_ref, dqkv_ref)
     sibling = SiblingSum(term_ref, acc_ref, sib_land, (sib_send, sib_recv), d, dps)
     sibling.start()
+    out_sum.step(2)
 
     def over_seq():
         sibling.add()
-        rows_sum.start()
+        rows_sum.step(1)
+        for t in range(3, seqs):
+            out_sum.step(t)
 
     rings = summed_products(
         part, land, f, [(dqkv_ref, w_ref)], s_send, s_recv, land.shape[0], (over_seq,)
     )
+    for t in range(2, seqs):
+        rows_sum.step(t)
     gsum[...] = jnp.zeros_like(gsum)
 
     def finish_rows(rows, grad):

time: 551 us -> 547 us (level)
  no operation moved by 1% of the time
where the time goes in v10:
time: 547 us; the launch traced here: 539 us
  Pallas kernels  410 us (75%)
  matrix products  66.7 us (12%)
  local copies, waits for them, and re-layouts  18.3 us (3%)
  waiting for transfers between devices  17 us (3%)
  between operations  14.7 us (3%)
  other arithmetic  12.1 us (2%)
    pallas_call x1, Pallas kernels, rows_back(): pl.pallas_call(rows_back_kernel, out_shape=(jax.ShapeDtypeStruct((parts,...  84.3 us
    pallas_call x1, Pallas kernels, opening(): pl.pallas_call(functools.partial(opening_kernel, seqs, dps), out_shape=(j...  74.9 us
    pallas_call x1, Pallas kernels, branch_step(): pl.pallas_call(branch_kernel, out_shape=(jax.ShapeDtypeStruct((parts, blo...  72.2 us
    pallas_call x1, Pallas kernels, attention_backward(): pl.pallas_call(functools.partial(backward_kernel, count, heads), out_shap...  71.7 us
    pallas_call x1, Pallas kernels, closing(): pl.pallas_call(functools.partial(closing_kernel, seqs, dps), out_shape=(j...  66.3 us
    dot_general x4, matrix products, dot(): lax.dot_general(a, b, (((1,), (0,)), ((), ())), preferred_element_type=f32)  43.3 us
    pallas_call x1, Pallas kernels, attention_forward(): pl.pallas_call(functools.partial(forward_kernel, count, heads), out_shape...  41 us
    all_gather x1, waiting for transfers between devices, local(): down_w = lax.all_gather(w_down.T, ('seq', 'dp'), axis=0, tiled=True)  15.5 us
  transfers between devices with their start and end apart: 6, of which 1 were waited for; matrix products, arithmetic and copies ran while one was open for 15% of the time, Pallas kernels for 76%

profile of v10, /device:TPU:0, one launch (start us, length us, event | category | flops | bytes accessed | tf_op | source)
XLA Modules:
  0.0 539.5 jit_solution(17451845187437616778)
XLA Ops:
  7.2 0.0 all-gather.6.cloned.1.call-start
  7.2 0.7 all-gather.6.cloned.1.call-update
  7.9 0.0 all-gather.12.cloned.1.call-start
  8.0 74.9 %opening.1 = (bf16[4,256,2048]{2,1,0:T(8,128)(2,1)}, bf16[4,4,2,64,640]{4,3,2,1,0:T(8,128)(2,1)}, f32[4,4,2,8,128]{4,3,2,1,0:T(8,128)}, bf16[4,64,512]{2,1,0:T(8,128)(2,1)}) custom-call(bf16[256,2048]{1,0:T(8,128)(2,1)} %bitcast.61, bf16[64,256]{1,0:T(8,128)(2,1)} %query_ref.1, bf16[64,256]{1,0:T(8,128)(2,1)} %key_ref.1, bf16[64,2048]{1,0:T(8,128)(2,1)} %value_ref.1, ...), custom_call_target="tpu_custom_call" | custom-call | bytes 1048576 | tf_op jit(solution)/shard_map/opening/pallas_call | solution.py:1067
  82.9 0.9 slice_bitcast_fusion.2
  83.8 0.1 slice_reduce_fusion
  83.9 0.1 mul.53
  84.0 3.3 fusion
  87.3 0.2 copy-done
  87.5 1.0 fusion.2.normed_hbm
  88.5 2.0 copy-done.1
  90.5 4.5 convolution_convert_fusion.2
  95.0 0.0 all-gather.8.cloned.1.call-start
  95.1 0.7 all-gather.8.cloned.1.call-update
  95.8 0.0 all-gather.10.cloned.1.call-start
  95.8 1.1 copy.35
  97.0 0.0 reduce-scatter.3.cloned.1.call-start
  97.0 0.6 fusion.6
  97.6 1.0 copy.37.segc_ref
  98.7 0.7 slice.30.gain_ref
  99.3 41.0 %attention_forward.1 = (bf16[4,256,512]{2,1,0:T(8,128)(2,1)}, f32[4,256,512]{2,1,0:T(8,128)}, bf16[4,4,160,128]{3,2,1,0:T(8,128)(2,1)}, f32[4,8,256]{2,1,0:T(8,128)}, bf16[4,256,2048]{2,1,0:T(8,128)(2,1)}) custom-call(bf16[4,256,640]{2,1,0:T(8,128)(2,1)} %bitcast.66, f32[4,256,1]{2,1,0:T(8,128)} %copy.37.segc_ref, f32[4,1,256]{2,1,0:T(1,128)} %get-tuple-element.112.segr_ref, ...), custom_call_target="tpu_custom_call" | custom-call | bytes 1048576 | tf_op jit(solution)/shard_map/attention_forward/pallas_call | solution.py:541
  140.4 0.0 all-gather.12.cloned.1.call-done
  140.4 72.2 %branch_step.1 = (bf16[4,256,2048]{2,1,0:T(8,128)(2,1)}, f32[256,2048]{1,0:T(8,128)}) custom-call(bf16[4,256,512]{2,1,0:T(8,128)(2,1)} %get-tuple-element.51.att_hbm, bf16[8,4,64,512]{3,2,1,0:T(8,128)(2,1)} %bitcast.64, bf16[256,2048]{1,0:T(8,128)(2,1)} %bitcast.62, f32[1,2048]{1,0:T(1,128)} %slice.30.gain_ref), custom_call_target="tpu_custom_call" | custom-call | bytes 1048576 | tf_op jit(solution)/shard_map/branch_step/pallas_call | solution.py:1289
  212.6 11.8 %fusion.7 = f32[1024,1408]{1,0:T(8,128)} fusion(bf16[1024,2048]{1,0:T(8,128)(2,1)} %bitcast.83, bf16[2048,1408]{1,0:T(8,128)(2,1)} %all-gather.6.cloned.1.call-done.wg_hbm), kind=kOutput, calls=%fused_computation.30 | convolution fusion | flops 5905580032 | bytes 15728640 | tf_op jit(solution)/shard_map/dot_general | solution.py:24
  224.4 12.9 %multiply_convert_fusion.2 = (bf16[1024,1408]{1,0:T(8,128)(2,1)S(1)}, f32[1024,1408]{1,0:T(8,128)}) fusion(f32[1024,1408]{1,0:T(8,128)} %fusion.7, bf16[1024,2048]{1,0:T(8,128)(2,1)} %bitcast.84, bf16[2048,1408]{1,0:T(8,128)(2,1)} %all-gather.8.cloned.1.call-done.wu_hbm), kind=kOutput, calls=%fused_computation.10 | convolution fusion | flops 5914230784 | bytes 24379392 | tf_op jit(solution)/shard_map/dot_general | solution.py:24
  237.3 8.2 %convolution_convert_fusion.1 = bf16[2048,1408]{0,1:T(8,128)(2,1)} fusion(bf16[1024,2048]{1,0:T(8,128)(2,1)S(1)} %bitcast.82, bf16[1024,1408]{1,0:T(8,128)(2,1)S(1)} %get-tuple-element.64), kind=kOutput, calls=%fused_computation.6 | convolution fusion | flops 5908463616 | bytes 12845056 | tf_op jit(solution)/shard_map/dot_general | solution.py:32
  245.5 0.0 reduce-scatter.5.cloned.1.call-start
  245.5 15.5 %all-gather.10.cloned.1.call-done.wd_hbm = bf16[2048,1408]{1,0:T(8,128)(2,1)} async-done(((bf16[256,1408]{1,0:T(8,128)(2,1)}), bf16[2048,1408]{1,0:T(8,128)(2,1)}) %all-gather.10.cloned.1.call-update) | async-done | bytes 5767184 | tf_op jit(solution)/shard_map/all_gather | solution.py:1718
  261.1 14.1 %fusion.5 = (bf16[1,1024,1408]{2,1,0:T(8,128)(2,1)S(1)}, bf16[1,1024,1408]{2,1,0:T(8,128)(2,1)S(1)}) fusion(f32[1024,1408]{1,0:T(8,128)} %fusion.7, f32[1024,1408]{1,0:T(8,128)} %get-tuple-element.115, bf16[1024,2048]{1,0:T(8,128)(2,1)} %bitcast.81, bf16[2048,1408]{1,0:T(8,128)(2,1)} %all-gather.10.cloned.1.call-done.wd_hbm), kind=kOutput, calls=%fused_computation.14 | convolution fusion | flops 5924323328 | bytes 27262976 | tf_op jit(solution)/shard_map/dot_general | solution.py:24
  275.2 3.4 pad_maximum_fusion
  278.6 0.5 copy-done.12
  279.1 15.3 %convolution_convert_fusion = bf16[2,1408,2048]{2,1,0:T(8,128)(2,1)} fusion(bf16[1024,2048,1]{1,0,2:T(8,128)(2,1)S(1)} %bitcast.85, bf16[1,1024,1408]{2,1,0:T(8,128)(2,1)S(1)} %get-tuple-element.106, bf16[1,1024,1408]{2,1,0:T(8,128)(2,1)S(1)} %get-tuple-element.105), kind=kOutput, calls=%fused_computation | convolution fusion | flops 11819810816 | bytes 21495808 | tf_op jit(solution)/shard_map/xtf,td->xfd/dot_general | solution.py:1742
  294.4 0.7 slice.31.gain_ref
  295.1 84.3 %rows_back.1 = (bf16[4,256,2048]{2,1,0:T(8,128)(2,1)}, f32[256,2048]{1,0:T(8,128)}, f32[1,2048]{1,0:T(1,128)}, bf16[4,256,2048]{2,1,0:T(8,128)(2,1)}, f32[4,256,512]{2,1,0:T(8,128)}) custom-call(bf16[2,4,256,1408]{3,2,1,0:T(8,128)(2,1)} %bitcast.59, bf16[2048,1408]{1,0:T(8,128)(2,1)} %all-gather.6.cloned.1.call-done.wg_hbm, ...), custom_call_target="tpu_custom_call" | custom-call | bytes 1048576 | tf_op jit(solution)/shard_map/rows_back/pallas_call | solution.py:1434
  379.4 71.7 %attention_backward.1 = (bf16[4,256,640]{2,1,0:T(8,128)(2,1)}, bf16[256,2048]{1,0:T(8,128)(2,1)}, bf16[4,4,64,512]{3,2,1,0:T(8,128)(2,1)}) custom-call(bf16[4,256,640]{2,1,0:T(8,128)(2,1)} %bitcast.67, f32[4,256,1]{2,1,0:T(8,128)} %copy.37.segc_ref, f32[4,1,256]{2,1,0:T(1,128)} %get-tuple-element.112.segr_ref, bf16[4,64,256]{2,1,0:T(8,128)(2,1)} %constant.25.clone.left_ref, ...), custom_call_target="tpu_custom_call" | custom-call | bytes 1048576 | tf_op jit(solution)/shard_map/attention_backward/pallas_call | solution.py:585
  451.1 2.3 convert_bitcast_fusion.2.down_hbm
  453.4 66.3 %closing.1 = (f32[256,2048]{1,0:T(8,128)}, f32[8,128]{1,0:T(8,128)}, f32[64,256]{1,0:T(8,128)}, f32[64,256]{1,0:T(8,128)}, f32[64,2048]{1,0:T(8,128)}, /*index=5*/f32[64,2048]{1,0:T(8,128)}) custom-call(bf16[4,256,640]{2,1,0:T(8,128)(2,1)} %get-tuple-element.69.dqkv_hbm, bf16[2048,640]{1,0:T(8,128)(2,1)} %bitcast.72, bf16[256,2048]{1,0:T(8,128)(2,1)} %bitcast.63, ...), custom_call_target="tpu_custom_call" | custom-call | bytes 1048576 | tf_op jit(solution)/shard_map/closing/pallas_call | solution.py:1644
  519.7 0.8 constant_dynamic-slice_fusion
  520.5 0.5 slice_bitcast_fusion.3
  521.0 1.5 convert_bitcast_fusion
  522.5 1.5 copy.39
  524.1 1.5 copy.38
  525.6 2.4 copy.48
  528.0 1.3 copy.49
  529.3 0.6 copy.50
  530.0 0.6 copy.51
  530.6 0.8 copy.52
  531.4 0.8 copy.53
  (32 shorter events, 0.1 us)
Async XLA Ops:
  7.2 87.8 %all-gather.6.cloned.1.call-start = ((), (), s32[]{:S(2)}) async-start(), calls=%async_computation.2 | async-start | bytes 6488064 | tf_op jit(solution)/shard_map/all_gather | solution.py:1707
  7.9 132.5 %all-gather.12.cloned.1.call-start = ((), (), s32[]{:S(2)}) async-start(), calls=%async_computation.7 | async-start | bytes 2359296 | tf_op jit(solution)/shard_map/all_gather | solution.py:1716
  84.0 3.5 copy-start
  87.5 3.0 copy-start.3
  88.5 2.0 copy-start.1
  90.5 5.3 copy-start.5
  90.5 6.5 %copy-start.10 = (s32[4,1,256]{2,1,0:T(1,128)S(1)}, s32[4,1,256]{2,1,0:T(1,128)}, u32[]{:S(2)}) copy-start(s32[4,1,256]{2,1,0:T(1,128)} %param.16) | copy-start | bytes 12292
  95.0 129.4 %all-gather.8.cloned.1.call-start = ((), (), s32[]{:S(2)}) async-start(), calls=%async_computation.3 | async-start | bytes 6488064 | tf_op jit(solution)/shard_map/all_gather | solution.py:1717
  95.8 165.3 %all-gather.10.cloned.1.call-start = ((), (), s32[]{:S(2)}) async-start(), calls=%async_computation.4 | async-start | bytes 6488064 | tf_op jit(solution)/shard_map/all_gather | solution.py:1718
  97.0 354.1 %reduce-scatter.3.cloned.1.call-start = ((), (), s32[]{:S(2)}) async-start(), calls=%async_computation.5 | async-start | bytes 6488064 | tf_op jit(solution)/shard_map/reduce_scatter | solution.py:1740
  224.4 12.9 %copy-start.11 = (bf16[4,256,2048]{2,1,0:T(8,128)(2,1)S(1)}, bf16[4,256,2048]{2,1,0:T(8,128)(2,1)}, u32[]{:S(2)}) copy-start(bf16[4,256,2048]{2,1,0:T(8,128)(2,1)} %get-tuple-element.59) | copy-start | bytes 12582916
  237.3 8.2 %copy-start.2 = (bf16[1024,1408]{1,0:T(8,128)(2,1)}, bf16[1024,1408]{1,0:T(8,128)(2,1)S(1)}, u32[]{:S(2)}) copy-start(bf16[1024,1408]{1,0:T(8,128)(2,1)S(1)} %get-tuple-element.64) | copy-start | bytes 8650756
  245.5 275.5 %reduce-scatter.5.cloned.1.call-start = ((), (), s32[]{:S(2)}) async-start(), calls=%async_computation.6 | async-start | bytes 12976128 | tf_op jit(solution)/shard_map/reduce_scatter | solution.py:1740
  275.2 3.9 copy-start.12
  524.1 4.0 copy-start.4
  525.6 3.7 copy-start.9
  525.6 4.4 copy-start.8
  525.6 5.0 copy-start.7
  525.6 5.8 %copy-start.6 = (f32[64,2048]{1,0:T(8,128)S(1)}, f32[64,2048]{1,0:T(8,128)}, u32[]{:S(2)}) copy-start(f32[64,2048]{1,0:T(8,128)} %get-tuple-element.79) | copy-start | bytes 1572868
Sparse Core Ops, SparseCore 0:
  9.7 84.0 all-gather.5
  95.4 39.3 all-gather.11
  136.5 63.3 all-gather.7
  201.9 59.1 all-gather.9
  263.2 63.5 reduce-scatter.2
  328.9 133.3 reduce-scatter.4

commit v11 on v10

--- a/solution.py
+++ b/solution.py
@@ -496,7 +496,7 @@
     ring.arrive()
 
     def add_up(rows, total):
-        final_ref[rows, :] = (res_ref[rows, :] + total).astype(bf16)
+        final_ref[rows, :] = res_ref[rows, :] + total
 
     by_rows(ring, add_up)
     ring.finish()
@@ -586,7 +586,7 @@
         functools.partial(backward_kernel, count, heads),
         out_shape=(
             jax.ShapeDtypeStruct((groups, block, wide), bf16),
-            jax.ShapeDtypeStruct(residual.shape, bf16),
+            jax.ShapeDtypeStruct(residual.shape, f32),
             jax.ShapeDtypeStruct((count, by_row[0]) + by_row[3:], bf16),
         ),
         in_specs=in_place(1)
@@ -1480,6 +1480,7 @@
     normed_hbm,
     oacc_hbm,
     down_hbm,
+    output_hbm,
     x_ref,
     tile_ref,
     query_ref,
@@ -1631,7 +1632,7 @@
         c.wait_send()
 
 
-def closing(dqkv, qkv_w, own, grad_residual, gain_one, gain_two_sum, normed, out_acc, down_grad):
+def closing(dqkv, qkv_w, own, grad_residual, gain_one, gain_two_sum, normed, out_acc, down_grad, output):
     parts, seqs, dps = (lax.axis_size(a) for a in ALL)
     block, width = own.shape
     others = max(dps - 1, 1)
@@ -1651,7 +1652,7 @@
             jax.ShapeDtypeStruct((rows_each, HEADS * HV), f32),
             jax.ShapeDtypeStruct((rows_each, HEADS * HV), f32),
         ),
-        in_specs=in_place(4) + whole_vmem(2) + in_place(3),
+        in_specs=in_place(4) + whole_vmem(2) + in_place(4),
         out_specs=tuple(whole_vmem(6)),
         scratch_shapes=square_scratch(parts, block, width)
         + [
@@ -1675,7 +1676,7 @@
         ),
         cost_estimate=pl.CostEstimate(flops=0, bytes_accessed=1 << 20, transcendentals=0),
         name="closing",
-    )(dqkv, qkv_w, own, grad_residual, gain_one, gain_two_sum, normed, out_acc, down_grad)
+    )(dqkv, qkv_w, own, grad_residual, gain_one, gain_two_sum, normed, out_acc, down_grad, output)
 
 
 def local(
@@ -1770,6 +1771,7 @@
         branch_all,
         heads,
     )
+    output = output.astype(bf16)
     down_grad = down_sum.T.astype(f32)
     x_grad, gain_grads, query_grad, key_grad, value_grad, out_grad = closing(
         dqkv,
@@ -1781,6 +1783,7 @@
         normed.reshape(parts, block, width),
         out_acc,
         down_grad,
+        output,
     )
     gain_each = gain_grads.shape[1] // lax.axis_size("dp")
     gain_grads = lax.dynamic_slice_in_dim(

time: 547 us -> 546 us (level)
    unnamed x34 -> x35, local copies, waits for them, and re-layouts: 12.4 us -> 10.5 us
  transfers between devices with their start and end apart: 6 -> 6, of which waited for: 1 -> 1; matrix products, arithmetic and copies ran while one was open for 15% -> 16% of each run, Pallas kernels for 76% -> 76%
where the time goes in v11:
time: 546 us; the launch traced here: 539 us
  Pallas kernels  408 us (75%)
  matrix products  66.7 us (12%)
  waiting for transfers between devices  17 us (3%)
  local copies, waits for them, and re-layouts  16.4 us (3%)
  other arithmetic  16.1 us (3%)
  between operations  14.8 us (3%)
    pallas_call x1, Pallas kernels, rows_back(): pl.pallas_call(rows_back_kernel, out_shape=(jax.ShapeDtypeStruct((parts,...  84.2 us
    pallas_call x1, Pallas kernels, opening(): pl.pallas_call(functools.partial(opening_kernel, seqs, dps), out_shape=(j...  74.9 us
    pallas_call x1, Pallas kernels, branch_step(): pl.pallas_call(branch_kernel, out_shape=(jax.ShapeDtypeStruct((parts, blo...  72.2 us
    pallas_call x1, Pallas kernels, attention_backward(): pl.pallas_call(functools.partial(backward_kernel, count, heads), out_shap...  72 us
    pallas_call x1, Pallas kernels, closing(): pl.pallas_call(functools.partial(closing_kernel, seqs, dps), out_shape=(j...  63.4 us
    dot_general x4, matrix products, dot(): lax.dot_general(a, b, (((1,), (0,)), ((), ())), preferred_element_type=f32)  43.3 us
    pallas_call x1, Pallas kernels, attention_forward(): pl.pallas_call(functools.partial(forward_kernel, count, heads), out_shape...  41 us
    all_gather x1, waiting for transfers between devices, local(): down_w = lax.all_gather(w_down.T, ('seq', 'dp'), axis=0, tiled=True)  15.5 us
  transfers between devices with their start and end apart: 6, of which 1 were waited for; matrix products, arithmetic and copies ran while one was open for 16% of the time, Pallas kernels for 76%

profile of v11, /device:TPU:0, one launch (start us, length us, event | category | flops | bytes accessed | tf_op | source)
XLA Modules:
  0.0 539.0 jit_solution(4848329248449237061)
XLA Ops:
  7.2 0.7 all-gather.6.cloned.1.call-update
  7.9 0.0 all-gather.12.cloned.1.call-start
  8.0 74.9 %opening.1 = (bf16[4,256,2048]{2,1,0:T(8,128)(2,1)}, bf16[4,4,2,64,640]{4,3,2,1,0:T(8,128)(2,1)}, f32[4,4,2,8,128]{4,3,2,1,0:T(8,128)}, bf16[4,64,512]{2,1,0:T(8,128)(2,1)}) custom-call(bf16[256,2048]{1,0:T(8,128)(2,1)} %bitcast.62, bf16[64,256]{1,0:T(8,128)(2,1)} %query_ref.1, bf16[64,256]{1,0:T(8,128)(2,1)} %key_ref.1, bf16[64,2048]{1,0:T(8,128)(2,1)} %value_ref.1, ...), custom_call_target="tpu_custom_call" | custom-call | bytes 1048576 | tf_op jit(solution)/shard_map/opening/pallas_call | solution.py:1067
  82.9 0.9 slice_bitcast_fusion.2
  83.8 0.1 slice_reduce_fusion
  83.9 0.1 mul.53
  84.0 3.3 fusion
  87.3 0.2 copy-done.1
  87.5 1.0 fusion.2.normed_hbm
  88.5 2.0 copy-done
  90.5 4.5 convolution_convert_fusion.2
  95.0 0.0 all-gather.8.cloned.1.call-start
  95.1 0.7 all-gather.8.cloned.1.call-update
  95.8 0.0 all-gather.10.cloned.1.call-start
  95.8 1.1 copy.35
  97.0 0.0 reduce-scatter.3.cloned.1.call-start
  97.0 0.6 fusion.6
  97.6 1.0 copy.37.segc_ref
  98.7 0.7 slice.30.gain_ref
  99.3 41.0 %attention_forward.1 = (bf16[4,256,512]{2,1,0:T(8,128)(2,1)}, f32[4,256,512]{2,1,0:T(8,128)}, bf16[4,4,160,128]{3,2,1,0:T(8,128)(2,1)}, f32[4,8,256]{2,1,0:T(8,128)}, bf16[4,256,2048]{2,1,0:T(8,128)(2,1)}) custom-call(bf16[4,256,640]{2,1,0:T(8,128)(2,1)} %bitcast.67, f32[4,256,1]{2,1,0:T(8,128)} %copy.37.segc_ref, f32[4,1,256]{2,1,0:T(1,128)} %get-tuple-element.112.segr_ref, ...), custom_call_target="tpu_custom_call" | custom-call | bytes 1048576 | tf_op jit(solution)/shard_map/attention_forward/pallas_call | solution.py:541
  140.4 72.2 %branch_step.1 = (bf16[4,256,2048]{2,1,0:T(8,128)(2,1)}, f32[256,2048]{1,0:T(8,128)}) custom-call(bf16[4,256,512]{2,1,0:T(8,128)(2,1)} %get-tuple-element.51.att_hbm, bf16[8,4,64,512]{3,2,1,0:T(8,128)(2,1)} %bitcast.65, bf16[256,2048]{1,0:T(8,128)(2,1)} %bitcast.63, f32[1,2048]{1,0:T(1,128)} %slice.30.gain_ref), custom_call_target="tpu_custom_call" | custom-call | bytes 1048576 | tf_op jit(solution)/shard_map/branch_step/pallas_call | solution.py:1289
  212.6 11.8 %fusion.7 = f32[1024,1408]{1,0:T(8,128)} fusion(bf16[1024,2048]{1,0:T(8,128)(2,1)} %bitcast.83, bf16[2048,1408]{1,0:T(8,128)(2,1)} %all-gather.6.cloned.1.call-done.wg_hbm), kind=kOutput, calls=%fused_computation.30 | convolution fusion | flops 5905580032 | bytes 15728640 | tf_op jit(solution)/shard_map/dot_general | solution.py:24
  224.4 12.9 %multiply_convert_fusion.2 = (bf16[1024,1408]{1,0:T(8,128)(2,1)S(1)}, f32[1024,1408]{1,0:T(8,128)}) fusion(f32[1024,1408]{1,0:T(8,128)} %fusion.7, bf16[1024,2048]{1,0:T(8,128)(2,1)} %bitcast.84, bf16[2048,1408]{1,0:T(8,128)(2,1)} %all-gather.8.cloned.1.call-done.wu_hbm), kind=kOutput, calls=%fused_computation.10 | convolution fusion | flops 5914230784 | bytes 24379392 | tf_op jit(solution)/shard_map/dot_general | solution.py:24
  237.3 8.2 %convolution_convert_fusion.1 = bf16[2048,1408]{0,1:T(8,128)(2,1)} fusion(bf16[1024,2048]{1,0:T(8,128)(2,1)S(1)} %bitcast.82, bf16[1024,1408]{1,0:T(8,128)(2,1)S(1)} %get-tuple-element.64), kind=kOutput, calls=%fused_computation.6 | convolution fusion | flops 5908463616 | bytes 12845056 | tf_op jit(solution)/shard_map/dot_general | solution.py:32
  245.5 0.0 reduce-scatter.5.cloned.1.call-start
  245.5 15.5 %all-gather.10.cloned.1.call-done.wd_hbm = bf16[2048,1408]{1,0:T(8,128)(2,1)} async-done(((bf16[256,1408]{1,0:T(8,128)(2,1)}), bf16[2048,1408]{1,0:T(8,128)(2,1)}) %all-gather.10.cloned.1.call-update) | async-done | bytes 5767184 | tf_op jit(solution)/shard_map/all_gather | solution.py:1719
  261.0 14.1 %fusion.5 = (bf16[1,1024,1408]{2,1,0:T(8,128)(2,1)S(1)}, bf16[1,1024,1408]{2,1,0:T(8,128)(2,1)S(1)}) fusion(f32[1024,1408]{1,0:T(8,128)} %fusion.7, f32[1024,1408]{1,0:T(8,128)} %get-tuple-element.115, bf16[1024,2048]{1,0:T(8,128)(2,1)} %bitcast.81, bf16[2048,1408]{1,0:T(8,128)(2,1)} %all-gather.10.cloned.1.call-done.wd_hbm), kind=kOutput, calls=%fused_computation.14 | convolution fusion | flops 5924323328 | bytes 27262976 | tf_op jit(solution)/shard_map/dot_general | solution.py:24
  275.2 3.4 pad_maximum_fusion
  278.6 0.5 copy-done.13
  279.1 15.3 %convolution_convert_fusion = bf16[2,1408,2048]{2,1,0:T(8,128)(2,1)} fusion(bf16[1024,2048,1]{1,0,2:T(8,128)(2,1)S(1)} %bitcast.85, bf16[1,1024,1408]{2,1,0:T(8,128)(2,1)S(1)} %get-tuple-element.106, bf16[1,1024,1408]{2,1,0:T(8,128)(2,1)S(1)} %get-tuple-element.105), kind=kOutput, calls=%fused_computation | convolution fusion | flops 11819810816 | bytes 21495808 | tf_op jit(solution)/shard_map/xtf,td->xfd/dot_general | solution.py:1743
  294.4 0.7 slice.31.gain_ref
  295.1 84.2 %rows_back.1 = (bf16[4,256,2048]{2,1,0:T(8,128)(2,1)}, f32[256,2048]{1,0:T(8,128)}, f32[1,2048]{1,0:T(1,128)}, bf16[4,256,2048]{2,1,0:T(8,128)(2,1)}, f32[4,256,512]{2,1,0:T(8,128)}) custom-call(bf16[2,4,256,1408]{3,2,1,0:T(8,128)(2,1)} %bitcast.60, bf16[2048,1408]{1,0:T(8,128)(2,1)} %all-gather.6.cloned.1.call-done.wg_hbm, ...), custom_call_target="tpu_custom_call" | custom-call | bytes 1048576 | tf_op jit(solution)/shard_map/rows_back/pallas_call | solution.py:1434
  379.3 72.0 %attention_backward.1 = (bf16[4,256,640]{2,1,0:T(8,128)(2,1)}, f32[256,2048]{1,0:T(8,128)}, bf16[4,4,64,512]{3,2,1,0:T(8,128)(2,1)}) custom-call(bf16[4,256,640]{2,1,0:T(8,128)(2,1)} %bitcast.68, f32[4,256,1]{2,1,0:T(8,128)} %copy.37.segc_ref, f32[4,1,256]{2,1,0:T(1,128)} %get-tuple-element.112.segr_ref, bf16[4,64,256]{2,1,0:T(8,128)(2,1)} %constant.25.clone.left_ref, ...), custom_call_target="tpu_custom_call" | custom-call | bytes 1048576 | tf_op jit(solution)/shard_map/attention_backward/pallas_call | solution.py:585
  451.4 2.9 convert_element_type.72.output_hbm
  454.2 1.1 convert_bitcast_fusion.4
  455.4 2.3 convert_bitcast_fusion.2.down_hbm
  457.7 63.4 %closing.1 = (f32[256,2048]{1,0:T(8,128)}, f32[8,128]{1,0:T(8,128)}, f32[64,256]{1,0:T(8,128)}, f32[64,256]{1,0:T(8,128)}, f32[64,2048]{1,0:T(8,128)}, /*index=5*/f32[64,2048]{1,0:T(8,128)}) custom-call(bf16[4,256,640]{2,1,0:T(8,128)(2,1)} %get-tuple-element.69.dqkv_hbm, bf16[2048,640]{1,0:T(8,128)(2,1)} %bitcast.73, bf16[256,2048]{1,0:T(8,128)(2,1)} %bitcast.64, ...), custom_call_target="tpu_custom_call" | custom-call | bytes 1048576 | tf_op jit(solution)/shard_map/closing/pallas_call | solution.py:1645
  521.1 0.8 constant_dynamic-slice_fusion
  521.9 0.5 slice_bitcast_fusion.3
  522.4 1.5 convert_bitcast_fusion
  523.9 1.5 copy.39
  525.5 1.5 copy.38
  527.0 0.5 copy-done.5
  527.5 1.3 copy.47
  528.8 0.6 copy.48
  529.4 0.6 copy.49
  530.1 0.8 copy.50
  530.9 0.8 copy.51
  (35 shorter events, 0.2 us)
Async XLA Ops:
  7.2 87.8 %all-gather.6.cloned.1.call-start = ((), (), s32[]{:S(2)}) async-start(), calls=%async_computation.2 | async-start | bytes 6488064 | tf_op jit(solution)/shard_map/all_gather | solution.py:1708
  7.9 132.5 %all-gather.12.cloned.1.call-start = ((), (), s32[]{:S(2)}) async-start(), calls=%async_computation.7 | async-start | bytes 2359296 | tf_op jit(solution)/shard_map/all_gather | solution.py:1717
  84.0 3.5 copy-start.1
  87.5 3.0 copy-start.4
  88.5 2.0 copy-start
  90.5 5.3 copy-start.6
  90.5 6.5 %copy-start.11 = (s32[4,1,256]{2,1,0:T(1,128)S(1)}, s32[4,1,256]{2,1,0:T(1,128)}, u32[]{:S(2)}) copy-start(s32[4,1,256]{2,1,0:T(1,128)} %param.16) | copy-start | bytes 12292
  95.0 129.4 %all-gather.8.cloned.1.call-start = ((), (), s32[]{:S(2)}) async-start(), calls=%async_computation.3 | async-start | bytes 6488064 | tf_op jit(solution)/shard_map/all_gather | solution.py:1718
  95.8 165.3 %all-gather.10.cloned.1.call-start = ((), (), s32[]{:S(2)}) async-start(), calls=%async_computation.4 | async-start | bytes 6488064 | tf_op jit(solution)/shard_map/all_gather | solution.py:1719
  97.0 358.4 %reduce-scatter.3.cloned.1.call-start = ((), (), s32[]{:S(2)}) async-start(), calls=%async_computation.5 | async-start | bytes 6488064 | tf_op jit(solution)/shard_map/reduce_scatter | solution.py:1741
  224.4 12.9 %copy-start.12 = (bf16[4,256,2048]{2,1,0:T(8,128)(2,1)S(1)}, bf16[4,256,2048]{2,1,0:T(8,128)(2,1)}, u32[]{:S(2)}) copy-start(bf16[4,256,2048]{2,1,0:T(8,128)(2,1)} %get-tuple-element.59) | copy-start | bytes 12582916
  237.3 8.2 %copy-start.3 = (bf16[1024,1408]{1,0:T(8,128)(2,1)}, bf16[1024,1408]{1,0:T(8,128)(2,1)S(1)}, u32[]{:S(2)}) copy-start(bf16[1024,1408]{1,0:T(8,128)(2,1)S(1)} %get-tuple-element.64) | copy-start | bytes 8650756
  245.5 276.9 %reduce-scatter.5.cloned.1.call-start = ((), (), s32[]{:S(2)}) async-start(), calls=%async_computation.6 | async-start | bytes 12976128 | tf_op jit(solution)/shard_map/reduce_scatter | solution.py:1741
  275.2 3.9 copy-start.13
  451.4 2.9 copy-start.2
  525.5 2.0 copy-start.5
  527.0 1.8 copy-start.10
  527.0 2.4 copy-start.9
  527.0 3.1 copy-start.8
  527.0 3.9 copy-start.7
Sparse Core Ops, SparseCore 0:
  9.7 84.0 all-gather.5
  95.4 39.3 all-gather.11
  136.5 63.3 all-gather.7
  201.9 59.1 all-gather.9
  263.2 63.5 reduce-scatter.2
  328.9 132.3 reduce-scatter.4

commit v12 on v11

--- a/solution.py
+++ b/solution.py
@@ -1269,7 +1269,7 @@
         c.wait()
 
 
-CHUNKS = 2
+CHUNKS = 4
 
 
 def square_scratch(parts, block, width, chunks=CHUNKS):

time: 546 us -> 546 us (level)
  no operation moved by 1% of the time
where the time goes in v12:
time: 546 us; the launch traced here: 538 us
  Pallas kernels  408 us (75%)
  matrix products  66.5 us (12%)
  local copies, waits for them, and re-layouts  16.3 us (3%)
  waiting for transfers between devices  16.1 us (3%)
  other arithmetic  16.1 us (3%)
  between operations  14.5 us (3%)
    pallas_call x1, Pallas kernels, rows_back(): pl.pallas_call(rows_back_kernel, out_shape=(jax.ShapeDtypeStruct((parts,...  84.7 us
    pallas_call x1, Pallas kernels, opening(): pl.pallas_call(functools.partial(opening_kernel, seqs, dps), out_shape=(j...  74.9 us
    pallas_call x1, Pallas kernels, branch_step(): pl.pallas_call(branch_kernel, out_shape=(jax.ShapeDtypeStruct((parts, blo...  72.7 us
    pallas_call x1, Pallas kernels, attention_backward(): pl.pallas_call(functools.partial(backward_kernel, count, heads), out_shap...  72.3 us
    pallas_call x1, Pallas kernels, closing(): pl.pallas_call(functools.partial(closing_kernel, seqs, dps), out_shape=(j...  62.4 us
    dot_general x4, matrix products, dot(): lax.dot_general(a, b, (((1,), (0,)), ((), ())), preferred_element_type=f32)  43.1 us
    pallas_call x1, Pallas kernels, attention_forward(): pl.pallas_call(functools.partial(forward_kernel, count, heads), out_shape...  41 us
    dot_general x1, matrix products, local(): jnp.einsum('xtf,td->xfd', grads, rows_all, preferred_element_type=f32)  15.2 us
  transfers between devices with their start and end apart: 6, of which 1 were waited for; matrix products, arithmetic and copies ran while one was open for 16% of the time, Pallas kernels for 76%

profile of v12, /device:TPU:0, one launch (start us, length us, event | category | flops | bytes accessed | tf_op | source)
XLA Modules:
  0.0 538.2 jit_solution(1283626409410747076)
XLA Ops:
  7.2 0.7 all-gather.6.cloned.1.call-update
  7.9 0.0 all-gather.12.cloned.1.call-start
  8.0 74.9 %opening.1 = (bf16[4,256,2048]{2,1,0:T(8,128)(2,1)}, bf16[4,4,2,64,640]{4,3,2,1,0:T(8,128)(2,1)}, f32[4,4,2,8,128]{4,3,2,1,0:T(8,128)}, bf16[4,64,512]{2,1,0:T(8,128)(2,1)}) custom-call(bf16[256,2048]{1,0:T(8,128)(2,1)} %bitcast.62, bf16[64,256]{1,0:T(8,128)(2,1)} %query_ref.1, bf16[64,256]{1,0:T(8,128)(2,1)} %key_ref.1, bf16[64,2048]{1,0:T(8,128)(2,1)} %value_ref.1, ...), custom_call_target="tpu_custom_call" | custom-call | bytes 1048576 | tf_op jit(solution)/shard_map/opening/pallas_call | solution.py:1067
  82.9 0.9 slice_bitcast_fusion.2
  83.8 0.1 slice_reduce_fusion
  83.9 0.1 mul.53
  84.0 3.3 fusion
  87.3 0.2 copy-done.1
  87.5 1.0 fusion.2.normed_hbm
  88.5 2.0 copy-done
  90.5 4.5 convolution_convert_fusion.2
  95.0 0.0 all-gather.8.cloned.1.call-start
  95.1 0.7 all-gather.8.cloned.1.call-update
  95.8 0.0 all-gather.10.cloned.1.call-start
  95.8 1.1 copy.35
  97.0 0.0 reduce-scatter.3.cloned.1.call-start
  97.0 0.6 fusion.6
  97.6 1.0 copy.37.segc_ref
  98.7 0.7 slice.30.gain_ref
  99.4 41.0 %attention_forward.1 = (bf16[4,256,512]{2,1,0:T(8,128)(2,1)}, f32[4,256,512]{2,1,0:T(8,128)}, bf16[4,4,160,128]{3,2,1,0:T(8,128)(2,1)}, f32[4,8,256]{2,1,0:T(8,128)}, bf16[4,256,2048]{2,1,0:T(8,128)(2,1)}) custom-call(bf16[4,256,640]{2,1,0:T(8,128)(2,1)} %bitcast.67, f32[4,256,1]{2,1,0:T(8,128)} %copy.37.segc_ref, f32[4,1,256]{2,1,0:T(1,128)} %get-tuple-element.112.segr_ref, ...), custom_call_target="tpu_custom_call" | custom-call | bytes 1048576 | tf_op jit(solution)/shard_map/attention_forward/pallas_call | solution.py:541
  140.4 72.7 %branch_step.1 = (bf16[4,256,2048]{2,1,0:T(8,128)(2,1)}, f32[256,2048]{1,0:T(8,128)}) custom-call(bf16[4,256,512]{2,1,0:T(8,128)(2,1)} %get-tuple-element.51.att_hbm, bf16[8,4,64,512]{3,2,1,0:T(8,128)(2,1)} %bitcast.65, bf16[256,2048]{1,0:T(8,128)(2,1)} %bitcast.63, f32[1,2048]{1,0:T(1,128)} %slice.30.gain_ref), custom_call_target="tpu_custom_call" | custom-call | bytes 1048576 | tf_op jit(solution)/shard_map/branch_step/pallas_call | solution.py:1289
  213.0 11.8 %fusion.7 = f32[1024,1408]{1,0:T(8,128)} fusion(bf16[1024,2048]{1,0:T(8,128)(2,1)} %bitcast.83, bf16[2048,1408]{1,0:T(8,128)(2,1)} %all-gather.6.cloned.1.call-done.wg_hbm), kind=kOutput, calls=%fused_computation.30 | convolution fusion | flops 5905580032 | bytes 15728640 | tf_op jit(solution)/shard_map/dot_general | solution.py:24
  224.8 12.9 %multiply_convert_fusion.2 = (bf16[1024,1408]{1,0:T(8,128)(2,1)S(1)}, f32[1024,1408]{1,0:T(8,128)}) fusion(f32[1024,1408]{1,0:T(8,128)} %fusion.7, bf16[1024,2048]{1,0:T(8,128)(2,1)} %bitcast.84, bf16[2048,1408]{1,0:T(8,128)(2,1)} %all-gather.8.cloned.1.call-done.wu_hbm), kind=kOutput, calls=%fused_computation.10 | convolution fusion | flops 5914230784 | bytes 24379392 | tf_op jit(solution)/shard_map/dot_general | solution.py:24
  237.7 8.2 %convolution_convert_fusion.1 = bf16[2048,1408]{0,1:T(8,128)(2,1)} fusion(bf16[1024,2048]{1,0:T(8,128)(2,1)S(1)} %bitcast.82, bf16[1024,1408]{1,0:T(8,128)(2,1)S(1)} %get-tuple-element.64), kind=kOutput, calls=%fused_computation.6 | convolution fusion | flops 5908463616 | bytes 12845056 | tf_op jit(solution)/shard_map/dot_general | solution.py:32
  245.9 0.4 reduce-scatter.5.cloned.1.call-start
  246.4 14.7 %all-gather.10.cloned.1.call-done.wd_hbm = bf16[2048,1408]{1,0:T(8,128)(2,1)} async-done(((bf16[256,1408]{1,0:T(8,128)(2,1)}), bf16[2048,1408]{1,0:T(8,128)(2,1)}) %all-gather.10.cloned.1.call-update) | async-done | bytes 5767184 | tf_op jit(solution)/shard_map/all_gather | solution.py:1719
  261.0 14.0 %fusion.5 = (bf16[1,1024,1408]{2,1,0:T(8,128)(2,1)S(1)}, bf16[1,1024,1408]{2,1,0:T(8,128)(2,1)S(1)}) fusion(f32[1024,1408]{1,0:T(8,128)} %fusion.7, f32[1024,1408]{1,0:T(8,128)} %get-tuple-element.115, bf16[1024,2048]{1,0:T(8,128)(2,1)} %bitcast.81, bf16[2048,1408]{1,0:T(8,128)(2,1)} %all-gather.10.cloned.1.call-done.wd_hbm), kind=kOutput, calls=%fused_computation.14 | convolution fusion | flops 5924323328 | bytes 27262976 | tf_op jit(solution)/shard_map/dot_general | solution.py:24
  275.0 3.3 pad_maximum_fusion
  278.3 0.5 copy-done.13
  278.8 15.2 %convolution_convert_fusion = bf16[2,1408,2048]{2,1,0:T(8,128)(2,1)} fusion(bf16[1024,2048,1]{1,0,2:T(8,128)(2,1)S(1)} %bitcast.85, bf16[1,1024,1408]{2,1,0:T(8,128)(2,1)S(1)} %get-tuple-element.106, bf16[1,1024,1408]{2,1,0:T(8,128)(2,1)S(1)} %get-tuple-element.105), kind=kOutput, calls=%fused_computation | convolution fusion | flops 11819810816 | bytes 21495808 | tf_op jit(solution)/shard_map/xtf,td->xfd/dot_general | solution.py:1743
  294.1 0.7 slice.31.gain_ref
  294.8 84.7 %rows_back.1 = (bf16[4,256,2048]{2,1,0:T(8,128)(2,1)}, f32[256,2048]{1,0:T(8,128)}, f32[1,2048]{1,0:T(1,128)}, bf16[4,256,2048]{2,1,0:T(8,128)(2,1)}, f32[4,256,512]{2,1,0:T(8,128)}) custom-call(bf16[2,4,256,1408]{3,2,1,0:T(8,128)(2,1)} %bitcast.60, bf16[2048,1408]{1,0:T(8,128)(2,1)} %all-gather.6.cloned.1.call-done.wg_hbm, ...), custom_call_target="tpu_custom_call" | custom-call | bytes 1048576 | tf_op jit(solution)/shard_map/rows_back/pallas_call | solution.py:1434
  379.5 72.3 %attention_backward.1 = (bf16[4,256,640]{2,1,0:T(8,128)(2,1)}, f32[256,2048]{1,0:T(8,128)}, bf16[4,4,64,512]{3,2,1,0:T(8,128)(2,1)}) custom-call(bf16[4,256,640]{2,1,0:T(8,128)(2,1)} %bitcast.68, f32[4,256,1]{2,1,0:T(8,128)} %copy.37.segc_ref, f32[4,1,256]{2,1,0:T(1,128)} %get-tuple-element.112.segr_ref, bf16[4,64,256]{2,1,0:T(8,128)(2,1)} %constant.25.clone.left_ref, ...), custom_call_target="tpu_custom_call" | custom-call | bytes 1048576 | tf_op jit(solution)/shard_map/attention_backward/pallas_call | solution.py:585
  451.8 2.9 convert_element_type.72.output_hbm
  454.6 1.1 convert_bitcast_fusion.4
  455.8 2.3 convert_bitcast_fusion.2.down_hbm
  458.1 62.4 %closing.1 = (f32[256,2048]{1,0:T(8,128)}, f32[8,128]{1,0:T(8,128)}, f32[64,256]{1,0:T(8,128)}, f32[64,256]{1,0:T(8,128)}, f32[64,2048]{1,0:T(8,128)}, /*index=5*/f32[64,2048]{1,0:T(8,128)}) custom-call(bf16[4,256,640]{2,1,0:T(8,128)(2,1)} %get-tuple-element.69.dqkv_hbm, bf16[2048,640]{1,0:T(8,128)(2,1)} %bitcast.73, bf16[256,2048]{1,0:T(8,128)(2,1)} %bitcast.64, ...), custom_call_target="tpu_custom_call" | custom-call | bytes 1048576 | tf_op jit(solution)/shard_map/closing/pallas_call | solution.py:1645
  520.5 0.8 constant_dynamic-slice_fusion
  521.3 0.5 slice_bitcast_fusion.3
  521.8 1.5 convert_bitcast_fusion
  523.4 1.5 copy.39
  524.9 1.5 copy.38
  526.4 0.5 copy-done.5
  526.9 1.3 copy.47
  528.2 0.6 copy.48
  528.9 0.6 copy.49
  529.5 0.8 copy.50
  530.3 0.8 copy.51
  (35 shorter events, 0.2 us)
Async XLA Ops:
  7.2 87.8 %all-gather.6.cloned.1.call-start = ((), (), s32[]{:S(2)}) async-start(), calls=%async_computation.2 | async-start | bytes 6488064 | tf_op jit(solution)/shard_map/all_gather | solution.py:1708
  7.9 132.5 %all-gather.12.cloned.1.call-start = ((), (), s32[]{:S(2)}) async-start(), calls=%async_computation.7 | async-start | bytes 2359296 | tf_op jit(solution)/shard_map/all_gather | solution.py:1717
  84.0 3.5 copy-start.1
  87.5 3.0 copy-start.4
  88.5 2.0 copy-start
  90.5 5.3 copy-start.6
  90.5 6.5 %copy-start.11 = (s32[4,1,256]{2,1,0:T(1,128)S(1)}, s32[4,1,256]{2,1,0:T(1,128)}, u32[]{:S(2)}) copy-start(s32[4,1,256]{2,1,0:T(1,128)} %param.16) | copy-start | bytes 12292
  95.0 129.8 %all-gather.8.cloned.1.call-start = ((), (), s32[]{:S(2)}) async-start(), calls=%async_computation.3 | async-start | bytes 6488064 | tf_op jit(solution)/shard_map/all_gather | solution.py:1718
  95.8 165.3 %all-gather.10.cloned.1.call-start = ((), (), s32[]{:S(2)}) async-start(), calls=%async_computation.4 | async-start | bytes 6488064 | tf_op jit(solution)/shard_map/all_gather | solution.py:1719
  97.0 358.8 %reduce-scatter.3.cloned.1.call-start = ((), (), s32[]{:S(2)}) async-start(), calls=%async_computation.5 | async-start | bytes 6488064 | tf_op jit(solution)/shard_map/reduce_scatter | solution.py:1741
  224.8 12.9 %copy-start.12 = (bf16[4,256,2048]{2,1,0:T(8,128)(2,1)S(1)}, bf16[4,256,2048]{2,1,0:T(8,128)(2,1)}, u32[]{:S(2)}) copy-start(bf16[4,256,2048]{2,1,0:T(8,128)(2,1)} %get-tuple-element.59) | copy-start | bytes 12582916
  237.7 8.2 %copy-start.3 = (bf16[1024,1408]{1,0:T(8,128)(2,1)}, bf16[1024,1408]{1,0:T(8,128)(2,1)S(1)}, u32[]{:S(2)}) copy-start(bf16[1024,1408]{1,0:T(8,128)(2,1)S(1)} %get-tuple-element.64) | copy-start | bytes 8650756
  245.9 275.9 %reduce-scatter.5.cloned.1.call-start = ((), (), s32[]{:S(2)}) async-start(), calls=%async_computation.6 | async-start | bytes 12976128 | tf_op jit(solution)/shard_map/reduce_scatter | solution.py:1741
  275.0 3.8 copy-start.13
  451.8 2.9 copy-start.2
  524.9 2.0 copy-start.5
  526.4 1.8 copy-start.10
  526.4 2.4 copy-start.9
  526.4 3.1 copy-start.8
  526.4 3.9 copy-start.7
Sparse Core Ops, SparseCore 0:
  9.7 84.0 all-gather.5
  95.4 39.3 all-gather.11
  136.4 63.3 all-gather.7
  201.9 59.1 all-gather.9
  263.2 63.5 reduce-scatter.2
  328.9 132.3 reduce-scatter.4
